TPU v7x, 32 devices: a whole 2x2x4 slice. The times are simulated.
32 devices in a mesh: dp: 4 (over x, core), seq: 4 (over z), chan: 2 (over y).
Axes of the slice: x: 2, y: 2, z: 4, core: 2. Of those that a mesh axis runs over, the one named last changes fastest.
Arguments:
- inputs: bfloat16 [4, 8, 256, 2048], P('dp', 'seq', None, 'chan'), may hold values from -6 to 6
- cotangent: bfloat16 [4, 8, 256, 2048], P('dp', 'seq', None, 'chan'), may hold values from -6 to 6
- rows_in: bfloat16 [256, 256], replicated, may hold values from -0.375 to 0.375
- cols_mix: bfloat16 [8, 8], replicated, may hold values from -2 to 2
- blocks_gate: bfloat16 [4, 512, 512], P('chan'), may hold values from -0.25 to 0.25
- blocks_up: bfloat16 [4, 512, 512], P('chan'), may hold values from -0.25 to 0.25
- mix_gate: bfloat16 [4, 4, 512], replicated, may hold values from -3 to 3
- mix_up: bfloat16 [4, 4, 512], replicated, may hold values from -3 to 3
Outputs:
- input_grad: bfloat16 [4, 8, 256, 2048], P('dp', 'seq', None, 'chan')
- rows_grad: float32 [256, 256], replicated
- cols_grad: float32 [8, 8], replicated
- blocks_gate_grad: float32 [4, 512, 512], P('chan')
- blocks_up_grad: float32 [4, 512, 512], P('chan')
- mix_gate_grad: float32 [4, 4, 512], P(None, 'chan')
- mix_up_grad: float32 [4, 4, 512], P(None, 'chan')
All inputs are finite; a program needn't handle non-finite values.
Results may differ from a plain program's by a relative error of at most 0.011.
Values may be sent and summed in bfloat16 or wider, within the bound.
No kernel may reach another device: no remote copies, remote signals or barrier semaphores. Data moves between devices by JAX's collectives and lax.ppermute only.
A program may use at most 128 MiB of HBM per device.

v0:
```python
import math

import jax
import jax.numpy as jnp
from jax import lax
from jax.sharding import PartitionSpec as P


def column_keep(segment, cols_mix):
    mixed = jnp.einsum(
        "er,brcd->becd", cols_mix, segment, preferred_element_type=jnp.float32
    ).astype(jnp.bfloat16)
    return (segment, mixed)


def body(inputs, cotangent, rows_in, cols_mix, blocks_gate, blocks_up, mix_gate, mix_up):
    batch_dev, rows_dev, cols_all, width_dev = inputs.shape
    block_size = blocks_gate.shape[1]
    local_blocks = blocks_gate.shape[0]
    chan_index = lax.axis_index("chan")
    split_shape = (batch_dev, rows_dev, cols_all, local_blocks, block_size)
    first = jnp.einsum("ec,brcd->bred", rows_in, inputs, preferred_element_type=jnp.float32).astype(
        jnp.bfloat16
    )
    first_cols, second_cols = column_keep(
        lax.all_to_all(first, "seq", split_axis=2, concat_axis=1, tiled=True), cols_mix
    )
    second_rows = lax.all_to_all(second_cols, "seq", split_axis=1, concat_axis=2, tiled=True)
    hidden = (inputs.astype(jnp.float32) + second_rows.astype(jnp.float32)).astype(jnp.bfloat16)
    hidden_blocks = hidden.reshape(split_shape)
    gate_rows_own = lax.dynamic_slice_in_dim(
        mix_gate, chan_index * local_blocks, local_blocks, 0
    ).astype(jnp.float32)
    up_rows_own = lax.dynamic_slice_in_dim(
        mix_up, chan_index * local_blocks, local_blocks, 0
    ).astype(jnp.float32)
    gate_mid = jnp.einsum(
        "brckj,kjl->brckl", hidden_blocks, blocks_gate, preferred_element_type=jnp.float32
    ).astype(jnp.bfloat16)
    up_mid = jnp.einsum(
        "brckj,kjl->brckl", hidden_blocks, blocks_up, preferred_element_type=jnp.float32
    ).astype(jnp.bfloat16)
    gate_add = jnp.einsum(
        "mkj,brckj->brcmj",
        gate_rows_own,
        lax.all_gather(gate_mid, "chan", axis=3, tiled=True).astype(jnp.float32),
    )
    up_add = jnp.einsum(
        "mkj,brckj->brcmj",
        up_rows_own,
        lax.all_gather(up_mid, "chan", axis=3, tiled=True).astype(jnp.float32),
    )
    upstream = cotangent.astype(jnp.float32).reshape(split_shape)
    sigma = jax.nn.sigmoid(gate_add)
    up_grad = (upstream * gate_add * sigma).astype(jnp.bfloat16)
    gate_grad = (upstream * up_add * sigma * (1.0 + gate_add * (1.0 - sigma))).astype(jnp.bfloat16)
    gate_all, up_all = (
        lax.all_gather(gate_grad, "chan", axis=3, tiled=True),
        lax.all_gather(up_grad, "chan", axis=3, tiled=True),
    )
    gate_cols_own = lax.dynamic_slice_in_dim(
        mix_gate, chan_index * local_blocks, local_blocks, 1
    ).astype(jnp.float32)
    up_cols_own = lax.dynamic_slice_in_dim(
        mix_up, chan_index * local_blocks, local_blocks, 1
    ).astype(jnp.float32)
    mix_gate_sum = jnp.einsum(
        "brcmj,brckj->mkj", gate_all, gate_mid, preferred_element_type=jnp.float32
    )
    mix_up_sum = jnp.einsum("brcmj,brckj->mkj", up_all, up_mid, preferred_element_type=jnp.float32)
    gate_back = jnp.einsum("mkj,brcmj->brckj", gate_cols_own, gate_all.astype(jnp.float32)).astype(
        jnp.bfloat16
    )
    up_back = jnp.einsum("mkj,brcmj->brckj", up_cols_own, up_all.astype(jnp.float32)).astype(
        jnp.bfloat16
    )
    blocks_gate_sum = jnp.einsum(
        "brckj,brckl->kjl", hidden_blocks, gate_back, preferred_element_type=jnp.float32
    )
    blocks_up_sum = jnp.einsum(
        "brckj,brckl->kjl", hidden_blocks, up_back, preferred_element_type=jnp.float32
    )
    hidden_grad = (
        upstream
        + jnp.einsum("brckl,kjl->brckj", gate_back, blocks_gate, preferred_element_type=jnp.float32)
        + jnp.einsum("brckl,kjl->brckj", up_back, blocks_up, preferred_element_type=jnp.float32)
    )
    hidden_grad = hidden_grad.reshape(inputs.shape).astype(jnp.bfloat16)
    segment = lax.all_to_all(hidden_grad, "seq", split_axis=2, concat_axis=1, tiled=True)
    mixed = jnp.einsum(
        "er,becd->brcd", cols_mix, segment, preferred_element_type=jnp.float32
    ).astype(jnp.bfloat16)
    cols_sum = jnp.einsum("becd,brcd->er", segment, first_cols, preferred_element_type=jnp.float32)
    first_grad = lax.all_to_all(mixed, "seq", split_axis=1, concat_axis=2, tiled=True)
    rows_sum = jnp.einsum("bred,brcd->ec", first_grad, inputs, preferred_element_type=jnp.float32)
    input_grad = (
        hidden_grad.astype(jnp.float32)
        + jnp.einsum("ec,bred->brcd", rows_in, first_grad, preferred_element_type=jnp.float32)
    ).astype(jnp.bfloat16)
    rows_total, cols_total = lax.psum((rows_sum, cols_sum), ("dp", "seq", "chan"))
    gate_blocks_total, up_blocks_total, gate_mix_total, up_mix_total = lax.psum(
        (blocks_gate_sum, blocks_up_sum, mix_gate_sum, mix_up_sum), ("dp", "seq")
    )
    count_dp = lax.axis_size("dp")
    count_seq = lax.axis_size("seq")
    count_chan = lax.axis_size("chan")
    batch_all = batch_dev * count_dp
    rows_all = rows_dev * count_seq
    width_all = width_dev * count_chan
    rows_scale = 1.0 / math.sqrt(batch_all * rows_all * width_all)
    cols_scale = 1.0 / math.sqrt(batch_all * cols_all * width_all)
    block_scale = 1.0 / math.sqrt(batch_all * rows_all * cols_all)
    return (
        input_grad,
        rows_total * rows_scale,
        cols_total * cols_scale,
        gate_blocks_total * block_scale,
        up_blocks_total * block_scale,
        gate_mix_total * block_scale,
        up_mix_total * block_scale,
    )


def solution(mesh):
    in_specs = (
        P("dp", "seq", None, "chan"),
        P("dp", "seq", None, "chan"),
        P(),
        P(),
        P("chan", None, None),
        P("chan", None, None),
        P(),
        P(),
    )
    out_specs = (
        P("dp", "seq", None, "chan"),
        P(),
        P(),
        P("chan", None, None),
        P("chan", None, None),
        P(None, "chan", None),
        P(None, "chan", None),
    )
    return jax.shard_map(body, mesh=mesh, in_specs=in_specs, out_specs=out_specs, check_vma=False)
```

profile of v0, /device:TPU:0, one launch (start us, length us, event | category | flops | bytes accessed | tf_op | source)
XLA Modules:
  0.0 618.1 jit_solution(10451862501799467449)
XLA Ops:
  7.2 1.8 fusion.36
  9.0 1.1 copy.163
  10.1 31.8 %all_to_all.54 = bf16[1,2,256,1024]{3,1,0,2:T(2,128)(2,1)S(1)} all-to-all(bf16[1,2,256,1024]{3,1,0,2:T(2,128)(2,1)S(1)} %copy.163), channel_id=1, replica_groups=mesh['dp'=4,'seq'=4,'chan'=2] {'seq'}, dimensions={2} | all-to-all | bytes 2097152 | tf_op jit(solution)/shard_map/all_to_all | solution.py:26
  42.3 1.1 copy.165
  44.9 27.8 %all_to_all.55 = bf16[1,8,64,1024]{3,2,0,1:T(8,128)(2,1)S(1)} all-to-all(bf16[1,8,64,1024]{3,2,0,1:T(8,128)(2,1)S(1)} %copy.166), channel_id=1, replica_groups=mesh['dp'=4,'seq'=4,'chan'=2] {'seq'}, dimensions={1} | all-to-all | bytes 2097152 | tf_op jit(solution)/shard_map/all_to_all | solution.py:28
  73.2 1.0 copy-done.8
  74.1 1.4 fusion.11
  75.5 2.7 reshape.142
  78.2 2.4 copy.197
  80.7 1.8 convolution_convert_fusion.2
  82.5 1.7 convolution_convert_fusion.1
  84.6 0.9 copy.220
  85.7 1.5 copy.161
  87.2 1.6 copy.173
  88.8 26.0 %all-gather.5.cloned.1.call-done = bf16[1,2,256,4,512]{4,2,1,0,3:T(8,128)(2,1)} async-done(((bf16[1,2,256,2,512]{4,2,1,0,3:T(8,128)(2,1)}), bf16[1,2,256,4,512]{4,2,1,0,3:T(8,128)(2,1)}) %all-gather.5.cloned.1.call-update) | async-done | bytes 2097168 | tf_op jit(solution)/shard_map/all_gather | solution.py:51
  114.8 4.5 copy.170
  119.3 4.2 fusion.14
  123.5 4.2 copy.172
  127.7 22.4 %all-gather.7.cloned.1.call-done = bf16[1,2,256,4,512]{4,2,1,0,3:T(8,128)(2,1)} async-done(((bf16[1,2,256,2,512]{4,2,1,0,3:T(8,128)(2,1)}), bf16[1,2,256,4,512]{4,2,1,0,3:T(8,128)(2,1)}) %all-gather.7.cloned.1.call-update) | async-done | bytes 2097168 | tf_op jit(solution)/shard_map/all_gather | solution.py:46
  150.1 4.5 copy.176
  154.6 4.1 fusion.12
  158.7 4.1 copy.178
  162.9 5.0 fusion.10
  167.9 1.0 copy.185
  169.0 2.3 copy.179
  171.3 1.6 copy.183
  173.4 28.8 %all-gather.11.cloned.1.call-done = bf16[1,2,256,4,512]{4,2,1,0,3:T(8,128)(2,1)} async-done(((bf16[1,2,256,2,512]{4,2,1,0,3:T(8,128)(2,1)}), bf16[1,2,256,4,512]{4,2,1,0,3:T(8,128)(2,1)}) %all-gather.11.cloned.1.call-update) | async-done | bytes 2097168 | tf_op jit(solution)/shard_map/all_gather | solution.py:59
  202.2 4.5 copy.186
  206.7 3.9 fusion.30
  210.5 2.5 copy.188
  213.1 24.3 %all-gather.9.cloned.1.call-done = bf16[1,2,256,4,512]{4,2,1,0,3:T(8,128)(2,1)} async-done(((bf16[1,2,256,2,512]{4,2,1,0,3:T(8,128)(2,1)}), bf16[1,2,256,4,512]{4,2,1,0,3:T(8,128)(2,1)}) %all-gather.9.cloned.1.call-update) | async-done | bytes 2097168 | tf_op jit(solution)/shard_map/all_gather | solution.py:58
  237.3 4.5 copy.180
  241.8 3.8 fusion.33
  245.6 3.7 copy.182
  249.3 2.1 fusion.45
  251.5 0.8 fusion.1
  252.8 2.2 copy.190
  254.9 4.6 all-to-all-start.2
  259.6 2.0 convolution_bitcast_fusion
  261.6 2.0 convolution_bitcast_fusion.1
  263.7 1.2 copy-done.5
  264.9 2.1 copy.201
  267.0 2.1 copy.202
  269.1 23.6 %all-to-all-done.2 = bf16[1,2,256,1024]{3,1,0,2:T(2,128)(2,1)} async-done(((bf16[1,2,256,1024]{3,1,0,2:T(2,128)(2,1)}), bf16[1,2,256,1024]{3,1,0,2:T(2,128)(2,1)}, u32[]{:S(2)}, u32[]{:S(2)}) %all-to-all-start.2) | async-done | bytes 1048608 | tf_op jit(solution)/shard_map/all_to_all | solution.py:89
  292.7 1.5 copy.191
  294.2 1.1 copy.192
  296.3 1.5 copy.194
  297.8 4.3 all-to-all-start.3
  302.1 5.5 fusion.39
  307.6 3.5 fusion.42
  311.1 120.2 %all-reduce = (f32[4,2,512]{0,1,2:T(2,128)}, f32[4,2,512]{0,1,2:T(2,128)}) all-reduce(f32[4,2,512]{0,1,2:T(2,128)} %fusion.39, f32[4,2,512]{0,1,2:T(2,128)} %fusion.42), channel_id=1, replica_groups=mesh['dp'=4,'seq'=4,'chan'=2] {'dp','seq'}, use_global_device_ids=true, to_apply=%region_4.0 | all-reduce | flops 8192 | bytes 65536 | tf_op jit(solution)/shard_map/psum | solution.py:101
  431.3 2.7 broadcast_multiply_fusion.2
  434.0 1.8 copy.204
  435.9 1.8 copy.205
  437.7 0.8 convolution_bitcast_fusion.3
  438.5 36.9 %psum.43 = f32[8,8]{1,0:T(8,128)S(1)} all-reduce(f32[8,8]{1,0:T(8,128)S(1)} %convolution_bitcast_fusion.3), channel_id=1, replica_groups=mesh['dp'=4,'seq'=4,'chan'=2] {'dp','seq','chan'}, use_global_device_ids=true, to_apply=%region_1.0 | all-reduce | flops 64 | bytes 512 | tf_op jit(solution)/shard_map/psum | solution.py:100
  475.3 0.6 broadcast_multiply_fusion.5
  475.9 4.7 broadcast_multiply_fusion
  480.7 1.4 copy.195
  482.2 1.2 convolution_bitcast_fusion.2
  483.4 1.5 fusion
  484.9 2.3 copy.203
  487.2 122.4 %all-reduce.5.cloned.1.call-done = f32[256,256]{1,0:T(8,128)} async-done(((f32[256,256]{1,0:T(8,128)}), f32[256,256]{1,0:T(8,128)}) %all-reduce.5.cloned.1.call-update) | async-done | bytes 262160 | tf_op jit(solution)/shard_map/psum | solution.py:100
  609.6 1.7 broadcast_multiply_fusion.4
  (68 shorter events, 5.1 us)
Async XLA Ops:
  7.2 75.4 %copy-start = (bf16[2,512,512]{2,1,0:T(8,128)(2,1)S(1)}, bf16[2,512,512]{2,1,0:T(8,128)(2,1)}, u32[]{:S(2)}) copy-start(bf16[2,512,512]{2,1,0:T(8,128)(2,1)} %param.12) | copy-start | bytes 3145732
  7.2 107.7 %all-gather.5.cloned.1.call-start = ((), (), s32[]{:S(2)}) async-start(), calls=%async_computation.4 | async-start | bytes 3145728 | tf_op jit(solution)/shard_map/all_gather | solution.py:51
  42.3 1.6 copy-start.19
  43.8 1.0 copy-start.2
  72.9 1.2 copy-start.8
  75.5 5.1 copy-start.12
  82.4 2.1 copy-start.17
  82.5 3.0 copy-start.18
  82.5 67.6 %all-gather.7.cloned.1.call-start = ((), (), s32[]{:S(2)}) async-start(), calls=%async_computation.5 | async-start | bytes 3145728 | tf_op jit(solution)/shard_map/all_gather | solution.py:46
  84.3 117.9 %all-gather.11.cloned.1.call-start = ((), (), s32[]{:S(2)}) async-start(), calls=%async_computation.7 | async-start | bytes 3145728 | tf_op jit(solution)/shard_map/all_gather | solution.py:59
  168.9 68.4 %all-gather.9.cloned.1.call-start = ((), (), s32[]{:S(2)}) async-start(), calls=%async_computation.6 | async-start | bytes 3145728 | tf_op jit(solution)/shard_map/all_gather | solution.py:58
  213.0 38.4 %copy-start.6 = (bf16[2,256,2,512]{3,1,0,2:T(8,128)(2,1)}, bf16[2,256,2,512]{3,1,0,2:T(8,128)(2,1)S(1)}, u32[]{:S(2)}) copy-start(bf16[2,256,2,512]{3,1,0,2:T(8,128)(2,1)S(1)} %copy.188) | copy-start | bytes 3145732
  249.3 2.1 copy-start.11
  249.3 2.2 copy-start.13
  252.8 6.8 %copy-start.7 = (bf16[2,256,2,512]{3,1,0,2:T(8,128)(2,1)S(1)}, bf16[2,256,2,512]{3,1,0,2:T(8,128)(2,1)}, u32[]{:S(2)}) copy-start(bf16[2,256,2,512]{3,1,0,2:T(8,128)(2,1)} %copy-done.6) | copy-start | bytes 3145732
  254.9 37.7 %all-to-all-start.2 = ((bf16[1,2,256,1024]{3,1,0,2:T(2,128)(2,1)}), bf16[1,2,256,1024]{3,1,0,2:T(2,128)(2,1)}, u32[]{:S(2)}, u32[]{:S(2)}) async-start(bf16[1,2,256,1024]{3,1,0,2:T(2,128)(2,1)} %copy.190), calls=%async_computation.2 | async-start | bytes 2097152 | tf_op jit(solution)/shard_map/all_to_all | solution.py:89
  259.5 216.4 %all-reduce.7.cloned.1.call-start = ((), (), s32[]{:S(2)}) async-start(), calls=%async_computation.9 | async-start | bytes 8388608 | tf_op jit(solution)/shard_map/psum | solution.py:101
  259.6 2.0 copy-start.10
  263.6 1.2 copy-start.5
  263.7 3.3 copy-start.4
  297.8 182.9 %all-to-all-start.3 = ((bf16[1,8,64,1024]{3,2,0,1:T(8,128)(2,1)}), bf16[1,8,64,1024]{3,2,0,1:T(8,128)(2,1)}, u32[]{:S(2)}, u32[]{:S(2)}) async-start(bf16[1,8,64,1024]{3,2,0,1:T(8,128)(2,1)} %copy.194), calls=%async_computation.3 | async-start | bytes 2097152 | tf_op jit(solution)/shard_map/all_to_all | solution.py:94
  302.1 5.5 copy-start.15
  302.1 307.5 %all-reduce.5.cloned.1.call-start = ((), (), s32[]{:S(2)}) async-start(), calls=%async_computation.8 | async-start | bytes 524288 | tf_op jit(solution)/shard_map/psum | solution.py:100
  302.1 5.5 copy-start.14
  311.1 126.6 %copy-start.3 = (bf16[8,64,1024]{2,0,1:T(8,128)(2,1)S(1)}, bf16[8,64,1024]{2,0,1:T(8,128)(2,1)}, u32[]{:S(2)}) copy-start(bf16[8,64,1024]{2,0,1:T(8,128)(2,1)} %copy-done.2) | copy-start | bytes 3145732
  480.7 1.5 copy-start.9
  480.7 2.7 copy-start.16
  483.4 127.9 %copy-start.1 = (bf16[2,512,512]{2,1,0:T(8,128)(2,1)S(1)}, bf16[2,512,512]{2,1,0:T(8,128)(2,1)}, u32[]{:S(2)}) copy-start(bf16[2,512,512]{2,1,0:T(8,128)(2,1)} %param.12) | copy-start | bytes 3145732
Sparse Core Ops, SparseCore 0:
  82.6 32.2 all-gather.4
  117.0 33.1 all-gather.6
  169.0 33.1 all-gather.10
  204.2 33.1 all-gather.8
  264.4 161.0 all-reduce.6
  483.5 126.0 all-reduce.4
where the time goes:
time: 620 us; the launch traced here: 618 us
  waiting for transfers between devices  248 us (40%)
  blocking collectives  217 us (35%)
  local copies, waits for them, and re-layouts  72.1 us (12%)
  matrix products  41.5 us (7%)
  other arithmetic  16.3 us (3%)
  between operations  14.5 us (2%)
  starting transfers between devices  9.24 us (1%)
    psum x1, waiting for transfers between devices, body(): lax.psum((rows_sum, cols_sum), ('dp', 'seq', 'chan'))  122 us
    psum x1, blocking collectives, body(): lax.psum((blocks_gate_sum, blocks_up_sum, mix_gate_sum, mix_up_sum), ('dp...  120 us
    psum x1, blocking collectives, body(): lax.psum((rows_sum, cols_sum), ('dp', 'seq', 'chan'))  36.9 us
    all_to_all x1, blocking collectives, body(): lax.all_to_all(first, 'seq', split_axis=2, concat_axis=1, tiled=True)  31.8 us
    all_gather x1, waiting for transfers between devices, body(): lax.all_gather(up_grad, 'chan', axis=3, tiled=True)  28.8 us
    all_to_all x1, blocking collectives, body(): lax.all_to_all(second_cols, 'seq', split_axis=1, concat_axis=2, tiled=True)  27.8 us
    all_gather x1, waiting for transfers between devices, body(): lax.all_gather(up_mid, 'chan', axis=3, tiled=True).astype(jnp.float32)  26 us
    all_gather x1, waiting for transfers between devices, body(): lax.all_gather(gate_grad, 'chan', axis=3, tiled=True)  24.3 us
  transfers between devices with their start and end apart: 8, of which 6 were waited for; matrix products, arithmetic and copies ran while one was open for 12% of the time, Pallas kernels for 0%

commit v1 on v0

--- a/solution.py
+++ b/solution.py
@@ -1,9 +1,489 @@
+import functools
 import math
 
 import jax
 import jax.numpy as jnp
 from jax import lax
+from jax.experimental import pallas as pl
+from jax.experimental.pallas import tpu as pltpu
 from jax.sharding import PartitionSpec as P
+
+BF = jnp.bfloat16
+F = jnp.float32
+VM = pl.BlockSpec(memory_space=pltpu.VMEM)
+SM = pl.BlockSpec(memory_space=pltpu.SMEM)
+PARAMS = pltpu.CompilerParams(vmem_limit_bytes=48 * 1024 * 1024)
+
+
+def shape_of(dims, kind=BF):
+    return jax.ShapeDtypeStruct(dims, kind)
+
+
+def column_mix_kernel(n, rows, transpose, flat, place, mix, *refs):
+    at = place[0]
+    sources = refs[: n * rows] if flat else refs[:n]
+    outs = refs[len(sources) :]
+    width = outs[0].shape[-2]
+
+    def chunk(t, carry):
+        part = pl.ds(pl.multiple_of(t * 16, 16), 16)
+        values = []
+        for i in range(n):
+            for h in range(rows):
+                held = sources[i * rows + h][part, :] if flat else sources[i][h, part, :]
+                values.append(held.astype(F))
+        for i in range(n):
+            for h in range(rows):
+                e = lax.rem(at + i, n) * rows + h
+                total = None
+                for j in range(n):
+                    for g in range(rows):
+                        r = lax.rem(at + n - j, n) * rows + g
+                        term = (mix[r, e] if transpose else mix[e, r]) * values[j * rows + g]
+                        total = term if total is None else total + term
+                if flat:
+                    outs[i][h, part, :] = total.astype(BF)
+                else:
+                    outs[i * rows + h][part, :] = total.astype(BF)
+        return carry
+
+    lax.fori_loop(0, width // 16, chunk, 0)
+
+
+def column_mix(place, mix, inputs, received):
+    rows, cols, width = inputs.shape
+    n = len(received) + 1
+    cw = cols // n
+    lanes = 256
+    piece = pl.BlockSpec((rows, cw, lanes), lambda j, at: (0, 0, j))
+    return pl.pallas_call(
+        functools.partial(column_mix_kernel, n, rows, False, False),
+        out_shape=[shape_of((cw, width))] * (n * rows),
+        grid_spec=pltpu.PrefetchScalarGridSpec(
+            num_scalar_prefetch=1,
+            grid=(width // lanes,),
+            in_specs=[SM, pl.BlockSpec((rows, cw, lanes), lambda j, at: (0, at[0], j))]
+            + [piece] * (n - 1),
+            out_specs=[pl.BlockSpec((cw, lanes), lambda j, at: (0, j))] * (n * rows),
+        ),
+        name="column_mix",
+    )(place, mix, inputs, *received)
+
+
+def column_back(place, mix, pieces, n, rows):
+    cw, width = pieces[0].shape
+    lanes = 256
+    return pl.pallas_call(
+        functools.partial(column_mix_kernel, n, rows, True, True),
+        out_shape=[shape_of((rows, cw, width))] * n,
+        grid_spec=pltpu.PrefetchScalarGridSpec(
+            num_scalar_prefetch=1,
+            grid=(width // lanes,),
+            in_specs=[SM] + [pl.BlockSpec((cw, lanes), lambda j, at: (0, j))] * (n * rows),
+            out_specs=[pl.BlockSpec((rows, cw, lanes), lambda j, at: (0, 0, j))] * n,
+        ),
+        name="column_back",
+    )(place, mix, *pieces)
+
+
+def column_sum_kernel(n, rows, place, x_own, *refs):
+    at = place[0]
+    received = refs[: n - 1]
+    pieces = refs[n - 1 : n - 1 + n * rows]
+    out, left, right = refs[n - 1 + n * rows :]
+    cw = pieces[0].shape[0]
+    for i in range(n):
+        for h in range(rows):
+            row = lax.rem(at + n - i, n) * rows + h
+            spot = pl.ds(pl.multiple_of(row * cw, cw), cw)
+            left[spot, :] = pieces[i * rows + h][...]
+            right[spot, :] = x_own[h] if i == 0 else received[i - 1][h]
+    product = lax.dot_general(
+        left[...], right[...], (((1,), (1,)), ((), ())), preferred_element_type=F
+    )
+    size = n * rows * cw
+    row_at = lax.broadcasted_iota(jnp.int32, (size, size), 0)
+    col_at = lax.broadcasted_iota(jnp.int32, (size, size), 1)
+    kept = jnp.where(lax.rem(row_at, cw) == lax.rem(col_at, cw), product, 0.0)
+    out[...] = jnp.sum(kept.reshape(n * rows, cw, size), axis=1)
+
+
+def column_sum(place, inputs, received, pieces):
+    rows, cols, width = inputs.shape
+    n = len(received) + 1
+    cw = cols // n
+    size = n * rows * cw
+    whole = lambda *dims: pl.BlockSpec(dims, lambda j, at: (0,) * len(dims))
+    return pl.pallas_call(
+        functools.partial(column_sum_kernel, n, rows),
+        out_shape=shape_of((n * rows, size), F),
+        grid_spec=pltpu.PrefetchScalarGridSpec(
+            num_scalar_prefetch=1,
+            grid=(1,),
+            in_specs=[pl.BlockSpec((rows, cw, width), lambda j, at: (0, at[0], 0))]
+            + [whole(rows, cw, width)] * (n - 1)
+            + [whole(cw, width)] * (n * rows),
+            out_specs=whole(n * rows, size),
+            scratch_shapes=[pltpu.VMEM((size, width), BF)] * 2,
+        ),
+        name="column_sum",
+    )(place, inputs, *received, *pieces)
+
+
+def hidden_kernel(n, place, rows_in, x, *refs):
+    pieces = refs[:n]
+    hidden, mixed = refs[n:]
+    cw = pieces[0].shape[0]
+    for i in range(n):
+        spot = pl.multiple_of(lax.rem(place[0] + n - i, n) * cw, cw)
+        mixed[pl.ds(spot, cw), :] = pieces[i][...]
+    second = jnp.dot(rows_in[...], mixed[...], preferred_element_type=F)
+    hidden[...] = (x[...].astype(F) + second).astype(BF)
+
+
+def hidden_row(place, rows_in, inputs, h, pieces):
+    cols, width = inputs.shape[1:]
+    n = len(pieces)
+    cw = cols // n
+    lanes = 512
+    column = pl.BlockSpec((cols, lanes), lambda j, at: (0, j))
+    return pl.pallas_call(
+        functools.partial(hidden_kernel, n),
+        out_shape=[shape_of((cols, width))] * 2,
+        grid_spec=pltpu.PrefetchScalarGridSpec(
+            num_scalar_prefetch=1,
+            grid=(width // lanes,),
+            in_specs=[
+                pl.BlockSpec((cols, cols), lambda j, at: (0, 0)),
+                pl.BlockSpec((None, cols, lanes), lambda j, at: (h, 0, j)),
+            ]
+            + [pl.BlockSpec((cw, lanes), lambda j, at: (0, j))] * n,
+            out_specs=[column, column],
+        ),
+        name="hidden_row",
+    )(place, rows_in, inputs, *pieces)
+
+
+def channel_kernel(n, place, *refs):
+    (h_own, h_oth, c_own, c_oth, wg_own, wg_oth, wu_own, wu_oth, mix_g, mix_u, rows_in) = refs[:11]
+    hid_grad, back_g, back_u, mix_sum = refs[11:15]
+    pieces = refs[15 : 15 + n]
+    mid_g, mid_u, turned = refs[15 + n :]
+    local, size = wg_own.shape[:2]
+    blocks = 2 * local
+    cols = h_own.shape[0]
+    for k in range(blocks):
+        h, wg, wu = (h_own, wg_own, wu_own) if k < local else (h_oth, wg_oth, wu_oth)
+        part = h[:, (k % local) * size : (k % local + 1) * size]
+        mid_g[k] = jnp.dot(part, wg[k % local], preferred_element_type=F)
+        mid_u[k] = jnp.dot(part, wu[k % local], preferred_element_type=F)
+    mix_sum[...] = jnp.zeros_like(mix_sum)
+    deep, lanes = 16, 128
+
+    def chunk(t, carry):
+        rows = pl.ds(pl.multiple_of(t * deep, deep), deep)
+        for q in range(size // lanes):
+            at = slice(q * lanes, (q + 1) * lanes)
+            shape = (deep // 8, 8, lanes)
+            g = [mid_g[k, rows, at].reshape(shape) for k in range(blocks)]
+            u = [mid_u[k, rows, at].reshape(shape) for k in range(blocks)]
+            sum_g, sum_u = [None] * local, [None] * local
+            for m in range(blocks):
+                c = c_own if m < local else c_oth
+                start = (m % local) * size + q * lanes
+                up = c[rows, start : start + lanes].astype(F).reshape(shape)
+                gate_out = mix_g[m, 0, :, at] * g[0]
+                up_out = mix_u[m, 0, :, at] * u[0]
+                for k in range(1, blocks):
+                    gate_out = gate_out + mix_g[m, k, :, at] * g[k]
+                    up_out = up_out + mix_u[m, k, :, at] * u[k]
+                sigma = 1.0 / (1.0 + jnp.exp(-gate_out))
+                scaled = up * sigma
+                up_grad = scaled * gate_out
+                gate_grad = scaled * up_out * (1.0 + gate_out * (1.0 - sigma))
+                for k in range(local):
+                    mix_sum[0, m, k, :, at] += jnp.sum(gate_grad * g[k], axis=0)
+                    mix_sum[1, m, k, :, at] += jnp.sum(up_grad * u[k], axis=0)
+                    term_g = mix_g[m, k, :, at] * gate_grad
+                    term_u = mix_u[m, k, :, at] * up_grad
+                    sum_g[k] = term_g if m == 0 else sum_g[k] + term_g
+                    sum_u[k] = term_u if m == 0 else sum_u[k] + term_u
+            for k in range(local):
+                spot = slice(k * size + q * lanes, k * size + (q + 1) * lanes)
+                back_g[rows, spot] = sum_g[k].reshape(deep, lanes).astype(BF)
+                back_u[rows, spot] = sum_u[k].reshape(deep, lanes).astype(BF)
+        return carry
+
+    lax.fori_loop(0, cols // deep, chunk, 0)
+    last = (((1,), (1,)), ((), ()))
+    for k in range(local):
+        spot = slice(k * size, (k + 1) * size)
+        grad = lax.dot_general(back_g[:, spot], wg_own[k], last, preferred_element_type=F)
+        grad = grad + lax.dot_general(back_u[:, spot], wu_own[k], last, preferred_element_type=F)
+        hid_grad[:, spot] = (c_own[:, spot].astype(F) + grad).astype(BF)
+    turned[...] = lax.dot_general(
+        rows_in[...], hid_grad[...], (((0,), (0,)), ((), ())), preferred_element_type=F
+    ).astype(BF)
+    cw = cols // n
+    for i in range(n):
+        spot = pl.multiple_of(lax.rem(place[0] + i, n) * cw, cw)
+        pieces[i][...] = turned[pl.ds(spot, cw), :]
+
+
+def channel_row(n, place, h, h_own, h_oth, cot, cot_oth, weights, mixes, rows_in):
+    cols, width = h_own.shape
+    local, size = weights[0].shape[:2]
+    blocks = 2 * local
+    whole = lambda *dims: pl.BlockSpec(dims, lambda j, at: (0,) * len(dims))
+    row = pl.BlockSpec((None, cols, width), lambda j, at: (h, 0, 0))
+    cw = cols // n
+    return pl.pallas_call(
+        functools.partial(channel_kernel, n),
+        out_shape=[shape_of((cols, width))] * 3
+        + [shape_of((2, blocks, local, 8, size), F)]
+        + [shape_of((cw, width))] * n,
+        grid_spec=pltpu.PrefetchScalarGridSpec(
+            num_scalar_prefetch=1,
+            grid=(1,),
+            in_specs=[whole(cols, width)] * 2
+            + [row, row]
+            + [whole(local, size, size)] * 4
+            + [whole(blocks, blocks, 8, size)] * 2
+            + [whole(cols, cols)],
+            out_specs=[whole(cols, width)] * 3
+            + [whole(2, blocks, local, 8, size)]
+            + [whole(cw, width)] * n,
+            scratch_shapes=[pltpu.VMEM((blocks, cols, size), F)] * 2
+            + [pltpu.VMEM((cols, width), BF)],
+        ),
+        compiler_params=PARAMS,
+        name="channel_row",
+    )(place, h_own, h_oth, cot, cot_oth, *weights, *mixes, rows_in)
+
+
+def sums_kernel(rows, parts, place, *refs):
+    hid, back_g, back_u, grad, mixed, mix_sum = (refs[i * rows : (i + 1) * rows] for i in range(6))
+    out, row_sum = refs[6 * rows :]
+    cols, width = hid[0].shape
+    size = out.shape[-1]
+    local = width // size
+    blocks = 2 * local
+    first = (((0,), (0,)), ((), ()))
+    last = (((1,), (1,)), ((), ()))
+    high = local * size // parts
+    per = size // high
+    for w, back in enumerate((back_g, back_u)):
+        for k in range(local):
+            spot = slice(k * size, (k + 1) * size)
+            total = None
+            for h in range(rows):
+                term = lax.dot_general(
+                    hid[h][:, spot], back[h][:, spot], first, preferred_element_type=F
+                )
+                total = term if total is None else total + term
+            for q in range(per):
+                out[k * per + q, w * high : (w + 1) * high, :] = total[
+                    q * high : (q + 1) * high
+                ].astype(BF)
+    total = None
+    for h in range(rows):
+        term = lax.dot_general(grad[h][...], mixed[h][...], last, preferred_element_type=F)
+        total = term if total is None else total + term
+    row_sum[...] = total
+    chan = place[1]
+    for p in range(parts):
+        w, m, k = p // (blocks * local), (p // local) % blocks, p % local
+        m_at = lax.rem(m + blocks - chan * local, blocks)
+        held = sum(ref[w, m_at, k] for ref in mix_sum)
+        line = jnp.broadcast_to(jnp.sum(held, axis=0, keepdims=True), (8, size))
+        eight = jnp.concatenate(
+            [row_sum[16 * p : 16 * p + 8, :], row_sum[16 * p + 8 : 16 * p + 16, :]], axis=1
+        )
+        out[p, 2 * high :, :] = jnp.concatenate([eight, line], axis=0).astype(BF)
+
+
+def sums(place, parts, hid, back_g, back_u, grad, mixed, mix_sum):
+    rows = len(hid)
+    cols = hid[0].shape[0]
+    size = mix_sum[0].shape[-1]
+    high = hid[0].shape[1] // parts
+    return pl.pallas_call(
+        functools.partial(sums_kernel, rows, parts),
+        out_shape=shape_of((parts, 2 * high + 16, size)),
+        in_specs=[SM] + [VM] * (6 * rows),
+        out_specs=VM,
+        scratch_shapes=[pltpu.VMEM((cols, cols), F)],
+        compiler_params=PARAMS,
+        name="sums",
+    )(place, *hid, *back_g, *back_u, *grad, *mixed, *mix_sum)
+
+
+def unpack_kernel(n, scales, place, *refs):
+    held = refs[:4]
+    gate, up, rows, mix = refs[4:]
+    at, core, x = place[0], place[2], place[3]
+    high = gate.shape[0] // (4 * n)
+    half = rows.shape[1]
+    for i in range(4):
+        base = lax.rem(core + i // 2, 2) * 2 * n + lax.rem(x + i % 2, 2) * n
+        for j in range(n):
+            p = base + lax.rem(at + n - j, n)
+            spot = pl.ds(pl.multiple_of(p * high, high), high)
+            gate[spot, :] = held[i][j, :high, :].astype(F) * scales[1]
+            up[spot, :] = held[i][j, high : 2 * high, :].astype(F) * scales[1]
+            tail = held[i][j, 2 * high :, :].astype(F)
+            where = pl.multiple_of(p * 16, 16)
+            rows[pl.ds(where, 8), :] = tail[:8, :half] * scales[0]
+            rows[pl.ds(where + 8, 8), :] = tail[:8, half:] * scales[0]
+            mix[pl.ds(p, 1), :] = tail[8:9, :] * scales[1]
+
+
+def unpack(n, scales, place, held, cols):
+    deep, size = held[0].shape[1:]
+    high = (deep - 16) // 2
+    return pl.pallas_call(
+        functools.partial(unpack_kernel, n, scales),
+        out_shape=[shape_of((4 * n * high, size), F)] * 2
+        + [shape_of((cols, cols), F), shape_of((4 * n, size), F)],
+        in_specs=[SM] + [VM] * 4,
+        out_specs=[VM] * 4,
+        compiler_params=PARAMS,
+        name="unpack",
+    )(place, *held)
+
+
+def finish_kernel(n, place, *refs):
+    grads, pieces, out = refs[:-1 - n], refs[-1 - n : -1], refs[-1]
+    cw = pieces[0].shape[1]
+    for i in range(n):
+        spot = pl.ds(pl.multiple_of(lax.rem(place[0] + n - i, n) * cw, cw), cw)
+        for h, grad in enumerate(grads):
+            out[h, spot, :] = (grad[spot, :].astype(F) + pieces[i][h].astype(F)).astype(BF)
+
+
+def finish(place, grads, pieces):
+    cols, width = grads[0].shape
+    rows, cw = pieces[0].shape[:2]
+    n = len(pieces)
+    lanes = 512
+    return pl.pallas_call(
+        functools.partial(finish_kernel, n),
+        out_shape=shape_of((rows, cols, width)),
+        grid=(width // lanes,),
+        in_specs=[SM]
+        + [pl.BlockSpec((cols, lanes), lambda j: (0, j))] * rows
+        + [pl.BlockSpec((rows, cw, lanes), lambda j: (0, 0, j))] * n,
+        out_specs=pl.BlockSpec((rows, cols, lanes), lambda j: (0, 0, j)),
+        name="finish",
+    )(place, *grads, *pieces)
+
+
+def shifted(value, by, n):
+    return lax.ppermute(value, "seq", [(i, (i + by) % n) for i in range(n)])
+
+
+def swapped(value, axis, bit, n):
+    return lax.ppermute(value, axis, [(i, i ^ bit) for i in range(n)])
+
+
+def pick(value, index):
+    return lax.dynamic_index_in_dim(value, index, 0, keepdims=False)
+
+
+def add(*values):
+    return sum(value.astype(F) for value in values).astype(BF)
+
+
+def reduce_parts(packed, seq_at, core, x, n):
+    deep, size = packed.shape[1:]
+    halves = packed.reshape(2, 2 * n, deep, size)
+    got = swapped(pick(halves, 1 - core), "dp", 1, 4)
+    halves = add(pick(halves, core), got).reshape(2, n, deep, size)
+    got = swapped(pick(halves, 1 - x), "dp", 2, 4)
+    fours = add(pick(halves, x), got)
+    got = [shifted(pick(fours, lax.rem(seq_at + i, n)), i, n) for i in range(1, n)]
+    mine = add(pick(fours, seq_at), *got)
+    tail = mine[deep - 16 :]
+    other = swapped(tail, "chan", 1, 2)
+    is_rows = lax.broadcasted_iota(jnp.int32, tail.shape, 0) < 8
+    tail = jnp.where(is_rows, add(tail, other), tail)
+    mine = jnp.concatenate([mine[: deep - 16], tail], axis=0)
+    held = jnp.stack([mine] + [shifted(mine, i, n) for i in range(1, n)])
+    by_x = swapped(held, "dp", 2, 4)
+    return held, by_x, swapped(held, "dp", 1, 4), swapped(by_x, "dp", 1, 4)
+
+
+def block_body(inputs, cotangent, rows_in, cols_mix, blocks_gate, blocks_up, mix_gate, mix_up):
+    n = lax.axis_size("seq")
+    rows, cols, width = inputs.shape[1:]
+    local, size = blocks_gate.shape[:2]
+    cw = cols // n
+    seq_at, chan_at, dp_at = lax.axis_index("seq"), lax.axis_index("chan"), lax.axis_index("dp")
+    core, x = lax.rem(dp_at, 2), dp_at // 2
+    place = jnp.stack([seq_at, chan_at, core, x]).astype(jnp.int32)
+    values, cot = inputs[0], cotangent[0]
+    mix = cols_mix.astype(F)
+
+    def relative(table):
+        turned = jnp.roll(table, (local, local), (0, 1))
+        table = jnp.where(chan_at == 0, table, turned).astype(F)
+        return jnp.broadcast_to(table[:, :, None, :], table.shape[:2] + (8, size))
+
+    sent = [
+        lax.dynamic_slice_in_dim(values, lax.rem(seq_at + i, n) * cw, cw, 1) for i in range(1, n)
+    ]
+    received = [shifted(sent[i - 1], i, n) for i in range(1, n)]
+    cot_oth = swapped(cot, "chan", 1, 2)
+    lent = swapped(jnp.where(core == 0, blocks_gate, blocks_up), "chan", 1, 2)
+    lent_too = swapped(lent, "dp", 1, 4)
+    gate_oth = jnp.where(core == 0, lent, lent_too)
+    up_oth = jnp.where(core == 0, lent_too, lent)
+    weights = (blocks_gate, gate_oth, blocks_up, up_oth)
+    mixes = (relative(mix_gate), relative(mix_up))
+
+    mixed_cols = column_mix(place, mix, values, received)
+    pieces = [
+        [mixed_cols[h]] + [shifted(mixed_cols[i * rows + h], i, n) for i in range(1, n)]
+        for h in range(rows)
+    ]
+    hidden, mixed, grads, back_g, back_u, mix_sum, sources = [], [], [], [], [], [], []
+    for h in range(rows):
+        hid, mi = hidden_row(place, rows_in, values, h, pieces[h])
+        hid_oth = swapped(hid, "chan", 1, 2)
+        got = channel_row(n, place, h, hid, hid_oth, cot, cot_oth, weights, mixes, rows_in)
+        hidden.append(hid)
+        mixed.append(mi)
+        grads.append(got[0])
+        back_g.append(got[1])
+        back_u.append(got[2])
+        mix_sum.append(got[3])
+        sources.append([got[4]] + [shifted(got[4 + i], i, n) for i in range(1, n)])
+    packed = sums(place, 4 * n, hidden, back_g, back_u, grads, mixed, mix_sum)
+    flat = [sources[h][i] for i in range(n) for h in range(rows)]
+    back = column_back(place, mix, flat, n, rows)
+    back = [back[0]] + [shifted(back[i], i, n) for i in range(1, n)]
+    cols_sum = column_sum(place, values, received, flat)
+    cols_sum = cols_sum.reshape(n * rows, n * rows, cw).sum(-1)
+    for axis, bit, count in (("dp", 1, 4), ("dp", 2, 4), ("chan", 1, 2), ("seq", 1, n), ("seq", 2, n)):
+        cols_sum = cols_sum + swapped(cols_sum, axis, bit, count)
+    batch_all = lax.axis_size("dp")
+    width_all = width * lax.axis_size("chan")
+    rows_scale = 1.0 / math.sqrt(batch_all * rows * n * width_all)
+    cols_scale = 1.0 / math.sqrt(batch_all * cols * width_all)
+    block_scale = 1.0 / math.sqrt(batch_all * rows * n * cols)
+    held = reduce_parts(packed, seq_at, core, x, n)
+    gate_sum, up_sum, rows_sum, mix_out = unpack(n, (rows_scale, block_scale), place, held, cols)
+    input_grad = finish(place, grads, back)
+    mix_out = mix_out.reshape(2, 2 * local, local, size)
+    return (
+        input_grad[None],
+        rows_sum,
+        cols_sum * cols_scale,
+        gate_sum.reshape(local, size, size),
+        up_sum.reshape(local, size, size),
+        mix_out[0],
+        mix_out[1],
+    )
 
 
 def column_keep(segment, cols_mix):
@@ -11,7 +491,6 @@
         "er,brcd->becd", cols_mix, segment, preferred_element_type=jnp.float32
     ).astype(jnp.bfloat16)
     return (segment, mixed)
-
 
 def body(inputs, cotangent, rows_in, cols_mix, blocks_gate, blocks_up, mix_gate, mix_up):
     batch_dev, rows_dev, cols_all, width_dev = inputs.shape
@@ -141,4 +620,6 @@
         P(None, "chan", None),
         P(None, "chan", None),
     )
-    return jax.shard_map(body, mesh=mesh, in_specs=in_specs, out_specs=out_specs, check_vma=False)
+    sizes = dict(mesh.shape)
+    fits = sizes["dp"] == 4 and sizes["seq"] == 4 and sizes["chan"] == 2
+    return jax.shard_map(block_body if fits else body, mesh=mesh, in_specs=in_specs, out_specs=out_specs, check_vma=False)

time: 620 us -> 273 us (0.44)
  blocking collectives: 217 us -> 0 us
  waiting for transfers between devices: 248 us -> 127 us
  starting transfers between devices: 9.24 us -> 74.1 us
  local copies, waits for them, and re-layouts: 72.1 us -> 11.5 us
  Pallas kernels: 0 us -> 45.3 us
  matrix products: 41.5 us -> 0 us
  between operations: 14.5 us -> 1.07 us
    psum x2 -> x0, blocking collectives: 157 us -> none  [the longest x1 120 us: body(): lax.psum((blocks_gate_sum, blocks_up_sum, mix_gate_sum, mix_up_sum), ('dp...]
    ppermute x0 -> x40, waiting for transfers between devices: none -> 127 us  [the longest x24 65.1 us: shifted(): return lax.ppermute(value, 'seq', [(i, (i + by) % n) for i in range(n)])]
    psum x2 -> x0, waiting for transfers between devices: 122 us -> none  [the longest x1 122 us: body(): lax.psum((rows_sum, cols_sum), ('dp', 'seq', 'chan'))]
    all_gather x4 -> x0, waiting for transfers between devices: 101 us -> none  [the longest x1 28.8 us: body(): lax.all_gather(up_grad, 'chan', axis=3, tiled=True)]
    ppermute x0 -> x40, starting transfers between devices: none -> 74.1 us  [the longest x24 53.6 us: shifted(): return lax.ppermute(value, 'seq', [(i, (i + by) % n) for i in range(n)])]
    all_to_all x2 -> x0, blocking collectives: 59.6 us -> none  [the longest x1 31.8 us: body(): lax.all_to_all(first, 'seq', split_axis=2, concat_axis=1, tiled=True)]
    pallas_call x0 -> x10, Pallas kernels: none -> 45.3 us  [the longest x2 16.7 us: channel_row(): pl.pallas_call(functools.partial(channel_kernel, n), out_shape=[shape_of(...]
    dot_general x18 -> x0, matrix products: 41.5 us -> none  [the longest x1 5.46 us: body(): jnp.einsum('brcmj,brckj->mkj', gate_all, gate_mid, preferred_element_type...]
  transfers between devices with their start and end apart: 8 -> 40, of which waited for: 6 -> 25; matrix products, arithmetic and copies ran while one was open for 12% -> 3% of each run, Pallas kernels for 0% -> 11%
where the time goes in v1:
time: 273 us; the launch traced here: 269 us
  waiting for transfers between devices  127 us (47%)
  starting transfers between devices  74.1 us (27%)
  Pallas kernels  45.3 us (17%)
  local copies, waits for them, and re-layouts  11.5 us (4%)
  other arithmetic  10.6 us (4%)
    ppermute x24, waiting for transfers between devices, shifted(): return lax.ppermute(value, 'seq', [(i, (i + by) % n) for i in range(n)])  65.1 us
    ppermute x16, waiting for transfers between devices, swapped(): return lax.ppermute(value, axis, [(i, i ^ bit) for i in range(n)])  61.4 us
    ppermute x24, starting transfers between devices, shifted(): return lax.ppermute(value, 'seq', [(i, (i + by) % n) for i in range(n)])  53.6 us
    ppermute x16, starting transfers between devices, swapped(): return lax.ppermute(value, axis, [(i, i ^ bit) for i in range(n)])  20.6 us
    pallas_call x2, Pallas kernels, channel_row(): pl.pallas_call(functools.partial(channel_kernel, n), out_shape=[shape_of(...  16.7 us
    pallas_call x2, Pallas kernels, hidden_row(): pl.pallas_call(functools.partial(hidden_kernel, n), out_shape=[shape_of((...  6.2 us
  transfers between devices with their start and end apart: 40, of which 25 were waited for; matrix products, arithmetic and copies ran while one was open for 3% of the time, Pallas kernels for 11%

profile of v1, /device:TPU:0, one launch (start us, length us, event | category | flops | bytes accessed | tf_op | source)
XLA Modules:
  0.0 269.1 jit_solution(5787859533645059093)
XLA Ops:
  0.7 1.4 broadcast_select_fusion.2
  2.1 3.0 %collective-permute-start.8 = (bf16[2,512,512]{2,1,0:T(8,128)(2,1)S(1)}, bf16[2,512,512]{2,1,0:T(8,128)(2,1)}, u32[]{:S(2)}, u32[]{:S(2)}) collective-permute-start(bf16[2,512,512]{2,1,0:T(8,128)(2,1)S(1)} %broadcast_select_fusion.2), channel_id=1, source_target_pairs={{0,1},{1,0},{2,3},{3,2},{4,5},{5,4},{6,7},{7,6},{8,9},{9,8},{10,11... | collective-permute-start | bytes 3145736 | tf_op jit(solution)/shard_map/ppermute | solution.py:386
  5.2 23.3 %collective-permute-done.8 = bf16[2,512,512]{2,1,0:T(8,128)(2,1)} collective-permute-done((bf16[2,512,512]{2,1,0:T(8,128)(2,1)S(1)}, bf16[2,512,512]{2,1,0:T(8,128)(2,1)}, u32[]{:S(2)}, u32[]{:S(2)}) %collective-permute-start.8) | collective-permute-done | bytes 1048608 | tf_op jit(solution)/shard_map/ppermute | solution.py:386
  29.3 1.8 collective-permute-start
  31.1 2.6 collective-permute-start.1
  33.7 1.3 collective-permute-start.2
  35.0 1.5 collective-permute-start.7
  37.8 2.8 %collective-permute-done.refs_1_.refs_0_ = bf16[2,64,1024]{2,1,0:T(8,128)(2,1)S(1)} collective-permute-done((bf16[2,64,1024]{2,1,0:T(8,128)(2,1)}, bf16[2,64,1024]{2,1,0:T(8,128)(2,1)S(1)}, u32[]{:S(2)}, u32[]{:S(2)}) %collective-permute-start) | collective-permute-done | bytes 262176 | tf_op jit(solution)/shard_map/ppermute | solution.py:382
  40.6 11.0 %collective-permute-done.1.refs_2_.refs_1_ = bf16[2,64,1024]{2,1,0:T(8,128)(2,1)S(1)} collective-permute-done((bf16[2,64,1024]{2,1,0:T(8,128)(2,1)}, bf16[2,64,1024]{2,1,0:T(8,128)(2,1)S(1)}, u32[]{:S(2)}, u32[]{:S(2)}) %collective-permute-start.1) | collective-permute-done | bytes 262176 | tf_op jit(solution)/shard_map/ppermute | solution.py:382
  52.4 4.9 %column_mix.1 = (bf16[64,1024]{1,0:T(8,128)(2,1)}, bf16[64,1024]{1,0:T(8,128)(2,1)}, bf16[64,1024]{1,0:T(8,128)(2,1)}, bf16[64,1024]{1,0:T(8,128)(2,1)}, bf16[64...) custom-call(s32[4]{0:T(128)} %pad_add_fusion.place, ...), custom_call_target="tpu_custom_call" | custom-call | tf_op jit(solution)/shard_map/column_mix/pallas_call | solution.py:59
  57.4 6.0 %collective-permute-start.10 = (bf16[64,1024]{1,0:T(8,128)(2,1)}, bf16[64,1024]{1,0:T(8,128)(2,1)S(1)}, u32[]{:S(2)}, u32[]{:S(2)}) collective-permute-start(bf16[64,1024]{1,0:T(8,128)(2,1)} %get-tuple-element.50), channel_id=1, source_target_pairs={{0,2},{2,4},{4,6},{6,0},{1,3},{3,5},{5,7},{7,1},{8,10},{10,12},{12... | collective-permute-start | bytes 393224 | tf_op jit(solution)/shard_map/ppermute | solution.py:382
  63.4 1.7 collective-permute-start.11
  65.9 3.3 %collective-permute-done.10.refs_1_ = bf16[64,1024]{1,0:T(8,128)(2,1)S(1)} collective-permute-done((bf16[64,1024]{1,0:T(8,128)(2,1)}, bf16[64,1024]{1,0:T(8,128)(2,1)S(1)}, u32[]{:S(2)}, u32[]{:S(2)}) %collective-permute-start.10) | collective-permute-done | bytes 131104 | tf_op jit(solution)/shard_map/ppermute | solution.py:382
  70.0 4.8 %collective-permute-done.11.refs_2_ = bf16[64,1024]{1,0:T(8,128)(2,1)S(1)} collective-permute-done((bf16[64,1024]{1,0:T(8,128)(2,1)}, bf16[64,1024]{1,0:T(8,128)(2,1)S(1)}, u32[]{:S(2)}, u32[]{:S(2)}) %collective-permute-start.11) | collective-permute-done | bytes 131104 | tf_op jit(solution)/shard_map/ppermute | solution.py:382
  74.9 4.0 %collective-permute-start.5 = (bf16[64,1024]{1,0:T(8,128)(2,1)}, bf16[64,1024]{1,0:T(8,128)(2,1)S(1)}, u32[]{:S(2)}, u32[]{:S(2)}) collective-permute-start(bf16[64,1024]{1,0:T(8,128)(2,1)} %get-tuple-element.46), channel_id=1, source_target_pairs={{0,6},{2,0},{4,2},{6,4},{1,7},{3,1},{5,3},{7,5},{8,14},{10,8},{12,... | collective-permute-start | bytes 393224 | tf_op jit(solution)/shard_map/ppermute | solution.py:382
  78.9 3.1 %hidden_row.3 = (bf16[256,1024]{1,0:T(8,128)(2,1)}, bf16[256,1024]{1,0:T(8,128)(2,1)}) custom-call(s32[4]{0:T(128)} %pad_add_fusion.place, bf16[256,256]{1,0:T(8,128)(2,1)} %refs_10_.3, bf16[2,256,1024]{2,1,0:T(8,128)(2,1)} %bitcast.45, bf16[64,1024]{1,0:T(8,128)(2,1)} %get-tuple-element.49.refs_0_, bf16[64,1024]{1,0:T(8,128)(2,1)} %copy-done.33, ...), custom_call_target="tpu_custom_call" | custom-call | tf_op jit(solution)/shard_map/hidden_row/pallas_call | solution.py:150
  82.1 1.6 collective-permute-start.13
  83.7 1.5 collective-permute-done.4.refs_2_
  85.1 2.7 %collective-permute-done.5.refs_3_ = bf16[64,1024]{1,0:T(8,128)(2,1)S(1)} collective-permute-done((bf16[64,1024]{1,0:T(8,128)(2,1)}, bf16[64,1024]{1,0:T(8,128)(2,1)S(1)}, u32[]{:S(2)}, u32[]{:S(2)}) %collective-permute-start.5) | collective-permute-done | bytes 131104 | tf_op jit(solution)/shard_map/ppermute | solution.py:382
  88.5 3.1 %hidden_row.2 = (bf16[256,1024]{1,0:T(8,128)(2,1)}, bf16[256,1024]{1,0:T(8,128)(2,1)}) custom-call(s32[4]{0:T(128)} %pad_add_fusion.place, bf16[256,256]{1,0:T(8,128)(2,1)} %refs_10_.3, bf16[2,256,1024]{2,1,0:T(8,128)(2,1)} %bitcast.46, bf16[64,1024]{1,0:T(8,128)(2,1)} %get-tuple-element.43.refs_0_, bf16[64,1024]{1,0:T(8,128)(2,1)} %copy-done.32, ...), custom_call_target="tpu_custom_call" | custom-call | tf_op jit(solution)/shard_map/hidden_row/pallas_call | solution.py:150
  91.6 1.5 collective-permute-start.6
  93.2 3.1 %broadcast_select_fusion = (bf16[2,512,512]{2,1,0:T(8,128)(2,1)}, bf16[2,512,512]{2,1,0:T(8,128)(2,1)}) fusion(bf16[2,512,512]{2,1,0:T(8,128)(2,1)} %collective-permute-done.9, bf16[2,512,512]{2,1,0:T(8,128)(2,1)} %collective-permute-done.8, pred[]{:T(512)S(6)} %eq.4), kind=kLoop, calls=%fused_computation.5 | loop fusion | flops 1048576 | bytes 4194305 | tf_op jit(solution)/shard_map/jit(_where)/select_n | solution.py:440
  96.4 8.4 %channel_row.3 = (bf16[256,1024]{1,0:T(8,128)(2,1)S(1)}, bf16[256,1024]{1,0:T(8,128)(2,1)S(1)}, bf16[256,1024]{1,0:T(8,128)(2,1)S(1)}, f32[2,4,2,8,512]{4,3,2,1,...) custom-call(s32[4]{0:T(128)S(1)} %copy-done.10, ...), custom_call_target="tpu_custom_call" | custom-call | tf_op jit(solution)/shard_map/channel_row/pallas_call | solution.py:240
  106.1 8.4 %channel_row.2 = (bf16[256,1024]{1,0:T(8,128)(2,1)S(1)}, bf16[256,1024]{1,0:T(8,128)(2,1)S(1)}, bf16[256,1024]{1,0:T(8,128)(2,1)S(1)}, f32[2,4,2,8,512]{4,3,2,1,...) custom-call(s32[4]{0:T(128)S(1)} %copy-done.10, ...), custom_call_target="tpu_custom_call" | custom-call | tf_op jit(solution)/shard_map/channel_row/pallas_call | solution.py:240
  115.1 3.6 %sums.1 = bf16[16,144,512]{2,1,0:T(8,128)(2,1)} custom-call(s32[4]{0:T(128)S(1)} %copy-done.10, bf16[256,1024]{1,0:T(8,128)(2,1)S(1)} %copy-done.3, bf16[256,1024]{1,0:T(8,128)(2,1)S(1)} %copy-done.2, bf16[256,1024]{1,0:T(8,128)(2,1)S(1)} %get-tuple-element.67.refs_2_, bf16[256,1024]{1,0:T(8,128)(2,1)S(1)} %get-tuple-element.68.refs_3_, ...), custom_call_target="tpu_custom_call" | custom-call | tf_op jit(solution)/shard_map/sums/pallas_call | solution.py:310
  118.7 2.5 dynamic-slice_bitcast_fusion
  121.2 3.2 %collective-permute-done.23 = bf16[8,144,512]{2,1,0:T(8,128)(2,1)} collective-permute-done((bf16[8,144,512]{2,1,0:T(8,128)(2,1)}, bf16[8,144,512]{2,1,0:T(8,128)(2,1)}, u32[]{:S(2)}, u32[]{:S(2)}) %collective-permute-start.23) | collective-permute-done | bytes 1179680 | tf_op jit(solution)/shard_map/ppermute | solution.py:386
  124.4 2.6 fusion
  128.1 1.6 collective-permute-start.24
  129.7 13.9 %collective-permute-done.24 = bf16[4,144,512]{2,1,0:T(8,128)(2,1)S(1)} collective-permute-done((bf16[4,144,512]{2,1,0:T(8,128)(2,1)S(1)}, bf16[4,144,512]{2,1,0:T(8,128)(2,1)S(1)}, u32[]{:S(2)}, u32[]{:S(2)}) %collective-permute-start.24) | collective-permute-done | bytes 589856 | tf_op jit(solution)/shard_map/ppermute | solution.py:386
  143.6 1.2 fusion.1
  144.8 5.9 %collective-permute-start.25 = (bf16[144,512]{1,0:T(8,128)(2,1)S(1)}, bf16[144,512]{1,0:T(8,128)(2,1)S(1)}, u32[]{:S(2)}, u32[]{:S(2)}) collective-permute-start(bf16[144,512]{1,0:T(8,128)(2,1)S(1)} %get-tuple-element.84), channel_id=1, source_target_pairs={{0,2},{2,4},{4,6},{6,0},{1,3},{3,5},{5,7},{7,1},{8,10},{10,12},{12... | collective-permute-start | bytes 442376 | tf_op jit(solution)/shard_map/ppermute | solution.py:382
  151.4 2.8 %collective-permute-start.27 = (bf16[144,512]{1,0:T(8,128)(2,1)S(1)}, bf16[144,512]{1,0:T(8,128)(2,1)S(1)}, u32[]{:S(2)}, u32[]{:S(2)}) collective-permute-start(bf16[144,512]{1,0:T(8,128)(2,1)S(1)} %get-tuple-element.85), channel_id=1, source_target_pairs={{0,6},{2,0},{4,2},{6,4},{1,7},{3,1},{5,3},{7,5},{8,14},{10,8},{12,... | collective-permute-start | bytes 442376 | tf_op jit(solution)/shard_map/ppermute | solution.py:382
  155.1 5.2 %collective-permute-done.26 = bf16[144,512]{1,0:T(8,128)(2,1)S(1)} collective-permute-done((bf16[144,512]{1,0:T(8,128)(2,1)S(1)}, bf16[144,512]{1,0:T(8,128)(2,1)S(1)}, u32[]{:S(2)}, u32[]{:S(2)}) %collective-permute-start.26) | collective-permute-done | bytes 147488 | tf_op jit(solution)/shard_map/ppermute | solution.py:382
  160.3 1.6 collective-permute-start.28
  161.9 2.2 collective-permute-done.28
  164.2 3.8 %collective-permute-start.29 = (bf16[144,512]{1,0:T(8,128)(2,1)S(1)}, bf16[144,512]{1,0:T(8,128)(2,1)S(1)}, u32[]{:S(2)}, u32[]{:S(2)}) collective-permute-start(bf16[144,512]{1,0:T(8,128)(2,1)S(1)} %get-tuple-element.88), channel_id=1, source_target_pairs={{0,2},{2,4},{4,6},{6,0},{1,3},{3,5},{5,7},{7,1},{8,10},{10,12},{12... | collective-permute-start | bytes 442376 | tf_op jit(solution)/shard_map/ppermute | solution.py:382
  168.1 3.4 %collective-permute-start.30 = (bf16[144,512]{1,0:T(8,128)(2,1)S(1)}, bf16[144,512]{1,0:T(8,128)(2,1)S(1)}, u32[]{:S(2)}, u32[]{:S(2)}) collective-permute-start(bf16[144,512]{1,0:T(8,128)(2,1)S(1)} %get-tuple-element.88), channel_id=1, source_target_pairs={{0,4},{2,6},{4,0},{6,2},{1,5},{3,7},{5,1},{7,3},{8,12},{10,14},{12... | collective-permute-start | bytes 442376 | tf_op jit(solution)/shard_map/ppermute | solution.py:382
  171.4 3.7 %collective-permute-done.29 = bf16[144,512]{1,0:T(8,128)(2,1)S(1)} collective-permute-done((bf16[144,512]{1,0:T(8,128)(2,1)S(1)}, bf16[144,512]{1,0:T(8,128)(2,1)S(1)}, u32[]{:S(2)}, u32[]{:S(2)}) %collective-permute-start.29) | collective-permute-done | bytes 147488 | tf_op jit(solution)/shard_map/ppermute | solution.py:382
  175.1 4.1 %collective-permute-done.30 = bf16[144,512]{1,0:T(8,128)(2,1)S(1)} collective-permute-done((bf16[144,512]{1,0:T(8,128)(2,1)S(1)}, bf16[144,512]{1,0:T(8,128)(2,1)S(1)}, u32[]{:S(2)}, u32[]{:S(2)}) %collective-permute-start.30) | collective-permute-done | bytes 147488 | tf_op jit(solution)/shard_map/ppermute | solution.py:382
  179.2 1.5 collective-permute-start.32
  180.8 11.9 %collective-permute-done.32.refs_1_ = bf16[4,144,512]{2,1,0:T(8,128)(2,1)S(1)} collective-permute-done((bf16[4,144,512]{2,1,0:T(8,128)(2,1)S(1)}, bf16[4,144,512]{2,1,0:T(8,128)(2,1)S(1)}, u32[]{:S(2)}, u32[]{:S(2)}) %collective-permute-start.32) | collective-permute-done | bytes 589856 | tf_op jit(solution)/shard_map/ppermute | solution.py:386
  192.7 3.7 %collective-permute-start.15 = (bf16[64,1024]{1,0:T(8,128)(2,1)S(1)}, bf16[64,1024]{1,0:T(8,128)(2,1)S(1)}, u32[]{:S(2)}, u32[]{:S(2)}) collective-permute-start(bf16[64,1024]{1,0:T(8,128)(2,1)S(1)} %copy-done.17), channel_id=1, source_target_pairs={{0,2},{2,4},{4,6},{6,0},{1,3},{3,5},{5,7},{7,1},{8,10},{10,12},{12... | collective-permute-start | bytes 393224 | tf_op jit(solution)/shard_map/ppermute | solution.py:382
  196.4 2.4 collective-permute-start.19
  198.9 2.0 collective-permute-done.15.refs_3_.refs_6_
  200.9 1.9 collective-permute-start.14
  202.7 3.8 %collective-permute-done.17.refs_5_.refs_8_ = bf16[64,1024]{1,0:T(8,128)(2,1)S(1)} collective-permute-done((bf16[64,1024]{1,0:T(8,128)(2,1)S(1)}, bf16[64,1024]{1,0:T(8,128)(2,1)S(1)}, u32[]{:S(2)}, u32[]{:S(2)}) %collective-permute-start.17) | collective-permute-done | bytes 131104 | tf_op jit(solution)/shard_map/ppermute | solution.py:382
  206.6 5.3 %collective-permute-start.18 = (bf16[64,1024]{1,0:T(8,128)(2,1)S(1)}, bf16[64,1024]{1,0:T(8,128)(2,1)S(1)}, u32[]{:S(2)}, u32[]{:S(2)}) collective-permute-start(bf16[64,1024]{1,0:T(8,128)(2,1)S(1)} %get-tuple-element.61), channel_id=1, source_target_pairs={{0,6},{2,0},{4,2},{6,4},{1,7},{3,1},{5,3},{7,5},{8,14},{10,8},{12,... | collective-permute-start | bytes 393224 | tf_op jit(solution)/shard_map/ppermute | solution.py:382
  211.9 5.5 %collective-permute-done.16.refs_4_.refs_7_ = bf16[64,1024]{1,0:T(8,128)(2,1)S(1)} collective-permute-done((bf16[64,1024]{1,0:T(8,128)(2,1)S(1)}, bf16[64,1024]{1,0:T(8,128)(2,1)S(1)}, u32[]{:S(2)}, u32[]{:S(2)}) %collective-permute-start.16) | collective-permute-done | bytes 131104 | tf_op jit(solution)/shard_map/ppermute | solution.py:382
  218.7 3.6 %column_sum.1 = f32[8,512]{1,0:T(8,128)} custom-call(s32[4]{0:T(128)} %pad_add_fusion.place, bf16[2,256,1024]{2,1,0:T(8,128)(2,1)} %bitcast.47, bf16[2,64,1024]{2,1,0:T(8,128)(2,1)} %copy-done.20, bf16[2,64,1024]{2,1,0:T(8,128)(2,1)} %copy-done.21, bf16[2,64,1024]{2,1,0:T(8,128)(2,1)} %copy-done.22, bf16[64,1024]{1,0:T(8,128)(2,1)} %copy-done.9, ...), custom_call_target="tpu_custom_call" | custom-call | tf_op jit(solution)/shard_map/column_sum/pallas_call | solution.py:117
  224.4 1.5 collective-permute-start.36
  225.9 2.1 collective-permute-done.36
  228.0 1.5 collective-permute-start.37
  229.5 2.1 collective-permute-done.37
  231.6 2.6 collective-permute-start.38
  234.2 1.6 collective-permute-done.38
  235.8 2.6 collective-permute-start.39
  238.4 4.8 %column_back.1 = (bf16[2,64,1024]{2,1,0:T(8,128)(2,1)}, bf16[2,64,1024]{2,1,0:T(8,128)(2,1)}, bf16[2,64,1024]{2,1,0:T(8,128)(2,1)}, bf16[2,64,1024]{2,1,0:T(8,128)(2,1)}) custom-call(s32[4]{0:T(128)} %pad_add_fusion.place, f32[8,8]{1,0:T(8,128)} %convert_element_type.60.mix, bf16[64,1024]{1,0:T(8,128)(2,1)} %copy-done.9, bf16[64,1024]{1,0:T(8,128)(2,1)} %copy-done.8, ...), custom_call_target="tpu_custom_call" | custom-call | tf_op jit(solution)/shard_map/column_back/pallas_call | solution.py:76
  243.2 2.1 collective-permute-start.20
  245.6 2.1 collective-permute-start.22
  248.3 6.2 %collective-permute-done.20.refs_3_ = bf16[2,64,1024]{2,1,0:T(8,128)(2,1)S(1)} collective-permute-done((bf16[2,64,1024]{2,1,0:T(8,128)(2,1)}, bf16[2,64,1024]{2,1,0:T(8,128)(2,1)S(1)}, u32[]{:S(2)}, u32[]{:S(2)}) %collective-permute-start.20) | collective-permute-done | bytes 262176 | tf_op jit(solution)/shard_map/ppermute | solution.py:382
  254.6 7.0 %collective-permute-done.21.refs_4_ = bf16[2,64,1024]{2,1,0:T(8,128)(2,1)S(1)} collective-permute-done((bf16[2,64,1024]{2,1,0:T(8,128)(2,1)}, bf16[2,64,1024]{2,1,0:T(8,128)(2,1)S(1)}, u32[]{:S(2)}, u32[]{:S(2)}) %collective-permute-start.21) | collective-permute-done | bytes 262176 | tf_op jit(solution)/shard_map/ppermute | solution.py:382
  262.4 2.5 finish.1
  264.9 3.0 %unpack.1 = (f32[1024,512]{1,0:T(8,128)}, f32[1024,512]{1,0:T(8,128)}, f32[256,256]{1,0:T(8,128)}, f32[16,512]{1,0:T(8,128)S(1)}) custom-call(s32[4]{0:T(128)S(1)} %copy-done.11, bf16[4,144,512]{2,1,0:T(8,128)(2,1)S(1)} %pad_maximum_fusion.refs_0_, bf16[4,144,512]{2,1,0:T(8,128)(2,1)S(1)} %collective-permute-done.32.refs_1_, ...), custom_call_target="tpu_custom_call" | custom-call | tf_op jit(solution)/shard_map/unpack/pallas_call | solution.py:344
  (142 shorter events, 16.5 us)
Async XLA Ops:
  0.6 27.8 %copy-start.18 = (bf16[1,2,256,1024]{3,2,1,0:T(8,128)(2,1)S(1)}, bf16[1,2,256,1024]{3,2,1,0:T(8,128)(2,1)}, u32[]{:S(2)}) copy-start(bf16[1,2,256,1024]{3,2,1,0:T(8,128)(2,1)} %param.8) | copy-start | bytes 3145732
  2.1 32.9 %copy-start = (bf16[1,2,256,1024]{3,2,1,0:T(8,128)(2,1)S(1)}, bf16[1,2,256,1024]{3,2,1,0:T(8,128)(2,1)}, u32[]{:S(2)}) copy-start(bf16[1,2,256,1024]{3,2,1,0:T(8,128)(2,1)} %param.9) | copy-start | bytes 3145732
  2.1 34.4 %copy-start.38 = (bf16[4,4,512]{2,1,0:T(4,128)(2,1)S(1)}, bf16[4,4,512]{2,1,0:T(4,128)(2,1)}, u32[]{:S(2)}) copy-start(bf16[4,4,512]{2,1,0:T(4,128)(2,1)} %param.15) | copy-start | bytes 49156
  2.1 35.1 %copy-start.40 = (bf16[8,8]{1,0:T(8,128)(2,1)S(1)}, bf16[8,8]{1,0:T(8,128)(2,1)}, u32[]{:S(2)}) copy-start(bf16[8,8]{1,0:T(8,128)(2,1)} %param.11) | copy-start | bytes 388
  2.1 26.3 %collective-permute-start.8 = (bf16[2,512,512]{2,1,0:T(8,128)(2,1)S(1)}, bf16[2,512,512]{2,1,0:T(8,128)(2,1)}, u32[]{:S(2)}, u32[]{:S(2)}) collective-permute-start(bf16[2,512,512]{2,1,0:T(8,128)(2,1)S(1)} %broadcast_select_fusion.2), channel_id=1, source_target_pairs={{0,1},{1,0},{2,3},{3,2},{4,5},{5,4},{6,7},{7,6},{8,9},{9,8},{10,11... | collective-permute-start | bytes 3145736 | tf_op jit(solution)/shard_map/ppermute | solution.py:386
  28.4 64.8 %collective-permute-start.9 = (bf16[2,512,512]{2,1,0:T(8,128)(2,1)}, bf16[2,512,512]{2,1,0:T(8,128)(2,1)}, u32[]{:S(2)}, u32[]{:S(2)}) collective-permute-start(bf16[2,512,512]{2,1,0:T(8,128)(2,1)} %collective-permute-done.8), channel_id=1, source_target_pairs={{0,8},{8,0},{16,24},{24,16},{1,9},{9,1},{17,25},{25,17},{2,10},{10... | collective-permute-start | bytes 3145736 | tf_op jit(solution)/shard_map/ppermute | solution.py:386
  29.3 36.6 %copy-start.39 = (bf16[4,4,512]{2,1,0:T(4,128)(2,1)S(1)}, bf16[4,4,512]{2,1,0:T(4,128)(2,1)}, u32[]{:S(2)}) copy-start(bf16[4,4,512]{2,1,0:T(4,128)(2,1)} %param.14) | copy-start | bytes 49156
  29.3 11.3 %collective-permute-start = (bf16[2,64,1024]{2,1,0:T(8,128)(2,1)}, bf16[2,64,1024]{2,1,0:T(8,128)(2,1)S(1)}, u32[]{:S(2)}, u32[]{:S(2)}) collective-permute-start(bf16[2,64,1024]{2,1,0:T(8,128)(2,1)} %get-tuple-element.82), channel_id=1, source_target_pairs={{0,2},{2,4},{4,6},{6,0},{1,3},{3,5},{5,7},{7,1},{8,10},{10,12},{12... | collective-permute-start | bytes 786440 | tf_op jit(solution)/shard_map/ppermute | solution.py:382
  31.1 20.6 %collective-permute-start.1 = (bf16[2,64,1024]{2,1,0:T(8,128)(2,1)}, bf16[2,64,1024]{2,1,0:T(8,128)(2,1)S(1)}, u32[]{:S(2)}, u32[]{:S(2)}) collective-permute-start(bf16[2,64,1024]{2,1,0:T(8,128)(2,1)} %get-tuple-element.83), channel_id=1, source_target_pairs={{0,4},{2,6},{4,0},{6,2},{1,5},{3,7},{5,1},{7,3},{8,12},{10,14},{12... | collective-permute-start | bytes 786440 | tf_op jit(solution)/shard_map/ppermute | solution.py:382
  33.7 18.0 %collective-permute-start.2 = (bf16[2,64,1024]{2,1,0:T(8,128)(2,1)S(1)}, bf16[2,64,1024]{2,1,0:T(8,128)(2,1)S(1)}, u32[]{:S(2)}, u32[]{:S(2)}) collective-permute-start(bf16[2,64,1024]{2,1,0:T(8,128)(2,1)S(1)} %get-tuple-element.81), channel_id=1, source_target_pairs={{0,6},{2,0},{4,2},{6,4},{1,7},{3,1},{5,3},{7,5},{8,14},{10,8},{12,... | collective-permute-start | bytes 786440 | tf_op jit(solution)/shard_map/ppermute | solution.py:382
  35.0 61.2 %collective-permute-start.7 = (bf16[2,256,1024]{2,1,0:T(8,128)(2,1)S(1)}, bf16[2,256,1024]{2,1,0:T(8,128)(2,1)S(1)}, u32[]{:S(2)}, u32[]{:S(2)}) collective-permute-start(bf16[2,256,1024]{2,1,0:T(8,128)(2,1)S(1)} %bitcast.41), channel_id=1, source_target_pairs={{0,1},{1,0},{2,3},{3,2},{4,5},{5,4},{6,7},{7,6},{8,9},{9,8},{10,11... | collective-permute-start | bytes 3145736 | tf_op jit(solution)/shard_map/ppermute | solution.py:386
  40.6 11.0 %copy-start.20 = (bf16[2,64,1024]{2,1,0:T(8,128)(2,1)}, bf16[2,64,1024]{2,1,0:T(8,128)(2,1)S(1)}, u32[]{:S(2)}) copy-start(bf16[2,64,1024]{2,1,0:T(8,128)(2,1)S(1)} %collective-permute-done.refs_1_.refs_0_) | copy-start | bytes 786436
  57.4 11.8 %collective-permute-start.10 = (bf16[64,1024]{1,0:T(8,128)(2,1)}, bf16[64,1024]{1,0:T(8,128)(2,1)S(1)}, u32[]{:S(2)}, u32[]{:S(2)}) collective-permute-start(bf16[64,1024]{1,0:T(8,128)(2,1)} %get-tuple-element.50), channel_id=1, source_target_pairs={{0,2},{2,4},{4,6},{6,0},{1,3},{3,5},{5,7},{7,1},{8,10},{10,12},{12... | collective-permute-start | bytes 393224 | tf_op jit(solution)/shard_map/ppermute | solution.py:382
  63.4 11.4 %collective-permute-start.11 = (bf16[64,1024]{1,0:T(8,128)(2,1)}, bf16[64,1024]{1,0:T(8,128)(2,1)S(1)}, u32[]{:S(2)}, u32[]{:S(2)}) collective-permute-start(bf16[64,1024]{1,0:T(8,128)(2,1)} %get-tuple-element.51), channel_id=1, source_target_pairs={{0,4},{2,6},{4,0},{6,2},{1,5},{3,7},{5,1},{7,3},{8,12},{10,14},{12... | collective-permute-start | bytes 393224 | tf_op jit(solution)/shard_map/ppermute | solution.py:382
  65.1 9.7 %collective-permute-start.12 = (bf16[64,1024]{1,0:T(8,128)(2,1)}, bf16[64,1024]{1,0:T(8,128)(2,1)S(1)}, u32[]{:S(2)}, u32[]{:S(2)}) collective-permute-start(bf16[64,1024]{1,0:T(8,128)(2,1)} %get-tuple-element.52), channel_id=1, source_target_pairs={{0,6},{2,0},{4,2},{6,4},{1,7},{3,1},{5,3},{7,5},{8,14},{10,8},{12,... | collective-permute-start | bytes 393224 | tf_op jit(solution)/shard_map/ppermute | solution.py:382
  69.2 9.7 %copy-start.33 = (bf16[64,1024]{1,0:T(8,128)(2,1)}, bf16[64,1024]{1,0:T(8,128)(2,1)S(1)}, u32[]{:S(2)}) copy-start(bf16[64,1024]{1,0:T(8,128)(2,1)S(1)} %collective-permute-done.10.refs_1_) | copy-start | bytes 393220
  69.2 12.8 %collective-permute-start.3 = (bf16[64,1024]{1,0:T(8,128)(2,1)}, bf16[64,1024]{1,0:T(8,128)(2,1)S(1)}, u32[]{:S(2)}, u32[]{:S(2)}) collective-permute-start(bf16[64,1024]{1,0:T(8,128)(2,1)} %get-tuple-element.44), channel_id=1, source_target_pairs={{0,2},{2,4},{4,6},{6,0},{1,3},{3,5},{5,7},{7,1},{8,10},{10,12},{12... | collective-permute-start | bytes 393224 | tf_op jit(solution)/shard_map/ppermute | solution.py:382
  74.8 4.1 %copy-start.35 = (bf16[64,1024]{1,0:T(8,128)(2,1)}, bf16[64,1024]{1,0:T(8,128)(2,1)S(1)}, u32[]{:S(2)}) copy-start(bf16[64,1024]{1,0:T(8,128)(2,1)S(1)} %collective-permute-done.11.refs_2_) | copy-start | bytes 393220
  74.9 10.3 %collective-permute-start.4 = (bf16[64,1024]{1,0:T(8,128)(2,1)}, bf16[64,1024]{1,0:T(8,128)(2,1)S(1)}, u32[]{:S(2)}, u32[]{:S(2)}) collective-permute-start(bf16[64,1024]{1,0:T(8,128)(2,1)} %get-tuple-element.45), channel_id=1, source_target_pairs={{0,4},{2,6},{4,0},{6,2},{1,5},{3,7},{5,1},{7,3},{8,12},{10,14},{12... | collective-permute-start | bytes 393224 | tf_op jit(solution)/shard_map/ppermute | solution.py:382
  74.9 4.1 %copy-start.36 = (bf16[64,1024]{1,0:T(8,128)(2,1)}, bf16[64,1024]{1,0:T(8,128)(2,1)S(1)}, u32[]{:S(2)}) copy-start(bf16[64,1024]{1,0:T(8,128)(2,1)S(1)} %collective-permute-done.12.refs_3_) | copy-start | bytes 393220
  74.9 13.0 %collective-permute-start.5 = (bf16[64,1024]{1,0:T(8,128)(2,1)}, bf16[64,1024]{1,0:T(8,128)(2,1)S(1)}, u32[]{:S(2)}, u32[]{:S(2)}) collective-permute-start(bf16[64,1024]{1,0:T(8,128)(2,1)} %get-tuple-element.46), channel_id=1, source_target_pairs={{0,6},{2,0},{4,2},{6,4},{1,7},{3,1},{5,3},{7,5},{8,14},{10,8},{12,... | collective-permute-start | bytes 393224 | tf_op jit(solution)/shard_map/ppermute | solution.py:382
  82.1 5.8 %copy-start.32 = (bf16[64,1024]{1,0:T(8,128)(2,1)}, bf16[64,1024]{1,0:T(8,128)(2,1)S(1)}, u32[]{:S(2)}) copy-start(bf16[64,1024]{1,0:T(8,128)(2,1)S(1)} %collective-permute-done.3.refs_1_) | copy-start | bytes 393220
  82.1 14.2 %collective-permute-start.13 = (bf16[256,1024]{1,0:T(8,128)(2,1)}, bf16[256,1024]{1,0:T(8,128)(2,1)S(1)}, u32[]{:S(2)}, u32[]{:S(2)}) collective-permute-start(bf16[256,1024]{1,0:T(8,128)(2,1)} %get-tuple-element.53.refs_0_.refs_1_), channel_id=1, source_target_pairs={{0,1},{1,0},{2,3},{3,2},{4,5},{5,4},{6,7},{7,6},{8,9},{9,8},{10,11... | collective-permute-start | bytes 1572872 | tf_op jit(solution)/shard_map/ppermute | solution.py:386
  91.6 14.5 %collective-permute-start.6 = (bf16[256,1024]{1,0:T(8,128)(2,1)}, bf16[256,1024]{1,0:T(8,128)(2,1)S(1)}, u32[]{:S(2)}, u32[]{:S(2)}) collective-permute-start(bf16[256,1024]{1,0:T(8,128)(2,1)} %get-tuple-element.47.refs_0_), channel_id=1, source_target_pairs={{0,1},{1,0},{2,3},{3,2},{4,5},{5,4},{6,7},{7,6},{8,9},{9,8},{10,11... | collective-permute-start | bytes 1572872 | tf_op jit(solution)/shard_map/ppermute | solution.py:386
  96.4 9.7 %copy-start.3 = (bf16[256,1024]{1,0:T(8,128)(2,1)S(1)}, bf16[256,1024]{1,0:T(8,128)(2,1)}, u32[]{:S(2)}) copy-start(bf16[256,1024]{1,0:T(8,128)(2,1)} %get-tuple-element.47.refs_0_) | copy-start | bytes 1572868
  106.0 8.4 %copy-start.8 = (bf16[64,1024]{1,0:T(8,128)(2,1)}, bf16[64,1024]{1,0:T(8,128)(2,1)S(1)}, u32[]{:S(2)}) copy-start(bf16[64,1024]{1,0:T(8,128)(2,1)S(1)} %get-tuple-element.56.refs_1_.refs_4_) | copy-start | bytes 393220
  106.0 9.1 %copy-start.4 = (bf16[256,1024]{1,0:T(8,128)(2,1)}, bf16[256,1024]{1,0:T(8,128)(2,1)S(1)}, u32[]{:S(2)}) copy-start(bf16[256,1024]{1,0:T(8,128)(2,1)S(1)} %get-tuple-element.54.refs_1_.refs_7_) | copy-start | bytes 1572868
  106.0 9.1 %copy-start.6 = (bf16[256,1024]{1,0:T(8,128)(2,1)S(1)}, bf16[256,1024]{1,0:T(8,128)(2,1)}, u32[]{:S(2)}) copy-start(bf16[256,1024]{1,0:T(8,128)(2,1)} %get-tuple-element.72.refs_9_) | copy-start | bytes 1572868
  106.0 9.1 %copy-start.7 = (bf16[256,1024]{1,0:T(8,128)(2,1)S(1)}, bf16[256,1024]{1,0:T(8,128)(2,1)}, u32[]{:S(2)}) copy-start(bf16[256,1024]{1,0:T(8,128)(2,1)} %get-tuple-element.71.refs_8_) | copy-start | bytes 1572868
  118.7 5.7 %copy-start.19 = (bf16[16,144,512]{2,1,0:T(8,128)(2,1)S(1)}, bf16[16,144,512]{2,1,0:T(8,128)(2,1)}, u32[]{:S(2)}) copy-start(bf16[16,144,512]{2,1,0:T(8,128)(2,1)} %sums.1) | copy-start | bytes 7077892
  121.2 3.2 %collective-permute-start.23 = (bf16[8,144,512]{2,1,0:T(8,128)(2,1)}, bf16[8,144,512]{2,1,0:T(8,128)(2,1)}, u32[]{:S(2)}, u32[]{:S(2)}) collective-permute-start(bf16[8,144,512]{2,1,0:T(8,128)(2,1)} %dynamic-slice_bitcast_fusion), channel_id=1, source_target_pairs={{0,8},{8,0},{16,24},{24,16},{1,9},{9,1},{17,25},{25,17},{2,10},{10... | collective-permute-start | bytes 3538952 | tf_op jit(solution)/shard_map/ppermute | solution.py:386
  128.1 15.4 %collective-permute-start.24 = (bf16[4,144,512]{2,1,0:T(8,128)(2,1)S(1)}, bf16[4,144,512]{2,1,0:T(8,128)(2,1)S(1)}, u32[]{:S(2)}, u32[]{:S(2)}) collective-permute-start(bf16[4,144,512]{2,1,0:T(8,128)(2,1)S(1)} %dynamic-slice_bitcast_fusion.1), channel_id=1, source_target_pairs={{0,16},{8,24},{16,0},{24,8},{1,17},{9,25},{17,1},{25,9},{2,18},{10... | collective-permute-start | bytes 1769480 | tf_op jit(solution)/shard_map/ppermute | solution.py:386
  144.8 10.2 %collective-permute-start.25 = (bf16[144,512]{1,0:T(8,128)(2,1)S(1)}, bf16[144,512]{1,0:T(8,128)(2,1)S(1)}, u32[]{:S(2)}, u32[]{:S(2)}) collective-permute-start(bf16[144,512]{1,0:T(8,128)(2,1)S(1)} %get-tuple-element.84), channel_id=1, source_target_pairs={{0,2},{2,4},{4,6},{6,0},{1,3},{3,5},{5,7},{7,1},{8,10},{10,12},{12... | collective-permute-start | bytes 442376 | tf_op jit(solution)/shard_map/ppermute | solution.py:382
  150.8 9.5 %collective-permute-start.26 = (bf16[144,512]{1,0:T(8,128)(2,1)S(1)}, bf16[144,512]{1,0:T(8,128)(2,1)S(1)}, u32[]{:S(2)}, u32[]{:S(2)}) collective-permute-start(bf16[144,512]{1,0:T(8,128)(2,1)S(1)} %get-tuple-element.86), channel_id=1, source_target_pairs={{0,4},{2,6},{4,0},{6,2},{1,5},{3,7},{5,1},{7,3},{8,12},{10,14},{12... | collective-permute-start | bytes 442376 | tf_op jit(solution)/shard_map/ppermute | solution.py:382
  151.4 8.8 %collective-permute-start.27 = (bf16[144,512]{1,0:T(8,128)(2,1)S(1)}, bf16[144,512]{1,0:T(8,128)(2,1)S(1)}, u32[]{:S(2)}, u32[]{:S(2)}) collective-permute-start(bf16[144,512]{1,0:T(8,128)(2,1)S(1)} %get-tuple-element.85), channel_id=1, source_target_pairs={{0,6},{2,0},{4,2},{6,4},{1,7},{3,1},{5,3},{7,5},{8,14},{10,8},{12,... | collective-permute-start | bytes 442376 | tf_op jit(solution)/shard_map/ppermute | solution.py:382
  154.3 38.4 %copy-start.17 = (bf16[64,1024]{1,0:T(8,128)(2,1)S(1)}, bf16[64,1024]{1,0:T(8,128)(2,1)}, u32[]{:S(2)}) copy-start(bf16[64,1024]{1,0:T(8,128)(2,1)} %copy-done.16) | copy-start | bytes 393220
  154.3 42.1 %copy-start.15 = (bf16[64,1024]{1,0:T(8,128)(2,1)S(1)}, bf16[64,1024]{1,0:T(8,128)(2,1)}, u32[]{:S(2)}) copy-start(bf16[64,1024]{1,0:T(8,128)(2,1)} %copy-done.14) | copy-start | bytes 393220
  154.3 46.6 %copy-start.13 = (bf16[64,1024]{1,0:T(8,128)(2,1)S(1)}, bf16[64,1024]{1,0:T(8,128)(2,1)}, u32[]{:S(2)}) copy-start(bf16[64,1024]{1,0:T(8,128)(2,1)} %copy-done.12) | copy-start | bytes 393220
  160.3 3.8 %collective-permute-start.28 = (bf16[16,512]{1,0:T(8,128)(2,1)S(1)}, bf16[16,512]{1,0:T(8,128)(2,1)S(1)}, u32[]{:S(2)}, u32[]{:S(2)}) collective-permute-start(bf16[16,512]{1,0:T(8,128)(2,1)S(1)} %slice.59), channel_id=1, source_target_pairs={{0,1},{1,0},{2,3},{3,2},{4,5},{5,4},{6,7},{7,6},{8,9},{9,8},{10,11... | collective-permute-start | bytes 49160 | tf_op jit(solution)/shard_map/ppermute | solution.py:386
  164.2 10.9 %collective-permute-start.29 = (bf16[144,512]{1,0:T(8,128)(2,1)S(1)}, bf16[144,512]{1,0:T(8,128)(2,1)S(1)}, u32[]{:S(2)}, u32[]{:S(2)}) collective-permute-start(bf16[144,512]{1,0:T(8,128)(2,1)S(1)} %get-tuple-element.88), channel_id=1, source_target_pairs={{0,2},{2,4},{4,6},{6,0},{1,3},{3,5},{5,7},{7,1},{8,10},{10,12},{12... | collective-permute-start | bytes 442376 | tf_op jit(solution)/shard_map/ppermute | solution.py:382
  168.1 11.1 %collective-permute-start.30 = (bf16[144,512]{1,0:T(8,128)(2,1)S(1)}, bf16[144,512]{1,0:T(8,128)(2,1)S(1)}, u32[]{:S(2)}, u32[]{:S(2)}) collective-permute-start(bf16[144,512]{1,0:T(8,128)(2,1)S(1)} %get-tuple-element.88), channel_id=1, source_target_pairs={{0,4},{2,6},{4,0},{6,2},{1,5},{3,7},{5,1},{7,3},{8,12},{10,14},{12... | collective-permute-start | bytes 442376 | tf_op jit(solution)/shard_map/ppermute | solution.py:382
  171.4 7.7 %collective-permute-start.31 = (bf16[144,512]{1,0:T(8,128)(2,1)S(1)}, bf16[144,512]{1,0:T(8,128)(2,1)S(1)}, u32[]{:S(2)}, u32[]{:S(2)}) collective-permute-start(bf16[144,512]{1,0:T(8,128)(2,1)S(1)} %get-tuple-element.88), channel_id=1, source_target_pairs={{0,6},{2,0},{4,2},{6,4},{1,7},{3,1},{5,3},{7,5},{8,14},{10,8},{12,... | collective-permute-start | bytes 442376 | tf_op jit(solution)/shard_map/ppermute | solution.py:382
  179.2 13.5 %collective-permute-start.32 = (bf16[4,144,512]{2,1,0:T(8,128)(2,1)S(1)}, bf16[4,144,512]{2,1,0:T(8,128)(2,1)S(1)}, u32[]{:S(2)}, u32[]{:S(2)}) collective-permute-start(bf16[4,144,512]{2,1,0:T(8,128)(2,1)S(1)} %pad_maximum_fusion.refs_0_), channel_id=1, source_target_pairs={{0,16},{8,24},{16,0},{24,8},{1,17},{9,25},{17,1},{25,9},{2,18},{10... | collective-permute-start | bytes 1769480 | tf_op jit(solution)/shard_map/ppermute | solution.py:386
  180.8 84.1 %collective-permute-start.33 = (bf16[4,144,512]{2,1,0:T(8,128)(2,1)S(1)}, bf16[4,144,512]{2,1,0:T(8,128)(2,1)S(1)}, u32[]{:S(2)}, u32[]{:S(2)}) collective-permute-start(bf16[4,144,512]{2,1,0:T(8,128)(2,1)S(1)} %pad_maximum_fusion.refs_0_), channel_id=1, source_target_pairs={{0,8},{8,0},{16,24},{24,16},{1,9},{9,1},{17,25},{25,17},{2,10},{10... | collective-permute-start | bytes 1769480 | tf_op jit(solution)/shard_map/ppermute | solution.py:386
  192.7 72.1 %collective-permute-start.34 = (bf16[4,144,512]{2,1,0:T(8,128)(2,1)S(1)}, bf16[4,144,512]{2,1,0:T(8,128)(2,1)S(1)}, u32[]{:S(2)}, u32[]{:S(2)}) collective-permute-start(bf16[4,144,512]{2,1,0:T(8,128)(2,1)S(1)} %collective-permute-done.32.refs_1_), channel_id=1, source_target_pairs={{0,8},{8,0},{16,24},{24,16},{1,9},{9,1},{17,25},{25,17},{2,10},{10... | collective-permute-start | bytes 1769480 | tf_op jit(solution)/shard_map/ppermute | solution.py:386
  192.7 8.2 %collective-permute-start.15 = (bf16[64,1024]{1,0:T(8,128)(2,1)S(1)}, bf16[64,1024]{1,0:T(8,128)(2,1)S(1)}, u32[]{:S(2)}, u32[]{:S(2)}) collective-permute-start(bf16[64,1024]{1,0:T(8,128)(2,1)S(1)} %copy-done.17), channel_id=1, source_target_pairs={{0,2},{2,4},{4,6},{6,0},{1,3},{3,5},{5,7},{7,1},{8,10},{10,12},{12... | collective-permute-start | bytes 393224 | tf_op jit(solution)/shard_map/ppermute | solution.py:382
  196.4 10.1 %collective-permute-start.17 = (bf16[64,1024]{1,0:T(8,128)(2,1)S(1)}, bf16[64,1024]{1,0:T(8,128)(2,1)S(1)}, u32[]{:S(2)}, u32[]{:S(2)}) collective-permute-start(bf16[64,1024]{1,0:T(8,128)(2,1)S(1)} %copy-done.15), channel_id=1, source_target_pairs={{0,4},{2,6},{4,0},{6,2},{1,5},{3,7},{5,1},{7,3},{8,12},{10,14},{12... | collective-permute-start | bytes 393224 | tf_op jit(solution)/shard_map/ppermute | solution.py:382
  196.4 10.1 %collective-permute-start.19 = (bf16[64,1024]{1,0:T(8,128)(2,1)S(1)}, bf16[64,1024]{1,0:T(8,128)(2,1)S(1)}, u32[]{:S(2)}, u32[]{:S(2)}) collective-permute-start(bf16[64,1024]{1,0:T(8,128)(2,1)S(1)} %get-tuple-element.62), channel_id=1, source_target_pairs={{0,6},{2,0},{4,2},{6,4},{1,7},{3,1},{5,3},{7,5},{8,14},{10,8},{12,... | collective-permute-start | bytes 393224 | tf_op jit(solution)/shard_map/ppermute | solution.py:382
  200.9 17.2 %copy-start.23 = (bf16[64,1024]{1,0:T(8,128)(2,1)}, bf16[64,1024]{1,0:T(8,128)(2,1)S(1)}, u32[]{:S(2)}) copy-start(bf16[64,1024]{1,0:T(8,128)(2,1)S(1)} %collective-permute-done.15.refs_3_.refs_6_) | copy-start | bytes 393220
  200.9 11.0 %collective-permute-start.14 = (bf16[64,1024]{1,0:T(8,128)(2,1)S(1)}, bf16[64,1024]{1,0:T(8,128)(2,1)S(1)}, u32[]{:S(2)}, u32[]{:S(2)}) collective-permute-start(bf16[64,1024]{1,0:T(8,128)(2,1)S(1)} %copy-done.13), channel_id=1, source_target_pairs={{0,2},{2,4},{4,6},{6,0},{1,3},{3,5},{5,7},{7,1},{8,10},{10,12},{12... | collective-permute-start | bytes 393224 | tf_op jit(solution)/shard_map/ppermute | solution.py:382
  206.5 11.6 %copy-start.24 = (bf16[64,1024]{1,0:T(8,128)(2,1)}, bf16[64,1024]{1,0:T(8,128)(2,1)S(1)}, u32[]{:S(2)}) copy-start(bf16[64,1024]{1,0:T(8,128)(2,1)S(1)} %collective-permute-done.17.refs_5_.refs_8_) | copy-start | bytes 393220
  206.5 10.9 %collective-permute-start.16 = (bf16[64,1024]{1,0:T(8,128)(2,1)S(1)}, bf16[64,1024]{1,0:T(8,128)(2,1)S(1)}, u32[]{:S(2)}, u32[]{:S(2)}) collective-permute-start(bf16[64,1024]{1,0:T(8,128)(2,1)S(1)} %get-tuple-element.59), channel_id=1, source_target_pairs={{0,4},{2,6},{4,0},{6,2},{1,5},{3,7},{5,1},{7,3},{8,12},{10,14},{12... | collective-permute-start | bytes 393224 | tf_op jit(solution)/shard_map/ppermute | solution.py:382
  206.5 11.5 %copy-start.25 = (bf16[64,1024]{1,0:T(8,128)(2,1)}, bf16[64,1024]{1,0:T(8,128)(2,1)S(1)}, u32[]{:S(2)}) copy-start(bf16[64,1024]{1,0:T(8,128)(2,1)S(1)} %collective-permute-done.19.refs_7_.refs_10_) | copy-start | bytes 393220
  206.6 11.5 %collective-permute-start.18 = (bf16[64,1024]{1,0:T(8,128)(2,1)S(1)}, bf16[64,1024]{1,0:T(8,128)(2,1)S(1)}, u32[]{:S(2)}, u32[]{:S(2)}) collective-permute-start(bf16[64,1024]{1,0:T(8,128)(2,1)S(1)} %get-tuple-element.61), channel_id=1, source_target_pairs={{0,6},{2,0},{4,2},{6,4},{1,7},{3,1},{5,3},{7,5},{8,14},{10,8},{12,... | collective-permute-start | bytes 393224 | tf_op jit(solution)/shard_map/ppermute | solution.py:382
  211.9 6.2 %copy-start.26 = (bf16[64,1024]{1,0:T(8,128)(2,1)}, bf16[64,1024]{1,0:T(8,128)(2,1)S(1)}, u32[]{:S(2)}) copy-start(bf16[64,1024]{1,0:T(8,128)(2,1)S(1)} %collective-permute-done.14.refs_2_.refs_5_) | copy-start | bytes 393220
  223.2 1.2 collective-permute-start.35
  224.4 3.6 %collective-permute-start.36 = (f32[8,8]{1,0:T(8,128)S(1)}, f32[8,8]{1,0:T(8,128)S(1)}, u32[]{:S(2)}, u32[]{:S(2)}) collective-permute-start(f32[8,8]{1,0:T(8,128)S(1)} %add.104), channel_id=1, source_target_pairs={{0,16},{8,24},{16,0},{24,8},{1,17},{9,25},{17,1},{25,9},{2,18},{10... | collective-permute-start | bytes 776 | tf_op jit(solution)/shard_map/ppermute | solution.py:386
  228.0 3.6 %collective-permute-start.37 = (f32[8,8]{1,0:T(8,128)S(1)}, f32[8,8]{1,0:T(8,128)S(1)}, u32[]{:S(2)}, u32[]{:S(2)}) collective-permute-start(f32[8,8]{1,0:T(8,128)S(1)} %add.105), channel_id=1, source_target_pairs={{0,1},{1,0},{2,3},{3,2},{4,5},{5,4},{6,7},{7,6},{8,9},{9,8},{10,11... | collective-permute-start | bytes 776 | tf_op jit(solution)/shard_map/ppermute | solution.py:386
  231.6 4.2 %collective-permute-start.38 = (f32[8,8]{1,0:T(8,128)S(1)}, f32[8,8]{1,0:T(8,128)S(1)}, u32[]{:S(2)}, u32[]{:S(2)}) collective-permute-start(f32[8,8]{1,0:T(8,128)S(1)} %add.106), channel_id=1, source_target_pairs={{0,2},{2,0},{4,6},{6,4},{1,3},{3,1},{5,7},{7,5},{8,10},{10,8},{12,... | collective-permute-start | bytes 776 | tf_op jit(solution)/shard_map/ppermute | solution.py:386
  235.8 9.8 %collective-permute-start.39 = (f32[8,8]{1,0:T(8,128)S(1)}, f32[8,8]{1,0:T(8,128)S(1)}, u32[]{:S(2)}, u32[]{:S(2)}) collective-permute-start(f32[8,8]{1,0:T(8,128)S(1)} %add.107), channel_id=1, source_target_pairs={{0,4},{2,6},{4,0},{6,2},{1,5},{3,7},{5,1},{7,3},{8,12},{10,14},{12... | collective-permute-start | bytes 776 | tf_op jit(solution)/shard_map/ppermute | solution.py:386
  243.2 11.4 %collective-permute-start.20 = (bf16[2,64,1024]{2,1,0:T(8,128)(2,1)}, bf16[2,64,1024]{2,1,0:T(8,128)(2,1)S(1)}, u32[]{:S(2)}, u32[]{:S(2)}) collective-permute-start(bf16[2,64,1024]{2,1,0:T(8,128)(2,1)} %get-tuple-element.64), channel_id=1, source_target_pairs={{0,2},{2,4},{4,6},{6,0},{1,3},{3,5},{5,7},{7,1},{8,10},{10,12},{12... | collective-permute-start | bytes 786440 | tf_op jit(solution)/shard_map/ppermute | solution.py:382
  245.3 16.3 %collective-permute-start.21 = (bf16[2,64,1024]{2,1,0:T(8,128)(2,1)}, bf16[2,64,1024]{2,1,0:T(8,128)(2,1)S(1)}, u32[]{:S(2)}, u32[]{:S(2)}) collective-permute-start(bf16[2,64,1024]{2,1,0:T(8,128)(2,1)} %get-tuple-element.65), channel_id=1, source_target_pairs={{0,4},{2,6},{4,0},{6,2},{1,5},{3,7},{5,1},{7,3},{8,12},{10,14},{12... | collective-permute-start | bytes 786440 | tf_op jit(solution)/shard_map/ppermute | solution.py:382
  245.6 16.0 %collective-permute-start.22 = (bf16[2,64,1024]{2,1,0:T(8,128)(2,1)}, bf16[2,64,1024]{2,1,0:T(8,128)(2,1)S(1)}, u32[]{:S(2)}, u32[]{:S(2)}) collective-permute-start(bf16[2,64,1024]{2,1,0:T(8,128)(2,1)} %get-tuple-element.66), channel_id=1, source_target_pairs={{0,6},{2,0},{4,2},{6,4},{1,7},{3,1},{5,3},{7,5},{8,14},{10,8},{12,... | collective-permute-start | bytes 786440 | tf_op jit(solution)/shard_map/ppermute | solution.py:382
  254.6 7.1 %copy-start.29 = (bf16[2,64,1024]{2,1,0:T(8,128)(2,1)}, bf16[2,64,1024]{2,1,0:T(8,128)(2,1)S(1)}, u32[]{:S(2)}) copy-start(bf16[2,64,1024]{2,1,0:T(8,128)(2,1)S(1)} %collective-permute-done.20.refs_3_) | copy-start | bytes 786436
  (17 other events, 28.8 us)

commit v2 on v0

--- a/solution.py
+++ b/solution.py
@@ -1,9 +1,476 @@
+import functools
 import math
 
 import jax
 import jax.numpy as jnp
 from jax import lax
+from jax.experimental import pallas as pl
+from jax.experimental.pallas import tpu as pltpu
 from jax.sharding import PartitionSpec as P
+
+BF = jnp.bfloat16
+F = jnp.float32
+VM = pl.BlockSpec(memory_space=pltpu.VMEM)
+SM = pl.BlockSpec(memory_space=pltpu.SMEM)
+PARAMS = pltpu.CompilerParams(vmem_limit_bytes=48 * 1024 * 1024)
+
+
+def shape_of(dims, kind=BF):
+    return jax.ShapeDtypeStruct(dims, kind)
+
+
+def mix_tables(mix, rows, cw):
+    size = mix.shape[0] * cw
+    same = lax.broadcasted_iota(jnp.int32, (1, cw, 1, cw), 1) == lax.broadcasted_iota(
+        jnp.int32, (1, cw, 1, cw), 3
+    )
+
+    def spread(table):
+        grown = jnp.where(same, table[:, None, :, None], jnp.zeros((), BF))
+        return grown.reshape(table.shape[0] * cw, table.shape[1] * cw)
+
+    ahead = jnp.stack([spread(mix[h::rows]) for h in range(rows)])
+    back = jnp.stack([spread(mix[h::rows].T) for h in range(rows)])
+    assert ahead.shape[2] == back.shape[1] == size
+    return ahead, back
+
+
+def column_mix_kernel(rows, table, x_cols, *outs):
+    for h in range(rows):
+        outs[h][...] = jnp.dot(table[h], x_cols[...], preferred_element_type=F).astype(BF)
+
+
+def column_mix(table, x_cols):
+    rows, deep, size = table.shape
+    width = x_cols.shape[-1]
+    lanes = 512
+    return pl.pallas_call(
+        functools.partial(column_mix_kernel, rows),
+        out_shape=[shape_of((deep, width))] * rows,
+        grid=(width // lanes,),
+        in_specs=[
+            pl.BlockSpec((rows, deep, size), lambda j: (0, 0, 0)),
+            pl.BlockSpec((size, lanes), lambda j: (0, j)),
+        ],
+        out_specs=[pl.BlockSpec((deep, lanes), lambda j: (0, j))] * rows,
+        name="column_mix",
+    )(table, x_cols)
+
+
+def column_back_kernel(rows, table, *refs):
+    total = None
+    for h in range(rows):
+        term = jnp.dot(table[h], refs[h][...], preferred_element_type=F)
+        total = term if total is None else total + term
+    refs[rows][...] = total.astype(BF)
+
+
+def column_back(table, pieces):
+    rows, size, deep = table.shape
+    width = pieces[0].shape[-1]
+    lanes = 512
+    return pl.pallas_call(
+        functools.partial(column_back_kernel, rows),
+        out_shape=shape_of((size, width)),
+        grid=(width // lanes,),
+        in_specs=[pl.BlockSpec((rows, size, deep), lambda j: (0, 0, 0))]
+        + [pl.BlockSpec((deep, lanes), lambda j: (0, j))] * rows,
+        out_specs=pl.BlockSpec((size, lanes), lambda j: (0, j)),
+        name="column_back",
+    )(table, *pieces)
+
+
+def column_sum_kernel(rows, x_cols, *refs):
+    pieces, (out, left) = refs[:rows], refs[rows:]
+    n, cw, width = pieces[0].shape
+    for i in range(n):
+        for h in range(rows):
+            row = i * rows + h
+            left[row * cw : (row + 1) * cw, :] = pieces[h][i]
+    size = n * rows * cw
+    product = lax.dot_general(
+        left[...],
+        x_cols[...].reshape(size, width),
+        (((1,), (1,)), ((), ())),
+        preferred_element_type=F,
+    )
+    row_at = lax.broadcasted_iota(jnp.int32, (size, size), 0)
+    col_at = lax.broadcasted_iota(jnp.int32, (size, size), 1)
+    kept = jnp.where(lax.rem(row_at, cw) == lax.rem(col_at, cw), product, 0.0)
+    out[...] = jnp.sum(kept.reshape(n * rows, cw, size), axis=1)
+
+
+def column_sum(x_cols, pieces):
+    n, rows, cw, width = x_cols.shape
+    size = n * rows * cw
+    return pl.pallas_call(
+        functools.partial(column_sum_kernel, rows),
+        out_shape=shape_of((n * rows, size), F),
+        in_specs=[VM] * (1 + rows),
+        out_specs=VM,
+        scratch_shapes=[pltpu.VMEM((size, width), BF)],
+        compiler_params=PARAMS,
+        name="column_sum",
+    )(x_cols, *pieces)
+
+
+def hidden_kernel(rows_in, x, mixed, hidden):
+    second = jnp.dot(rows_in[...], mixed[...], preferred_element_type=F)
+    hidden[...] = (x[...].astype(F) + second).astype(BF)
+
+
+def hidden_row(rows_in, inputs, h, mixed):
+    cols, width = mixed.shape
+    lanes = 512
+    column = pl.BlockSpec((cols, lanes), lambda j: (0, j))
+    return pl.pallas_call(
+        hidden_kernel,
+        out_shape=shape_of((cols, width)),
+        grid=(width // lanes,),
+        in_specs=[
+            pl.BlockSpec((cols, cols), lambda j: (0, 0)),
+            pl.BlockSpec((None, cols, lanes), lambda j: (h, 0, j)),
+            column,
+        ],
+        out_specs=column,
+        name="hidden_row",
+    )(rows_in, inputs, mixed)
+
+
+def channel_kernel(*refs):
+    (h_own, h_oth, c_own, c_oth, wg_own, wg_oth, wu_own, wu_oth, mix_g, mix_u, rows_in) = refs[:11]
+    hid_grad, back_g, back_u, turned, mix_sum, mid_g, mid_u = refs[11:]
+    local, size = wg_own.shape[:2]
+    blocks = 2 * local
+    cols = h_own.shape[0]
+    for k in range(blocks):
+        h, wg, wu = (h_own, wg_own, wu_own) if k < local else (h_oth, wg_oth, wu_oth)
+        part = h[:, (k % local) * size : (k % local + 1) * size]
+        mid_g[k] = jnp.dot(part, wg[k % local], preferred_element_type=F)
+        mid_u[k] = jnp.dot(part, wu[k % local], preferred_element_type=F)
+    mix_sum[...] = jnp.zeros_like(mix_sum)
+    deep, lanes = 16, 128
+
+    def chunk(t, carry):
+        rows = pl.ds(pl.multiple_of(t * deep, deep), deep)
+        for q in range(size // lanes):
+            at = slice(q * lanes, (q + 1) * lanes)
+            shape = (deep // 8, 8, lanes)
+            g = [mid_g[k, rows, at].reshape(shape) for k in range(blocks)]
+            u = [mid_u[k, rows, at].reshape(shape) for k in range(blocks)]
+            sum_g, sum_u = [None] * local, [None] * local
+            for m in range(blocks):
+                c = c_own if m < local else c_oth
+                start = (m % local) * size + q * lanes
+                up = c[rows, start : start + lanes].astype(F).reshape(shape)
+                gate_out = mix_g[m, 0, :, at] * g[0]
+                up_out = mix_u[m, 0, :, at] * u[0]
+                for k in range(1, blocks):
+                    gate_out = gate_out + mix_g[m, k, :, at] * g[k]
+                    up_out = up_out + mix_u[m, k, :, at] * u[k]
+                sigma = 0.5 * jnp.tanh(0.5 * gate_out) + 0.5
+                scaled = up * sigma
+                up_grad = scaled * gate_out
+                gate_grad = scaled * up_out * (1.0 + gate_out * (1.0 - sigma))
+                for k in range(local):
+                    mix_sum[0, m, k, :, at] += jnp.sum(gate_grad * g[k], axis=0)
+                    mix_sum[1, m, k, :, at] += jnp.sum(up_grad * u[k], axis=0)
+                    term_g = mix_g[m, k, :, at] * gate_grad
+                    term_u = mix_u[m, k, :, at] * up_grad
+                    sum_g[k] = term_g if m == 0 else sum_g[k] + term_g
+                    sum_u[k] = term_u if m == 0 else sum_u[k] + term_u
+            for k in range(local):
+                spot = slice(k * size + q * lanes, k * size + (q + 1) * lanes)
+                back_g[rows, spot] = sum_g[k].reshape(deep, lanes).astype(BF)
+                back_u[rows, spot] = sum_u[k].reshape(deep, lanes).astype(BF)
+        return carry
+
+    lax.fori_loop(0, cols // deep, chunk, 0)
+    last = (((1,), (1,)), ((), ()))
+    for k in range(local):
+        spot = slice(k * size, (k + 1) * size)
+        grad = lax.dot_general(back_g[:, spot], wg_own[k], last, preferred_element_type=F)
+        grad = grad + lax.dot_general(back_u[:, spot], wu_own[k], last, preferred_element_type=F)
+        hid_grad[:, spot] = (c_own[:, spot].astype(F) + grad).astype(BF)
+    turned[...] = lax.dot_general(
+        rows_in[...], hid_grad[...], (((0,), (0,)), ((), ())), preferred_element_type=F
+    ).astype(BF)
+
+
+def channel_row(h, h_own, h_oth, cot, cot_oth, weights, mixes, rows_in):
+    cols, width = h_own.shape
+    local, size = weights[0].shape[:2]
+    blocks = 2 * local
+    row = pl.BlockSpec((None, cols, width), lambda j: (h, 0, 0))
+    return pl.pallas_call(
+        channel_kernel,
+        out_shape=[shape_of((cols, width))] * 4 + [shape_of((2, blocks, local, 8, size), F)],
+        grid=(1,),
+        in_specs=[VM] * 2 + [row, row] + [VM] * 7,
+        out_specs=[VM] * 5,
+        scratch_shapes=[pltpu.VMEM((blocks, cols, size), F)] * 2,
+        compiler_params=PARAMS,
+        name="channel_row",
+    )(h_own, h_oth, cot, cot_oth, *weights, *mixes, rows_in)
+
+
+def sums_kernel(rows, parts, place, *refs):
+    hid, back_g, back_u, grad, mixed, mix_sum = (refs[i * rows : (i + 1) * rows] for i in range(6))
+    outs, row_sum = refs[6 * rows : -1], refs[-1]
+    cols, width = hid[0].shape
+    size = outs[0].shape[-1]
+    local = width // size
+    blocks = 2 * local
+    first = (((0,), (0,)), ((), ()))
+    last = (((1,), (1,)), ((), ()))
+    high = local * size // parts
+    per = size // high
+    total = None
+    for h in range(rows):
+        term = lax.dot_general(grad[h][...], mixed[h][...], last, preferred_element_type=F)
+        total = term if total is None else total + term
+    row_sum[...] = total
+    chan, core = place[1], place[2]
+    for part, out in ((1, outs[1]), (0, outs[0])):
+        k = core if part == 0 else 1 - core
+        spot = pl.ds(pl.multiple_of(k * size, size), size)
+        for w, back in enumerate((back_g, back_u)):
+            total = None
+            for h in range(rows):
+                term = lax.dot_general(
+                    hid[h][:, spot], back[h][:, spot], first, preferred_element_type=F
+                )
+                total = term if total is None else total + term
+            for q in range(per):
+                out[q, w * high : (w + 1) * high, :] = total[q * high : (q + 1) * high].astype(BF)
+        for q in range(per):
+            p = k * per + q
+            m_at = lax.rem(p // (2 * local) + blocks - chan * local, blocks)
+            k_at = lax.rem(p // 2, local)
+            lines = [
+                jnp.sum(sum(ref[w, m_at, k_at] for ref in mix_sum), axis=0, keepdims=True)
+                for w in range(2)
+            ]
+            at = pl.multiple_of(p * 16, 16)
+            eight = jnp.concatenate(
+                [row_sum[pl.ds(at, 8), :], row_sum[pl.ds(at + 8, 8), :]], axis=1
+            )
+            blank = jnp.zeros((6, size), F)
+            out[q, 2 * high :, :] = jnp.concatenate([eight, *lines, blank], axis=0).astype(BF)
+
+
+def sums(place, parts, hid, back_g, back_u, grad, mixed, mix_sum):
+    rows = len(hid)
+    cols = hid[0].shape[0]
+    size = mix_sum[0].shape[-1]
+    high = hid[0].shape[1] // parts
+    return pl.pallas_call(
+        functools.partial(sums_kernel, rows, parts),
+        out_shape=[shape_of((parts // 2, 2 * high + 16, size))] * 2,
+        in_specs=[SM] + [VM] * (6 * rows),
+        out_specs=[VM] * 2,
+        scratch_shapes=[pltpu.VMEM((cols, cols), F)],
+        compiler_params=PARAMS,
+        name="sums",
+    )(place, *hid, *back_g, *back_u, *grad, *mixed, *mix_sum)
+
+
+def unpack_kernel(n, scales, place, *refs):
+    held = refs[:4]
+    gate, up, rows, mix_g, mix_u, cols_out, lines = refs[4:]
+    local = mix_g.shape[1]
+    at, core, x = place[0], place[2], place[3]
+    high = gate.shape[0] // (4 * n)
+    half = rows.shape[1]
+    for i in range(4):
+        base = lax.rem(core + i // 2, 2) * 2 * n + lax.rem(x + i % 2, 2) * n
+        for j in range(n):
+            p = base + lax.rem(at + n - j, n)
+            spot = pl.ds(pl.multiple_of(p * high, high), high)
+            gate[spot, :] = held[i][j, :high, :].astype(F) * scales[1]
+            up[spot, :] = held[i][j, high : 2 * high, :].astype(F) * scales[1]
+            tail = held[i][j, 2 * high :, :].astype(F)
+            where = pl.multiple_of(p * 16, 16)
+            rows[pl.ds(where, 8), :] = tail[:8, :half] * scales[0]
+            rows[pl.ds(where + 8, 8), :] = tail[:8, half:] * scales[0]
+            for w, out in enumerate((mix_g, mix_u)):
+                spot = (pl.ds(p // (2 * local), 1), pl.ds(lax.rem(p // 2, local), 1), slice(None))
+                out[spot] = tail[None, 8 + w : 9 + w, :] * scales[1]
+            lines[pl.ds(p, 1), :] = tail[10:11, :] + tail[11:12, :]
+    total = jnp.sum(lines[...], axis=0, keepdims=True) * scales[2]
+    count = cols_out.shape[0]
+    for r in range(count):
+        cols_out[r : r + 1, :] = total[:, r * count : (r + 1) * count]
+
+
+def unpack(n, rows, local, scales, place, held, cols):
+    deep, size = held[0].shape[1:]
+    high = (deep - 16) // 2
+    return pl.pallas_call(
+        functools.partial(unpack_kernel, n, scales),
+        out_shape=[shape_of((4 * n * high, size), F)] * 2
+        + [shape_of((cols, cols), F)]
+        + [shape_of((2 * local, local, size), F)] * 2
+        + [shape_of((n * rows, n * rows), F)],
+        in_specs=[SM] + [VM] * 4,
+        out_specs=[VM] * 6,
+        scratch_shapes=[pltpu.VMEM((4 * n, size), F)],
+        compiler_params=PARAMS,
+        name="unpack",
+    )(place, *held)
+
+
+def finish_kernel(*refs):
+    grads, (back, out) = refs[:-2], refs[-2:]
+    n, rows, cw = back.shape[:3]
+    for i in range(n):
+        spot = slice(i * cw, (i + 1) * cw)
+        for h in range(rows):
+            out[h, spot, :] = (grads[h][spot, :].astype(F) + back[i, h].astype(F)).astype(BF)
+
+
+def finish(grads, back):
+    cols, width = grads[0].shape
+    n, rows, cw = back.shape[:3]
+    lanes = 512
+    return pl.pallas_call(
+        finish_kernel,
+        out_shape=shape_of((rows, cols, width)),
+        grid=(width // lanes,),
+        in_specs=[pl.BlockSpec((cols, lanes), lambda j: (0, j))] * rows
+        + [pl.BlockSpec((n, rows, cw, lanes), lambda j: (0, 0, 0, j))],
+        out_specs=pl.BlockSpec((rows, cols, lanes), lambda j: (0, 0, j)),
+        name="finish",
+    )(*grads, back)
+
+
+def shifted(value, by, n):
+    return lax.ppermute(value, "seq", [(i, (i + by) % n) for i in range(n)])
+
+
+def swapped(value, axis, bit, n):
+    return lax.ppermute(value, axis, [(i, i ^ bit) for i in range(n)])
+
+
+def traded(value):
+    return lax.all_to_all(value, "seq", split_axis=0, concat_axis=0, tiled=True)
+
+
+def pick(value, index):
+    return lax.dynamic_index_in_dim(value, index, 0, keepdims=False)
+
+
+def add(*values):
+    return sum(value.astype(F) for value in values).astype(BF)
+
+
+def two_lines(line):
+    upper = line.astype(BF)
+    return upper, (line - upper.astype(F)).astype(BF)
+
+
+def reduce_parts(kept, sent, early, later, cols_sum, place_at, n):
+    seq_at, x = place_at
+    deep, size = kept.shape[1:]
+    sent, _ = lax.optimization_barrier((sent, early))
+    got = swapped(sent, "dp", 1, 4)
+    halves = add(kept, got).reshape(2, n, deep, size)
+    got = swapped(pick(halves, 1 - x), "dp", 2, 4)
+    fours = add(pick(halves, x), got)
+    got = [shifted(pick(fours, lax.rem(seq_at + i, n)), i, n) for i in range(1, n)]
+    got, _ = lax.optimization_barrier((got, later))
+    mine = add(pick(fours, seq_at), *got)
+    tail = mine[deep - 16 :]
+    count = cols_sum.size
+    line = jnp.pad(cols_sum.reshape(1, count), ((0, 0), (0, size - count)))
+    blank = jnp.zeros((4, size), BF)
+    tail = jnp.concatenate([tail[:10], *two_lines(line), blank], axis=0)
+    other = swapped(tail, "chan", 1, 2)
+    both = tail.astype(F) + other.astype(F)
+    lines = two_lines(both[10:11] + both[11:12])
+    tail = jnp.concatenate([both[:8].astype(BF), tail[8:10], *lines, blank], axis=0)
+    mine = jnp.concatenate([mine[: deep - 16], tail], axis=0)
+    held = jnp.stack([mine] + [shifted(mine, i, n) for i in range(1, n)])
+    return held, swapped(held, "dp", 2, 4), swapped(held, "dp", 1, 4)
+
+
+def block_body(inputs, cotangent, rows_in, cols_mix, blocks_gate, blocks_up, mix_gate, mix_up):
+    n = lax.axis_size("seq")
+    rows, cols, width = inputs.shape[1:]
+    local, size = blocks_gate.shape[:2]
+    cw = cols // n
+    seq_at, chan_at, dp_at = lax.axis_index("seq"), lax.axis_index("chan"), lax.axis_index("dp")
+    core, x = lax.rem(dp_at, 2), dp_at // 2
+    place = jnp.stack([seq_at, chan_at, core, x]).astype(jnp.int32)
+    values, cot = inputs[0], cotangent[0]
+    ahead, behind = mix_tables(cols_mix, rows, cw)
+
+    def relative(table):
+        turned = jnp.roll(table, (local, local), (0, 1))
+        table = jnp.where(chan_at == 0, table, turned).astype(F)
+        return jnp.broadcast_to(table[:, :, None, :], table.shape[:2] + (8, size))
+
+    x_cols = traded(values.reshape(rows, n, cw, width).transpose(1, 0, 2, 3))
+    cot_oth = swapped(cot, "chan", 1, 2)
+    lent = jnp.where(core == 0, blocks_gate, blocks_up)
+    lent, _ = lax.optimization_barrier((lent, cot_oth))
+    lent = swapped(lent, "chan", 1, 2)
+    lent_too = swapped(lent, "dp", 1, 4)
+    gate_oth = jnp.where(core == 0, lent, lent_too)
+    up_oth = jnp.where(core == 0, lent_too, lent)
+    weights = (blocks_gate, gate_oth, blocks_up, up_oth)
+    mixes = (relative(mix_gate), relative(mix_up))
+
+    x_cols, ahead, behind, mixes, cot_oth = lax.optimization_barrier(
+        (x_cols, ahead, behind, mixes, cot_oth)
+    )
+    parts = column_mix(ahead, x_cols.reshape(n * rows * cw, width))
+    mixed = [traded(part.reshape(n, cw, width)).reshape(cols, width) for part in parts]
+    hidden = [hidden_row(rows_in, values, h, mixed[h]) for h in range(rows)]
+    leaving = list(hidden)
+    leaving[0], _ = lax.optimization_barrier((leaving[0], lent))
+    others = [swapped(hid, "chan", 1, 2) for hid in leaving]
+    others[0], hidden[-1] = lax.optimization_barrier((others[0], hidden[-1]))
+    grads, back_g, back_u, mix_sum, pieces = [], [], [], [], []
+    for h in range(rows):
+        got = channel_row(h, hidden[h], others[h], cot, cot_oth, weights, mixes, rows_in)
+        for held, value in zip((grads, back_g, back_u, pieces, mix_sum), got):
+            held.append(value)
+        if h == 0:
+            pieces[0], others[-1] = lax.optimization_barrier((pieces[0], others[-1]))
+        pieces[h] = traded(pieces[h].reshape(n, cw, width))
+    kept, sent = sums(place, 4 * n, hidden, back_g, back_u, grads, mixed, mix_sum)
+    flat = [piece.reshape(cols, width) for piece in pieces]
+    turned = column_back(behind, flat)
+    back = traded(turned.reshape(n, rows, cw, width))
+    cols_sum = column_sum(x_cols, pieces)
+    cols_sum = cols_sum.reshape(n * rows, n * rows, cw).sum(-1)
+    batch_all = lax.axis_size("dp")
+    width_all = width * lax.axis_size("chan")
+    rows_scale = 1.0 / math.sqrt(batch_all * rows * n * width_all)
+    cols_scale = 1.0 / math.sqrt(batch_all * cols * width_all)
+    block_scale = 1.0 / math.sqrt(batch_all * rows * n * cols)
+    held, by_x, by_core = reduce_parts(kept, sent, pieces[0], turned, cols_sum, (seq_at, x), n)
+    input_grad = finish(grads, back)
+    by_x, input_grad = lax.optimization_barrier((by_x, input_grad))
+    gate_sum, up_sum, rows_sum, mix_g, mix_u, cols_sum = unpack(
+        n,
+        rows,
+        local,
+        (rows_scale, block_scale, cols_scale),
+        place,
+        (held, by_x, by_core, swapped(by_x, "dp", 1, 4)),
+        cols,
+    )
+    return (
+        input_grad[None],
+        rows_sum,
+        cols_sum,
+        gate_sum.reshape(local, size, size),
+        up_sum.reshape(local, size, size),
+        mix_g,
+        mix_u,
+    )
 
 
 def column_keep(segment, cols_mix):
@@ -11,7 +478,6 @@
         "er,brcd->becd", cols_mix, segment, preferred_element_type=jnp.float32
     ).astype(jnp.bfloat16)
     return (segment, mixed)
-
 
 def body(inputs, cotangent, rows_in, cols_mix, blocks_gate, blocks_up, mix_gate, mix_up):
     batch_dev, rows_dev, cols_all, width_dev = inputs.shape
@@ -141,4 +607,6 @@
         P(None, "chan", None),
         P(None, "chan", None),
     )
-    return jax.shard_map(body, mesh=mesh, in_specs=in_specs, out_specs=out_specs, check_vma=False)
+    sizes = dict(mesh.shape)
+    fits = sizes["dp"] == 4 and sizes["seq"] == 4 and sizes["chan"] == 2
+    return jax.shard_map(block_body if fits else body, mesh=mesh, in_specs=in_specs, out_specs=out_specs, check_vma=False)

time: 620 us -> 212 us (0.34)
  blocking collectives: 217 us -> 0 us
  waiting for transfers between devices: 248 us -> 91 us
  local copies, waits for them, and re-layouts: 72.1 us -> 17.3 us
  starting transfers between devices: 9.24 us -> 52.9 us
  matrix products: 41.5 us -> 0 us
  Pallas kernels: 0 us -> 36 us
  between operations: 14.5 us -> 1 us
    psum x2 -> x0, blocking collectives: 157 us -> none  [the longest x1 120 us: body(): lax.psum((blocks_gate_sum, blocks_up_sum, mix_gate_sum, mix_up_sum), ('dp...]
    psum x2 -> x0, waiting for transfers between devices: 122 us -> none  [the longest x1 122 us: body(): lax.psum((rows_sum, cols_sum), ('dp', 'seq', 'chan'))]
    all_gather x4 -> x0, waiting for transfers between devices: 101 us -> none  [the longest x1 28.8 us: body(): lax.all_gather(up_grad, 'chan', axis=3, tiled=True)]
    ppermute x0 -> x17, waiting for transfers between devices: none -> 68.6 us  [the longest x11 42.9 us: swapped(): return lax.ppermute(value, axis, [(i, i ^ bit) for i in range(n)])]
    all_to_all x2 -> x0, blocking collectives: 59.6 us -> none  [the longest x1 31.8 us: body(): lax.all_to_all(first, 'seq', split_axis=2, concat_axis=1, tiled=True)]
    dot_general x18 -> x0, matrix products: 41.5 us -> none  [the longest x1 5.46 us: body(): jnp.einsum('brcmj,brckj->mkj', gate_all, gate_mid, preferred_element_type...]
    pallas_call x0 -> x10, Pallas kernels: none -> 36 us  [the longest x2 16.3 us: channel_row(): pl.pallas_call(channel_kernel, out_shape=[shape_of((cols, width))] * 4 +...]
    ppermute x0 -> x17, starting transfers between devices: none -> 25.1 us  [the longest x6 15.4 us: shifted(): return lax.ppermute(value, 'seq', [(i, (i + by) % n) for i in range(n)])]
  transfers between devices with their start and end apart: 8 -> 23, of which waited for: 6 -> 12; matrix products, arithmetic and copies ran while one was open for 12% -> 8% of each run, Pallas kernels for 0% -> 16%
where the time goes in v2:
time: 212 us; the launch traced here: 211 us
  waiting for transfers between devices  91 us (43%)
  starting transfers between devices  52.9 us (25%)
  Pallas kernels  36 us (17%)
  local copies, waits for them, and re-layouts  17.3 us (8%)
  other arithmetic  13 us (6%)
    ppermute x11, waiting for transfers between devices, swapped(): return lax.ppermute(value, axis, [(i, i ^ bit) for i in range(n)])  42.9 us
    all_to_all x6, starting transfers between devices, traded(): return lax.all_to_all(value, 'seq', split_axis=0, concat_axis=0, tiled=True)  27.8 us
    ppermute x6, waiting for transfers between devices, shifted(): return lax.ppermute(value, 'seq', [(i, (i + by) % n) for i in range(n)])  25.7 us
    all_to_all x6, waiting for transfers between devices, traded(): return lax.all_to_all(value, 'seq', split_axis=0, concat_axis=0, tiled=True)  22.4 us
    pallas_call x2, Pallas kernels, channel_row(): pl.pallas_call(channel_kernel, out_shape=[shape_of((cols, width))] * 4 +...  16.3 us
    ppermute x6, starting transfers between devices, shifted(): return lax.ppermute(value, 'seq', [(i, (i + by) % n) for i in range(n)])  15.4 us
    ppermute x11, starting transfers between devices, swapped(): return lax.ppermute(value, axis, [(i, i ^ bit) for i in range(n)])  9.78 us
    unnamed x56, local copies, waits for them, and re-layouts  9.56 us
  transfers between devices with their start and end apart: 23, of which 12 were waited for; matrix products, arithmetic and copies ran while one was open for 8% of the time, Pallas kernels for 16%

profile of v2, /device:TPU:0, one launch (start us, length us, event | category | flops | bytes accessed | tf_op | source)
XLA Modules:
  0.0 211.2 jit_solution(13969436748789082742)
XLA Ops:
  0.6 2.3 %copy.21 = bf16[2,4,64,1024]{3,2,0,1:T(8,128)(2,1)} copy(bf16[2,4,64,1024]{3,2,1,0:T(8,128)(2,1)} %bitcast.59) | data formatting | bytes 2097152 | tf_op jit(solution)/shard_map/reshape;squeeze | solution.py:413
  2.9 6.4 %all-to-all-start = ((bf16[4,2,64,1024]{3,2,1,0:T(8,128)(2,1)}), bf16[4,2,64,1024]{3,2,1,0:T(8,128)(2,1)S(1)}, u32[]{:S(2)}, u32[]{:S(2)}) async-start(bf16[4,2,64,1024]{3,2,1,0:T(8,128)(2,1)} %bitcast.65), calls=%async_computation | async-start | bytes 2097152 | tf_op jit(solution)/shard_map/all_to_all | solution.py:356
  9.4 1.5 collective-permute-start
  11.0 0.1 copy.18
  11.1 0.5 broadcast_select_fusion.4
  11.6 1.1 broadcast_select_fusion.6
  12.7 1.4 select_n.111
  14.1 2.1 select_n.109
  16.2 1.0 select_n.115
  17.3 0.3 select_n.113
  17.7 1.8 pad_maximum_fusion.1.table
  19.5 0.9 pad_maximum_fusion.2.table
  20.3 2.3 %broadcast_select_fusion.2 = bf16[2,512,512]{2,1,0:T(8,128)(2,1)} fusion(bf16[2,512,512]{2,1,0:T(8,128)(2,1)} %refs_4_.3, bf16[2,512,512]{2,1,0:T(8,128)(2,1)} %refs_6_.3, pred[]{:T(512)S(6)} %eq.25), kind=kLoop, calls=%fused_computation.6 | loop fusion | flops 524288 | bytes 3145729 | tf_op jit(solution)/shard_map/jit(_where)/select_n | solution.py:415
  22.6 11.4 %collective-permute-done.refs_3_ = bf16[2,256,1024]{2,1,0:T(8,128)(2,1)} collective-permute-done((bf16[2,256,1024]{2,1,0:T(8,128)(2,1)S(1)}, bf16[2,256,1024]{2,1,0:T(8,128)(2,1)}, u32[]{:S(2)}, u32[]{:S(2)}) %collective-permute-start) | collective-permute-done | bytes 1048608 | tf_op jit(solution)/shard_map/ppermute | solution.py:352
  34.1 1.5 collective-permute-start.1
  35.8 0.9 copy-done
  36.7 2.8 %column_mix.1 = (bf16[256,1024]{1,0:T(8,128)(2,1)}, bf16[256,1024]{1,0:T(8,128)(2,1)}) custom-call(bf16[2,256,512]{2,1,0:T(8,128)(2,1)} %pad_maximum_fusion.1.table, bf16[512,1024]{1,0:T(8,128)(2,1)} %bitcast.48), custom_call_target="tpu_custom_call" | custom-call | tf_op jit(solution)/shard_map/column_mix/pallas_call | solution.py:47
  39.5 4.8 %all-to-all-start.1 = ((bf16[4,64,1024]{2,1,0:T(8,128)(2,1)}), bf16[4,64,1024]{2,1,0:T(8,128)(2,1)S(1)}, u32[]{:S(2)}, u32[]{:S(2)}) async-start(bf16[4,64,1024]{2,1,0:T(8,128)(2,1)} %bitcast.69), calls=%async_computation.1 | async-start | bytes 1048576 | tf_op jit(solution)/shard_map/all_to_all | solution.py:356
  44.3 13.8 %collective-permute-done.1 = bf16[2,512,512]{2,1,0:T(8,128)(2,1)} collective-permute-done((bf16[2,512,512]{2,1,0:T(8,128)(2,1)}, bf16[2,512,512]{2,1,0:T(8,128)(2,1)}, u32[]{:S(2)}, u32[]{:S(2)}) %collective-permute-start.1) | collective-permute-done | bytes 1048608 | tf_op jit(solution)/shard_map/ppermute | solution.py:352
  58.1 4.5 %all-to-all-start.2 = ((bf16[4,64,1024]{2,1,0:T(8,128)(2,1)}), bf16[4,64,1024]{2,1,0:T(8,128)(2,1)S(1)}, u32[]{:S(2)}, u32[]{:S(2)}) async-start(bf16[4,64,1024]{2,1,0:T(8,128)(2,1)} %bitcast.68), calls=%async_computation.2 | async-start | bytes 1048576 | tf_op jit(solution)/shard_map/all_to_all | solution.py:356
  62.6 2.3 %hidden_row.2.refs_0_ = bf16[256,1024]{1,0:T(8,128)(2,1)} custom-call(bf16[256,256]{1,0:T(8,128)(2,1)} %refs_10_.3, bf16[2,256,1024]{2,1,0:T(8,128)(2,1)} %bitcast.60, bf16[256,1024]{1,0:T(8,128)(2,1)} %bitcast.49), custom_call_target="tpu_custom_call" | custom-call | tf_op jit(solution)/shard_map/hidden_row/pallas_call | solution.py:126
  64.9 1.5 collective-permute-start.2
  66.4 11.3 %all-to-all-done.2 = bf16[4,64,1024]{2,1,0:T(8,128)(2,1)S(1)} async-done(((bf16[4,64,1024]{2,1,0:T(8,128)(2,1)}), bf16[4,64,1024]{2,1,0:T(8,128)(2,1)S(1)}, u32[]{:S(2)}, u32[]{:S(2)}) %all-to-all-start.2) | async-done | bytes 524320 | tf_op jit(solution)/shard_map/all_to_all | solution.py:356
  77.8 0.8 copy-done.4
  78.6 2.3 %hidden_row.3.refs_0_.refs_1_ = bf16[256,1024]{1,0:T(8,128)(2,1)} custom-call(bf16[256,256]{1,0:T(8,128)(2,1)} %refs_10_.3, bf16[2,256,1024]{2,1,0:T(8,128)(2,1)} %bitcast.61, bf16[256,1024]{1,0:T(8,128)(2,1)} %bitcast.51), custom_call_target="tpu_custom_call" | custom-call | tf_op jit(solution)/shard_map/hidden_row/pallas_call | solution.py:126
  80.9 1.5 collective-permute-start.4
  82.5 3.0 %broadcast_select_fusion = (bf16[2,512,512]{2,1,0:T(8,128)(2,1)}, bf16[2,512,512]{2,1,0:T(8,128)(2,1)}) fusion(bf16[2,512,512]{2,1,0:T(8,128)(2,1)} %collective-permute-done.3, bf16[2,512,512]{2,1,0:T(8,128)(2,1)} %collective-permute-done.1, pred[]{:T(512)S(6)} %eq.25), kind=kLoop, calls=%fused_computation.4 | loop fusion | flops 1048576 | bytes 4194305 | tf_op jit(solution)/shard_map/jit(_where)/select_n | solution.py:420
  85.5 7.7 %channel_row.2 = (bf16[256,1024]{1,0:T(8,128)(2,1)S(1)}, bf16[256,1024]{1,0:T(8,128)(2,1)S(1)}, bf16[256,1024]{1,0:T(8,128)(2,1)S(1)}, bf16[256,1024]{1,0:T(8,128)(2,1)S(1)}, f32[2,4,2,8,512]{4,3,2,1,0:T(8,128)S(1)}) custom-call(bf16[256,1024]{1,0:T(8,128)(2,1)S(1)} %copy-done.8, bf16[256,1024]{1,0:T(8,128)(2,1)S(1)} %collective-permute-done.2.refs_1_, ...), custom_call_target="tpu_custom_call" | custom-call | tf_op jit(solution)/shard_map/channel_row/pallas_call | solution.py:205
  93.2 0.8 copy-done.12
  93.9 0.8 copy-done.15
  94.7 0.8 copy-done.17
  95.5 0.8 copy-done.19
  96.3 0.8 copy-done.20
  97.1 3.5 %all-to-all-start.3 = ((bf16[4,64,1024]{2,1,0:T(8,128)(2,1)}), bf16[4,64,1024]{2,1,0:T(8,128)(2,1)S(1)}, u32[]{:S(2)}, u32[]{:S(2)}) async-start(bf16[4,64,1024]{2,1,0:T(8,128)(2,1)} %bitcast.58), calls=%async_computation.3 | async-start | bytes 1048576 | tf_op jit(solution)/shard_map/all_to_all | solution.py:356
  100.7 1.0 copy-done.21
  101.8 8.6 %channel_row.3 = (bf16[256,1024]{1,0:T(8,128)(2,1)S(1)}, bf16[256,1024]{1,0:T(8,128)(2,1)S(1)}, bf16[256,1024]{1,0:T(8,128)(2,1)S(1)}, bf16[256,1024]{1,0:T(8,128)(2,1)}, f32[2,4,2,8,512]{4,3,2,1,0:T(8,128)S(1)}) custom-call(bf16[256,1024]{1,0:T(8,128)(2,1)S(1)} %copy-done.9, bf16[256,1024]{1,0:T(8,128)(2,1)S(1)} %copy-done.21, ...), custom_call_target="tpu_custom_call" | custom-call | tf_op jit(solution)/shard_map/channel_row/pallas_call | solution.py:205
  110.4 3.3 %sums.1 = (bf16[8,144,512]{2,1,0:T(8,128)(2,1)}, bf16[8,144,512]{2,1,0:T(8,128)(2,1)}) custom-call(s32[4]{0:T(128)S(1)} %pad_add_fusion.place, bf16[256,1024]{1,0:T(8,128)(2,1)S(1)} %copy-done.8, bf16[256,1024]{1,0:T(8,128)(2,1)S(1)} %copy-done.9, bf16[256,1024]{1,0:T(8,128)(2,1)S(1)} %copy-done.16, bf16[256,1024]{1,0:T(8,128)(2,1)S(1)} %get-tuple-element.59.refs_3_, ...), custom_call_target="tpu_custom_call" | custom-call | tf_op jit(solution)/shard_map/sums/pallas_call | solution.py:267
  113.8 0.8 copy-done.14
  114.6 5.0 %all-to-all-start.4 = ((bf16[4,64,1024]{2,1,0:T(8,128)(2,1)}), bf16[4,64,1024]{2,1,0:T(8,128)(2,1)S(1)}, u32[]{:S(2)}, u32[]{:S(2)}) async-start(bf16[4,64,1024]{2,1,0:T(8,128)(2,1)} %bitcast.24), calls=%async_computation.4 | async-start | bytes 1048576 | tf_op jit(solution)/shard_map/all_to_all | solution.py:356
  119.6 1.6 add_convert_fusion
  121.2 1.0 copy-done.22
  122.3 1.6 collective-permute-start.6
  123.8 10.9 %all-to-all-done.4.refs_1_ = bf16[4,64,1024]{2,1,0:T(8,128)(2,1)S(1)} async-done(((bf16[4,64,1024]{2,1,0:T(8,128)(2,1)}), bf16[4,64,1024]{2,1,0:T(8,128)(2,1)S(1)}, u32[]{:S(2)}, u32[]{:S(2)}) %all-to-all-start.4) | async-done | bytes 524320 | tf_op jit(solution)/shard_map/all_to_all | solution.py:356
  134.8 0.8 column_sum.1
  135.8 2.1 %collective-permute-done.6 = bf16[4,144,512]{2,1,0:T(8,128)(2,1)} collective-permute-done((bf16[4,144,512]{2,1,0:T(8,128)(2,1)S(1)}, bf16[4,144,512]{2,1,0:T(8,128)(2,1)}, u32[]{:S(2)}, u32[]{:S(2)}) %collective-permute-start.6) | collective-permute-done | bytes 589856 | tf_op jit(solution)/shard_map/ppermute | solution.py:352
  137.9 1.4 fusion
  139.3 1.8 collective-permute-start.7
  141.1 2.4 %collective-permute-start.8 = (bf16[144,512]{1,0:T(8,128)(2,1)S(1)}, bf16[144,512]{1,0:T(8,128)(2,1)S(1)}, u32[]{:S(2)}, u32[]{:S(2)}) collective-permute-start(bf16[144,512]{1,0:T(8,128)(2,1)S(1)} %get-tuple-element.86), channel_id=1, source_target_pairs={{0,4},{2,6},{4,0},{6,2},{1,5},{3,7},{5,1},{7,3},{8,12},{10,14},{12... | collective-permute-start | bytes 442376 | tf_op jit(solution)/shard_map/ppermute | solution.py:348
  143.5 1.5 collective-permute-start.9
  145.0 2.9 %column_back.1 = bf16[512,1024]{1,0:T(8,128)(2,1)} custom-call(bf16[2,512,256]{2,1,0:T(8,128)(2,1)} %pad_maximum_fusion.2.table, bf16[256,1024]{1,0:T(8,128)(2,1)} %bitcast.53, bf16[256,1024]{1,0:T(8,128)(2,1)} %bitcast.54), custom_call_target="tpu_custom_call" | custom-call | tf_op jit(solution)/shard_map/column_back/pallas_call | solution.py:72
  147.9 3.5 %all-to-all-start.5 = ((bf16[4,2,64,1024]{3,2,1,0:T(8,128)(2,1)}), bf16[4,2,64,1024]{3,2,1,0:T(8,128)(2,1)S(1)}, u32[]{:S(2)}, u32[]{:S(2)}) async-start(bf16[4,2,64,1024]{3,2,1,0:T(8,128)(2,1)} %bitcast.64), calls=%async_computation.5 | async-start | bytes 2097152 | tf_op jit(solution)/shard_map/all_to_all | solution.py:356
  151.4 1.3 collective-permute-done.8
  152.9 0.6 collective-permute-start.10
  153.5 3.2 %collective-permute-done.10 = bf16[16,512]{1,0:T(8,128)(2,1)S(1)} collective-permute-done((bf16[16,512]{1,0:T(8,128)(2,1)S(1)}, bf16[16,512]{1,0:T(8,128)(2,1)S(1)}, u32[]{:S(2)}, u32[]{:S(2)}) %collective-permute-start.10) | collective-permute-done | bytes 16416 | tf_op jit(solution)/shard_map/ppermute | solution.py:352
  156.8 8.1 %collective-permute-start.13 = (bf16[144,512]{1,0:T(8,128)(2,1)S(1)}, bf16[144,512]{1,0:T(8,128)(2,1)S(1)}, u32[]{:S(2)}, u32[]{:S(2)}) collective-permute-start(bf16[144,512]{1,0:T(8,128)(2,1)S(1)} %concatenate.25), channel_id=1, source_target_pairs={{0,6},{2,0},{4,2},{6,4},{1,7},{3,1},{5,3},{7,5},{8,14},{10,8},{12,... | collective-permute-start | bytes 442376 | tf_op jit(solution)/shard_map/ppermute | solution.py:348
  164.9 1.6 collective-permute-start.12
  166.5 6.3 %collective-permute-done.13 = bf16[144,512]{1,0:T(8,128)(2,1)S(1)} collective-permute-done((bf16[144,512]{1,0:T(8,128)(2,1)S(1)}, bf16[144,512]{1,0:T(8,128)(2,1)S(1)}, u32[]{:S(2)}, u32[]{:S(2)}) %collective-permute-start.13) | collective-permute-done | bytes 147488 | tf_op jit(solution)/shard_map/ppermute | solution.py:348
  172.8 18.1 %collective-permute-done.12 = bf16[144,512]{1,0:T(8,128)(2,1)S(1)} collective-permute-done((bf16[144,512]{1,0:T(8,128)(2,1)S(1)}, bf16[144,512]{1,0:T(8,128)(2,1)S(1)}, u32[]{:S(2)}, u32[]{:S(2)}) %collective-permute-start.12) | collective-permute-done | bytes 147488 | tf_op jit(solution)/shard_map/ppermute | solution.py:348
  191.0 1.6 collective-permute-start.14
  192.6 1.0 copy-done.23
  193.5 2.4 %finish.1 = bf16[2,256,1024]{2,1,0:T(8,128)(2,1)} custom-call(bf16[256,1024]{1,0:T(8,128)(2,1)} %copy-done.12, bf16[256,1024]{1,0:T(8,128)(2,1)} %copy-done.14, bf16[4,2,64,1024]{3,2,1,0:T(8,128)(2,1)} %copy-done.23), custom_call_target="tpu_custom_call" | custom-call | tf_op jit(solution)/shard_map/finish/pallas_call | solution.py:336
  196.0 10.4 %collective-permute-done.14.refs_1_ = bf16[4,144,512]{2,1,0:T(8,128)(2,1)S(1)} collective-permute-done((bf16[4,144,512]{2,1,0:T(8,128)(2,1)S(1)}, bf16[4,144,512]{2,1,0:T(8,128)(2,1)S(1)}, u32[]{:S(2)}, u32[]{:S(2)}) %collective-permute-start.14) | collective-permute-done | bytes 589856 | tf_op jit(solution)/shard_map/ppermute | solution.py:352
  206.3 2.0 collective-permute-done.16.refs_3_
  208.3 2.9 %unpack.1 = (f32[1024,512]{1,0:T(8,128)}, f32[1024,512]{1,0:T(8,128)}, f32[256,256]{1,0:T(8,128)}, f32[4,2,512]{2,1,0:T(2,128)}, f32[4,2,512]{2,1,0:T(2,128)}, /*index=5*/f32[8,8]{1,0:T(8,128)}) custom-call(s32[4]{0:T(128)S(1)} %pad_add_fusion.place, bf16[4,144,512]{2,1,0:T(8,128)(2,1)S(1)} %pad_maximum_fusion.refs_0_, ...), custom_call_target="tpu_custom_call" | custom-call | tf_op jit(solution)/shard_map/unpack/pallas_call | solution.py:309
  (92 shorter events, 1.2 us)
Async XLA Ops:
  2.9 6.5 %copy-start.10 = (bf16[1,2,256,1024]{3,2,1,0:T(8,128)(2,1)S(1)}, bf16[1,2,256,1024]{3,2,1,0:T(8,128)(2,1)}, u32[]{:S(2)}) copy-start(bf16[1,2,256,1024]{3,2,1,0:T(8,128)(2,1)} %param.9) | copy-start | bytes 3145732
  2.9 8.0 %copy-start.27 = (bf16[8,8]{1,0:T(8,128)(2,1)S(1)}, bf16[8,8]{1,0:T(8,128)(2,1)}, u32[]{:S(2)}) copy-start(bf16[8,8]{1,0:T(8,128)(2,1)} %param.11) | copy-start | bytes 388
  2.9 32.8 %all-to-all-start = ((bf16[4,2,64,1024]{3,2,1,0:T(8,128)(2,1)}), bf16[4,2,64,1024]{3,2,1,0:T(8,128)(2,1)S(1)}, u32[]{:S(2)}, u32[]{:S(2)}) async-start(bf16[4,2,64,1024]{3,2,1,0:T(8,128)(2,1)} %bitcast.65), calls=%async_computation | async-start | bytes 2097152 | tf_op jit(solution)/shard_map/all_to_all | solution.py:356
  9.4 24.7 %collective-permute-start = (bf16[2,256,1024]{2,1,0:T(8,128)(2,1)S(1)}, bf16[2,256,1024]{2,1,0:T(8,128)(2,1)}, u32[]{:S(2)}, u32[]{:S(2)}) collective-permute-start(bf16[2,256,1024]{2,1,0:T(8,128)(2,1)S(1)} %bitcast.55), channel_id=1, source_target_pairs={{0,1},{1,0},{2,3},{3,2},{4,5},{5,4},{6,7},{7,6},{8,9},{9,8},{10,11... | collective-permute-start | bytes 3145736 | tf_op jit(solution)/shard_map/ppermute | solution.py:352
  14.1 3.5 %copy-start.25 = (bf16[4,4,512]{2,1,0:T(4,128)(2,1)S(1)}, bf16[4,4,512]{2,1,0:T(4,128)(2,1)}, u32[]{:S(2)}) copy-start(bf16[4,4,512]{2,1,0:T(4,128)(2,1)} %param.15) | copy-start | bytes 49156
  17.2 2.2 %copy-start.24 = (bf16[1,512,256]{2,1,0:T(8,128)(2,1)S(1)}, bf16[1,512,256]{2,1,0:T(8,128)(2,1)}, u32[]{:S(2)}) copy-start(bf16[1,512,256]{2,1,0:T(8,128)(2,1)} %select_n.115) | copy-start | bytes 786436
  17.6 2.7 %copy-start.26 = (bf16[4,4,512]{2,1,0:T(4,128)(2,1)S(1)}, bf16[4,4,512]{2,1,0:T(4,128)(2,1)}, u32[]{:S(2)}) copy-start(bf16[4,4,512]{2,1,0:T(4,128)(2,1)} %param.14) | copy-start | bytes 49156
  34.1 24.0 %collective-permute-start.1 = (bf16[2,512,512]{2,1,0:T(8,128)(2,1)}, bf16[2,512,512]{2,1,0:T(8,128)(2,1)}, u32[]{:S(2)}, u32[]{:S(2)}) collective-permute-start(bf16[2,512,512]{2,1,0:T(8,128)(2,1)} %broadcast_select_fusion.2), channel_id=1, source_target_pairs={{0,1},{1,0},{2,3},{3,2},{4,5},{5,4},{6,7},{7,6},{8,9},{9,8},{10,11... | collective-permute-start | bytes 3145736 | tf_op jit(solution)/shard_map/ppermute | solution.py:352
  35.7 1.0 copy-start
  39.5 18.6 %all-to-all-start.1 = ((bf16[4,64,1024]{2,1,0:T(8,128)(2,1)}), bf16[4,64,1024]{2,1,0:T(8,128)(2,1)S(1)}, u32[]{:S(2)}, u32[]{:S(2)}) async-start(bf16[4,64,1024]{2,1,0:T(8,128)(2,1)} %bitcast.69), calls=%async_computation.1 | async-start | bytes 1048576 | tf_op jit(solution)/shard_map/all_to_all | solution.py:356
  58.1 24.3 %collective-permute-start.3 = (bf16[2,512,512]{2,1,0:T(8,128)(2,1)}, bf16[2,512,512]{2,1,0:T(8,128)(2,1)}, u32[]{:S(2)}, u32[]{:S(2)}) collective-permute-start(bf16[2,512,512]{2,1,0:T(8,128)(2,1)} %collective-permute-done.1), channel_id=1, source_target_pairs={{0,8},{8,0},{16,24},{24,16},{1,9},{9,1},{17,25},{25,17},{2,10},{10... | collective-permute-start | bytes 3145736 | tf_op jit(solution)/shard_map/ppermute | solution.py:352
  58.1 4.5 %copy-start.2 = (bf16[4,64,1024]{2,1,0:T(8,128)(2,1)}, bf16[4,64,1024]{2,1,0:T(8,128)(2,1)S(1)}, u32[]{:S(2)}) copy-start(bf16[4,64,1024]{2,1,0:T(8,128)(2,1)S(1)} %all-to-all-done.1) | copy-start | bytes 1572868
  58.1 19.7 %all-to-all-start.2 = ((bf16[4,64,1024]{2,1,0:T(8,128)(2,1)}), bf16[4,64,1024]{2,1,0:T(8,128)(2,1)S(1)}, u32[]{:S(2)}, u32[]{:S(2)}) async-start(bf16[4,64,1024]{2,1,0:T(8,128)(2,1)} %bitcast.68), calls=%async_computation.2 | async-start | bytes 1048576 | tf_op jit(solution)/shard_map/all_to_all | solution.py:356
  64.9 17.5 %collective-permute-start.2 = (bf16[256,1024]{1,0:T(8,128)(2,1)}, bf16[256,1024]{1,0:T(8,128)(2,1)S(1)}, u32[]{:S(2)}, u32[]{:S(2)}) collective-permute-start(bf16[256,1024]{1,0:T(8,128)(2,1)} %hidden_row.2.refs_0_), channel_id=1, source_target_pairs={{0,1},{1,0},{2,3},{3,2},{4,5},{5,4},{6,7},{7,6},{8,9},{9,8},{10,11... | collective-permute-start | bytes 1572872 | tf_op jit(solution)/shard_map/ppermute | solution.py:352
  77.8 0.8 copy-start.4
  80.9 4.5 %copy-start.8 = (bf16[256,1024]{1,0:T(8,128)(2,1)S(1)}, bf16[256,1024]{1,0:T(8,128)(2,1)}, u32[]{:S(2)}) copy-start(bf16[256,1024]{1,0:T(8,128)(2,1)} %hidden_row.2.refs_0_) | copy-start | bytes 1572868
  80.9 4.5 %copy-start.11 = (bf16[256,256]{1,0:T(8,128)(2,1)S(1)}, bf16[256,256]{1,0:T(8,128)(2,1)}, u32[]{:S(2)}) copy-start(bf16[256,256]{1,0:T(8,128)(2,1)} %refs_10_.3) | copy-start | bytes 393220
  80.9 15.4 %collective-permute-start.4 = (bf16[256,1024]{1,0:T(8,128)(2,1)}, bf16[256,1024]{1,0:T(8,128)(2,1)S(1)}, u32[]{:S(2)}, u32[]{:S(2)}) collective-permute-start(bf16[256,1024]{1,0:T(8,128)(2,1)} %hidden_row.3.refs_0_.refs_1_), channel_id=1, source_target_pairs={{0,1},{1,0},{2,3},{3,2},{4,5},{5,4},{6,7},{7,6},{8,9},{9,8},{10,11... | collective-permute-start | bytes 1572872 | tf_op jit(solution)/shard_map/ppermute | solution.py:352
  93.1 0.8 copy-start.12
  93.9 0.8 copy-start.15
  94.7 0.8 copy-start.17
  95.5 0.8 copy-start.19
  96.3 4.4 %copy-start.9 = (bf16[256,1024]{1,0:T(8,128)(2,1)S(1)}, bf16[256,1024]{1,0:T(8,128)(2,1)}, u32[]{:S(2)}) copy-start(bf16[256,1024]{1,0:T(8,128)(2,1)} %hidden_row.3.refs_0_.refs_1_) | copy-start | bytes 1572868
  96.3 0.8 copy-start.20
  97.1 17.5 %all-to-all-start.3 = ((bf16[4,64,1024]{2,1,0:T(8,128)(2,1)}), bf16[4,64,1024]{2,1,0:T(8,128)(2,1)S(1)}, u32[]{:S(2)}, u32[]{:S(2)}) async-start(bf16[4,64,1024]{2,1,0:T(8,128)(2,1)} %bitcast.58), calls=%async_computation.3 | async-start | bytes 1048576 | tf_op jit(solution)/shard_map/all_to_all | solution.py:356
  100.7 1.0 copy-start.21
  101.7 8.7 %copy-start.3 = (bf16[4,64,1024]{2,1,0:T(8,128)(2,1)S(1)}, bf16[4,64,1024]{2,1,0:T(8,128)(2,1)}, u32[]{:S(2)}) copy-start(bf16[4,64,1024]{2,1,0:T(8,128)(2,1)} %copy-done.2) | copy-start | bytes 1572868
  101.7 8.7 %copy-start.5 = (bf16[4,64,1024]{2,1,0:T(8,128)(2,1)S(1)}, bf16[4,64,1024]{2,1,0:T(8,128)(2,1)}, u32[]{:S(2)}) copy-start(bf16[4,64,1024]{2,1,0:T(8,128)(2,1)} %copy-done.4) | copy-start | bytes 1572868
  101.7 8.7 %copy-start.13 = (bf16[256,1024]{1,0:T(8,128)(2,1)S(1)}, bf16[256,1024]{1,0:T(8,128)(2,1)}, u32[]{:S(2)}) copy-start(bf16[256,1024]{1,0:T(8,128)(2,1)} %copy-done.12) | copy-start | bytes 1572868
  101.7 8.7 %copy-start.16 = (bf16[256,1024]{1,0:T(8,128)(2,1)S(1)}, bf16[256,1024]{1,0:T(8,128)(2,1)}, u32[]{:S(2)}) copy-start(bf16[256,1024]{1,0:T(8,128)(2,1)} %copy-done.15) | copy-start | bytes 1572868
  101.8 8.7 %copy-start.18 = (bf16[256,1024]{1,0:T(8,128)(2,1)S(1)}, bf16[256,1024]{1,0:T(8,128)(2,1)}, u32[]{:S(2)}) copy-start(bf16[256,1024]{1,0:T(8,128)(2,1)} %copy-done.17) | copy-start | bytes 1572868
  113.8 0.8 copy-start.14
  114.6 20.1 %copy-start.6 = (bf16[4,64,1024]{2,1,0:T(8,128)(2,1)}, bf16[4,64,1024]{2,1,0:T(8,128)(2,1)S(1)}, u32[]{:S(2)}) copy-start(bf16[4,64,1024]{2,1,0:T(8,128)(2,1)S(1)} %all-to-all-done.3.refs_0_) | copy-start | bytes 1572868
  114.6 5.0 %collective-permute-start.5 = (bf16[8,144,512]{2,1,0:T(8,128)(2,1)}, bf16[8,144,512]{2,1,0:T(8,128)(2,1)S(1)}, u32[]{:S(2)}, u32[]{:S(2)}) collective-permute-start(bf16[8,144,512]{2,1,0:T(8,128)(2,1)} %get-tuple-element.69), channel_id=1, source_target_pairs={{0,8},{8,0},{16,24},{24,16},{1,9},{9,1},{17,25},{25,17},{2,10},{10... | collective-permute-start | bytes 3538952 | tf_op jit(solution)/shard_map/ppermute | solution.py:352
  114.6 20.1 %all-to-all-start.4 = ((bf16[4,64,1024]{2,1,0:T(8,128)(2,1)}), bf16[4,64,1024]{2,1,0:T(8,128)(2,1)S(1)}, u32[]{:S(2)}, u32[]{:S(2)}) async-start(bf16[4,64,1024]{2,1,0:T(8,128)(2,1)} %bitcast.24), calls=%async_computation.4 | async-start | bytes 1048576 | tf_op jit(solution)/shard_map/all_to_all | solution.py:356
  121.2 1.0 copy-start.22
  121.2 13.5 %copy-start.1 = (bf16[4,2,64,1024]{3,2,1,0:T(8,128)(2,1)S(1)}, bf16[4,2,64,1024]{3,2,1,0:T(8,128)(2,1)}, u32[]{:S(2)}) copy-start(bf16[4,2,64,1024]{3,2,1,0:T(8,128)(2,1)} %copy-done) | copy-start | bytes 3145732
  122.3 15.6 %collective-permute-start.6 = (bf16[4,144,512]{2,1,0:T(8,128)(2,1)S(1)}, bf16[4,144,512]{2,1,0:T(8,128)(2,1)}, u32[]{:S(2)}, u32[]{:S(2)}) collective-permute-start(bf16[4,144,512]{2,1,0:T(8,128)(2,1)S(1)} %dynamic-slice_bitcast_fusion), channel_id=1, source_target_pairs={{0,16},{8,24},{16,0},{24,8},{1,17},{9,25},{17,1},{25,9},{2,18},{10... | collective-permute-start | bytes 1769480 | tf_op jit(solution)/shard_map/ppermute | solution.py:352
  134.8 4.5 %copy-start.7 = (bf16[4,64,1024]{2,1,0:T(8,128)(2,1)}, bf16[4,64,1024]{2,1,0:T(8,128)(2,1)S(1)}, u32[]{:S(2)}) copy-start(bf16[4,64,1024]{2,1,0:T(8,128)(2,1)S(1)} %all-to-all-done.4.refs_1_) | copy-start | bytes 1572868
  139.3 12.1 %collective-permute-start.7 = (bf16[144,512]{1,0:T(8,128)(2,1)S(1)}, bf16[144,512]{1,0:T(8,128)(2,1)S(1)}, u32[]{:S(2)}, u32[]{:S(2)}) collective-permute-start(bf16[144,512]{1,0:T(8,128)(2,1)S(1)} %get-tuple-element.87), channel_id=1, source_target_pairs={{0,2},{2,4},{4,6},{6,0},{1,3},{3,5},{5,7},{7,1},{8,10},{10,12},{12... | collective-permute-start | bytes 442376 | tf_op jit(solution)/shard_map/ppermute | solution.py:348
  141.1 11.6 %collective-permute-start.8 = (bf16[144,512]{1,0:T(8,128)(2,1)S(1)}, bf16[144,512]{1,0:T(8,128)(2,1)S(1)}, u32[]{:S(2)}, u32[]{:S(2)}) collective-permute-start(bf16[144,512]{1,0:T(8,128)(2,1)S(1)} %get-tuple-element.86), channel_id=1, source_target_pairs={{0,4},{2,6},{4,0},{6,2},{1,5},{3,7},{5,1},{7,3},{8,12},{10,14},{12... | collective-permute-start | bytes 442376 | tf_op jit(solution)/shard_map/ppermute | solution.py:348
  143.5 9.2 %collective-permute-start.9 = (bf16[144,512]{1,0:T(8,128)(2,1)S(1)}, bf16[144,512]{1,0:T(8,128)(2,1)S(1)}, u32[]{:S(2)}, u32[]{:S(2)}) collective-permute-start(bf16[144,512]{1,0:T(8,128)(2,1)S(1)} %get-tuple-element.85), channel_id=1, source_target_pairs={{0,6},{2,0},{4,2},{6,4},{1,7},{3,1},{5,3},{7,5},{8,14},{10,8},{12,... | collective-permute-start | bytes 442376 | tf_op jit(solution)/shard_map/ppermute | solution.py:348
  147.9 44.7 %all-to-all-start.5 = ((bf16[4,2,64,1024]{3,2,1,0:T(8,128)(2,1)}), bf16[4,2,64,1024]{3,2,1,0:T(8,128)(2,1)S(1)}, u32[]{:S(2)}, u32[]{:S(2)}) async-start(bf16[4,2,64,1024]{3,2,1,0:T(8,128)(2,1)} %bitcast.64), calls=%async_computation.5 | async-start | bytes 2097152 | tf_op jit(solution)/shard_map/all_to_all | solution.py:356
  152.9 3.8 %collective-permute-start.10 = (bf16[16,512]{1,0:T(8,128)(2,1)S(1)}, bf16[16,512]{1,0:T(8,128)(2,1)S(1)}, u32[]{:S(2)}, u32[]{:S(2)}) collective-permute-start(bf16[16,512]{1,0:T(8,128)(2,1)S(1)} %pad_maximum_fusion.5), channel_id=1, source_target_pairs={{0,1},{1,0},{2,3},{3,2},{4,5},{5,4},{6,7},{7,6},{8,9},{9,8},{10,11... | collective-permute-start | bytes 49160 | tf_op jit(solution)/shard_map/ppermute | solution.py:352
  156.8 16.0 %collective-permute-start.13 = (bf16[144,512]{1,0:T(8,128)(2,1)S(1)}, bf16[144,512]{1,0:T(8,128)(2,1)S(1)}, u32[]{:S(2)}, u32[]{:S(2)}) collective-permute-start(bf16[144,512]{1,0:T(8,128)(2,1)S(1)} %concatenate.25), channel_id=1, source_target_pairs={{0,6},{2,0},{4,2},{6,4},{1,7},{3,1},{5,3},{7,5},{8,14},{10,8},{12,... | collective-permute-start | bytes 442376 | tf_op jit(solution)/shard_map/ppermute | solution.py:348
  164.9 26.0 %collective-permute-start.12 = (bf16[144,512]{1,0:T(8,128)(2,1)S(1)}, bf16[144,512]{1,0:T(8,128)(2,1)S(1)}, u32[]{:S(2)}, u32[]{:S(2)}) collective-permute-start(bf16[144,512]{1,0:T(8,128)(2,1)S(1)} %concatenate.25), channel_id=1, source_target_pairs={{0,4},{2,6},{4,0},{6,2},{1,5},{3,7},{5,1},{7,3},{8,12},{10,14},{12... | collective-permute-start | bytes 442376 | tf_op jit(solution)/shard_map/ppermute | solution.py:348
  166.5 24.4 %collective-permute-start.11 = (bf16[144,512]{1,0:T(8,128)(2,1)S(1)}, bf16[144,512]{1,0:T(8,128)(2,1)S(1)}, u32[]{:S(2)}, u32[]{:S(2)}) collective-permute-start(bf16[144,512]{1,0:T(8,128)(2,1)S(1)} %concatenate.25), channel_id=1, source_target_pairs={{0,2},{2,4},{4,6},{6,0},{1,3},{3,5},{5,7},{7,1},{8,10},{10,12},{12... | collective-permute-start | bytes 442376 | tf_op jit(solution)/shard_map/ppermute | solution.py:348
  191.0 15.3 %collective-permute-start.14 = (bf16[4,144,512]{2,1,0:T(8,128)(2,1)S(1)}, bf16[4,144,512]{2,1,0:T(8,128)(2,1)S(1)}, u32[]{:S(2)}, u32[]{:S(2)}) collective-permute-start(bf16[4,144,512]{2,1,0:T(8,128)(2,1)S(1)} %pad_maximum_fusion.refs_0_), channel_id=1, source_target_pairs={{0,16},{8,24},{16,0},{24,8},{1,17},{9,25},{17,1},{25,9},{2,18},{10... | collective-permute-start | bytes 1769480 | tf_op jit(solution)/shard_map/ppermute | solution.py:352
  192.6 1.0 copy-start.23
  196.0 10.4 %collective-permute-start.15 = (bf16[4,144,512]{2,1,0:T(8,128)(2,1)S(1)}, bf16[4,144,512]{2,1,0:T(8,128)(2,1)S(1)}, u32[]{:S(2)}, u32[]{:S(2)}) collective-permute-start(bf16[4,144,512]{2,1,0:T(8,128)(2,1)S(1)} %pad_maximum_fusion.refs_0_), channel_id=1, source_target_pairs={{0,8},{8,0},{16,24},{24,16},{1,9},{9,1},{17,25},{25,17},{2,10},{10... | collective-permute-start | bytes 1769480 | tf_op jit(solution)/shard_map/ppermute | solution.py:352
  206.3 2.0 collective-permute-start.16

commit v3 on v2

--- a/solution.py
+++ b/solution.py
@@ -12,15 +12,45 @@
 F = jnp.float32
 VM = pl.BlockSpec(memory_space=pltpu.VMEM)
 SM = pl.BlockSpec(memory_space=pltpu.SMEM)
-PARAMS = pltpu.CompilerParams(vmem_limit_bytes=48 * 1024 * 1024)
+PARAMS = pltpu.CompilerParams(vmem_limit_bytes=20 * 1024 * 1024)
+
+
+def whole(*dims):
+    return pl.BlockSpec(dims, lambda j: (0,) * len(dims))
+
+
+def wholes(*values):
+    return [whole(*value.shape) for value in values]
+
+
+def once(kernel):
+    def run(*refs):
+        @pl.when(pl.program_id(0) == 0)
+        def _():
+            kernel(*refs)
+
+    return run
+
+
+def held_in_hbm(*values):
+    return [pltpu.with_memory_space_constraint(value, pltpu.HBM) for value in values]
 
 
 def shape_of(dims, kind=BF):
-    return jax.ShapeDtypeStruct(dims, kind)
-
-
-def mix_tables(mix, rows, cw):
-    size = mix.shape[0] * cw
+    return pltpu.HBM(dims, kind)
+
+
+def turned_blocks(table, at, n, rows):
+    return jnp.concatenate(
+        [
+            lax.dynamic_slice_in_dim(table, lax.rem(at + n - j, n) * rows, rows, 1)
+            for j in range(n)
+        ],
+        axis=1,
+    )
+
+
+def mix_tables(mix, at, n, rows, cw):
     same = lax.broadcasted_iota(jnp.int32, (1, cw, 1, cw), 1) == lax.broadcasted_iota(
         jnp.int32, (1, cw, 1, cw), 3
     )
@@ -29,89 +59,70 @@
         grown = jnp.where(same, table[:, None, :, None], jnp.zeros((), BF))
         return grown.reshape(table.shape[0] * cw, table.shape[1] * cw)
 
-    ahead = jnp.stack([spread(mix[h::rows]) for h in range(rows)])
-    back = jnp.stack([spread(mix[h::rows].T) for h in range(rows)])
-    assert ahead.shape[2] == back.shape[1] == size
+    ahead = turned_blocks(mix, at, n, rows)
+    ahead = jnp.stack([spread(ahead[h::rows]) for h in range(rows)])
+    by_row = mix.reshape(n, rows, -1).transpose(1, 0, 2).reshape(mix.shape)
+    back = jnp.stack([spread(by_row[:, h::rows].T) for h in range(rows)])
     return ahead, back
 
 
-def column_mix_kernel(rows, table, x_cols, *outs):
+def column_mix_kernel(rows, table, *refs):
+    sources, outs = refs[:-rows], refs[-rows:]
     for h in range(rows):
-        outs[h][...] = jnp.dot(table[h], x_cols[...], preferred_element_type=F).astype(BF)
-
-
-def column_mix(table, x_cols):
+        total = None
+        for j, source in enumerate(sources):
+            deep = source.shape[0]
+            term = jnp.dot(
+                table[h, :, j * deep : (j + 1) * deep], source[...], preferred_element_type=F
+            )
+            total = term if total is None else total + term
+        outs[h][...] = total.astype(BF)
+
+
+def column_mix(table, sources, name):
     rows, deep, size = table.shape
-    width = x_cols.shape[-1]
+    width = sources[0].shape[-1]
     lanes = 512
     return pl.pallas_call(
         functools.partial(column_mix_kernel, rows),
         out_shape=[shape_of((deep, width))] * rows,
         grid=(width // lanes,),
-        in_specs=[
-            pl.BlockSpec((rows, deep, size), lambda j: (0, 0, 0)),
-            pl.BlockSpec((size, lanes), lambda j: (0, j)),
-        ],
+        in_specs=[pl.BlockSpec((rows, deep, size), lambda j: (0, 0, 0))]
+        + [pl.BlockSpec((source.shape[0], lanes), lambda j: (0, j)) for source in sources],
         out_specs=[pl.BlockSpec((deep, lanes), lambda j: (0, j))] * rows,
-        name="column_mix",
-    )(table, x_cols)
-
-
-def column_back_kernel(rows, table, *refs):
-    total = None
-    for h in range(rows):
-        term = jnp.dot(table[h], refs[h][...], preferred_element_type=F)
-        total = term if total is None else total + term
-    refs[rows][...] = total.astype(BF)
-
-
-def column_back(table, pieces):
-    rows, size, deep = table.shape
-    width = pieces[0].shape[-1]
-    lanes = 512
-    return pl.pallas_call(
-        functools.partial(column_back_kernel, rows),
-        out_shape=shape_of((size, width)),
-        grid=(width // lanes,),
-        in_specs=[pl.BlockSpec((rows, size, deep), lambda j: (0, 0, 0))]
-        + [pl.BlockSpec((deep, lanes), lambda j: (0, j))] * rows,
-        out_specs=pl.BlockSpec((size, lanes), lambda j: (0, j)),
-        name="column_back",
-    )(table, *pieces)
-
-
-def column_sum_kernel(rows, x_cols, *refs):
-    pieces, (out, left) = refs[:rows], refs[rows:]
-    n, cw, width = pieces[0].shape
-    for i in range(n):
-        for h in range(rows):
-            row = i * rows + h
-            left[row * cw : (row + 1) * cw, :] = pieces[h][i]
-    size = n * rows * cw
+        name=name,
+    )(*held_in_hbm(table, *sources))
+
+
+def column_sum_kernel(cw, rows, *refs):
+    pieces, sources, (out, left, right) = refs[:rows], refs[rows:-3], refs[-3:]
+    for side, parts in ((left, pieces), (right, sources)):
+        deep = parts[0].shape[0]
+        for j, part in enumerate(parts):
+            side[j * deep : (j + 1) * deep, :] = part[...]
     product = lax.dot_general(
-        left[...],
-        x_cols[...].reshape(size, width),
-        (((1,), (1,)), ((), ())),
-        preferred_element_type=F,
-    )
+        left[...], right[...], (((1,), (1,)), ((), ())), preferred_element_type=F
+    )
+    size = product.shape[0]
     row_at = lax.broadcasted_iota(jnp.int32, (size, size), 0)
     col_at = lax.broadcasted_iota(jnp.int32, (size, size), 1)
     kept = jnp.where(lax.rem(row_at, cw) == lax.rem(col_at, cw), product, 0.0)
-    out[...] = jnp.sum(kept.reshape(n * rows, cw, size), axis=1)
-
-
-def column_sum(x_cols, pieces):
-    n, rows, cw, width = x_cols.shape
-    size = n * rows * cw
-    return pl.pallas_call(
-        functools.partial(column_sum_kernel, rows),
-        out_shape=shape_of((n * rows, size), F),
-        in_specs=[VM] * (1 + rows),
-        out_specs=VM,
-        scratch_shapes=[pltpu.VMEM((size, width), BF)],
+    out[...] = jnp.sum(kept.reshape(size // cw, cw, size), axis=1)
+
+
+def column_sum(cw, sources, pieces):
+    width = pieces[0].shape[1]
+    size = sum(piece.shape[0] for piece in pieces)
+    return pl.pallas_call(
+        once(functools.partial(column_sum_kernel, cw, len(pieces))),
+        out_shape=shape_of((size // cw, size), F),
+        grid=(2,),
+        in_specs=wholes(*pieces, *sources),
+        out_specs=whole(size // cw, size),
+        scratch_shapes=[pltpu.VMEM((size, width), BF)] * 2,
         compiler_params=PARAMS,
         name="column_sum",
-    )(x_cols, *pieces)
+    )(*held_in_hbm(*pieces, *sources))
 
 
 def hidden_kernel(rows_in, x, mixed, hidden):
@@ -134,20 +145,33 @@
         ],
         out_specs=column,
         name="hidden_row",
-    )(rows_in, inputs, mixed)
-
-
-def channel_kernel(*refs):
-    (h_own, h_oth, c_own, c_oth, wg_own, wg_oth, wu_own, wu_oth, mix_g, mix_u, rows_in) = refs[:11]
-    hid_grad, back_g, back_u, turned, mix_sum, mid_g, mid_u = refs[11:]
+    )(*held_in_hbm(rows_in, inputs, mixed))
+
+
+def channel_kernel(first, *refs):
+    (place, h_own, h_oth, c_own, c_oth, wg_own, wu_own, lent, lent_too, mix_g, mix_u) = refs[:11]
+    rows_in, mixed, *before = refs[11 : 13 if first else 14]
+    hid_grad, back_g, back_u, turned, mix_sum, row_sum, mid_g, mid_u = refs[-8:]
     local, size = wg_own.shape[:2]
     blocks = 2 * local
     cols = h_own.shape[0]
-    for k in range(blocks):
-        h, wg, wu = (h_own, wg_own, wu_own) if k < local else (h_oth, wg_oth, wu_oth)
-        part = h[:, (k % local) * size : (k % local + 1) * size]
-        mid_g[k] = jnp.dot(part, wg[k % local], preferred_element_type=F)
-        mid_u[k] = jnp.dot(part, wu[k % local], preferred_element_type=F)
+
+    def middle(base, h, wg, wu):
+        for k in range(local):
+            part = h[:, k * size : (k + 1) * size]
+            mid_g[base + k] = jnp.dot(part, wg[k], preferred_element_type=F)
+            mid_u[base + k] = jnp.dot(part, wu[k], preferred_element_type=F)
+
+    middle(0, h_own, wg_own, wu_own)
+
+    @pl.when(place[2] == 0)
+    def _():
+        middle(local, h_oth, lent, lent_too)
+
+    @pl.when(place[2] != 0)
+    def _():
+        middle(local, h_oth, lent_too, lent)
+
     mix_sum[...] = jnp.zeros_like(mix_sum)
     deep, lanes = 16, 128
 
@@ -195,41 +219,51 @@
     turned[...] = lax.dot_general(
         rows_in[...], hid_grad[...], (((0,), (0,)), ((), ())), preferred_element_type=F
     ).astype(BF)
-
-
-def channel_row(h, h_own, h_oth, cot, cot_oth, weights, mixes, rows_in):
+    total = lax.dot_general(hid_grad[...], mixed[...], last, preferred_element_type=F)
+    for held in before:
+        total = held[...] + total
+    row_sum[...] = total
+
+
+def channel_row(place, h, h_own, h_oth, cot, cot_oth, weights, mixes, rows_in, mixed, before):
     cols, width = h_own.shape
     local, size = weights[0].shape[:2]
     blocks = 2 * local
     row = pl.BlockSpec((None, cols, width), lambda j: (h, 0, 0))
     return pl.pallas_call(
-        channel_kernel,
-        out_shape=[shape_of((cols, width))] * 4 + [shape_of((2, blocks, local, 8, size), F)],
-        grid=(1,),
-        in_specs=[VM] * 2 + [row, row] + [VM] * 7,
-        out_specs=[VM] * 5,
+        once(functools.partial(channel_kernel, not before)),
+        out_shape=[shape_of((cols, width))] * 4
+        + [shape_of((2, blocks, local, 8, size), F), shape_of((cols, cols), F)],
+        grid=(2,),
+        in_specs=[SM]
+        + wholes(h_own, h_oth)
+        + [row, row]
+        + [VM] * 7
+        + wholes(mixed, *before),
+        out_specs=[whole(cols, width)] * 4
+        + [whole(2, blocks, local, 8, size), whole(cols, cols)],
         scratch_shapes=[pltpu.VMEM((blocks, cols, size), F)] * 2,
         compiler_params=PARAMS,
         name="channel_row",
-    )(h_own, h_oth, cot, cot_oth, *weights, *mixes, rows_in)
-
-
-def sums_kernel(rows, parts, place, *refs):
-    hid, back_g, back_u, grad, mixed, mix_sum = (refs[i * rows : (i + 1) * rows] for i in range(6))
-    outs, row_sum = refs[6 * rows : -1], refs[-1]
-    cols, width = hid[0].shape
+    )(
+        place,
+        *held_in_hbm(h_own, h_oth, cot, cot_oth),
+        *weights,
+        *mixes,
+        rows_in,
+        *held_in_hbm(mixed, *before),
+    )
+
+
+def sums_kernel(rows, parts, place, row_sum, *refs):
+    hid, back_g, back_u, mix_sum = (refs[i * rows : (i + 1) * rows] for i in range(4))
+    outs = refs[4 * rows :]
     size = outs[0].shape[-1]
-    local = width // size
+    local = hid[0].shape[1] // size
     blocks = 2 * local
     first = (((0,), (0,)), ((), ()))
-    last = (((1,), (1,)), ((), ()))
     high = local * size // parts
     per = size // high
-    total = None
-    for h in range(rows):
-        term = lax.dot_general(grad[h][...], mixed[h][...], last, preferred_element_type=F)
-        total = term if total is None else total + term
-    row_sum[...] = total
     chan, core = place[1], place[2]
     for part, out in ((1, outs[1]), (0, outs[0])):
         k = core if part == 0 else 1 - core
@@ -255,24 +289,46 @@
             eight = jnp.concatenate(
                 [row_sum[pl.ds(at, 8), :], row_sum[pl.ds(at + 8, 8), :]], axis=1
             )
-            blank = jnp.zeros((6, size), F)
-            out[q, 2 * high :, :] = jnp.concatenate([eight, *lines, blank], axis=0).astype(BF)
-
-
-def sums(place, parts, hid, back_g, back_u, grad, mixed, mix_sum):
+            tail = jnp.concatenate([eight, *lines, jnp.zeros((6, size), F)], axis=0)
+            out[q, 2 * high :, :] = tail.astype(BF)
+
+
+def sums(place, parts, row_sum, hid, back_g, back_u, mix_sum):
     rows = len(hid)
-    cols = hid[0].shape[0]
     size = mix_sum[0].shape[-1]
     high = hid[0].shape[1] // parts
-    return pl.pallas_call(
-        functools.partial(sums_kernel, rows, parts),
-        out_shape=[shape_of((parts // 2, 2 * high + 16, size))] * 2,
-        in_specs=[SM] + [VM] * (6 * rows),
-        out_specs=[VM] * 2,
-        scratch_shapes=[pltpu.VMEM((cols, cols), F)],
+    dims = (parts // 2, 2 * high + 16, size)
+    return pl.pallas_call(
+        once(functools.partial(sums_kernel, rows, parts)),
+        out_shape=[shape_of(dims)] * 2,
+        grid=(2,),
+        in_specs=[SM] + wholes(row_sum, *hid, *back_g, *back_u, *mix_sum),
+        out_specs=[whole(*dims)] * 2,
         compiler_params=PARAMS,
         name="sums",
-    )(place, *hid, *back_g, *back_u, *grad, *mixed, *mix_sum)
+    )(place, *held_in_hbm(row_sum, *hid, *back_g, *back_u, *mix_sum))
+
+
+def core_add_kernel(n, place, kept, got, *outs):
+    at, x = place[0], place[3]
+    for i in range(n):
+        for part in range(2):
+            q = (x if part else 1 - x) * n + lax.rem(at + i, n)
+            out = outs[n].at[i] if part else outs[i]
+            out[...] = (kept[q].astype(F) + got[q].astype(F)).astype(BF)
+
+
+def core_add(n, place, kept, got):
+    deep, size = kept.shape[1:]
+    return pl.pallas_call(
+        once(functools.partial(core_add_kernel, n)),
+        out_shape=[shape_of((deep, size))] * n + [shape_of((n, deep, size))],
+        grid=(2,),
+        in_specs=[SM] + wholes(kept, got),
+        out_specs=[whole(deep, size)] * n + [whole(n, deep, size)],
+        compiler_params=PARAMS,
+        name="core_add",
+    )(place, *held_in_hbm(kept, got))
 
 
 def unpack_kernel(n, scales, place, *refs):
@@ -312,36 +368,37 @@
         + [shape_of((cols, cols), F)]
         + [shape_of((2 * local, local, size), F)] * 2
         + [shape_of((n * rows, n * rows), F)],
-        in_specs=[SM] + [VM] * 4,
-        out_specs=[VM] * 6,
+        grid=(1,),
+        in_specs=[SM] + wholes(*held),
+        out_specs=[whole(4 * n * high, size)] * 2
+        + [whole(cols, cols)]
+        + [whole(2 * local, local, size)] * 2
+        + [whole(n * rows, n * rows)],
         scratch_shapes=[pltpu.VMEM((4 * n, size), F)],
         compiler_params=PARAMS,
         name="unpack",
-    )(place, *held)
-
-
-def finish_kernel(*refs):
-    grads, (back, out) = refs[:-2], refs[-2:]
-    n, rows, cw = back.shape[:3]
-    for i in range(n):
-        spot = slice(i * cw, (i + 1) * cw)
-        for h in range(rows):
-            out[h, spot, :] = (grads[h][spot, :].astype(F) + back[i, h].astype(F)).astype(BF)
-
-
-def finish(grads, back):
+    )(place, *held_in_hbm(*held))
+
+
+def finish_kernel(rows, *refs):
+    grads, backs, out = refs[:rows], refs[rows:-1], refs[-1]
+    for h in range(rows):
+        out[h] = (grads[h][...].astype(F) + backs[h][...].astype(F)).astype(BF)
+
+
+def finish(grads, backs):
+    rows = len(grads)
     cols, width = grads[0].shape
-    n, rows, cw = back.shape[:3]
     lanes = 512
-    return pl.pallas_call(
-        finish_kernel,
+    column = pl.BlockSpec((cols, lanes), lambda j: (0, j))
+    return pl.pallas_call(
+        functools.partial(finish_kernel, rows),
         out_shape=shape_of((rows, cols, width)),
         grid=(width // lanes,),
-        in_specs=[pl.BlockSpec((cols, lanes), lambda j: (0, j))] * rows
-        + [pl.BlockSpec((n, rows, cw, lanes), lambda j: (0, 0, 0, j))],
+        in_specs=[column] * (2 * rows),
         out_specs=pl.BlockSpec((rows, cols, lanes), lambda j: (0, 0, j)),
         name="finish",
-    )(*grads, back)
+    )(*held_in_hbm(*grads, *backs))
 
 
 def shifted(value, by, n):
@@ -369,29 +426,27 @@
     return upper, (line - upper.astype(F)).astype(BF)
 
 
-def reduce_parts(kept, sent, early, later, cols_sum, place_at, n):
-    seq_at, x = place_at
-    deep, size = kept.shape[1:]
-    sent, _ = lax.optimization_barrier((sent, early))
-    got = swapped(sent, "dp", 1, 4)
-    halves = add(kept, got).reshape(2, n, deep, size)
-    got = swapped(pick(halves, 1 - x), "dp", 2, 4)
-    fours = add(pick(halves, x), got)
-    got = [shifted(pick(fours, lax.rem(seq_at + i, n)), i, n) for i in range(1, n)]
-    got, _ = lax.optimization_barrier((got, later))
-    mine = add(pick(fours, seq_at), *got)
-    tail = mine[deep - 16 :]
+def two_lines(line):
+    upper = line.astype(BF)
+    return upper, (line - upper.astype(F)).astype(BF)
+
+
+def scatter_seq(by_x, fours, cols_sum, n):
+    deep, size = fours.shape[1:]
+    arrived = []
+    for i in [*range(1, n), 0]:
+        shard = add(fours[i], by_x[i])
+        arrived.append(shifted(shard, i, n) if i else shard)
     count = cols_sum.size
     line = jnp.pad(cols_sum.reshape(1, count), ((0, 0), (0, size - count)))
-    blank = jnp.zeros((4, size), BF)
-    tail = jnp.concatenate([tail[:10], *two_lines(line), blank], axis=0)
+    lines = jnp.pad(jnp.concatenate(two_lines(line), axis=0), ((deep - 6, 4), (0, 0)))
+    mine = add(*arrived, lines)
+    tail = mine[deep - 16 :]
     other = swapped(tail, "chan", 1, 2)
     both = tail.astype(F) + other.astype(F)
     lines = two_lines(both[10:11] + both[11:12])
-    tail = jnp.concatenate([both[:8].astype(BF), tail[8:10], *lines, blank], axis=0)
-    mine = jnp.concatenate([mine[: deep - 16], tail], axis=0)
-    held = jnp.stack([mine] + [shifted(mine, i, n) for i in range(1, n)])
-    return held, swapped(held, "dp", 2, 4), swapped(held, "dp", 1, 4)
+    tail = jnp.concatenate([both[:8].astype(BF), tail[8:10], *lines, tail[12:]], axis=0)
+    return jnp.concatenate([mine[: deep - 16], tail], axis=0)
 
 
 def block_body(inputs, cotangent, rows_in, cols_mix, blocks_gate, blocks_up, mix_gate, mix_up):
@@ -403,56 +458,84 @@
     core, x = lax.rem(dp_at, 2), dp_at // 2
     place = jnp.stack([seq_at, chan_at, core, x]).astype(jnp.int32)
     values, cot = inputs[0], cotangent[0]
-    ahead, behind = mix_tables(cols_mix, rows, cw)
+    ahead, behind = mix_tables(cols_mix, seq_at, n, rows, cw)
 
     def relative(table):
         turned = jnp.roll(table, (local, local), (0, 1))
         table = jnp.where(chan_at == 0, table, turned).astype(F)
         return jnp.broadcast_to(table[:, :, None, :], table.shape[:2] + (8, size))
 
-    x_cols = traded(values.reshape(rows, n, cw, width).transpose(1, 0, 2, 3))
+    ways = [
+        lax.dynamic_slice_in_dim(values, lax.rem(seq_at + i, n) * cw, cw, 1) for i in range(n)
+    ]
+    x_cols = [ways[0]] + [shifted(ways[i], i, n) for i in range(1, n)]
+    x_cols = [part.reshape(rows * cw, width) for part in x_cols]
     cot_oth = swapped(cot, "chan", 1, 2)
     lent = jnp.where(core == 0, blocks_gate, blocks_up)
     lent, _ = lax.optimization_barrier((lent, cot_oth))
     lent = swapped(lent, "chan", 1, 2)
-    lent_too = swapped(lent, "dp", 1, 4)
-    gate_oth = jnp.where(core == 0, lent, lent_too)
-    up_oth = jnp.where(core == 0, lent_too, lent)
-    weights = (blocks_gate, gate_oth, blocks_up, up_oth)
     mixes = (relative(mix_gate), relative(mix_up))
 
-    x_cols, ahead, behind, mixes, cot_oth = lax.optimization_barrier(
-        (x_cols, ahead, behind, mixes, cot_oth)
-    )
-    parts = column_mix(ahead, x_cols.reshape(n * rows * cw, width))
+    x_cols, ahead, behind, mixes = lax.optimization_barrier((x_cols, ahead, behind, mixes))
+    parts = column_mix(ahead, x_cols, "column_mix")
+    parts, cot_oth = lax.optimization_barrier((parts, cot_oth))
     mixed = [traded(part.reshape(n, cw, width)).reshape(cols, width) for part in parts]
     hidden = [hidden_row(rows_in, values, h, mixed[h]) for h in range(rows)]
     leaving = list(hidden)
+    lender, _ = lax.optimization_barrier((lent, hidden[0]))
+    lent_too = swapped(lender, "dp", 1, 4)
+    weights = (blocks_gate, blocks_up, lent, lent_too)
     leaving[0], _ = lax.optimization_barrier((leaving[0], lent))
     others = [swapped(hid, "chan", 1, 2) for hid in leaving]
     others[0], hidden[-1] = lax.optimization_barrier((others[0], hidden[-1]))
-    grads, back_g, back_u, mix_sum, pieces = [], [], [], [], []
+    grads, back_g, back_u, pieces, mix_sum, rows_sum = [], [], [], [], [], []
     for h in range(rows):
-        got = channel_row(h, hidden[h], others[h], cot, cot_oth, weights, mixes, rows_in)
+        got = channel_row(
+            place,
+            h,
+            hidden[h],
+            others[h],
+            cot,
+            cot_oth,
+            weights,
+            mixes,
+            rows_in,
+            mixed[h],
+            rows_sum,
+        )
         for held, value in zip((grads, back_g, back_u, pieces, mix_sum), got):
             held.append(value)
-        if h == 0:
-            pieces[0], others[-1] = lax.optimization_barrier((pieces[0], others[-1]))
-        pieces[h] = traded(pieces[h].reshape(n, cw, width))
-    kept, sent = sums(place, 4 * n, hidden, back_g, back_u, grads, mixed, mix_sum)
-    flat = [piece.reshape(cols, width) for piece in pieces]
-    turned = column_back(behind, flat)
-    back = traded(turned.reshape(n, rows, cw, width))
-    cols_sum = column_sum(x_cols, pieces)
-    cols_sum = cols_sum.reshape(n * rows, n * rows, cw).sum(-1)
+        rows_sum = got[5:]
+    kept, sent = sums(place, 4 * n, rows_sum[0], hidden, back_g, back_u, mix_sum)
+    pieces[0], _ = lax.optimization_barrier((pieces[0], others[-1]))
+    pieces[0] = traded(pieces[0].reshape(n, cw, width)).reshape(cols, width)
+    sent, _ = lax.optimization_barrier((sent, pieces[0]))
+    pieces[1], _ = lax.optimization_barrier((pieces[1], kept))
+    pieces[1] = traded(pieces[1].reshape(n, cw, width)).reshape(cols, width)
+    *leaving, fours = core_add(n, place, kept, swapped(sent, "dp", 1, 4))
+    by_x = [swapped(shard, "dp", 2, 4) for shard in leaving]
+    pieces[1], _ = lax.optimization_barrier((pieces[1], by_x[1]))
+    turned = column_mix(behind, pieces, "column_back")
+    backs = [traded(turned[0].reshape(n, cw, width))]
+    late, _ = lax.optimization_barrier((pieces[1], turned[0]))
+    cols_sum = column_sum(cw, x_cols, [pieces[0], late])
+    cols_sum = cols_sum.reshape(rows, n, n * rows, cw).sum(-1).transpose(1, 0, 2)
+    cols_sum = turned_blocks(cols_sum.reshape(n * rows, n * rows), seq_at, n, rows)
+    mine = scatter_seq(by_x, fours, cols_sum, n)
+    held = [mine] + [shifted(mine, i, n) for i in range(1, n)]
+    for part in turned[1:]:
+        part, _ = lax.optimization_barrier((part, held[1:]))
+        backs.append(traded(part.reshape(n, cw, width)))
+    backs = [part.reshape(cols, width) for part in backs]
     batch_all = lax.axis_size("dp")
     width_all = width * lax.axis_size("chan")
     rows_scale = 1.0 / math.sqrt(batch_all * rows * n * width_all)
     cols_scale = 1.0 / math.sqrt(batch_all * cols * width_all)
     block_scale = 1.0 / math.sqrt(batch_all * rows * n * cols)
-    held, by_x, by_core = reduce_parts(kept, sent, pieces[0], turned, cols_sum, (seq_at, x), n)
-    input_grad = finish(grads, back)
-    by_x, input_grad = lax.optimization_barrier((by_x, input_grad))
+    by_x = jnp.stack([swapped(shard, "dp", 2, 4) for shard in held])
+    held = jnp.stack(held)
+    by_core = swapped(held, "dp", 1, 4)
+    input_grad = finish(grads, backs)
     gate_sum, up_sum, rows_sum, mix_g, mix_u, cols_sum = unpack(
         n,
         rows,

time: 212 us -> 192 us (0.906)
  waiting for transfers between devices: 91 us -> 56.4 us
  blocking collectives: 0 us -> 17.8 us
  Pallas kernels: 36 us -> 47 us
  other arithmetic: 13 us -> 6.41 us
  local copies, waits for them, and re-layouts: 17.3 us -> 12.6 us
  starting transfers between devices: 52.9 us -> 50.1 us
    ppermute x11 -> x17, waiting for transfers between devices: 42.9 us -> 10.7 us  [swapped(): return lax.ppermute(value, axis, [(i, i ^ bit) for i in range(n)])]
    all_to_all x0 -> x1, blocking collectives: none -> 17.8 us  [traded(): return lax.all_to_all(value, 'seq', split_axis=0, concat_axis=0, tiled=True)]
    all_to_all x6 -> x5, starting transfers between devices: 27.8 us -> 20.4 us  [traded(): return lax.all_to_all(value, 'seq', split_axis=0, concat_axis=0, tiled=True)]
    pallas_call x6, Pallas kernels: 25.7 us -> 32 us  [the longest x2 18.7 us: channel_row(): pl.pallas_call(once(functools.partial(channel_kernel, not before)), out_s...]
    unnamed x56 -> x34, local copies, waits for them, and re-layouts: 9.56 us -> 4.59 us
    ppermute x11 -> x17, starting transfers between devices: 9.78 us -> 14.1 us  [swapped(): return lax.ppermute(value, axis, [(i, i ^ bit) for i in range(n)])]
    pallas_call x1 -> x2, Pallas kernels: 2.83 us -> 6.46 us  [column_mix(): pl.pallas_call(functools.partial(column_mix_kernel, rows), out_shape=[sha...]
    select_n x1 -> x0, other arithmetic: 3 us -> none  [block_body(): up_oth = jnp.where(core == 0, lent_too, lent)]
  transfers between devices with their start and end apart: 23 -> 31, of which waited for: 12 -> 15; matrix products, arithmetic and copies ran while one was open for 8% -> 6% of each run, Pallas kernels for 16% -> 23%
where the time goes in v3:
time: 192 us; the launch traced here: 191 us
  waiting for transfers between devices  56.4 us (29%)
  starting transfers between devices  50.1 us (26%)
  Pallas kernels  47 us (24%)
  blocking collectives  17.8 us (9%)
  local copies, waits for them, and re-layouts  12.6 us (7%)
  other arithmetic  6.41 us (3%)
    ppermute x9, waiting for transfers between devices, shifted(): return lax.ppermute(value, 'seq', [(i, (i + by) % n) for i in range(n)])  23.9 us
    all_to_all x5, waiting for transfers between devices, traded(): return lax.all_to_all(value, 'seq', split_axis=0, concat_axis=0, tiled=True)  21.8 us
    all_to_all x5, starting transfers between devices, traded(): return lax.all_to_all(value, 'seq', split_axis=0, concat_axis=0, tiled=True)  20.4 us
    pallas_call x2, Pallas kernels, channel_row(): pl.pallas_call(once(functools.partial(channel_kernel, not before)), out_s...  18.7 us
    all_to_all x1, blocking collectives, traded(): return lax.all_to_all(value, 'seq', split_axis=0, concat_axis=0, tiled=True)  17.8 us
    ppermute x9, starting transfers between devices, shifted(): return lax.ppermute(value, 'seq', [(i, (i + by) % n) for i in range(n)])  15.6 us
    ppermute x17, starting transfers between devices, swapped(): return lax.ppermute(value, axis, [(i, i ^ bit) for i in range(n)])  14.1 us
    ppermute x17, waiting for transfers between devices, swapped(): return lax.ppermute(value, axis, [(i, i ^ bit) for i in range(n)])  10.7 us
  transfers between devices with their start and end apart: 31, of which 15 were waited for; matrix products, arithmetic and copies ran while one was open for 6% of the time, Pallas kernels for 23%

profile of v3, /device:TPU:0, one launch (start us, length us, event | category | flops | bytes accessed | tf_op | source)
XLA Modules:
  0.0 191.4 jit_solution(5571859488250026352)
XLA Ops:
  0.7 2.3 %dynamic-slice_bitcast_fusion = (bf16[2,64,1024]{2,1,0:T(8,128)(2,1)}, bf16[2,64,1024]{2,1,0:T(8,128)(2,1)}, bf16[1,2,64,1024]{3,2,1,0:T(8,128)(2,1)}, bf16[2,64,1024]{2,1,0:T(8,128)(2,1)}) fusion(bf16[1,2,256,1024]{3,2,1,0:T(8,128)(2,1)} %param.8, s32[]{:T(128)S(6)} %select_n.110, s32[]{:T(128)S(6)} %select_n.108, s32[]{:T(128)S(6)} %select_n.107, ...), kind=kLoop, calls=%fused_computation.21 | loop fusion | bytes 2097168 | tf_op jit(solution)/shard_map/dynamic_slice | solution.py:469
  3.0 5.0 %collective-permute-start.2 = (bf16[2,64,1024]{2,1,0:T(8,128)(2,1)}, bf16[2,64,1024]{2,1,0:T(8,128)(2,1)}, u32[]{:S(2)}, u32[]{:S(2)}) collective-permute-start(bf16[2,64,1024]{2,1,0:T(8,128)(2,1)} %get-tuple-element.109), channel_id=1, source_target_pairs={{0,6},{2,0},{4,2},{6,4},{1,7},{3,1},{5,3},{7,5},{8,14},{10,8},{12,... | collective-permute-start | bytes 786440 | tf_op jit(solution)/shard_map/ppermute | solution.py:405
  8.0 1.0 collective-permute-start.1
  9.1 1.5 collective-permute-start.3
  11.8 1.0 select_n.118
  12.8 1.0 select_n.122
  13.9 1.0 select_n.116
  14.9 2.3 %pad_maximum_fusion.2 = (bf16[2,256,512]{2,1,0:T(8,128)(2,1)}, bf16[2,256,512]{2,1,0:T(8,128)(2,1)}) fusion(bf16[1,256,512]{2,1,0:T(8,128)(2,1)} %select_n.118, bf16[1,256,512]{2,1,0:T(8,128)(2,1)} %select_n.116, bf16[1,256,512]{2,1,0:T(8,128)(2,1)} %select_n.122, bf16[1,256,512]{2,1,0:T(8,128)(2,1)S(1)} %select_n.120), kind=kLoop, calls=%fused_computation.3 | loop fusion | flops 524288 | bytes 2097152 | tf_op jit(solution)/shard_map/stack | solution.py:63
  17.3 1.1 broadcast_select_fusion
  18.4 3.3 %collective-permute-done = bf16[2,64,1024]{2,1,0:T(8,128)(2,1)} collective-permute-done((bf16[2,64,1024]{2,1,0:T(8,128)(2,1)}, bf16[2,64,1024]{2,1,0:T(8,128)(2,1)}, u32[]{:S(2)}, u32[]{:S(2)}) %collective-permute-start) | collective-permute-done | bytes 262176 | tf_op jit(solution)/shard_map/ppermute | solution.py:405
  21.7 9.0 %collective-permute-done.1 = bf16[2,64,1024]{2,1,0:T(8,128)(2,1)} collective-permute-done((bf16[2,64,1024]{2,1,0:T(8,128)(2,1)}, bf16[2,64,1024]{2,1,0:T(8,128)(2,1)}, u32[]{:S(2)}, u32[]{:S(2)}) %collective-permute-start.1) | collective-permute-done | bytes 262176 | tf_op jit(solution)/shard_map/ppermute | solution.py:405
  30.7 0.7 broadcast_in_dim.78.refs_9_
  31.4 3.5 %column_mix.1 = (bf16[256,1024]{1,0:T(8,128)(2,1)}, bf16[256,1024]{1,0:T(8,128)(2,1)}) custom-call(bf16[2,256,512]{2,1,0:T(8,128)(2,1)} %get-tuple-element.58.table, bf16[128,1024]{1,0:T(8,128)(2,1)} %bitcast.76, bf16[128,1024]{1,0:T(8,128)(2,1)} %bitcast.7.refs_1_.refs_3_, bf16[128,1024]{1,0:T(8,128)(2,1)} %bitcast.9.refs_2_.refs_4_, ...), custom_call_target="tpu_custom_call" | custom-call | tf_op jit(solution)/shard_map/column_mix/pallas_call | solution.py:86
  35.0 1.6 collective-permute-start.4
  36.5 17.8 %all_to_all.30 = bf16[4,64,1024]{2,1,0:T(8,128)(2,1)} all-to-all(bf16[4,64,1024]{2,1,0:T(8,128)(2,1)} %bitcast.84), channel_id=1, replica_groups=mesh['dp'=4,'seq'=4,'chan'=2] {'seq'}, dimensions={0} | all-to-all | bytes 1048576 | tf_op jit(solution)/shard_map/all_to_all | solution.py:413
  54.4 4.1 %all-to-all-start.1 = ((bf16[4,64,1024]{2,1,0:T(8,128)(2,1)}), bf16[4,64,1024]{2,1,0:T(8,128)(2,1)}, u32[]{:S(2)}, u32[]{:S(2)}) async-start(bf16[4,64,1024]{2,1,0:T(8,128)(2,1)} %bitcast.83), calls=%async_computation.1 | async-start | bytes 1048576 | tf_op jit(solution)/shard_map/all_to_all | solution.py:413
  58.5 2.3 %hidden_row.2.refs_1_.refs_2_ = bf16[256,1024]{1,0:T(8,128)(2,1)} custom-call(bf16[256,256]{1,0:T(8,128)(2,1)} %refs_11_.3, bf16[2,256,1024]{2,1,0:T(8,128)(2,1)} %bitcast.67, bf16[256,1024]{1,0:T(8,128)(2,1)} %bitcast.69), custom_call_target="tpu_custom_call" | custom-call | tf_op jit(solution)/shard_map/hidden_row/pallas_call | solution.py:137
  60.9 0.6 collective-permute-start.5
  61.5 10.6 %all-to-all-done.1 = bf16[4,64,1024]{2,1,0:T(8,128)(2,1)} async-done(((bf16[4,64,1024]{2,1,0:T(8,128)(2,1)}), bf16[4,64,1024]{2,1,0:T(8,128)(2,1)}, u32[]{:S(2)}, u32[]{:S(2)}) %all-to-all-start.1) | async-done | bytes 524320 | tf_op jit(solution)/shard_map/all_to_all | solution.py:413
  72.1 2.3 %hidden_row.3.refs_1_.refs_3_ = bf16[256,1024]{1,0:T(8,128)(2,1)} custom-call(bf16[256,256]{1,0:T(8,128)(2,1)} %refs_11_.3, bf16[2,256,1024]{2,1,0:T(8,128)(2,1)} %bitcast.68, bf16[256,1024]{1,0:T(8,128)(2,1)} %bitcast.21.mixed.refs_12_), custom_call_target="tpu_custom_call" | custom-call | tf_op jit(solution)/shard_map/hidden_row/pallas_call | solution.py:137
  75.0 0.6 collective-permute-done.5.refs_2_
  75.6 0.9 copy-done.2
  76.5 9.3 %channel_row.2 = (bf16[256,1024]{1,0:T(8,128)(2,1)}, bf16[256,1024]{1,0:T(8,128)(2,1)}, bf16[256,1024]{1,0:T(8,128)(2,1)}, bf16[256,1024]{1,0:T(8,128)(2,1)}, f3...) custom-call(s32[4]{0:T(128)S(1)} %pad_add_fusion.refs_0_.place, bf16[256,1024]{1,0:T(8,128)(2,1)} %hidden_row.2.refs_1_.refs_2_, ...), custom_call_target="tpu_custom_call" | custom-call | tf_op jit(solution)/shard_map/channel_row/pallas_call | solution.py:233
  85.8 1.8 collective-permute-done.7.refs_2_
  87.6 4.2 %all-to-all-start.2 = ((bf16[4,64,1024]{2,1,0:T(8,128)(2,1)}), bf16[4,64,1024]{2,1,0:T(8,128)(2,1)}, u32[]{:S(2)}, u32[]{:S(2)}) async-start(bf16[4,64,1024]{2,1,0:T(8,128)(2,1)} %bitcast.82), calls=%async_computation.2 | async-start | bytes 1048576 | tf_op jit(solution)/shard_map/all_to_all | solution.py:413
  91.8 0.9 copy-done.3
  92.8 9.4 %channel_row.3 = (bf16[256,1024]{1,0:T(8,128)(2,1)}, bf16[256,1024]{1,0:T(8,128)(2,1)}, bf16[256,1024]{1,0:T(8,128)(2,1)}, bf16[256,1024]{1,0:T(8,128)(2,1)}, f3...) custom-call(s32[4]{0:T(128)S(1)} %pad_add_fusion.refs_0_.place, bf16[256,1024]{1,0:T(8,128)(2,1)} %hidden_row.3.refs_1_.refs_3_, ...), custom_call_target="tpu_custom_call" | custom-call | tf_op jit(solution)/shard_map/channel_row/pallas_call | solution.py:233
  102.1 5.1 %sums.1 = (bf16[8,144,512]{2,1,0:T(8,128)(2,1)}, bf16[8,144,512]{2,1,0:T(8,128)(2,1)}) custom-call(s32[4]{0:T(128)S(1)} %pad_add_fusion.refs_0_.place, f32[256,256]{1,0:T(8,128)} %get-tuple-element.82.refs_1_, bf16[256,1024]{1,0:T(8,128)(2,1)} %hidden_row.2.refs_1_.refs_2_, bf16[256,1024]{1,0:T(8,128)(2,1)} %hidden_row.3.refs_1_.refs_3_, ...), custom_call_target="tpu_custom_call" | custom-call | tf_op jit(solution)/shard_map/sums/pallas_call | solution.py:301
  107.3 5.1 %all-to-all-start.3 = ((bf16[4,64,1024]{2,1,0:T(8,128)(2,1)}), bf16[4,64,1024]{2,1,0:T(8,128)(2,1)S(1)}, u32[]{:S(2)}, u32[]{:S(2)}) async-start(bf16[4,64,1024]{2,1,0:T(8,128)(2,1)} %bitcast.24), calls=%async_computation.3 | async-start | bytes 1048576 | tf_op jit(solution)/shard_map/all_to_all | solution.py:413
  112.4 1.0 copy-done.11
  113.4 3.0 %core_add.1 = (bf16[144,512]{1,0:T(8,128)(2,1)}, bf16[144,512]{1,0:T(8,128)(2,1)}, bf16[144,512]{1,0:T(8,128)(2,1)}, bf16[144,512]{1,0:T(8,128)(2,1)}, bf16[4,144,512]{2,1,0:T(8,128)(2,1)}) custom-call(s32[4]{0:T(128)S(1)} %pad_add_fusion.refs_0_.place, bf16[8,144,512]{2,1,0:T(8,128)(2,1)} %get-tuple-element.89.refs_1_, bf16[8,144,512]{2,1,0:T(8,128)(2,1)} %copy-done.11), custom_call_target="tpu_custom_call" | custom-call | tf_op jit(solution)/shard_map/core_add/pallas_call | solution.py:323
  116.3 1.5 collective-permute-start.9
  118.4 1.5 collective-permute-start.13
  120.4 7.1 %all-to-all-done.3 = bf16[4,64,1024]{2,1,0:T(8,128)(2,1)S(1)} async-done(((bf16[4,64,1024]{2,1,0:T(8,128)(2,1)}), bf16[4,64,1024]{2,1,0:T(8,128)(2,1)S(1)}, u32[]{:S(2)}, u32[]{:S(2)}) %all-to-all-start.3) | async-done | bytes 524320 | tf_op jit(solution)/shard_map/all_to_all | solution.py:413
  127.5 2.0 %collective-permute-done.13 = bf16[144,512]{1,0:T(8,128)(2,1)S(1)} collective-permute-done((bf16[144,512]{1,0:T(8,128)(2,1)}, bf16[144,512]{1,0:T(8,128)(2,1)S(1)}, u32[]{:S(2)}, u32[]{:S(2)}) %collective-permute-start.13) | collective-permute-done | bytes 147488 | tf_op jit(solution)/shard_map/ppermute | solution.py:409
  129.6 1.2 fusion.3
  130.7 2.1 %collective-permute-start.10 = (bf16[144,512]{1,0:T(8,128)(2,1)S(1)}, bf16[144,512]{1,0:T(8,128)(2,1)S(1)}, u32[]{:S(2)}, u32[]{:S(2)}) collective-permute-start(bf16[144,512]{1,0:T(8,128)(2,1)S(1)} %get-tuple-element.113), channel_id=1, source_target_pairs={{0,2},{2,4},{4,6},{6,0},{1,3},{3,5},{5,7},{7,1},{8,10},{10,12},{12... | collective-permute-start | bytes 442376 | tf_op jit(solution)/shard_map/ppermute | solution.py:405
  132.8 2.0 %collective-permute-start.14 = (bf16[144,512]{1,0:T(8,128)(2,1)S(1)}, bf16[144,512]{1,0:T(8,128)(2,1)S(1)}, u32[]{:S(2)}, u32[]{:S(2)}) collective-permute-start(bf16[144,512]{1,0:T(8,128)(2,1)S(1)} %get-tuple-element.114), channel_id=1, source_target_pairs={{0,6},{2,0},{4,2},{6,4},{1,7},{3,1},{5,3},{7,5},{8,14},{10,8},{12,... | collective-permute-start | bytes 442376 | tf_op jit(solution)/shard_map/ppermute | solution.py:405
  134.9 0.9 collective-permute-start.12
  135.8 2.9 %column_back.1 = (bf16[256,1024]{1,0:T(8,128)(2,1)}, bf16[256,1024]{1,0:T(8,128)(2,1)}) custom-call(bf16[2,256,512]{2,1,0:T(8,128)(2,1)} %get-tuple-element.78.table, bf16[256,1024]{1,0:T(8,128)(2,1)} %bitcast.23.refs_0_, bf16[256,1024]{1,0:T(8,128)(2,1)} %bitcast.71), custom_call_target="tpu_custom_call" | custom-call | tf_op jit(solution)/shard_map/column_back/pallas_call | solution.py:86
  138.7 2.9 %column_sum.1 = f32[8,512]{1,0:T(8,128)} custom-call(bf16[256,1024]{1,0:T(8,128)(2,1)} %bitcast.23.refs_0_, bf16[256,1024]{1,0:T(8,128)(2,1)} %bitcast.72, bf16[128,1024]{1,0:T(8,128)(2,1)} %bitcast.77, bf16[128,1024]{1,0:T(8,128)(2,1)} %bitcast.7.refs_1_.refs_3_, bf16[128,1024]{1,0:T(8,128)(2,1)} %bitcast.9.refs_2_.refs_4_, ...), custom_call_target="tpu_custom_call" | custom-call | tf_op jit(solution)/shard_map/column_sum/pallas_call | solution.py:116
  141.6 3.5 %all-to-all-start.4 = ((bf16[4,64,1024]{2,1,0:T(8,128)(2,1)}), bf16[4,64,1024]{2,1,0:T(8,128)(2,1)S(1)}, u32[]{:S(2)}, u32[]{:S(2)}) async-start(bf16[4,64,1024]{2,1,0:T(8,128)(2,1)} %bitcast.26), calls=%async_computation.4 | async-start | bytes 1048576 | tf_op jit(solution)/shard_map/all_to_all | solution.py:413
  145.1 0.8 reshape.218
  146.3 2.2 %collective-permute-done.12 = bf16[144,512]{1,0:T(8,128)(2,1)S(1)} collective-permute-done((bf16[144,512]{1,0:T(8,128)(2,1)S(1)}, bf16[144,512]{1,0:T(8,128)(2,1)S(1)}, u32[]{:S(2)}, u32[]{:S(2)}) %collective-permute-start.12) | collective-permute-done | bytes 147488 | tf_op jit(solution)/shard_map/ppermute | solution.py:405
  148.4 1.0 add_convert_fusion
  149.4 0.6 collective-permute-start.16
  150.0 3.2 %collective-permute-done.16 = bf16[16,512]{1,0:T(8,128)(2,1)S(1)} collective-permute-done((bf16[16,512]{1,0:T(8,128)(2,1)S(1)}, bf16[16,512]{1,0:T(8,128)(2,1)S(1)}, u32[]{:S(2)}, u32[]{:S(2)}) %collective-permute-start.16) | collective-permute-done | bytes 16416 | tf_op jit(solution)/shard_map/ppermute | solution.py:409
  153.3 3.9 %collective-permute-start.19 = (bf16[144,512]{1,0:T(8,128)(2,1)S(1)}, bf16[144,512]{1,0:T(8,128)(2,1)S(1)}, u32[]{:S(2)}, u32[]{:S(2)}) collective-permute-start(bf16[144,512]{1,0:T(8,128)(2,1)S(1)} %concatenate.33), channel_id=1, source_target_pairs={{0,6},{2,0},{4,2},{6,4},{1,7},{3,1},{5,3},{7,5},{8,14},{10,8},{12,... | collective-permute-start | bytes 442376 | tf_op jit(solution)/shard_map/ppermute | solution.py:405
  157.2 0.6 collective-permute-start.17
  157.8 1.5 collective-permute-start.20
  159.3 0.6 collective-permute-done.19
  159.9 1.5 collective-permute-start.23
  161.4 8.9 %collective-permute-done.18 = bf16[144,512]{1,0:T(8,128)(2,1)S(1)} collective-permute-done((bf16[144,512]{1,0:T(8,128)(2,1)S(1)}, bf16[144,512]{1,0:T(8,128)(2,1)S(1)}, u32[]{:S(2)}, u32[]{:S(2)}) %collective-permute-start.18) | collective-permute-done | bytes 147488 | tf_op jit(solution)/shard_map/ppermute | solution.py:405
  170.3 1.5 collective-permute-start.22
  171.8 0.5 collective-permute-start.21
  172.4 3.5 %all-to-all-start.5 = ((bf16[4,64,1024]{2,1,0:T(8,128)(2,1)}), bf16[4,64,1024]{2,1,0:T(8,128)(2,1)S(1)}, u32[]{:S(2)}, u32[]{:S(2)}) async-start(bf16[4,64,1024]{2,1,0:T(8,128)(2,1)} %bitcast.34), calls=%async_computation.5 | async-start | bytes 1048576 | tf_op jit(solution)/shard_map/all_to_all | solution.py:413
  176.1 1.1 collective-permute-done.21
  177.4 0.6 collective-permute-done.24.refs_2_
  178.0 1.3 collective-permute-done.25.refs_3_
  179.4 0.8 copy-done.13
  180.2 3.9 %unpack.1 = (f32[1024,512]{1,0:T(8,128)}, f32[1024,512]{1,0:T(8,128)}, f32[256,256]{1,0:T(8,128)}, f32[4,2,512]{2,1,0:T(2,128)}, f32[4,2,512]{2,1,0:T(2,128)}, /*index=5*/f32[8,8]{1,0:T(8,128)}) custom-call(s32[4]{0:T(128)S(1)} %pad_add_fusion.refs_0_.place, bf16[4,144,512]{2,1,0:T(8,128)(2,1)} %copy-done.7, bf16[4,144,512]{2,1,0:T(8,128)(2,1)} %copy-done.8, ...), custom_call_target="tpu_custom_call" | custom-call | tf_op jit(solution)/shard_map/unpack/pallas_call | solution.py:365
  184.1 4.0 %all-to-all-done.5 = bf16[4,64,1024]{2,1,0:T(8,128)(2,1)S(1)} async-done(((bf16[4,64,1024]{2,1,0:T(8,128)(2,1)}), bf16[4,64,1024]{2,1,0:T(8,128)(2,1)S(1)}, u32[]{:S(2)}, u32[]{:S(2)}) %all-to-all-start.5) | async-done | bytes 524320 | tf_op jit(solution)/shard_map/all_to_all | solution.py:413
  188.1 0.8 copy-done.10
  189.0 2.4 %finish.1 = bf16[2,256,1024]{2,1,0:T(8,128)(2,1)} custom-call(bf16[256,1024]{1,0:T(8,128)(2,1)} %get-tuple-element.74.refs_0_, bf16[256,1024]{1,0:T(8,128)(2,1)} %get-tuple-element.77.refs_1_, bf16[256,1024]{1,0:T(8,128)(2,1)} %bitcast.78, bf16[256,1024]{1,0:T(8,128)(2,1)} %bitcast.79), custom_call_target="tpu_custom_call" | custom-call | tf_op jit(solution)/shard_map/finish/pallas_call | solution.py:394
  (90 shorter events, 3.8 us)
Async XLA Ops:
  0.6 8.4 %copy-start.6 = (bf16[1,2,256,1024]{3,2,1,0:T(8,128)(2,1)S(1)}, bf16[1,2,256,1024]{3,2,1,0:T(8,128)(2,1)}, u32[]{:S(2)}) copy-start(bf16[1,2,256,1024]{3,2,1,0:T(8,128)(2,1)} %param.9) | copy-start | bytes 3145732
  0.6 9.9 %copy-start.16 = (bf16[8,8]{1,0:T(8,128)(2,1)S(1)}, bf16[8,8]{1,0:T(8,128)(2,1)}, u32[]{:S(2)}) copy-start(bf16[8,8]{1,0:T(8,128)(2,1)} %param.11) | copy-start | bytes 388
  0.7 10.6 %copy-start.15 = (bf16[4,4,512]{2,1,0:T(4,128)(2,1)S(1)}, bf16[4,4,512]{2,1,0:T(4,128)(2,1)}, u32[]{:S(2)}) copy-start(bf16[4,4,512]{2,1,0:T(4,128)(2,1)} %param.14) | copy-start | bytes 49156
  3.0 15.4 %collective-permute-start.2 = (bf16[2,64,1024]{2,1,0:T(8,128)(2,1)}, bf16[2,64,1024]{2,1,0:T(8,128)(2,1)}, u32[]{:S(2)}, u32[]{:S(2)}) collective-permute-start(bf16[2,64,1024]{2,1,0:T(8,128)(2,1)} %get-tuple-element.109), channel_id=1, source_target_pairs={{0,6},{2,0},{4,2},{6,4},{1,7},{3,1},{5,3},{7,5},{8,14},{10,8},{12,... | collective-permute-start | bytes 786440 | tf_op jit(solution)/shard_map/ppermute | solution.py:405
  8.0 13.7 %collective-permute-start = (bf16[2,64,1024]{2,1,0:T(8,128)(2,1)}, bf16[2,64,1024]{2,1,0:T(8,128)(2,1)}, u32[]{:S(2)}, u32[]{:S(2)}) collective-permute-start(bf16[2,64,1024]{2,1,0:T(8,128)(2,1)} %get-tuple-element.110), channel_id=1, source_target_pairs={{0,2},{2,4},{4,6},{6,0},{1,3},{3,5},{5,7},{7,1},{8,10},{10,12},{12... | collective-permute-start | bytes 786440 | tf_op jit(solution)/shard_map/ppermute | solution.py:405
  8.0 22.6 %collective-permute-start.1 = (bf16[2,64,1024]{2,1,0:T(8,128)(2,1)}, bf16[2,64,1024]{2,1,0:T(8,128)(2,1)}, u32[]{:S(2)}, u32[]{:S(2)}) collective-permute-start(bf16[2,64,1024]{2,1,0:T(8,128)(2,1)} %get-tuple-element.112), channel_id=1, source_target_pairs={{0,4},{2,6},{4,0},{6,2},{1,5},{3,7},{5,1},{7,3},{8,12},{10,14},{12... | collective-permute-start | bytes 786440 | tf_op jit(solution)/shard_map/ppermute | solution.py:405
  9.1 25.9 %collective-permute-start.3 = (bf16[2,256,1024]{2,1,0:T(8,128)(2,1)S(1)}, bf16[2,256,1024]{2,1,0:T(8,128)(2,1)}, u32[]{:S(2)}, u32[]{:S(2)}) collective-permute-start(bf16[2,256,1024]{2,1,0:T(8,128)(2,1)S(1)} %bitcast.75), channel_id=1, source_target_pairs={{0,1},{1,0},{2,3},{3,2},{4,5},{5,4},{6,7},{7,6},{8,9},{9,8},{10,11... | collective-permute-start | bytes 3145736 | tf_op jit(solution)/shard_map/ppermute | solution.py:409
  13.9 3.4 %copy-start.14 = (bf16[4,4,512]{2,1,0:T(4,128)(2,1)S(1)}, bf16[4,4,512]{2,1,0:T(4,128)(2,1)}, u32[]{:S(2)}) copy-start(bf16[4,4,512]{2,1,0:T(4,128)(2,1)} %param.15) | copy-start | bytes 49156
  14.9 2.3 %copy-start = (bf16[2,512,512]{2,1,0:T(8,128)(2,1)S(1)}, bf16[2,512,512]{2,1,0:T(8,128)(2,1)}, u32[]{:S(2)}) copy-start(bf16[2,512,512]{2,1,0:T(8,128)(2,1)} %refs_5_.3) | copy-start | bytes 3145732
  14.9 2.3 %copy-start.1 = (bf16[2,512,512]{2,1,0:T(8,128)(2,1)S(1)}, bf16[2,512,512]{2,1,0:T(8,128)(2,1)}, u32[]{:S(2)}) copy-start(bf16[2,512,512]{2,1,0:T(8,128)(2,1)} %refs_6_.3) | copy-start | bytes 3145732
  35.0 25.9 %collective-permute-start.4 = (bf16[2,512,512]{2,1,0:T(8,128)(2,1)}, bf16[2,512,512]{2,1,0:T(8,128)(2,1)S(1)}, u32[]{:S(2)}, u32[]{:S(2)}) collective-permute-start(bf16[2,512,512]{2,1,0:T(8,128)(2,1)} %broadcast_select_fusion), channel_id=1, source_target_pairs={{0,1},{1,0},{2,3},{3,2},{4,5},{5,4},{6,7},{7,6},{8,9},{9,8},{10,11... | collective-permute-start | bytes 3145736 | tf_op jit(solution)/shard_map/ppermute | solution.py:409
  54.4 17.8 %all-to-all-start.1 = ((bf16[4,64,1024]{2,1,0:T(8,128)(2,1)}), bf16[4,64,1024]{2,1,0:T(8,128)(2,1)}, u32[]{:S(2)}, u32[]{:S(2)}) async-start(bf16[4,64,1024]{2,1,0:T(8,128)(2,1)} %bitcast.83), calls=%async_computation.1 | async-start | bytes 1048576 | tf_op jit(solution)/shard_map/all_to_all | solution.py:413
  60.8 14.7 %copy-start.4 = (bf16[256,256]{1,0:T(8,128)(2,1)S(1)}, bf16[256,256]{1,0:T(8,128)(2,1)}, u32[]{:S(2)}) copy-start(bf16[256,256]{1,0:T(8,128)(2,1)} %refs_11_.3) | copy-start | bytes 393220
  60.8 14.7 %collective-permute-start.6 = (bf16[2,512,512]{2,1,0:T(8,128)(2,1)S(1)}, bf16[2,512,512]{2,1,0:T(8,128)(2,1)}, u32[]{:S(2)}, u32[]{:S(2)}) collective-permute-start(bf16[2,512,512]{2,1,0:T(8,128)(2,1)S(1)} %collective-permute-done.4.refs_7_), channel_id=1, source_target_pairs={{0,8},{8,0},{16,24},{24,16},{1,9},{9,1},{17,25},{25,17},{2,10},{10... | collective-permute-start | bytes 3145736 | tf_op jit(solution)/shard_map/ppermute | solution.py:409
  60.9 14.7 %collective-permute-start.5 = (bf16[256,1024]{1,0:T(8,128)(2,1)}, bf16[256,1024]{1,0:T(8,128)(2,1)}, u32[]{:S(2)}, u32[]{:S(2)}) collective-permute-start(bf16[256,1024]{1,0:T(8,128)(2,1)} %hidden_row.2.refs_1_.refs_2_), channel_id=1, source_target_pairs={{0,1},{1,0},{2,3},{3,2},{4,5},{5,4},{6,7},{7,6},{8,9},{9,8},{10,11... | collective-permute-start | bytes 1572872 | tf_op jit(solution)/shard_map/ppermute | solution.py:409
  74.4 13.2 %collective-permute-start.7 = (bf16[256,1024]{1,0:T(8,128)(2,1)}, bf16[256,1024]{1,0:T(8,128)(2,1)}, u32[]{:S(2)}, u32[]{:S(2)}) collective-permute-start(bf16[256,1024]{1,0:T(8,128)(2,1)} %hidden_row.3.refs_1_.refs_3_), channel_id=1, source_target_pairs={{0,1},{1,0},{2,3},{3,2},{4,5},{5,4},{6,7},{7,6},{8,9},{9,8},{10,11... | collective-permute-start | bytes 1572872 | tf_op jit(solution)/shard_map/ppermute | solution.py:409
  75.6 1.0 copy-start.2
  87.6 19.7 %all-to-all-start.2 = ((bf16[4,64,1024]{2,1,0:T(8,128)(2,1)}), bf16[4,64,1024]{2,1,0:T(8,128)(2,1)}, u32[]{:S(2)}, u32[]{:S(2)}) async-start(bf16[4,64,1024]{2,1,0:T(8,128)(2,1)} %bitcast.82), calls=%async_computation.2 | async-start | bytes 1048576 | tf_op jit(solution)/shard_map/all_to_all | solution.py:413
  91.8 0.9 copy-start.3
  107.2 5.1 %collective-permute-start.8 = (bf16[8,144,512]{2,1,0:T(8,128)(2,1)}, bf16[8,144,512]{2,1,0:T(8,128)(2,1)S(1)}, u32[]{:S(2)}, u32[]{:S(2)}) collective-permute-start(bf16[8,144,512]{2,1,0:T(8,128)(2,1)} %get-tuple-element.92), channel_id=1, source_target_pairs={{0,8},{8,0},{16,24},{24,16},{1,9},{9,1},{17,25},{25,17},{2,10},{10... | collective-permute-start | bytes 3538952 | tf_op jit(solution)/shard_map/ppermute | solution.py:409
  107.3 20.3 %all-to-all-start.3 = ((bf16[4,64,1024]{2,1,0:T(8,128)(2,1)}), bf16[4,64,1024]{2,1,0:T(8,128)(2,1)S(1)}, u32[]{:S(2)}, u32[]{:S(2)}) async-start(bf16[4,64,1024]{2,1,0:T(8,128)(2,1)} %bitcast.24), calls=%async_computation.3 | async-start | bytes 1048576 | tf_op jit(solution)/shard_map/all_to_all | solution.py:413
  112.4 1.0 copy-start.11
  116.3 11.2 %collective-permute-start.9 = (bf16[144,512]{1,0:T(8,128)(2,1)}, bf16[144,512]{1,0:T(8,128)(2,1)S(1)}, u32[]{:S(2)}, u32[]{:S(2)}) collective-permute-start(bf16[144,512]{1,0:T(8,128)(2,1)} %get-tuple-element.93), channel_id=1, source_target_pairs={{0,16},{8,24},{16,0},{24,8},{1,17},{9,25},{17,1},{25,9},{2,18},{10... | collective-permute-start | bytes 442376 | tf_op jit(solution)/shard_map/ppermute | solution.py:409
  117.8 9.7 %collective-permute-start.11 = (bf16[144,512]{1,0:T(8,128)(2,1)}, bf16[144,512]{1,0:T(8,128)(2,1)S(1)}, u32[]{:S(2)}, u32[]{:S(2)}) collective-permute-start(bf16[144,512]{1,0:T(8,128)(2,1)} %get-tuple-element.98), channel_id=1, source_target_pairs={{0,16},{8,24},{16,0},{24,8},{1,17},{9,25},{17,1},{25,9},{2,18},{10... | collective-permute-start | bytes 442376 | tf_op jit(solution)/shard_map/ppermute | solution.py:409
  118.4 11.2 %collective-permute-start.13 = (bf16[144,512]{1,0:T(8,128)(2,1)}, bf16[144,512]{1,0:T(8,128)(2,1)S(1)}, u32[]{:S(2)}, u32[]{:S(2)}) collective-permute-start(bf16[144,512]{1,0:T(8,128)(2,1)} %get-tuple-element.99), channel_id=1, source_target_pairs={{0,16},{8,24},{16,0},{24,8},{1,17},{9,25},{17,1},{25,9},{2,18},{10... | collective-permute-start | bytes 442376 | tf_op jit(solution)/shard_map/ppermute | solution.py:409
  119.9 26.4 %collective-permute-start.15 = (bf16[144,512]{1,0:T(8,128)(2,1)}, bf16[144,512]{1,0:T(8,128)(2,1)S(1)}, u32[]{:S(2)}, u32[]{:S(2)}) collective-permute-start(bf16[144,512]{1,0:T(8,128)(2,1)} %get-tuple-element.100), channel_id=1, source_target_pairs={{0,16},{8,24},{16,0},{24,8},{1,17},{9,25},{17,1},{25,9},{2,18},{10... | collective-permute-start | bytes 442376 | tf_op jit(solution)/shard_map/ppermute | solution.py:409
  127.5 8.3 %copy-start.5 = (bf16[4,64,1024]{2,1,0:T(8,128)(2,1)}, bf16[4,64,1024]{2,1,0:T(8,128)(2,1)S(1)}, u32[]{:S(2)}) copy-start(bf16[4,64,1024]{2,1,0:T(8,128)(2,1)S(1)} %all-to-all-done.3) | copy-start | bytes 1572868
  130.7 15.5 %collective-permute-start.10 = (bf16[144,512]{1,0:T(8,128)(2,1)S(1)}, bf16[144,512]{1,0:T(8,128)(2,1)S(1)}, u32[]{:S(2)}, u32[]{:S(2)}) collective-permute-start(bf16[144,512]{1,0:T(8,128)(2,1)S(1)} %get-tuple-element.113), channel_id=1, source_target_pairs={{0,2},{2,4},{4,6},{6,0},{1,3},{3,5},{5,7},{7,1},{8,10},{10,12},{12... | collective-permute-start | bytes 442376 | tf_op jit(solution)/shard_map/ppermute | solution.py:405
  132.8 13.4 %collective-permute-start.14 = (bf16[144,512]{1,0:T(8,128)(2,1)S(1)}, bf16[144,512]{1,0:T(8,128)(2,1)S(1)}, u32[]{:S(2)}, u32[]{:S(2)}) collective-permute-start(bf16[144,512]{1,0:T(8,128)(2,1)S(1)} %get-tuple-element.114), channel_id=1, source_target_pairs={{0,6},{2,0},{4,2},{6,4},{1,7},{3,1},{5,3},{7,5},{8,14},{10,8},{12,... | collective-permute-start | bytes 442376 | tf_op jit(solution)/shard_map/ppermute | solution.py:405
  134.9 13.5 %collective-permute-start.12 = (bf16[144,512]{1,0:T(8,128)(2,1)S(1)}, bf16[144,512]{1,0:T(8,128)(2,1)S(1)}, u32[]{:S(2)}, u32[]{:S(2)}) collective-permute-start(bf16[144,512]{1,0:T(8,128)(2,1)S(1)} %get-tuple-element.115), channel_id=1, source_target_pairs={{0,4},{2,6},{4,0},{6,2},{1,5},{3,7},{5,1},{7,3},{8,12},{10,14},{12... | collective-permute-start | bytes 442376 | tf_op jit(solution)/shard_map/ppermute | solution.py:405
  141.6 30.8 %all-to-all-start.4 = ((bf16[4,64,1024]{2,1,0:T(8,128)(2,1)}), bf16[4,64,1024]{2,1,0:T(8,128)(2,1)S(1)}, u32[]{:S(2)}, u32[]{:S(2)}) async-start(bf16[4,64,1024]{2,1,0:T(8,128)(2,1)} %bitcast.26), calls=%async_computation.4 | async-start | bytes 1048576 | tf_op jit(solution)/shard_map/all_to_all | solution.py:413
  149.4 3.8 %collective-permute-start.16 = (bf16[16,512]{1,0:T(8,128)(2,1)S(1)}, bf16[16,512]{1,0:T(8,128)(2,1)S(1)}, u32[]{:S(2)}, u32[]{:S(2)}) collective-permute-start(bf16[16,512]{1,0:T(8,128)(2,1)S(1)} %slice.104), channel_id=1, source_target_pairs={{0,1},{1,0},{2,3},{3,2},{4,5},{5,4},{6,7},{7,6},{8,9},{9,8},{10,11... | collective-permute-start | bytes 49160 | tf_op jit(solution)/shard_map/ppermute | solution.py:409
  153.3 6.6 %collective-permute-start.19 = (bf16[144,512]{1,0:T(8,128)(2,1)S(1)}, bf16[144,512]{1,0:T(8,128)(2,1)S(1)}, u32[]{:S(2)}, u32[]{:S(2)}) collective-permute-start(bf16[144,512]{1,0:T(8,128)(2,1)S(1)} %concatenate.33), channel_id=1, source_target_pairs={{0,6},{2,0},{4,2},{6,4},{1,7},{3,1},{5,3},{7,5},{8,14},{10,8},{12,... | collective-permute-start | bytes 442376 | tf_op jit(solution)/shard_map/ppermute | solution.py:405
  157.2 13.2 %collective-permute-start.18 = (bf16[144,512]{1,0:T(8,128)(2,1)S(1)}, bf16[144,512]{1,0:T(8,128)(2,1)S(1)}, u32[]{:S(2)}, u32[]{:S(2)}) collective-permute-start(bf16[144,512]{1,0:T(8,128)(2,1)S(1)} %concatenate.33), channel_id=1, source_target_pairs={{0,4},{2,6},{4,0},{6,2},{1,5},{3,7},{5,1},{7,3},{8,12},{10,14},{12... | collective-permute-start | bytes 442376 | tf_op jit(solution)/shard_map/ppermute | solution.py:405
  157.2 14.7 %collective-permute-start.17 = (bf16[144,512]{1,0:T(8,128)(2,1)S(1)}, bf16[144,512]{1,0:T(8,128)(2,1)S(1)}, u32[]{:S(2)}, u32[]{:S(2)}) collective-permute-start(bf16[144,512]{1,0:T(8,128)(2,1)S(1)} %concatenate.33), channel_id=1, source_target_pairs={{0,2},{2,4},{4,6},{6,0},{1,3},{3,5},{5,7},{7,1},{8,10},{10,12},{12... | collective-permute-start | bytes 442376 | tf_op jit(solution)/shard_map/ppermute | solution.py:405
  157.8 18.2 %collective-permute-start.20 = (bf16[144,512]{1,0:T(8,128)(2,1)S(1)}, bf16[144,512]{1,0:T(8,128)(2,1)S(1)}, u32[]{:S(2)}, u32[]{:S(2)}) collective-permute-start(bf16[144,512]{1,0:T(8,128)(2,1)S(1)} %concatenate.33), channel_id=1, source_target_pairs={{0,16},{8,24},{16,0},{24,8},{1,17},{9,25},{17,1},{25,9},{2,18},{10... | collective-permute-start | bytes 442376 | tf_op jit(solution)/shard_map/ppermute | solution.py:409
  159.9 16.1 %collective-permute-start.23 = (bf16[144,512]{1,0:T(8,128)(2,1)S(1)}, bf16[144,512]{1,0:T(8,128)(2,1)S(1)}, u32[]{:S(2)}, u32[]{:S(2)}) collective-permute-start(bf16[144,512]{1,0:T(8,128)(2,1)S(1)} %collective-permute-done.19), channel_id=1, source_target_pairs={{0,16},{8,24},{16,0},{24,8},{1,17},{9,25},{17,1},{25,9},{2,18},{10... | collective-permute-start | bytes 442376 | tf_op jit(solution)/shard_map/ppermute | solution.py:409
  170.3 5.7 %collective-permute-start.22 = (bf16[144,512]{1,0:T(8,128)(2,1)S(1)}, bf16[144,512]{1,0:T(8,128)(2,1)S(1)}, u32[]{:S(2)}, u32[]{:S(2)}) collective-permute-start(bf16[144,512]{1,0:T(8,128)(2,1)S(1)} %collective-permute-done.18), channel_id=1, source_target_pairs={{0,16},{8,24},{16,0},{24,8},{1,17},{9,25},{17,1},{25,9},{2,18},{10... | collective-permute-start | bytes 442376 | tf_op jit(solution)/shard_map/ppermute | solution.py:409
  171.8 5.4 %collective-permute-start.21 = (bf16[144,512]{1,0:T(8,128)(2,1)S(1)}, bf16[144,512]{1,0:T(8,128)(2,1)S(1)}, u32[]{:S(2)}, u32[]{:S(2)}) collective-permute-start(bf16[144,512]{1,0:T(8,128)(2,1)S(1)} %collective-permute-done.17), channel_id=1, source_target_pairs={{0,16},{8,24},{16,0},{24,8},{1,17},{9,25},{17,1},{25,9},{2,18},{10... | collective-permute-start | bytes 442376 | tf_op jit(solution)/shard_map/ppermute | solution.py:409
  172.4 4.9 %copy-start.9 = (bf16[4,64,1024]{2,1,0:T(8,128)(2,1)}, bf16[4,64,1024]{2,1,0:T(8,128)(2,1)S(1)}, u32[]{:S(2)}) copy-start(bf16[4,64,1024]{2,1,0:T(8,128)(2,1)S(1)} %all-to-all-done.4) | copy-start | bytes 1572868
  172.4 15.8 %all-to-all-start.5 = ((bf16[4,64,1024]{2,1,0:T(8,128)(2,1)}), bf16[4,64,1024]{2,1,0:T(8,128)(2,1)S(1)}, u32[]{:S(2)}, u32[]{:S(2)}) async-start(bf16[4,64,1024]{2,1,0:T(8,128)(2,1)} %bitcast.34), calls=%async_computation.5 | async-start | bytes 1048576 | tf_op jit(solution)/shard_map/all_to_all | solution.py:413
  175.9 3.4 %copy-start.7 = (bf16[4,144,512]{2,1,0:T(8,128)(2,1)}, bf16[4,144,512]{2,1,0:T(8,128)(2,1)S(1)}, u32[]{:S(2)}) copy-start(bf16[4,144,512]{2,1,0:T(8,128)(2,1)S(1)} %pad_maximum_fusion.refs_0_) | copy-start | bytes 1769476
  176.0 2.1 %collective-permute-start.24 = (bf16[4,144,512]{2,1,0:T(8,128)(2,1)S(1)}, bf16[4,144,512]{2,1,0:T(8,128)(2,1)S(1)}, u32[]{:S(2)}, u32[]{:S(2)}) collective-permute-start(bf16[4,144,512]{2,1,0:T(8,128)(2,1)S(1)} %pad_maximum_fusion.refs_0_), channel_id=1, source_target_pairs={{0,8},{8,0},{16,24},{24,16},{1,9},{9,1},{17,25},{25,17},{2,10},{10... | collective-permute-start | bytes 1769480 | tf_op jit(solution)/shard_map/ppermute | solution.py:409
  177.3 2.1 %copy-start.8 = (bf16[4,144,512]{2,1,0:T(8,128)(2,1)}, bf16[4,144,512]{2,1,0:T(8,128)(2,1)S(1)}, u32[]{:S(2)}) copy-start(bf16[4,144,512]{2,1,0:T(8,128)(2,1)S(1)} %pad_maximum_fusion.1.refs_1_) | copy-start | bytes 1769476
  177.3 2.1 %collective-permute-start.25 = (bf16[4,144,512]{2,1,0:T(8,128)(2,1)S(1)}, bf16[4,144,512]{2,1,0:T(8,128)(2,1)S(1)}, u32[]{:S(2)}, u32[]{:S(2)}) collective-permute-start(bf16[4,144,512]{2,1,0:T(8,128)(2,1)S(1)} %pad_maximum_fusion.1.refs_1_), channel_id=1, source_target_pairs={{0,8},{8,0},{16,24},{24,16},{1,9},{9,1},{17,25},{25,17},{2,10},{10... | collective-permute-start | bytes 1769480 | tf_op jit(solution)/shard_map/ppermute | solution.py:409
  178.0 1.4 copy-start.12
  179.4 0.8 copy-start.13
  188.1 0.8 copy-start.10

commit v4 on v3

--- a/solution.py
+++ b/solution.py
@@ -40,58 +40,54 @@
     return pltpu.HBM(dims, kind)
 
 
-def turned_blocks(table, at, n, rows):
+def turned_blocks(table, at, step, n, rows, axis):
     return jnp.concatenate(
         [
-            lax.dynamic_slice_in_dim(table, lax.rem(at + n - j, n) * rows, rows, 1)
+            lax.dynamic_slice_in_dim(table, lax.rem(at + n + step * j, n) * rows, rows, axis)
             for j in range(n)
         ],
-        axis=1,
+        axis=axis,
     )
 
 
 def mix_tables(mix, at, n, rows, cw):
+    size = mix.shape[0]
     same = lax.broadcasted_iota(jnp.int32, (1, cw, 1, cw), 1) == lax.broadcasted_iota(
         jnp.int32, (1, cw, 1, cw), 3
     )
 
     def spread(table):
         grown = jnp.where(same, table[:, None, :, None], jnp.zeros((), BF))
-        return grown.reshape(table.shape[0] * cw, table.shape[1] * cw)
-
-    ahead = turned_blocks(mix, at, n, rows)
-    ahead = jnp.stack([spread(ahead[h::rows]) for h in range(rows)])
-    by_row = mix.reshape(n, rows, -1).transpose(1, 0, 2).reshape(mix.shape)
-    back = jnp.stack([spread(by_row[:, h::rows].T) for h in range(rows)])
-    return ahead, back
-
-
-def column_mix_kernel(rows, table, *refs):
-    sources, outs = refs[:-rows], refs[-rows:]
-    for h in range(rows):
-        total = None
-        for j, source in enumerate(sources):
-            deep = source.shape[0]
-            term = jnp.dot(
-                table[h, :, j * deep : (j + 1) * deep], source[...], preferred_element_type=F
-            )
-            total = term if total is None else total + term
-        outs[h][...] = total.astype(BF)
-
-
-def column_mix(table, sources, name):
-    rows, deep, size = table.shape
+        return grown.reshape(size * cw, size * cw)
+
+    ahead = turned_blocks(turned_blocks(mix, at, -1, n, rows, 1), at, 1, n, rows, 0)
+    back = mix.T.reshape(n, rows, n, rows).transpose(1, 0, 3, 2).reshape(size, size)
+    return spread(ahead), spread(back)
+
+
+def column_mix_kernel(count, table, *refs):
+    sources, outs = refs[:count], refs[count:]
+    whole_source = jnp.concatenate([source[...] for source in sources], axis=0)
+    total = jnp.dot(table[...], whole_source, preferred_element_type=F).astype(BF)
+    deep = outs[0].shape[0]
+    for i, out in enumerate(outs):
+        out[...] = total[i * deep : (i + 1) * deep]
+
+
+def column_mix(table, sources, outs, name):
+    size = table.shape[0]
     width = sources[0].shape[-1]
     lanes = 512
+    deep = size // outs
     return pl.pallas_call(
-        functools.partial(column_mix_kernel, rows),
-        out_shape=[shape_of((deep, width))] * rows,
+        functools.partial(column_mix_kernel, len(sources)),
+        out_shape=[shape_of((deep, width))] * outs,
         grid=(width // lanes,),
-        in_specs=[pl.BlockSpec((rows, deep, size), lambda j: (0, 0, 0))]
+        in_specs=[pl.BlockSpec((size, size), lambda j: (0, 0))]
         + [pl.BlockSpec((source.shape[0], lanes), lambda j: (0, j)) for source in sources],
-        out_specs=[pl.BlockSpec((deep, lanes), lambda j: (0, j))] * rows,
+        out_specs=[pl.BlockSpec((deep, lanes), lambda j: (0, j))] * outs,
         name=name,
-    )(*held_in_hbm(table, *sources))
+    )(*held_in_hbm(table), *sources)
 
 
 def column_sum_kernel(cw, rows, *refs):
@@ -125,53 +121,56 @@
     )(*held_in_hbm(*pieces, *sources))
 
 
-def hidden_kernel(rows_in, x, mixed, hidden):
+def hidden_kernel(n, place, rows_in, x, own, *refs):
+    received, (hidden, mixed) = refs[: n - 1], refs[n - 1 :]
+    cw, lanes = own.shape
+    side = pl.ds(pl.multiple_of(pl.program_id(0) * lanes, lanes), lanes)
+    for i in range(n):
+        spot = pl.multiple_of(lax.rem(place[0] + n - i, n) * cw, cw)
+        mixed[pl.ds(spot, cw), :] = own[...] if i == 0 else received[i - 1][:, side]
     second = jnp.dot(rows_in[...], mixed[...], preferred_element_type=F)
     hidden[...] = (x[...].astype(F) + second).astype(BF)
 
 
-def hidden_row(rows_in, inputs, h, mixed):
-    cols, width = mixed.shape
+def hidden_row(place, rows_in, inputs, h, pieces):
+    cols, width = inputs.shape[1:]
+    n = len(pieces)
     lanes = 512
     column = pl.BlockSpec((cols, lanes), lambda j: (0, j))
     return pl.pallas_call(
-        hidden_kernel,
-        out_shape=shape_of((cols, width)),
+        functools.partial(hidden_kernel, n),
+        out_shape=[shape_of((cols, width))] * 2,
         grid=(width // lanes,),
         in_specs=[
+            SM,
             pl.BlockSpec((cols, cols), lambda j: (0, 0)),
             pl.BlockSpec((None, cols, lanes), lambda j: (h, 0, j)),
-            column,
-        ],
-        out_specs=column,
+            pl.BlockSpec((cols // n, lanes), lambda j: (0, j)),
+        ]
+        + [VM] * (n - 1),
+        out_specs=[column, column],
         name="hidden_row",
-    )(*held_in_hbm(rows_in, inputs, mixed))
+    )(place, *held_in_hbm(rows_in, inputs, pieces[0]), *pieces[1:])
 
 
 def channel_kernel(first, *refs):
-    (place, h_own, h_oth, c_own, c_oth, wg_own, wu_own, lent, lent_too, mix_g, mix_u) = refs[:11]
-    rows_in, mixed, *before = refs[11 : 13 if first else 14]
-    hid_grad, back_g, back_u, turned, mix_sum, row_sum, mid_g, mid_u = refs[-8:]
+    (place, h_own, h_oth, c_own, c_oth, wg_own, wu_own, *lent) = refs[:11]
+    mix_g, mix_u, rows_in, mixed, *before = refs[11 : 15 if first else 16]
+    hid_grad, back_g, back_u, turned, mix_sum, row_sum, mid = refs[-7:]
+    mid_g, mid_u = mid.at[0], mid.at[1]
     local, size = wg_own.shape[:2]
     blocks = 2 * local
     cols = h_own.shape[0]
-
-    def middle(base, h, wg, wu):
-        for k in range(local):
-            part = h[:, k * size : (k + 1) * size]
-            mid_g[base + k] = jnp.dot(part, wg[k], preferred_element_type=F)
-            mid_u[base + k] = jnp.dot(part, wu[k], preferred_element_type=F)
-
-    middle(0, h_own, wg_own, wu_own)
-
-    @pl.when(place[2] == 0)
-    def _():
-        middle(local, h_oth, lent, lent_too)
-
-    @pl.when(place[2] != 0)
-    def _():
-        middle(local, h_oth, lent_too, lent)
-
+    for k in range(local):
+        part = h_own[:, k * size : (k + 1) * size]
+        mid_g[k] = jnp.dot(part, wg_own[k], preferred_element_type=F)
+        mid_u[k] = jnp.dot(part, wu_own[k], preferred_element_type=F)
+    core, x = place[2], place[3]
+    for i, block in enumerate(lent):
+        table = core if i < 2 else 1 - core
+        k = x if i % 2 == 0 else 1 - x
+        part = h_oth[:, pl.ds(pl.multiple_of(k * size, size), size)]
+        mid[table, local + k] = jnp.dot(part, block[...], preferred_element_type=F)
     mix_sum[...] = jnp.zeros_like(mix_sum)
     deep, lanes = 16, 128
 
@@ -238,20 +237,18 @@
         in_specs=[SM]
         + wholes(h_own, h_oth)
         + [row, row]
-        + [VM] * 7
-        + wholes(mixed, *before),
+        + [VM] * 2
+        + wholes(*weights[2:], *mixes, rows_in, mixed, *before),
         out_specs=[whole(cols, width)] * 4
         + [whole(2, blocks, local, 8, size), whole(cols, cols)],
-        scratch_shapes=[pltpu.VMEM((blocks, cols, size), F)] * 2,
+        scratch_shapes=[pltpu.VMEM((2, blocks, cols, size), F)],
         compiler_params=PARAMS,
         name="channel_row",
     )(
         place,
         *held_in_hbm(h_own, h_oth, cot, cot_oth),
-        *weights,
-        *mixes,
-        rows_in,
-        *held_in_hbm(mixed, *before),
+        *weights[:2],
+        *held_in_hbm(*weights[2:], *mixes, rows_in, mixed, *before),
     )
 
 
@@ -328,7 +325,7 @@
         out_specs=[whole(deep, size)] * n + [whole(n, deep, size)],
         compiler_params=PARAMS,
         name="core_add",
-    )(place, *held_in_hbm(kept, got))
+    )(place, *held_in_hbm(kept), got)
 
 
 def unpack_kernel(n, scales, place, *refs):
@@ -377,28 +374,28 @@
         scratch_shapes=[pltpu.VMEM((4 * n, size), F)],
         compiler_params=PARAMS,
         name="unpack",
-    )(place, *held_in_hbm(*held))
-
-
-def finish_kernel(rows, *refs):
-    grads, backs, out = refs[:rows], refs[rows:-1], refs[-1]
-    for h in range(rows):
-        out[h] = (grads[h][...].astype(F) + backs[h][...].astype(F)).astype(BF)
-
-
-def finish(grads, backs):
-    rows = len(grads)
-    cols, width = grads[0].shape
+    )(place, *held)
+
+
+def finish_kernel(grad, back, *refs):
+    lanes = grad.shape[1]
+    side = pl.ds(pl.multiple_of(pl.program_id(0) * lanes, lanes), lanes)
+    refs[-1][...] = (grad[...].astype(F) + back[:, side].astype(F)).astype(BF)
+
+
+def finish(h, rows, grad, back, before):
+    cols, width = grad.shape
     lanes = 512
-    column = pl.BlockSpec((cols, lanes), lambda j: (0, j))
     return pl.pallas_call(
-        functools.partial(finish_kernel, rows),
+        finish_kernel,
         out_shape=shape_of((rows, cols, width)),
         grid=(width // lanes,),
-        in_specs=[column] * (2 * rows),
-        out_specs=pl.BlockSpec((rows, cols, lanes), lambda j: (0, 0, j)),
+        in_specs=[pl.BlockSpec((cols, lanes), lambda j: (0, j)), VM]
+        + [pl.BlockSpec(memory_space=pltpu.HBM)] * len(before),
+        out_specs=pl.BlockSpec((None, cols, lanes), lambda j: (h, 0, j)),
+        input_output_aliases={2: 0} if before else {},
         name="finish",
-    )(*held_in_hbm(*grads, *backs))
+    )(*held_in_hbm(grad), back, *before)
 
 
 def shifted(value, by, n):
@@ -470,23 +467,34 @@
     ]
     x_cols = [ways[0]] + [shifted(ways[i], i, n) for i in range(1, n)]
     x_cols = [part.reshape(rows * cw, width) for part in x_cols]
-    cot_oth = swapped(cot, "chan", 1, 2)
-    lent = jnp.where(core == 0, blocks_gate, blocks_up)
-    lent, _ = lax.optimization_barrier((lent, cot_oth))
+    lent = pick(jnp.where(core == 0, blocks_gate, blocks_up), x)
     lent = swapped(lent, "chan", 1, 2)
+    leaving, _ = lax.optimization_barrier((cot, lent))
+    cot_oth = swapped(leaving, "chan", 1, 2)
+    lent = [lent, swapped(lent, "dp", 2, 4)]
     mixes = (relative(mix_gate), relative(mix_up))
 
     x_cols, ahead, behind, mixes = lax.optimization_barrier((x_cols, ahead, behind, mixes))
-    parts = column_mix(ahead, x_cols, "column_mix")
-    parts, cot_oth = lax.optimization_barrier((parts, cot_oth))
-    mixed = [traded(part.reshape(n, cw, width)).reshape(cols, width) for part in parts]
-    hidden = [hidden_row(rows_in, values, h, mixed[h]) for h in range(rows)]
-    leaving = list(hidden)
-    lender, _ = lax.optimization_barrier((lent, hidden[0]))
-    lent_too = swapped(lender, "dp", 1, 4)
-    weights = (blocks_gate, blocks_up, lent, lent_too)
-    leaving[0], _ = lax.optimization_barrier((leaving[0], lent))
-    others = [swapped(hid, "chan", 1, 2) for hid in leaving]
+    parts = column_mix(ahead, x_cols, n * rows, "column_mix")
+    parts, lent = lax.optimization_barrier((parts, lent))
+    passed = [swapped(block, "dp", 1, 4) for block in lent]
+    parts = list(parts)
+    held_up = [i for i in range(n * rows) if i not in (0, rows, 2 * rows)]
+    late, passed = lax.optimization_barrier(([parts[i] for i in held_up], passed))
+    for i, part in zip(held_up, late):
+        parts[i] = part
+    lent = lent + passed
+    got = [
+        [parts[h]] + [shifted(parts[i * rows + h], i, n) for i in range(1, n)]
+        for h in range(rows)
+    ]
+    got[0], cot_oth = lax.optimization_barrier((got[0], cot_oth))
+    hidden, mixed = [], []
+    for h in range(rows):
+        for held, value in zip((hidden, mixed), hidden_row(place, rows_in, values, h, got[h])):
+            held.append(value)
+    weights = (blocks_gate, blocks_up, *lent)
+    others = [swapped(hid, "chan", 1, 2) for hid in hidden]
     others[0], hidden[-1] = lax.optimization_barrier((others[0], hidden[-1]))
     grads, back_g, back_u, pieces, mix_sum, rows_sum = [], [], [], [], [], []
     for h in range(rows):
@@ -515,16 +523,16 @@
     *leaving, fours = core_add(n, place, kept, swapped(sent, "dp", 1, 4))
     by_x = [swapped(shard, "dp", 2, 4) for shard in leaving]
     pieces[1], _ = lax.optimization_barrier((pieces[1], by_x[1]))
-    turned = column_mix(behind, pieces, "column_back")
+    turned = column_mix(behind, pieces, rows, "column_back")
     backs = [traded(turned[0].reshape(n, cw, width))]
     late, _ = lax.optimization_barrier((pieces[1], turned[0]))
     cols_sum = column_sum(cw, x_cols, [pieces[0], late])
     cols_sum = cols_sum.reshape(rows, n, n * rows, cw).sum(-1).transpose(1, 0, 2)
-    cols_sum = turned_blocks(cols_sum.reshape(n * rows, n * rows), seq_at, n, rows)
+    cols_sum = turned_blocks(cols_sum.reshape(n * rows, n * rows), seq_at, -1, n, rows, 1)
     mine = scatter_seq(by_x, fours, cols_sum, n)
     held = [mine] + [shifted(mine, i, n) for i in range(1, n)]
     for part in turned[1:]:
-        part, _ = lax.optimization_barrier((part, held[1:]))
+        part, _ = lax.optimization_barrier((part, held[1]))
         backs.append(traded(part.reshape(n, cw, width)))
     backs = [part.reshape(cols, width) for part in backs]
     batch_all = lax.axis_size("dp")
@@ -535,7 +543,10 @@
     by_x = jnp.stack([swapped(shard, "dp", 2, 4) for shard in held])
     held = jnp.stack(held)
     by_core = swapped(held, "dp", 1, 4)
-    input_grad = finish(grads, backs)
+    done = []
+    for h in range(rows):
+        done = [finish(h, rows, grads[h], backs[h], done)]
+    input_grad = done[0]
     gate_sum, up_sum, rows_sum, mix_g, mix_u, cols_sum = unpack(
         n,
         rows,

time: 192 us -> 188 us (0.979)
  blocking collectives: 17.8 us -> 0 us
  starting transfers between devices: 50.1 us -> 59.3 us
  waiting for transfers between devices: 56.4 us -> 61.8 us
    all_to_all x1 -> x0, blocking collectives: 17.8 us -> none  [traded(): return lax.all_to_all(value, 'seq', split_axis=0, concat_axis=0, tiled=True)]
    ppermute x9 -> x15, starting transfers between devices: 15.6 us -> 24.6 us  [shifted(): return lax.ppermute(value, 'seq', [(i, (i + by) % n) for i in range(n)])]
    ppermute x17 -> x19, waiting for transfers between devices: 10.7 us -> 18.9 us  [swapped(): return lax.ppermute(value, axis, [(i, i ^ bit) for i in range(n)])]
    all_to_all x5 -> x4, waiting for transfers between devices: 21.8 us -> 14.3 us  [traded(): return lax.all_to_all(value, 'seq', split_axis=0, concat_axis=0, tiled=True)]
    ppermute x9 -> x15, waiting for transfers between devices: 23.9 us -> 28.6 us  [shifted(): return lax.ppermute(value, 'seq', [(i, (i + by) % n) for i in range(n)])]
    ppermute x17 -> x19, starting transfers between devices: 14.1 us -> 18.4 us  [swapped(): return lax.ppermute(value, axis, [(i, i ^ bit) for i in range(n)])]
    all_to_all x5 -> x4, starting transfers between devices: 20.4 us -> 16.3 us  [traded(): return lax.all_to_all(value, 'seq', split_axis=0, concat_axis=0, tiled=True)]
    another operation x1 -> x0, other arithmetic: 2.32 us -> none  [mix_tables(): ahead = jnp.stack([spread(ahead[h::rows]) for h in range(rows)])]
  transfers between devices with their start and end apart: 31 -> 38, of which waited for: 15 -> 14; matrix products, arithmetic and copies ran while one was open for 6% -> 7% of each run, Pallas kernels for 23% -> 25%
where the time goes in v4:
time: 188 us
  waiting for transfers between devices  61.8 us (33%)
  starting transfers between devices  59.3 us (32%)
  Pallas kernels  48.5 us (26%)
  local copies, waits for them, and re-layouts  11.3 us (6%)
  other arithmetic  5.83 us (3%)
    ppermute x15, waiting for transfers between devices, shifted(): return lax.ppermute(value, 'seq', [(i, (i + by) % n) for i in range(n)])  28.6 us
    ppermute x15, starting transfers between devices, shifted(): return lax.ppermute(value, 'seq', [(i, (i + by) % n) for i in range(n)])  24.6 us
    pallas_call x2, Pallas kernels, channel_row(): pl.pallas_call(once(functools.partial(channel_kernel, not before)), out_s...  20 us
    ppermute x19, waiting for transfers between devices, swapped(): return lax.ppermute(value, axis, [(i, i ^ bit) for i in range(n)])  18.9 us
    ppermute x19, starting transfers between devices, swapped(): return lax.ppermute(value, axis, [(i, i ^ bit) for i in range(n)])  18.4 us
    all_to_all x4, starting transfers between devices, traded(): return lax.all_to_all(value, 'seq', split_axis=0, concat_axis=0, tiled=True)  16.3 us
    all_to_all x4, waiting for transfers between devices, traded(): return lax.all_to_all(value, 'seq', split_axis=0, concat_axis=0, tiled=True)  14.3 us
    pallas_call x2, Pallas kernels, column_mix(): pl.pallas_call(functools.partial(column_mix_kernel, len(sources)), out_sh...  5.95 us
  transfers between devices with their start and end apart: 38, of which 14 were waited for; matrix products, arithmetic and copies ran while one was open for 7% of the time, Pallas kernels for 25%

profile of v4, /device:TPU:0, one launch (start us, length us, event | category | flops | bytes accessed | tf_op | source)
XLA Modules:
  0.0 187.8 jit_solution(7035723945307831353)
XLA Ops:
  0.7 1.3 fusion
  2.0 3.0 %collective-permute-start.3 = (bf16[512,512]{1,0:T(8,128)(2,1)S(1)}, bf16[512,512]{1,0:T(8,128)(2,1)}, u32[]{:S(2)}, u32[]{:S(2)}) collective-permute-start(bf16[512,512]{1,0:T(8,128)(2,1)S(1)} %fusion), channel_id=1, source_target_pairs={{0,1},{1,0},{2,3},{3,2},{4,5},{5,4},{6,7},{7,6},{8,9},{9,8},{10,11... | collective-permute-start | bytes 1572872 | tf_op jit(solution)/shard_map/ppermute | solution.py:406
  5.1 1.0 dynamic-slice_bitcast_fusion
  6.0 3.6 %collective-permute-start.2 = (bf16[2,64,1024]{2,1,0:T(8,128)(2,1)}, bf16[2,64,1024]{2,1,0:T(8,128)(2,1)S(1)}, u32[]{:S(2)}, u32[]{:S(2)}) collective-permute-start(bf16[2,64,1024]{2,1,0:T(8,128)(2,1)} %get-tuple-element.163), channel_id=1, source_target_pairs={{0,6},{2,0},{4,2},{6,4},{1,7},{3,1},{5,3},{7,5},{8,14},{10,8},{12,... | collective-permute-start | bytes 786440 | tf_op jit(solution)/shard_map/ppermute | solution.py:402
  9.6 1.0 collective-permute-start.1
  11.3 1.2 broadcast_select_fusion
  12.5 4.6 %collective-permute-done.3.refs_7_ = bf16[512,512]{1,0:T(8,128)(2,1)} collective-permute-done((bf16[512,512]{1,0:T(8,128)(2,1)S(1)}, bf16[512,512]{1,0:T(8,128)(2,1)}, u32[]{:S(2)}, u32[]{:S(2)}) %collective-permute-start.3) | collective-permute-done | bytes 524320 | tf_op jit(solution)/shard_map/ppermute | solution.py:406
  17.1 1.7 collective-permute-start.4
  18.8 1.6 collective-permute-start.10
  20.5 2.6 %select_n.97.table = bf16[512,512]{1,0:T(8,128)(2,1)} reshape(bf16[8,64,8,64]{3,2,1,0:T(8,128)(2,1)} %get-tuple-element.176) | data formatting | bytes 1048576 | tf_op jit(solution)/shard_map/jit(_where)/select_n | solution.py:60
  23.0 1.4 select_n.95.table
  24.5 7.5 %collective-permute-done.1 = bf16[2,64,1024]{2,1,0:T(8,128)(2,1)} collective-permute-done((bf16[2,64,1024]{2,1,0:T(8,128)(2,1)}, bf16[2,64,1024]{2,1,0:T(8,128)(2,1)}, u32[]{:S(2)}, u32[]{:S(2)}) %collective-permute-start.1) | collective-permute-done | bytes 262176 | tf_op jit(solution)/shard_map/ppermute | solution.py:402
  32.0 0.7 broadcast_in_dim.55.refs_12_
  32.7 0.7 broadcast_in_dim.54.refs_11_
  33.5 3.0 %column_mix.1 = (bf16[64,1024]{1,0:T(8,128)(2,1)}, bf16[64,1024]{1,0:T(8,128)(2,1)}, bf16[64,1024]{1,0:T(8,128)(2,1)}, bf16[64,1024]{1,0:T(8,128)(2,1)}, bf16[64...) custom-call(bf16[512,512]{1,0:T(8,128)(2,1)} %select_n.95.table, ...), custom_call_target="tpu_custom_call" | custom-call | tf_op jit(solution)/shard_map/column_mix/pallas_call | solution.py:82
  37.1 3.2 %collective-permute-start.6 = (bf16[64,1024]{1,0:T(8,128)(2,1)}, bf16[64,1024]{1,0:T(8,128)(2,1)S(1)}, u32[]{:S(2)}, u32[]{:S(2)}) collective-permute-start(bf16[64,1024]{1,0:T(8,128)(2,1)} %get-tuple-element.100), channel_id=1, source_target_pairs={{0,4},{2,6},{4,0},{6,2},{1,5},{3,7},{5,1},{7,3},{8,12},{10,14},{12... | collective-permute-start | bytes 393224 | tf_op jit(solution)/shard_map/ppermute | solution.py:402
  40.3 1.9 %collective-permute-start.9 = (bf16[64,1024]{1,0:T(8,128)(2,1)}, bf16[64,1024]{1,0:T(8,128)(2,1)S(1)}, u32[]{:S(2)}, u32[]{:S(2)}) collective-permute-start(bf16[64,1024]{1,0:T(8,128)(2,1)} %get-tuple-element.108), channel_id=1, source_target_pairs={{0,6},{2,0},{4,2},{6,4},{1,7},{3,1},{5,3},{7,5},{8,14},{10,8},{12,... | collective-permute-start | bytes 393224 | tf_op jit(solution)/shard_map/ppermute | solution.py:402
  42.3 3.2 %collective-permute-done.5.refs_0_ = bf16[64,1024]{1,0:T(8,128)(2,1)S(1)} collective-permute-done((bf16[64,1024]{1,0:T(8,128)(2,1)}, bf16[64,1024]{1,0:T(8,128)(2,1)S(1)}, u32[]{:S(2)}, u32[]{:S(2)}) %collective-permute-start.5) | collective-permute-done | bytes 131104 | tf_op jit(solution)/shard_map/ppermute | solution.py:402
  45.5 5.6 %collective-permute-done.6.refs_1_ = bf16[64,1024]{1,0:T(8,128)(2,1)S(1)} collective-permute-done((bf16[64,1024]{1,0:T(8,128)(2,1)}, bf16[64,1024]{1,0:T(8,128)(2,1)S(1)}, u32[]{:S(2)}, u32[]{:S(2)}) %collective-permute-start.6) | collective-permute-done | bytes 131104 | tf_op jit(solution)/shard_map/ppermute | solution.py:402
  51.1 5.1 %collective-permute-start.14 = (bf16[64,1024]{1,0:T(8,128)(2,1)}, bf16[64,1024]{1,0:T(8,128)(2,1)}, u32[]{:S(2)}, u32[]{:S(2)}) collective-permute-start(bf16[64,1024]{1,0:T(8,128)(2,1)} %get-tuple-element.118), channel_id=1, source_target_pairs={{0,6},{2,0},{4,2},{6,4},{1,7},{3,1},{5,3},{7,5},{8,14},{10,8},{12,... | collective-permute-start | bytes 393224 | tf_op jit(solution)/shard_map/ppermute | solution.py:402
  56.2 0.6 pad_add_fusion.place.refs_0_
  56.9 0.7 copy-done.16
  57.8 2.6 %hidden_row.2 = (bf16[256,1024]{1,0:T(8,128)(2,1)}, bf16[256,1024]{1,0:T(8,128)(2,1)}) custom-call(s32[4]{0:T(128)} %pad_add_fusion.place.refs_0_, bf16[256,256]{1,0:T(8,128)(2,1)} %refs_13_.3, bf16[2,256,1024]{2,1,0:T(8,128)(2,1)} %bitcast.57, bf16[64,1024]{1,0:T(8,128)(2,1)} %get-tuple-element.110.own, bf16[64,1024]{1,0:T(8,128)(2,1)} %copy-done.13, ...), custom_call_target="tpu_custom_call" | custom-call | tf_op jit(solution)/shard_map/hidden_row/pallas_call | solution.py:140
  60.5 0.6 collective-permute-start.11
  62.1 2.5 %hidden_row.3 = (bf16[256,1024]{1,0:T(8,128)(2,1)}, bf16[256,1024]{1,0:T(8,128)(2,1)}) custom-call(s32[4]{0:T(128)} %pad_add_fusion.place.refs_0_, bf16[256,256]{1,0:T(8,128)(2,1)} %refs_13_.3, bf16[2,256,1024]{2,1,0:T(8,128)(2,1)} %bitcast.58, bf16[64,1024]{1,0:T(8,128)(2,1)} %get-tuple-element.115.own, bf16[64,1024]{1,0:T(8,128)(2,1)} %copy-done.12, ...), custom_call_target="tpu_custom_call" | custom-call | tf_op jit(solution)/shard_map/hidden_row/pallas_call | solution.py:140
  64.6 1.1 collective-permute-start.15
  65.8 9.0 %collective-permute-done.11.refs_2_ = bf16[256,1024]{1,0:T(8,128)(2,1)} collective-permute-done((bf16[256,1024]{1,0:T(8,128)(2,1)}, bf16[256,1024]{1,0:T(8,128)(2,1)}, u32[]{:S(2)}, u32[]{:S(2)}) %collective-permute-start.11) | collective-permute-done | bytes 524320 | tf_op jit(solution)/shard_map/ppermute | solution.py:406
  74.8 9.9 %channel_row.2 = (bf16[256,1024]{1,0:T(8,128)(2,1)}, bf16[256,1024]{1,0:T(8,128)(2,1)}, bf16[256,1024]{1,0:T(8,128)(2,1)}, bf16[256,1024]{1,0:T(8,128)(2,1)}, f3...) custom-call(s32[4]{0:T(128)S(1)} %copy-done.2, bf16[256,1024]{1,0:T(8,128)(2,1)} %get-tuple-element.114.refs_1_.refs_2_, ...), custom_call_target="tpu_custom_call" | custom-call | tf_op jit(solution)/shard_map/channel_row/pallas_call | solution.py:232
  84.8 0.8 copy-done.11
  85.5 4.2 %all-to-all-start = ((bf16[4,64,1024]{2,1,0:T(8,128)(2,1)}), bf16[4,64,1024]{2,1,0:T(8,128)(2,1)S(1)}, u32[]{:S(2)}, u32[]{:S(2)}) async-start(bf16[4,64,1024]{2,1,0:T(8,128)(2,1)} %bitcast.74), calls=%async_computation | async-start | bytes 1048576 | tf_op jit(solution)/shard_map/all_to_all | solution.py:410
  89.8 10.1 %channel_row.3 = (bf16[256,1024]{1,0:T(8,128)(2,1)}, bf16[256,1024]{1,0:T(8,128)(2,1)}, bf16[256,1024]{1,0:T(8,128)(2,1)}, bf16[256,1024]{1,0:T(8,128)(2,1)}, f3...) custom-call(s32[4]{0:T(128)S(1)} %copy-done.2, bf16[256,1024]{1,0:T(8,128)(2,1)} %get-tuple-element.120.refs_1_.refs_3_, ...), custom_call_target="tpu_custom_call" | custom-call | tf_op jit(solution)/shard_map/channel_row/pallas_call | solution.py:232
  99.8 5.1 %sums.1 = (bf16[8,144,512]{2,1,0:T(8,128)(2,1)}, bf16[8,144,512]{2,1,0:T(8,128)(2,1)}) custom-call(s32[4]{0:T(128)S(1)} %copy-done.2, f32[256,256]{1,0:T(8,128)} %get-tuple-element.135.refs_1_, bf16[256,1024]{1,0:T(8,128)(2,1)} %get-tuple-element.114.refs_1_.refs_2_, bf16[256,1024]{1,0:T(8,128)(2,1)} %get-tuple-element.120.refs_1_.refs_3_, ...), custom_call_target="tpu_custom_call" | custom-call | tf_op jit(solution)/shard_map/sums/pallas_call | solution.py:298
  105.0 5.1 %all-to-all-start.1 = ((bf16[4,64,1024]{2,1,0:T(8,128)(2,1)}), bf16[4,64,1024]{2,1,0:T(8,128)(2,1)S(1)}, u32[]{:S(2)}, u32[]{:S(2)}) async-start(bf16[4,64,1024]{2,1,0:T(8,128)(2,1)} %bitcast.18), calls=%async_computation.1 | async-start | bytes 1048576 | tf_op jit(solution)/shard_map/all_to_all | solution.py:410
  110.1 2.6 %core_add.1 = (bf16[144,512]{1,0:T(8,128)(2,1)}, bf16[144,512]{1,0:T(8,128)(2,1)}, bf16[144,512]{1,0:T(8,128)(2,1)}, bf16[144,512]{1,0:T(8,128)(2,1)}, bf16[4,144,512]{2,1,0:T(8,128)(2,1)}) custom-call(s32[4]{0:T(128)S(1)} %copy-done.2, bf16[8,144,512]{2,1,0:T(8,128)(2,1)} %get-tuple-element.142.refs_1_, bf16[8,144,512]{2,1,0:T(8,128)(2,1)S(1)} %collective-permute-done.16.refs_2_), custom_call_target="tpu_custom_call" | custom-call | tf_op jit(solution)/shard_map/core_add/pallas_call | solution.py:320
  112.8 1.5 collective-permute-start.17
  114.8 1.5 collective-permute-start.21
  116.8 8.4 %all-to-all-done.1 = bf16[4,64,1024]{2,1,0:T(8,128)(2,1)S(1)} async-done(((bf16[4,64,1024]{2,1,0:T(8,128)(2,1)}), bf16[4,64,1024]{2,1,0:T(8,128)(2,1)S(1)}, u32[]{:S(2)}, u32[]{:S(2)}) %all-to-all-start.1) | async-done | bytes 524320 | tf_op jit(solution)/shard_map/all_to_all | solution.py:410
  125.3 0.7 collective-permute-done.21
  126.0 1.2 fusion.4
  127.1 2.1 %collective-permute-start.18 = (bf16[144,512]{1,0:T(8,128)(2,1)S(1)}, bf16[144,512]{1,0:T(8,128)(2,1)S(1)}, u32[]{:S(2)}, u32[]{:S(2)}) collective-permute-start(bf16[144,512]{1,0:T(8,128)(2,1)S(1)} %get-tuple-element.167), channel_id=1, source_target_pairs={{0,2},{2,4},{4,6},{6,0},{1,3},{3,5},{5,7},{7,1},{8,10},{10,12},{12... | collective-permute-start | bytes 442376 | tf_op jit(solution)/shard_map/ppermute | solution.py:402
  129.2 2.0 %collective-permute-start.22 = (bf16[144,512]{1,0:T(8,128)(2,1)S(1)}, bf16[144,512]{1,0:T(8,128)(2,1)S(1)}, u32[]{:S(2)}, u32[]{:S(2)}) collective-permute-start(bf16[144,512]{1,0:T(8,128)(2,1)S(1)} %get-tuple-element.168), channel_id=1, source_target_pairs={{0,6},{2,0},{4,2},{6,4},{1,7},{3,1},{5,3},{7,5},{8,14},{10,8},{12,... | collective-permute-start | bytes 442376 | tf_op jit(solution)/shard_map/ppermute | solution.py:402
  131.3 0.9 collective-permute-start.20
  132.2 2.9 %column_back.1 = (bf16[256,1024]{1,0:T(8,128)(2,1)}, bf16[256,1024]{1,0:T(8,128)(2,1)}) custom-call(bf16[512,512]{1,0:T(8,128)(2,1)} %select_n.97.table, bf16[256,1024]{1,0:T(8,128)(2,1)} %bitcast.59, bf16[256,1024]{1,0:T(8,128)(2,1)} %bitcast.61), custom_call_target="tpu_custom_call" | custom-call | tf_op jit(solution)/shard_map/column_back/pallas_call | solution.py:82
  135.1 2.9 %column_sum.1 = f32[8,512]{1,0:T(8,128)} custom-call(bf16[256,1024]{1,0:T(8,128)(2,1)} %bitcast.60, bf16[256,1024]{1,0:T(8,128)(2,1)} %bitcast.62, bf16[128,1024]{1,0:T(8,128)(2,1)} %bitcast.68, bf16[128,1024]{1,0:T(8,128)(2,1)} %bitcast.7.refs_1_.refs_3_, bf16[128,1024]{1,0:T(8,128)(2,1)} %bitcast.9.refs_2_.refs_4_, bf16[128,1024]{1,0:T(8,128)(2,1)} %bitcast.72), custom_call_target="tpu_custom_call" | custom-call | tf_op jit(solution)/shard_map/column_sum/pallas_call | solution.py:112
  138.0 3.5 %all-to-all-start.3 = ((bf16[4,64,1024]{2,1,0:T(8,128)(2,1)}), bf16[4,64,1024]{2,1,0:T(8,128)(2,1)S(1)}, u32[]{:S(2)}, u32[]{:S(2)}) async-start(bf16[4,64,1024]{2,1,0:T(8,128)(2,1)} %bitcast.28), calls=%async_computation.3 | async-start | bytes 1048576 | tf_op jit(solution)/shard_map/all_to_all | solution.py:410
  141.5 0.8 reshape.112
  142.7 2.4 %collective-permute-done.20 = bf16[144,512]{1,0:T(8,128)(2,1)S(1)} collective-permute-done((bf16[144,512]{1,0:T(8,128)(2,1)S(1)}, bf16[144,512]{1,0:T(8,128)(2,1)S(1)}, u32[]{:S(2)}, u32[]{:S(2)}) %collective-permute-start.20) | collective-permute-done | bytes 147488 | tf_op jit(solution)/shard_map/ppermute | solution.py:402
  145.0 1.0 add_convert_fusion
  146.1 0.6 collective-permute-start.24
  146.7 3.2 %collective-permute-done.24 = bf16[16,512]{1,0:T(8,128)(2,1)S(1)} collective-permute-done((bf16[16,512]{1,0:T(8,128)(2,1)S(1)}, bf16[16,512]{1,0:T(8,128)(2,1)S(1)}, u32[]{:S(2)}, u32[]{:S(2)}) %collective-permute-start.24) | collective-permute-done | bytes 16416 | tf_op jit(solution)/shard_map/ppermute | solution.py:406
  149.9 3.9 %collective-permute-start.27 = (bf16[144,512]{1,0:T(8,128)(2,1)S(1)}, bf16[144,512]{1,0:T(8,128)(2,1)S(1)}, u32[]{:S(2)}, u32[]{:S(2)}) collective-permute-start(bf16[144,512]{1,0:T(8,128)(2,1)S(1)} %concatenate.37), channel_id=1, source_target_pairs={{0,6},{2,0},{4,2},{6,4},{1,7},{3,1},{5,3},{7,5},{8,14},{10,8},{12,... | collective-permute-start | bytes 442376 | tf_op jit(solution)/shard_map/ppermute | solution.py:402
  153.9 0.6 collective-permute-start.25
  154.5 1.5 collective-permute-start.28
  156.0 0.6 collective-permute-done.27
  156.6 1.5 collective-permute-start.31
  158.1 8.9 %collective-permute-done.26 = bf16[144,512]{1,0:T(8,128)(2,1)S(1)} collective-permute-done((bf16[144,512]{1,0:T(8,128)(2,1)S(1)}, bf16[144,512]{1,0:T(8,128)(2,1)S(1)}, u32[]{:S(2)}, u32[]{:S(2)}) %collective-permute-start.26) | collective-permute-done | bytes 147488 | tf_op jit(solution)/shard_map/ppermute | solution.py:402
  167.0 1.5 collective-permute-start.30
  169.0 3.5 %all-to-all-start.2 = ((bf16[4,64,1024]{2,1,0:T(8,128)(2,1)}), bf16[4,64,1024]{2,1,0:T(8,128)(2,1)S(1)}, u32[]{:S(2)}, u32[]{:S(2)}) async-start(bf16[4,64,1024]{2,1,0:T(8,128)(2,1)} %bitcast.26), calls=%async_computation.2 | async-start | bytes 1048576 | tf_op jit(solution)/shard_map/all_to_all | solution.py:410
  172.7 1.3 collective-permute-done.29
  174.2 2.0 %finish.2.refs_0_ = bf16[2,256,1024]{2,1,0:T(8,128)(2,1)} custom-call(bf16[256,1024]{1,0:T(8,128)(2,1)} %get-tuple-element.156.grad, bf16[256,1024]{1,0:T(8,128)(2,1)} %bitcast.69), custom_call_target="tpu_custom_call" | custom-call | tf_op jit(solution)/shard_map/finish/pallas_call | solution.py:389
  176.2 2.9 %unpack.1 = (f32[1024,512]{1,0:T(8,128)}, f32[1024,512]{1,0:T(8,128)}, f32[256,256]{1,0:T(8,128)}, f32[4,2,512]{2,1,0:T(2,128)}, f32[4,2,512]{2,1,0:T(2,128)}, /*index=5*/f32[8,8]{1,0:T(8,128)}) custom-call(s32[4]{0:T(128)S(1)} %copy-done.2, bf16[4,144,512]{2,1,0:T(8,128)(2,1)S(1)} %pad_maximum_fusion.refs_0_, ...), custom_call_target="tpu_custom_call" | custom-call | tf_op jit(solution)/shard_map/unpack/pallas_call | solution.py:362
  179.1 5.9 %all-to-all-done.2 = bf16[4,64,1024]{2,1,0:T(8,128)(2,1)S(1)} async-done(((bf16[4,64,1024]{2,1,0:T(8,128)(2,1)}), bf16[4,64,1024]{2,1,0:T(8,128)(2,1)S(1)}, u32[]{:S(2)}, u32[]{:S(2)}) %all-to-all-start.2) | async-done | bytes 524320 | tf_op jit(solution)/shard_map/all_to_all | solution.py:410
  184.9 0.8 copy-done.9
  185.8 2.0 %finish.3 = bf16[2,256,1024]{2,1,0:T(8,128)(2,1)} custom-call(bf16[256,1024]{1,0:T(8,128)(2,1)} %get-tuple-element.130.grad, bf16[256,1024]{1,0:T(8,128)(2,1)} %bitcast.70, bf16[2,256,1024]{2,1,0:T(8,128)(2,1)} %finish.2.refs_0_), custom_call_target="tpu_custom_call", output_to_operand_aliasing={{}: (2, {})} | custom-call | tf_op jit(solution)/shard_map/finish/pallas_call | solution.py:389
  (106 shorter events, 5.3 us)
Async XLA Ops:
  0.6 4.4 %copy-start.3 = (bf16[1,2,256,1024]{3,2,1,0:T(8,128)(2,1)S(1)}, bf16[1,2,256,1024]{3,2,1,0:T(8,128)(2,1)}, u32[]{:S(2)}) copy-start(bf16[1,2,256,1024]{3,2,1,0:T(8,128)(2,1)} %param.8) | copy-start | bytes 3145732
  2.0 8.7 %copy-start.19 = (bf16[8,8]{1,0:T(8,128)(2,1)S(1)}, bf16[8,8]{1,0:T(8,128)(2,1)}, u32[]{:S(2)}) copy-start(bf16[8,8]{1,0:T(8,128)(2,1)} %param.11) | copy-start | bytes 388
  2.0 15.1 %collective-permute-start.3 = (bf16[512,512]{1,0:T(8,128)(2,1)S(1)}, bf16[512,512]{1,0:T(8,128)(2,1)}, u32[]{:S(2)}, u32[]{:S(2)}) collective-permute-start(bf16[512,512]{1,0:T(8,128)(2,1)S(1)} %fusion), channel_id=1, source_target_pairs={{0,1},{1,0},{2,3},{3,2},{4,5},{5,4},{6,7},{7,6},{8,9},{9,8},{10,11... | collective-permute-start | bytes 1572872 | tf_op jit(solution)/shard_map/ppermute | solution.py:406
  5.1 6.3 %copy-start.18 = (bf16[4,4,512]{2,1,0:T(4,128)(2,1)S(1)}, bf16[4,4,512]{2,1,0:T(4,128)(2,1)}, u32[]{:S(2)}) copy-start(bf16[4,4,512]{2,1,0:T(4,128)(2,1)} %param.14) | copy-start | bytes 49156
  6.0 12.8 %copy-start.17 = (bf16[4,4,512]{2,1,0:T(4,128)(2,1)S(1)}, bf16[4,4,512]{2,1,0:T(4,128)(2,1)}, u32[]{:S(2)}) copy-start(bf16[4,4,512]{2,1,0:T(4,128)(2,1)} %param.15) | copy-start | bytes 49156
  6.0 18.4 %collective-permute-start.2 = (bf16[2,64,1024]{2,1,0:T(8,128)(2,1)}, bf16[2,64,1024]{2,1,0:T(8,128)(2,1)S(1)}, u32[]{:S(2)}, u32[]{:S(2)}) collective-permute-start(bf16[2,64,1024]{2,1,0:T(8,128)(2,1)} %get-tuple-element.163), channel_id=1, source_target_pairs={{0,6},{2,0},{4,2},{6,4},{1,7},{3,1},{5,3},{7,5},{8,14},{10,8},{12,... | collective-permute-start | bytes 786440 | tf_op jit(solution)/shard_map/ppermute | solution.py:402
  9.6 14.9 %collective-permute-start = (bf16[2,64,1024]{2,1,0:T(8,128)(2,1)}, bf16[2,64,1024]{2,1,0:T(8,128)(2,1)}, u32[]{:S(2)}, u32[]{:S(2)}) collective-permute-start(bf16[2,64,1024]{2,1,0:T(8,128)(2,1)} %get-tuple-element.164), channel_id=1, source_target_pairs={{0,2},{2,4},{4,6},{6,0},{1,3},{3,5},{5,7},{7,1},{8,10},{10,12},{12... | collective-permute-start | bytes 786440 | tf_op jit(solution)/shard_map/ppermute | solution.py:402
  9.6 22.3 %collective-permute-start.1 = (bf16[2,64,1024]{2,1,0:T(8,128)(2,1)}, bf16[2,64,1024]{2,1,0:T(8,128)(2,1)}, u32[]{:S(2)}, u32[]{:S(2)}) collective-permute-start(bf16[2,64,1024]{2,1,0:T(8,128)(2,1)} %get-tuple-element.166), channel_id=1, source_target_pairs={{0,4},{2,6},{4,0},{6,2},{1,5},{3,7},{5,1},{7,3},{8,12},{10,14},{12... | collective-permute-start | bytes 786440 | tf_op jit(solution)/shard_map/ppermute | solution.py:402
  10.7 8.2 %copy-start.6 = (bf16[1,2,256,1024]{3,2,1,0:T(8,128)(2,1)S(1)}, bf16[1,2,256,1024]{3,2,1,0:T(8,128)(2,1)}, u32[]{:S(2)}) copy-start(bf16[1,2,256,1024]{3,2,1,0:T(8,128)(2,1)} %param.9) | copy-start | bytes 3145732
  17.1 19.4 %collective-permute-start.4 = (bf16[512,512]{1,0:T(8,128)(2,1)}, bf16[512,512]{1,0:T(8,128)(2,1)}, u32[]{:S(2)}, u32[]{:S(2)}) collective-permute-start(bf16[512,512]{1,0:T(8,128)(2,1)} %collective-permute-done.3.refs_7_), channel_id=1, source_target_pairs={{0,16},{8,24},{16,0},{24,8},{1,17},{9,25},{17,1},{25,9},{2,18},{10... | collective-permute-start | bytes 1572872 | tf_op jit(solution)/shard_map/ppermute | solution.py:406
  18.8 38.0 %collective-permute-start.10 = (bf16[2,256,1024]{2,1,0:T(8,128)(2,1)S(1)}, bf16[2,256,1024]{2,1,0:T(8,128)(2,1)S(1)}, u32[]{:S(2)}, u32[]{:S(2)}) collective-permute-start(bf16[2,256,1024]{2,1,0:T(8,128)(2,1)S(1)} %bitcast.65), channel_id=1, source_target_pairs={{0,1},{1,0},{2,3},{3,2},{4,5},{5,4},{6,7},{7,6},{8,9},{9,8},{10,11... | collective-permute-start | bytes 3145736 | tf_op jit(solution)/shard_map/ppermute | solution.py:406
  24.5 9.0 %copy-start.10 = (bf16[2,64,1024]{2,1,0:T(8,128)(2,1)}, bf16[2,64,1024]{2,1,0:T(8,128)(2,1)S(1)}, u32[]{:S(2)}) copy-start(bf16[2,64,1024]{2,1,0:T(8,128)(2,1)S(1)} %collective-permute-done.2) | copy-start | bytes 786436
  36.5 3.8 %collective-permute-start.7 = (bf16[512,512]{1,0:T(8,128)(2,1)}, bf16[512,512]{1,0:T(8,128)(2,1)}, u32[]{:S(2)}, u32[]{:S(2)}) collective-permute-start(bf16[512,512]{1,0:T(8,128)(2,1)} %collective-permute-done.3.refs_7_), channel_id=1, source_target_pairs={{0,8},{8,0},{16,24},{24,16},{1,9},{9,1},{17,25},{25,17},{2,10},{10... | collective-permute-start | bytes 1572872 | tf_op jit(solution)/shard_map/ppermute | solution.py:406
  36.6 3.7 %collective-permute-start.8 = (bf16[512,512]{1,0:T(8,128)(2,1)}, bf16[512,512]{1,0:T(8,128)(2,1)}, u32[]{:S(2)}, u32[]{:S(2)}) collective-permute-start(bf16[512,512]{1,0:T(8,128)(2,1)} %collective-permute-done.4.refs_8_), channel_id=1, source_target_pairs={{0,8},{8,0},{16,24},{24,16},{1,9},{9,1},{17,25},{25,17},{2,10},{10... | collective-permute-start | bytes 1572872 | tf_op jit(solution)/shard_map/ppermute | solution.py:406
  37.1 8.5 %collective-permute-start.5 = (bf16[64,1024]{1,0:T(8,128)(2,1)}, bf16[64,1024]{1,0:T(8,128)(2,1)S(1)}, u32[]{:S(2)}, u32[]{:S(2)}) collective-permute-start(bf16[64,1024]{1,0:T(8,128)(2,1)} %get-tuple-element.99), channel_id=1, source_target_pairs={{0,2},{2,4},{4,6},{6,0},{1,3},{3,5},{5,7},{7,1},{8,10},{10,12},{12... | collective-permute-start | bytes 393224 | tf_op jit(solution)/shard_map/ppermute | solution.py:402
  37.1 14.1 %collective-permute-start.6 = (bf16[64,1024]{1,0:T(8,128)(2,1)}, bf16[64,1024]{1,0:T(8,128)(2,1)S(1)}, u32[]{:S(2)}, u32[]{:S(2)}) collective-permute-start(bf16[64,1024]{1,0:T(8,128)(2,1)} %get-tuple-element.100), channel_id=1, source_target_pairs={{0,4},{2,6},{4,0},{6,2},{1,5},{3,7},{5,1},{7,3},{8,12},{10,14},{12... | collective-permute-start | bytes 393224 | tf_op jit(solution)/shard_map/ppermute | solution.py:402
  40.3 16.6 %collective-permute-start.9 = (bf16[64,1024]{1,0:T(8,128)(2,1)}, bf16[64,1024]{1,0:T(8,128)(2,1)S(1)}, u32[]{:S(2)}, u32[]{:S(2)}) collective-permute-start(bf16[64,1024]{1,0:T(8,128)(2,1)} %get-tuple-element.108), channel_id=1, source_target_pairs={{0,6},{2,0},{4,2},{6,4},{1,7},{3,1},{5,3},{7,5},{8,14},{10,8},{12,... | collective-permute-start | bytes 393224 | tf_op jit(solution)/shard_map/ppermute | solution.py:402
  42.2 18.9 %collective-permute-start.12 = (bf16[64,1024]{1,0:T(8,128)(2,1)}, bf16[64,1024]{1,0:T(8,128)(2,1)S(1)}, u32[]{:S(2)}, u32[]{:S(2)}) collective-permute-start(bf16[64,1024]{1,0:T(8,128)(2,1)} %get-tuple-element.116), channel_id=1, source_target_pairs={{0,2},{2,4},{4,6},{6,0},{1,3},{3,5},{5,7},{7,1},{8,10},{10,12},{12... | collective-permute-start | bytes 393224 | tf_op jit(solution)/shard_map/ppermute | solution.py:402
  45.5 12.0 %copy-start.13 = (bf16[64,1024]{1,0:T(8,128)(2,1)}, bf16[64,1024]{1,0:T(8,128)(2,1)S(1)}, u32[]{:S(2)}) copy-start(bf16[64,1024]{1,0:T(8,128)(2,1)S(1)} %collective-permute-done.5.refs_0_) | copy-start | bytes 393220
  45.5 16.0 %collective-permute-start.13 = (bf16[64,1024]{1,0:T(8,128)(2,1)}, bf16[64,1024]{1,0:T(8,128)(2,1)S(1)}, u32[]{:S(2)}, u32[]{:S(2)}) collective-permute-start(bf16[64,1024]{1,0:T(8,128)(2,1)} %get-tuple-element.117), channel_id=1, source_target_pairs={{0,4},{2,6},{4,0},{6,2},{1,5},{3,7},{5,1},{7,3},{8,12},{10,14},{12... | collective-permute-start | bytes 393224 | tf_op jit(solution)/shard_map/ppermute | solution.py:402
  51.1 5.7 %copy-start.15 = (bf16[64,1024]{1,0:T(8,128)(2,1)}, bf16[64,1024]{1,0:T(8,128)(2,1)S(1)}, u32[]{:S(2)}) copy-start(bf16[64,1024]{1,0:T(8,128)(2,1)S(1)} %collective-permute-done.6.refs_1_) | copy-start | bytes 393220
  51.1 10.4 %collective-permute-start.14 = (bf16[64,1024]{1,0:T(8,128)(2,1)}, bf16[64,1024]{1,0:T(8,128)(2,1)}, u32[]{:S(2)}, u32[]{:S(2)}) collective-permute-start(bf16[64,1024]{1,0:T(8,128)(2,1)} %get-tuple-element.118), channel_id=1, source_target_pairs={{0,6},{2,0},{4,2},{6,4},{1,7},{3,1},{5,3},{7,5},{8,14},{10,8},{12,... | collective-permute-start | bytes 393224 | tf_op jit(solution)/shard_map/ppermute | solution.py:402
  56.8 1.0 copy-start.7
  56.8 0.7 copy-start.16
  57.8 17.0 %copy-start.1 = (bf16[2,512,512]{2,1,0:T(8,128)(2,1)S(1)}, bf16[2,512,512]{2,1,0:T(8,128)(2,1)}, u32[]{:S(2)}) copy-start(bf16[2,512,512]{2,1,0:T(8,128)(2,1)} %refs_6_.3) | copy-start | bytes 3145732
  60.5 14.4 %copy-start = (bf16[2,512,512]{2,1,0:T(8,128)(2,1)S(1)}, bf16[2,512,512]{2,1,0:T(8,128)(2,1)}, u32[]{:S(2)}) copy-start(bf16[2,512,512]{2,1,0:T(8,128)(2,1)} %refs_5_.3) | copy-start | bytes 3145732
  60.5 14.3 %copy-start.2 = (s32[4]{0:T(128)S(1)}, s32[4]{0:T(128)}, u32[]{:S(2)}) copy-start(s32[4]{0:T(128)} %pad_add_fusion.place.refs_0_) | copy-start | bytes 52
  60.5 14.3 %collective-permute-start.11 = (bf16[256,1024]{1,0:T(8,128)(2,1)}, bf16[256,1024]{1,0:T(8,128)(2,1)}, u32[]{:S(2)}, u32[]{:S(2)}) collective-permute-start(bf16[256,1024]{1,0:T(8,128)(2,1)} %get-tuple-element.114.refs_1_.refs_2_), channel_id=1, source_target_pairs={{0,1},{1,0},{2,3},{3,2},{4,5},{5,4},{6,7},{7,6},{8,9},{9,8},{10,11... | collective-permute-start | bytes 1572872 | tf_op jit(solution)/shard_map/ppermute | solution.py:406
  61.1 0.6 copy-start.12
  61.5 0.6 copy-start.14
  64.6 20.1 %collective-permute-start.15 = (bf16[256,1024]{1,0:T(8,128)(2,1)}, bf16[256,1024]{1,0:T(8,128)(2,1)S(1)}, u32[]{:S(2)}, u32[]{:S(2)}) collective-permute-start(bf16[256,1024]{1,0:T(8,128)(2,1)} %get-tuple-element.120.refs_1_.refs_3_), channel_id=1, source_target_pairs={{0,1},{1,0},{2,3},{3,2},{4,5},{5,4},{6,7},{7,6},{8,9},{9,8},{10,11... | collective-permute-start | bytes 1572872 | tf_op jit(solution)/shard_map/ppermute | solution.py:406
  84.8 0.8 copy-start.11
  85.5 19.4 %all-to-all-start = ((bf16[4,64,1024]{2,1,0:T(8,128)(2,1)}), bf16[4,64,1024]{2,1,0:T(8,128)(2,1)S(1)}, u32[]{:S(2)}, u32[]{:S(2)}) async-start(bf16[4,64,1024]{2,1,0:T(8,128)(2,1)} %bitcast.74), calls=%async_computation | async-start | bytes 1048576 | tf_op jit(solution)/shard_map/all_to_all | solution.py:410
  105.0 7.8 %copy-start.4 = (bf16[4,64,1024]{2,1,0:T(8,128)(2,1)}, bf16[4,64,1024]{2,1,0:T(8,128)(2,1)S(1)}, u32[]{:S(2)}) copy-start(bf16[4,64,1024]{2,1,0:T(8,128)(2,1)S(1)} %all-to-all-done) | copy-start | bytes 1572868
  105.0 5.2 %collective-permute-start.16 = (bf16[8,144,512]{2,1,0:T(8,128)(2,1)}, bf16[8,144,512]{2,1,0:T(8,128)(2,1)S(1)}, u32[]{:S(2)}, u32[]{:S(2)}) collective-permute-start(bf16[8,144,512]{2,1,0:T(8,128)(2,1)} %get-tuple-element.145), channel_id=1, source_target_pairs={{0,8},{8,0},{16,24},{24,16},{1,9},{9,1},{17,25},{25,17},{2,10},{10... | collective-permute-start | bytes 3538952 | tf_op jit(solution)/shard_map/ppermute | solution.py:406
  105.0 20.2 %all-to-all-start.1 = ((bf16[4,64,1024]{2,1,0:T(8,128)(2,1)}), bf16[4,64,1024]{2,1,0:T(8,128)(2,1)S(1)}, u32[]{:S(2)}, u32[]{:S(2)}) async-start(bf16[4,64,1024]{2,1,0:T(8,128)(2,1)} %bitcast.18), calls=%async_computation.1 | async-start | bytes 1048576 | tf_op jit(solution)/shard_map/all_to_all | solution.py:410
  112.8 12.5 %collective-permute-start.17 = (bf16[144,512]{1,0:T(8,128)(2,1)}, bf16[144,512]{1,0:T(8,128)(2,1)S(1)}, u32[]{:S(2)}, u32[]{:S(2)}) collective-permute-start(bf16[144,512]{1,0:T(8,128)(2,1)} %get-tuple-element.146), channel_id=1, source_target_pairs={{0,16},{8,24},{16,0},{24,8},{1,17},{9,25},{17,1},{25,9},{2,18},{10... | collective-permute-start | bytes 442376 | tf_op jit(solution)/shard_map/ppermute | solution.py:406
  114.2 11.0 %collective-permute-start.19 = (bf16[144,512]{1,0:T(8,128)(2,1)}, bf16[144,512]{1,0:T(8,128)(2,1)S(1)}, u32[]{:S(2)}, u32[]{:S(2)}) collective-permute-start(bf16[144,512]{1,0:T(8,128)(2,1)} %get-tuple-element.150), channel_id=1, source_target_pairs={{0,16},{8,24},{16,0},{24,8},{1,17},{9,25},{17,1},{25,9},{2,18},{10... | collective-permute-start | bytes 442376 | tf_op jit(solution)/shard_map/ppermute | solution.py:406
  114.8 11.2 %collective-permute-start.21 = (bf16[144,512]{1,0:T(8,128)(2,1)}, bf16[144,512]{1,0:T(8,128)(2,1)S(1)}, u32[]{:S(2)}, u32[]{:S(2)}) collective-permute-start(bf16[144,512]{1,0:T(8,128)(2,1)} %get-tuple-element.151), channel_id=1, source_target_pairs={{0,16},{8,24},{16,0},{24,8},{1,17},{9,25},{17,1},{25,9},{2,18},{10... | collective-permute-start | bytes 442376 | tf_op jit(solution)/shard_map/ppermute | solution.py:406
  116.3 26.4 %collective-permute-start.23 = (bf16[144,512]{1,0:T(8,128)(2,1)}, bf16[144,512]{1,0:T(8,128)(2,1)S(1)}, u32[]{:S(2)}, u32[]{:S(2)}) collective-permute-start(bf16[144,512]{1,0:T(8,128)(2,1)} %get-tuple-element.152), channel_id=1, source_target_pairs={{0,16},{8,24},{16,0},{24,8},{1,17},{9,25},{17,1},{25,9},{2,18},{10... | collective-permute-start | bytes 442376 | tf_op jit(solution)/shard_map/ppermute | solution.py:406
  125.2 6.9 %copy-start.5 = (bf16[4,64,1024]{2,1,0:T(8,128)(2,1)}, bf16[4,64,1024]{2,1,0:T(8,128)(2,1)S(1)}, u32[]{:S(2)}) copy-start(bf16[4,64,1024]{2,1,0:T(8,128)(2,1)S(1)} %all-to-all-done.1) | copy-start | bytes 1572868
  127.1 15.5 %collective-permute-start.18 = (bf16[144,512]{1,0:T(8,128)(2,1)S(1)}, bf16[144,512]{1,0:T(8,128)(2,1)S(1)}, u32[]{:S(2)}, u32[]{:S(2)}) collective-permute-start(bf16[144,512]{1,0:T(8,128)(2,1)S(1)} %get-tuple-element.167), channel_id=1, source_target_pairs={{0,2},{2,4},{4,6},{6,0},{1,3},{3,5},{5,7},{7,1},{8,10},{10,12},{12... | collective-permute-start | bytes 442376 | tf_op jit(solution)/shard_map/ppermute | solution.py:402
  129.2 13.4 %collective-permute-start.22 = (bf16[144,512]{1,0:T(8,128)(2,1)S(1)}, bf16[144,512]{1,0:T(8,128)(2,1)S(1)}, u32[]{:S(2)}, u32[]{:S(2)}) collective-permute-start(bf16[144,512]{1,0:T(8,128)(2,1)S(1)} %get-tuple-element.168), channel_id=1, source_target_pairs={{0,6},{2,0},{4,2},{6,4},{1,7},{3,1},{5,3},{7,5},{8,14},{10,8},{12,... | collective-permute-start | bytes 442376 | tf_op jit(solution)/shard_map/ppermute | solution.py:402
  131.3 13.7 %collective-permute-start.20 = (bf16[144,512]{1,0:T(8,128)(2,1)S(1)}, bf16[144,512]{1,0:T(8,128)(2,1)S(1)}, u32[]{:S(2)}, u32[]{:S(2)}) collective-permute-start(bf16[144,512]{1,0:T(8,128)(2,1)S(1)} %get-tuple-element.169), channel_id=1, source_target_pairs={{0,4},{2,6},{4,0},{6,2},{1,5},{3,7},{5,1},{7,3},{8,12},{10,14},{12... | collective-permute-start | bytes 442376 | tf_op jit(solution)/shard_map/ppermute | solution.py:402
  138.0 31.0 %all-to-all-start.3 = ((bf16[4,64,1024]{2,1,0:T(8,128)(2,1)}), bf16[4,64,1024]{2,1,0:T(8,128)(2,1)S(1)}, u32[]{:S(2)}, u32[]{:S(2)}) async-start(bf16[4,64,1024]{2,1,0:T(8,128)(2,1)} %bitcast.28), calls=%async_computation.3 | async-start | bytes 1048576 | tf_op jit(solution)/shard_map/all_to_all | solution.py:410
  146.1 3.8 %collective-permute-start.24 = (bf16[16,512]{1,0:T(8,128)(2,1)S(1)}, bf16[16,512]{1,0:T(8,128)(2,1)S(1)}, u32[]{:S(2)}, u32[]{:S(2)}) collective-permute-start(bf16[16,512]{1,0:T(8,128)(2,1)S(1)} %slice.88), channel_id=1, source_target_pairs={{0,1},{1,0},{2,3},{3,2},{4,5},{5,4},{6,7},{7,6},{8,9},{9,8},{10,11... | collective-permute-start | bytes 49160 | tf_op jit(solution)/shard_map/ppermute | solution.py:406
  149.9 6.6 %collective-permute-start.27 = (bf16[144,512]{1,0:T(8,128)(2,1)S(1)}, bf16[144,512]{1,0:T(8,128)(2,1)S(1)}, u32[]{:S(2)}, u32[]{:S(2)}) collective-permute-start(bf16[144,512]{1,0:T(8,128)(2,1)S(1)} %concatenate.37), channel_id=1, source_target_pairs={{0,6},{2,0},{4,2},{6,4},{1,7},{3,1},{5,3},{7,5},{8,14},{10,8},{12,... | collective-permute-start | bytes 442376 | tf_op jit(solution)/shard_map/ppermute | solution.py:402
  153.9 13.1 %collective-permute-start.26 = (bf16[144,512]{1,0:T(8,128)(2,1)S(1)}, bf16[144,512]{1,0:T(8,128)(2,1)S(1)}, u32[]{:S(2)}, u32[]{:S(2)}) collective-permute-start(bf16[144,512]{1,0:T(8,128)(2,1)S(1)} %concatenate.37), channel_id=1, source_target_pairs={{0,4},{2,6},{4,0},{6,2},{1,5},{3,7},{5,1},{7,3},{8,12},{10,14},{12... | collective-permute-start | bytes 442376 | tf_op jit(solution)/shard_map/ppermute | solution.py:402
  153.9 14.6 %collective-permute-start.25 = (bf16[144,512]{1,0:T(8,128)(2,1)S(1)}, bf16[144,512]{1,0:T(8,128)(2,1)S(1)}, u32[]{:S(2)}, u32[]{:S(2)}) collective-permute-start(bf16[144,512]{1,0:T(8,128)(2,1)S(1)} %concatenate.37), channel_id=1, source_target_pairs={{0,2},{2,4},{4,6},{6,0},{1,3},{3,5},{5,7},{7,1},{8,10},{10,12},{12... | collective-permute-start | bytes 442376 | tf_op jit(solution)/shard_map/ppermute | solution.py:402
  154.5 18.1 %collective-permute-start.28 = (bf16[144,512]{1,0:T(8,128)(2,1)S(1)}, bf16[144,512]{1,0:T(8,128)(2,1)S(1)}, u32[]{:S(2)}, u32[]{:S(2)}) collective-permute-start(bf16[144,512]{1,0:T(8,128)(2,1)S(1)} %concatenate.37), channel_id=1, source_target_pairs={{0,16},{8,24},{16,0},{24,8},{1,17},{9,25},{17,1},{25,9},{2,18},{10... | collective-permute-start | bytes 442376 | tf_op jit(solution)/shard_map/ppermute | solution.py:406
  156.6 16.1 %collective-permute-start.31 = (bf16[144,512]{1,0:T(8,128)(2,1)S(1)}, bf16[144,512]{1,0:T(8,128)(2,1)S(1)}, u32[]{:S(2)}, u32[]{:S(2)}) collective-permute-start(bf16[144,512]{1,0:T(8,128)(2,1)S(1)} %collective-permute-done.27), channel_id=1, source_target_pairs={{0,16},{8,24},{16,0},{24,8},{1,17},{9,25},{17,1},{25,9},{2,18},{10... | collective-permute-start | bytes 442376 | tf_op jit(solution)/shard_map/ppermute | solution.py:406
  167.0 5.7 %collective-permute-start.30 = (bf16[144,512]{1,0:T(8,128)(2,1)S(1)}, bf16[144,512]{1,0:T(8,128)(2,1)S(1)}, u32[]{:S(2)}, u32[]{:S(2)}) collective-permute-start(bf16[144,512]{1,0:T(8,128)(2,1)S(1)} %collective-permute-done.26), channel_id=1, source_target_pairs={{0,16},{8,24},{16,0},{24,8},{1,17},{9,25},{17,1},{25,9},{2,18},{10... | collective-permute-start | bytes 442376 | tf_op jit(solution)/shard_map/ppermute | solution.py:406
  168.5 5.5 %collective-permute-start.29 = (bf16[144,512]{1,0:T(8,128)(2,1)S(1)}, bf16[144,512]{1,0:T(8,128)(2,1)S(1)}, u32[]{:S(2)}, u32[]{:S(2)}) collective-permute-start(bf16[144,512]{1,0:T(8,128)(2,1)S(1)} %collective-permute-done.25), channel_id=1, source_target_pairs={{0,16},{8,24},{16,0},{24,8},{1,17},{9,25},{17,1},{25,9},{2,18},{10... | collective-permute-start | bytes 442376 | tf_op jit(solution)/shard_map/ppermute | solution.py:406
  169.0 5.1 %copy-start.8 = (bf16[4,64,1024]{2,1,0:T(8,128)(2,1)}, bf16[4,64,1024]{2,1,0:T(8,128)(2,1)S(1)}, u32[]{:S(2)}) copy-start(bf16[4,64,1024]{2,1,0:T(8,128)(2,1)S(1)} %all-to-all-done.3) | copy-start | bytes 1572868
  169.0 15.9 %all-to-all-start.2 = ((bf16[4,64,1024]{2,1,0:T(8,128)(2,1)}), bf16[4,64,1024]{2,1,0:T(8,128)(2,1)S(1)}, u32[]{:S(2)}, u32[]{:S(2)}) async-start(bf16[4,64,1024]{2,1,0:T(8,128)(2,1)} %bitcast.26), calls=%async_computation.2 | async-start | bytes 1048576 | tf_op jit(solution)/shard_map/all_to_all | solution.py:410
  172.6 3.6 %collective-permute-start.32 = (bf16[4,144,512]{2,1,0:T(8,128)(2,1)S(1)}, bf16[4,144,512]{2,1,0:T(8,128)(2,1)S(1)}, u32[]{:S(2)}, u32[]{:S(2)}) collective-permute-start(bf16[4,144,512]{2,1,0:T(8,128)(2,1)S(1)} %pad_maximum_fusion.refs_0_), channel_id=1, source_target_pairs={{0,8},{8,0},{16,24},{24,16},{1,9},{9,1},{17,25},{25,17},{2,10},{10... | collective-permute-start | bytes 1769480 | tf_op jit(solution)/shard_map/ppermute | solution.py:406
  174.1 2.1 %collective-permute-start.33 = (bf16[4,144,512]{2,1,0:T(8,128)(2,1)S(1)}, bf16[4,144,512]{2,1,0:T(8,128)(2,1)S(1)}, u32[]{:S(2)}, u32[]{:S(2)}) collective-permute-start(bf16[4,144,512]{2,1,0:T(8,128)(2,1)S(1)} %pad_maximum_fusion.1.refs_1_), channel_id=1, source_target_pairs={{0,8},{8,0},{16,24},{24,16},{1,9},{9,1},{17,25},{25,17},{2,10},{10... | collective-permute-start | bytes 1769480 | tf_op jit(solution)/shard_map/ppermute | solution.py:406
  184.9 0.8 copy-start.9

commit v5 on v4

--- a/solution.py
+++ b/solution.py
@@ -153,24 +153,45 @@
     )(place, *held_in_hbm(rows_in, inputs, pieces[0]), *pieces[1:])
 
 
-def channel_kernel(first, *refs):
-    (place, h_own, h_oth, c_own, c_oth, wg_own, wu_own, *lent) = refs[:11]
-    mix_g, mix_u, rows_in, mixed, *before = refs[11 : 15 if first else 16]
-    hid_grad, back_g, back_u, turned, mix_sum, row_sum, mid = refs[-7:]
+def started(pairs, done):
+    copies = [
+        pltpu.make_async_copy(source, target, done.at[i])
+        for i, (source, target) in enumerate(pairs)
+    ]
+    for copy in copies:
+        copy.start()
+    return copies
+
+
+def channel_kernel(h, count, place, wg_own, wu_own, *refs):
+    sources, results, held = refs[:count], refs[count : count + 6], refs[count + 6 : -3]
+    mid, come, gone = refs[-3:]
+    inputs, outs = held[:count], held[count:]
+    views = [source.at[h] if len(source.shape) == len(buffer.shape) + 1 else source
+             for source, buffer in zip(sources, inputs)]
+    copies = started(list(zip(views, inputs)), come)
+    h_own, h_oth, *lent = inputs[:6]
+    mix_g, mix_u, c_own, c_oth, rows_in, mixed, *before = inputs[6:]
+    hid_grad, back_g, back_u, turned, mix_sum, row_sum = outs
     mid_g, mid_u = mid.at[0], mid.at[1]
     local, size = wg_own.shape[:2]
     blocks = 2 * local
     cols = h_own.shape[0]
+    copies[0].wait()
     for k in range(local):
         part = h_own[:, k * size : (k + 1) * size]
         mid_g[k] = jnp.dot(part, wg_own[k], preferred_element_type=F)
         mid_u[k] = jnp.dot(part, wu_own[k], preferred_element_type=F)
     core, x = place[2], place[3]
+    copies[1].wait()
     for i, block in enumerate(lent):
         table = core if i < 2 else 1 - core
         k = x if i % 2 == 0 else 1 - x
+        copies[2 + i].wait()
         part = h_oth[:, pl.ds(pl.multiple_of(k * size, size), size)]
         mid[table, local + k] = jnp.dot(part, block[...], preferred_element_type=F)
+    for copy in copies[6:10]:
+        copy.wait()
     mix_sum[...] = jnp.zeros_like(mix_sum)
     deep, lanes = 16, 128
 
@@ -209,6 +230,10 @@
         return carry
 
     lax.fori_loop(0, cols // deep, chunk, 0)
+    leaving = [(outs[i], results[i]) for i in (1, 2, 4)]
+    going = started(leaving, gone)
+    for copy in copies[10:]:
+        copy.wait()
     last = (((1,), (1,)), ((), ()))
     for k in range(local):
         spot = slice(k * size, (k + 1) * size)
@@ -218,38 +243,42 @@
     turned[...] = lax.dot_general(
         rows_in[...], hid_grad[...], (((0,), (0,)), ((), ())), preferred_element_type=F
     ).astype(BF)
+    going += started([(outs[i], results[i]) for i in (0, 3)], gone.at[pl.ds(3, 2)])
     total = lax.dot_general(hid_grad[...], mixed[...], last, preferred_element_type=F)
-    for held in before:
-        total = held[...] + total
+    for value in before:
+        total = value[...] + total
     row_sum[...] = total
+    going += started([(outs[5], results[5])], gone.at[pl.ds(5, 1)])
+    for copy in going:
+        copy.wait()
 
 
 def channel_row(place, h, h_own, h_oth, cot, cot_oth, weights, mixes, rows_in, mixed, before):
     cols, width = h_own.shape
     local, size = weights[0].shape[:2]
     blocks = 2 * local
-    row = pl.BlockSpec((None, cols, width), lambda j: (h, 0, 0))
+    sources = (h_own, h_oth, *weights[2:], *mixes, cot, cot_oth, rows_in, mixed, *before)
+    results = [((cols, width), BF)] * 4 + [((2, blocks, local, 8, size), F), ((cols, cols), F)]
+    count = len(sources)
+    buffers = [
+        pltpu.VMEM(value.shape[1:] if value is cot or value is cot_oth else value.shape, value.dtype)
+        for value in sources
+    ]
+    buffers += [pltpu.VMEM(*result) for result in results]
     return pl.pallas_call(
-        once(functools.partial(channel_kernel, not before)),
-        out_shape=[shape_of((cols, width))] * 4
-        + [shape_of((2, blocks, local, 8, size), F), shape_of((cols, cols), F)],
-        grid=(2,),
-        in_specs=[SM]
-        + wholes(h_own, h_oth)
-        + [row, row]
-        + [VM] * 2
-        + wholes(*weights[2:], *mixes, rows_in, mixed, *before),
-        out_specs=[whole(cols, width)] * 4
-        + [whole(2, blocks, local, 8, size), whole(cols, cols)],
-        scratch_shapes=[pltpu.VMEM((2, blocks, cols, size), F)],
+        functools.partial(channel_kernel, h, count),
+        out_shape=[shape_of(*result) for result in results],
+        in_specs=[SM] + [VM] * 2 + [pl.BlockSpec(memory_space=pltpu.HBM)] * count,
+        out_specs=[pl.BlockSpec(memory_space=pltpu.HBM)] * 6,
+        scratch_shapes=buffers
+        + [
+            pltpu.VMEM((2, blocks, cols, size), F),
+            pltpu.SemaphoreType.DMA((count,)),
+            pltpu.SemaphoreType.DMA((6,)),
+        ],
         compiler_params=PARAMS,
         name="channel_row",
-    )(
-        place,
-        *held_in_hbm(h_own, h_oth, cot, cot_oth),
-        *weights[:2],
-        *held_in_hbm(*weights[2:], *mixes, rows_in, mixed, *before),
-    )
+    )(place, *weights[:2], *held_in_hbm(*sources))
 
 
 def sums_kernel(rows, parts, place, row_sum, *refs):

time: 188 us -> 187 us (level)
  Pallas kernels: 48.5 us -> 46.6 us
    pallas_call x2, Pallas kernels: 20 us -> 18 us  [channel_row(): pl.pallas_call(functools.partial(channel_kernel, h, count), out_shape=[sh...]
  transfers between devices with their start and end apart: 38 -> 38, of which waited for: 14 -> 14; matrix products, arithmetic and copies ran while one was open for 7% -> 7% of each run, Pallas kernels for 25% -> 24%
where the time goes in v5:
time: 187 us; the launch traced here: 186 us
  waiting for transfers between devices  61.8 us (33%)
  starting transfers between devices  59.3 us (32%)
  Pallas kernels  46.6 us (25%)
  local copies, waits for them, and re-layouts  11.3 us (6%)
  other arithmetic  5.83 us (3%)
    ppermute x15, waiting for transfers between devices, shifted(): return lax.ppermute(value, 'seq', [(i, (i + by) % n) for i in range(n)])  28.6 us
    ppermute x15, starting transfers between devices, shifted(): return lax.ppermute(value, 'seq', [(i, (i + by) % n) for i in range(n)])  24.5 us
    ppermute x19, waiting for transfers between devices, swapped(): return lax.ppermute(value, axis, [(i, i ^ bit) for i in range(n)])  18.9 us
    ppermute x19, starting transfers between devices, swapped(): return lax.ppermute(value, axis, [(i, i ^ bit) for i in range(n)])  18.5 us
    pallas_call x2, Pallas kernels, channel_row(): pl.pallas_call(functools.partial(channel_kernel, h, count), out_shape=[sh...  18 us
    all_to_all x4, starting transfers between devices, traded(): return lax.all_to_all(value, 'seq', split_axis=0, concat_axis=0, tiled=True)  16.3 us
    all_to_all x4, waiting for transfers between devices, traded(): return lax.all_to_all(value, 'seq', split_axis=0, concat_axis=0, tiled=True)  14.3 us
    pallas_call x2, Pallas kernels, column_mix(): pl.pallas_call(functools.partial(column_mix_kernel, len(sources)), out_sh...  5.95 us
  transfers between devices with their start and end apart: 38, of which 14 were waited for; matrix products, arithmetic and copies ran while one was open for 7% of the time, Pallas kernels for 24%

profile of v5, /device:TPU:0, one launch (start us, length us, event | category | flops | bytes accessed | tf_op | source)
XLA Modules:
  0.0 185.8 jit_solution(11394334750141649930)
XLA Ops:
  0.7 1.3 fusion
  2.0 3.0 %collective-permute-start.3 = (bf16[512,512]{1,0:T(8,128)(2,1)S(1)}, bf16[512,512]{1,0:T(8,128)(2,1)}, u32[]{:S(2)}, u32[]{:S(2)}) collective-permute-start(bf16[512,512]{1,0:T(8,128)(2,1)S(1)} %fusion), channel_id=1, source_target_pairs={{0,1},{1,0},{2,3},{3,2},{4,5},{5,4},{6,7},{7,6},{8,9},{9,8},{10,11... | collective-permute-start | bytes 1572872 | tf_op jit(solution)/shard_map/ppermute | solution.py:435
  5.1 1.0 dynamic-slice_bitcast_fusion
  6.0 3.6 %collective-permute-start.2 = (bf16[2,64,1024]{2,1,0:T(8,128)(2,1)}, bf16[2,64,1024]{2,1,0:T(8,128)(2,1)S(1)}, u32[]{:S(2)}, u32[]{:S(2)}) collective-permute-start(bf16[2,64,1024]{2,1,0:T(8,128)(2,1)} %get-tuple-element.163), channel_id=1, source_target_pairs={{0,6},{2,0},{4,2},{6,4},{1,7},{3,1},{5,3},{7,5},{8,14},{10,8},{12,... | collective-permute-start | bytes 786440 | tf_op jit(solution)/shard_map/ppermute | solution.py:431
  9.6 1.0 collective-permute-start.1
  11.3 1.2 broadcast_select_fusion
  12.5 4.6 %collective-permute-done.3.refs_2_ = bf16[512,512]{1,0:T(8,128)(2,1)} collective-permute-done((bf16[512,512]{1,0:T(8,128)(2,1)S(1)}, bf16[512,512]{1,0:T(8,128)(2,1)}, u32[]{:S(2)}, u32[]{:S(2)}) %collective-permute-start.3) | collective-permute-done | bytes 524320 | tf_op jit(solution)/shard_map/ppermute | solution.py:435
  17.1 1.7 collective-permute-start.4
  18.8 1.6 collective-permute-start.10
  20.5 2.6 %select_n.97.table = bf16[512,512]{1,0:T(8,128)(2,1)} reshape(bf16[8,64,8,64]{3,2,1,0:T(8,128)(2,1)} %get-tuple-element.176) | data formatting | bytes 1048576 | tf_op jit(solution)/shard_map/jit(_where)/select_n | solution.py:60
  23.0 1.4 select_n.95.table
  24.5 7.5 %collective-permute-done.1 = bf16[2,64,1024]{2,1,0:T(8,128)(2,1)} collective-permute-done((bf16[2,64,1024]{2,1,0:T(8,128)(2,1)}, bf16[2,64,1024]{2,1,0:T(8,128)(2,1)}, u32[]{:S(2)}, u32[]{:S(2)}) %collective-permute-start.1) | collective-permute-done | bytes 262176 | tf_op jit(solution)/shard_map/ppermute | solution.py:431
  32.0 0.7 broadcast_in_dim.55.refs_7_
  32.7 0.7 broadcast_in_dim.54.refs_6_
  33.5 3.0 %column_mix.1 = (bf16[64,1024]{1,0:T(8,128)(2,1)}, bf16[64,1024]{1,0:T(8,128)(2,1)}, bf16[64,1024]{1,0:T(8,128)(2,1)}, bf16[64,1024]{1,0:T(8,128)(2,1)}, bf16[64...) custom-call(bf16[512,512]{1,0:T(8,128)(2,1)} %select_n.95.table, ...), custom_call_target="tpu_custom_call" | custom-call | tf_op jit(solution)/shard_map/column_mix/pallas_call | solution.py:82
  37.1 3.2 %collective-permute-start.6 = (bf16[64,1024]{1,0:T(8,128)(2,1)}, bf16[64,1024]{1,0:T(8,128)(2,1)S(1)}, u32[]{:S(2)}, u32[]{:S(2)}) collective-permute-start(bf16[64,1024]{1,0:T(8,128)(2,1)} %get-tuple-element.100), channel_id=1, source_target_pairs={{0,4},{2,6},{4,0},{6,2},{1,5},{3,7},{5,1},{7,3},{8,12},{10,14},{12... | collective-permute-start | bytes 393224 | tf_op jit(solution)/shard_map/ppermute | solution.py:431
  40.3 1.9 %collective-permute-start.9 = (bf16[64,1024]{1,0:T(8,128)(2,1)}, bf16[64,1024]{1,0:T(8,128)(2,1)S(1)}, u32[]{:S(2)}, u32[]{:S(2)}) collective-permute-start(bf16[64,1024]{1,0:T(8,128)(2,1)} %get-tuple-element.108), channel_id=1, source_target_pairs={{0,6},{2,0},{4,2},{6,4},{1,7},{3,1},{5,3},{7,5},{8,14},{10,8},{12,... | collective-permute-start | bytes 393224 | tf_op jit(solution)/shard_map/ppermute | solution.py:431
  42.3 3.2 %collective-permute-done.5.refs_0_ = bf16[64,1024]{1,0:T(8,128)(2,1)S(1)} collective-permute-done((bf16[64,1024]{1,0:T(8,128)(2,1)}, bf16[64,1024]{1,0:T(8,128)(2,1)S(1)}, u32[]{:S(2)}, u32[]{:S(2)}) %collective-permute-start.5) | collective-permute-done | bytes 131104 | tf_op jit(solution)/shard_map/ppermute | solution.py:431
  45.5 5.6 %collective-permute-done.6.refs_1_ = bf16[64,1024]{1,0:T(8,128)(2,1)S(1)} collective-permute-done((bf16[64,1024]{1,0:T(8,128)(2,1)}, bf16[64,1024]{1,0:T(8,128)(2,1)S(1)}, u32[]{:S(2)}, u32[]{:S(2)}) %collective-permute-start.6) | collective-permute-done | bytes 131104 | tf_op jit(solution)/shard_map/ppermute | solution.py:431
  51.1 5.1 %collective-permute-start.14 = (bf16[64,1024]{1,0:T(8,128)(2,1)}, bf16[64,1024]{1,0:T(8,128)(2,1)}, u32[]{:S(2)}, u32[]{:S(2)}) collective-permute-start(bf16[64,1024]{1,0:T(8,128)(2,1)} %get-tuple-element.118), channel_id=1, source_target_pairs={{0,6},{2,0},{4,2},{6,4},{1,7},{3,1},{5,3},{7,5},{8,14},{10,8},{12,... | collective-permute-start | bytes 393224 | tf_op jit(solution)/shard_map/ppermute | solution.py:431
  56.2 0.6 pad_add_fusion.place.refs_0_
  56.9 0.7 copy-done.16
  57.8 2.6 %hidden_row.2 = (bf16[256,1024]{1,0:T(8,128)(2,1)}, bf16[256,1024]{1,0:T(8,128)(2,1)}) custom-call(s32[4]{0:T(128)} %pad_add_fusion.place.refs_0_, bf16[256,256]{1,0:T(8,128)(2,1)} %refs_10_.3, bf16[2,256,1024]{2,1,0:T(8,128)(2,1)} %bitcast.57, bf16[64,1024]{1,0:T(8,128)(2,1)} %get-tuple-element.110.own, bf16[64,1024]{1,0:T(8,128)(2,1)} %copy-done.13, ...), custom_call_target="tpu_custom_call" | custom-call | tf_op jit(solution)/shard_map/hidden_row/pallas_call | solution.py:140
  60.5 0.6 collective-permute-start.11
  62.1 2.5 %hidden_row.3 = (bf16[256,1024]{1,0:T(8,128)(2,1)}, bf16[256,1024]{1,0:T(8,128)(2,1)}) custom-call(s32[4]{0:T(128)} %pad_add_fusion.place.refs_0_, bf16[256,256]{1,0:T(8,128)(2,1)} %refs_10_.3, bf16[2,256,1024]{2,1,0:T(8,128)(2,1)} %bitcast.58, bf16[64,1024]{1,0:T(8,128)(2,1)} %get-tuple-element.115.own, bf16[64,1024]{1,0:T(8,128)(2,1)} %copy-done.12, ...), custom_call_target="tpu_custom_call" | custom-call | tf_op jit(solution)/shard_map/hidden_row/pallas_call | solution.py:140
  64.6 1.1 collective-permute-start.15
  65.8 9.0 %collective-permute-done.11.refs_1_ = bf16[256,1024]{1,0:T(8,128)(2,1)} collective-permute-done((bf16[256,1024]{1,0:T(8,128)(2,1)}, bf16[256,1024]{1,0:T(8,128)(2,1)}, u32[]{:S(2)}, u32[]{:S(2)}) %collective-permute-start.11) | collective-permute-done | bytes 524320 | tf_op jit(solution)/shard_map/ppermute | solution.py:435
  74.8 9.0 %channel_row.2 = (bf16[256,1024]{1,0:T(8,128)(2,1)}, bf16[256,1024]{1,0:T(8,128)(2,1)}, bf16[256,1024]{1,0:T(8,128)(2,1)}, bf16[256,1024]{1,0:T(8,128)(2,1)}, f3...) custom-call(s32[4]{0:T(128)S(1)} %copy-done.2, bf16[2,512,512]{2,1,0:T(8,128)(2,1)S(1)} %copy-done, ...), custom_call_target="tpu_custom_call" | custom-call | tf_op jit(solution)/shard_map/channel_row/pallas_call | solution.py:268
  83.9 0.8 copy-done.11
  84.6 4.2 %all-to-all-start = ((bf16[4,64,1024]{2,1,0:T(8,128)(2,1)}), bf16[4,64,1024]{2,1,0:T(8,128)(2,1)S(1)}, u32[]{:S(2)}, u32[]{:S(2)}) async-start(bf16[4,64,1024]{2,1,0:T(8,128)(2,1)} %bitcast.74), calls=%async_computation | async-start | bytes 1048576 | tf_op jit(solution)/shard_map/all_to_all | solution.py:439
  88.9 9.0 %channel_row.3 = (bf16[256,1024]{1,0:T(8,128)(2,1)}, bf16[256,1024]{1,0:T(8,128)(2,1)}, bf16[256,1024]{1,0:T(8,128)(2,1)}, bf16[256,1024]{1,0:T(8,128)(2,1)}, f3...) custom-call(s32[4]{0:T(128)S(1)} %copy-done.2, bf16[2,512,512]{2,1,0:T(8,128)(2,1)S(1)} %copy-done, ...), custom_call_target="tpu_custom_call" | custom-call | tf_op jit(solution)/shard_map/channel_row/pallas_call | solution.py:268
  97.9 5.1 %sums.1 = (bf16[8,144,512]{2,1,0:T(8,128)(2,1)}, bf16[8,144,512]{2,1,0:T(8,128)(2,1)}) custom-call(s32[4]{0:T(128)S(1)} %copy-done.2, f32[256,256]{1,0:T(8,128)} %get-tuple-element.135.refs_1_, bf16[256,1024]{1,0:T(8,128)(2,1)} %get-tuple-element.114.refs_0_.refs_2_, bf16[256,1024]{1,0:T(8,128)(2,1)} %get-tuple-element.120.refs_0_.refs_3_, ...), custom_call_target="tpu_custom_call" | custom-call | tf_op jit(solution)/shard_map/sums/pallas_call | solution.py:327
  103.1 5.1 %all-to-all-start.1 = ((bf16[4,64,1024]{2,1,0:T(8,128)(2,1)}), bf16[4,64,1024]{2,1,0:T(8,128)(2,1)S(1)}, u32[]{:S(2)}, u32[]{:S(2)}) async-start(bf16[4,64,1024]{2,1,0:T(8,128)(2,1)} %bitcast.18), calls=%async_computation.1 | async-start | bytes 1048576 | tf_op jit(solution)/shard_map/all_to_all | solution.py:439
  108.2 2.6 %core_add.1 = (bf16[144,512]{1,0:T(8,128)(2,1)}, bf16[144,512]{1,0:T(8,128)(2,1)}, bf16[144,512]{1,0:T(8,128)(2,1)}, bf16[144,512]{1,0:T(8,128)(2,1)}, bf16[4,144,512]{2,1,0:T(8,128)(2,1)}) custom-call(s32[4]{0:T(128)S(1)} %copy-done.2, bf16[8,144,512]{2,1,0:T(8,128)(2,1)} %get-tuple-element.142.refs_1_, bf16[8,144,512]{2,1,0:T(8,128)(2,1)S(1)} %collective-permute-done.16.refs_2_), custom_call_target="tpu_custom_call" | custom-call | tf_op jit(solution)/shard_map/core_add/pallas_call | solution.py:349
  110.8 1.5 collective-permute-start.17
  112.9 1.5 collective-permute-start.21
  114.9 8.4 %all-to-all-done.1 = bf16[4,64,1024]{2,1,0:T(8,128)(2,1)S(1)} async-done(((bf16[4,64,1024]{2,1,0:T(8,128)(2,1)}), bf16[4,64,1024]{2,1,0:T(8,128)(2,1)S(1)}, u32[]{:S(2)}, u32[]{:S(2)}) %all-to-all-start.1) | async-done | bytes 524320 | tf_op jit(solution)/shard_map/all_to_all | solution.py:439
  123.3 0.7 collective-permute-done.21
  124.1 1.2 fusion.4
  125.2 2.1 %collective-permute-start.18 = (bf16[144,512]{1,0:T(8,128)(2,1)S(1)}, bf16[144,512]{1,0:T(8,128)(2,1)S(1)}, u32[]{:S(2)}, u32[]{:S(2)}) collective-permute-start(bf16[144,512]{1,0:T(8,128)(2,1)S(1)} %get-tuple-element.167), channel_id=1, source_target_pairs={{0,2},{2,4},{4,6},{6,0},{1,3},{3,5},{5,7},{7,1},{8,10},{10,12},{12... | collective-permute-start | bytes 442376 | tf_op jit(solution)/shard_map/ppermute | solution.py:431
  127.3 2.0 %collective-permute-start.22 = (bf16[144,512]{1,0:T(8,128)(2,1)S(1)}, bf16[144,512]{1,0:T(8,128)(2,1)S(1)}, u32[]{:S(2)}, u32[]{:S(2)}) collective-permute-start(bf16[144,512]{1,0:T(8,128)(2,1)S(1)} %get-tuple-element.168), channel_id=1, source_target_pairs={{0,6},{2,0},{4,2},{6,4},{1,7},{3,1},{5,3},{7,5},{8,14},{10,8},{12,... | collective-permute-start | bytes 442376 | tf_op jit(solution)/shard_map/ppermute | solution.py:431
  129.4 0.9 collective-permute-start.20
  130.3 2.9 %column_back.1 = (bf16[256,1024]{1,0:T(8,128)(2,1)}, bf16[256,1024]{1,0:T(8,128)(2,1)}) custom-call(bf16[512,512]{1,0:T(8,128)(2,1)} %select_n.97.table, bf16[256,1024]{1,0:T(8,128)(2,1)} %bitcast.59, bf16[256,1024]{1,0:T(8,128)(2,1)} %bitcast.61), custom_call_target="tpu_custom_call" | custom-call | tf_op jit(solution)/shard_map/column_back/pallas_call | solution.py:82
  133.2 2.9 %column_sum.1 = f32[8,512]{1,0:T(8,128)} custom-call(bf16[256,1024]{1,0:T(8,128)(2,1)} %bitcast.60, bf16[256,1024]{1,0:T(8,128)(2,1)} %bitcast.62, bf16[128,1024]{1,0:T(8,128)(2,1)} %bitcast.68, bf16[128,1024]{1,0:T(8,128)(2,1)} %bitcast.7.refs_1_.refs_3_, bf16[128,1024]{1,0:T(8,128)(2,1)} %bitcast.9.refs_2_.refs_4_, bf16[128,1024]{1,0:T(8,128)(2,1)} %bitcast.72), custom_call_target="tpu_custom_call" | custom-call | tf_op jit(solution)/shard_map/column_sum/pallas_call | solution.py:112
  136.1 3.5 %all-to-all-start.3 = ((bf16[4,64,1024]{2,1,0:T(8,128)(2,1)}), bf16[4,64,1024]{2,1,0:T(8,128)(2,1)S(1)}, u32[]{:S(2)}, u32[]{:S(2)}) async-start(bf16[4,64,1024]{2,1,0:T(8,128)(2,1)} %bitcast.28), calls=%async_computation.3 | async-start | bytes 1048576 | tf_op jit(solution)/shard_map/all_to_all | solution.py:439
  139.6 0.8 reshape.112
  140.8 2.4 %collective-permute-done.20 = bf16[144,512]{1,0:T(8,128)(2,1)S(1)} collective-permute-done((bf16[144,512]{1,0:T(8,128)(2,1)S(1)}, bf16[144,512]{1,0:T(8,128)(2,1)S(1)}, u32[]{:S(2)}, u32[]{:S(2)}) %collective-permute-start.20) | collective-permute-done | bytes 147488 | tf_op jit(solution)/shard_map/ppermute | solution.py:431
  143.1 1.0 add_convert_fusion
  144.1 0.6 collective-permute-start.24
  144.7 3.2 %collective-permute-done.24 = bf16[16,512]{1,0:T(8,128)(2,1)S(1)} collective-permute-done((bf16[16,512]{1,0:T(8,128)(2,1)S(1)}, bf16[16,512]{1,0:T(8,128)(2,1)S(1)}, u32[]{:S(2)}, u32[]{:S(2)}) %collective-permute-start.24) | collective-permute-done | bytes 16416 | tf_op jit(solution)/shard_map/ppermute | solution.py:435
  148.0 3.9 %collective-permute-start.27 = (bf16[144,512]{1,0:T(8,128)(2,1)S(1)}, bf16[144,512]{1,0:T(8,128)(2,1)S(1)}, u32[]{:S(2)}, u32[]{:S(2)}) collective-permute-start(bf16[144,512]{1,0:T(8,128)(2,1)S(1)} %concatenate.37), channel_id=1, source_target_pairs={{0,6},{2,0},{4,2},{6,4},{1,7},{3,1},{5,3},{7,5},{8,14},{10,8},{12,... | collective-permute-start | bytes 442376 | tf_op jit(solution)/shard_map/ppermute | solution.py:431
  151.9 0.6 collective-permute-start.25
  152.6 1.5 collective-permute-start.28
  154.1 0.6 collective-permute-done.27
  154.7 1.5 collective-permute-start.31
  156.2 8.9 %collective-permute-done.26 = bf16[144,512]{1,0:T(8,128)(2,1)S(1)} collective-permute-done((bf16[144,512]{1,0:T(8,128)(2,1)S(1)}, bf16[144,512]{1,0:T(8,128)(2,1)S(1)}, u32[]{:S(2)}, u32[]{:S(2)}) %collective-permute-start.26) | collective-permute-done | bytes 147488 | tf_op jit(solution)/shard_map/ppermute | solution.py:431
  165.0 1.5 collective-permute-start.30
  167.1 3.5 %all-to-all-start.2 = ((bf16[4,64,1024]{2,1,0:T(8,128)(2,1)}), bf16[4,64,1024]{2,1,0:T(8,128)(2,1)S(1)}, u32[]{:S(2)}, u32[]{:S(2)}) async-start(bf16[4,64,1024]{2,1,0:T(8,128)(2,1)} %bitcast.26), calls=%async_computation.2 | async-start | bytes 1048576 | tf_op jit(solution)/shard_map/all_to_all | solution.py:439
  170.8 1.3 collective-permute-done.29
  172.3 2.0 %finish.2.refs_0_ = bf16[2,256,1024]{2,1,0:T(8,128)(2,1)} custom-call(bf16[256,1024]{1,0:T(8,128)(2,1)} %get-tuple-element.156.grad, bf16[256,1024]{1,0:T(8,128)(2,1)} %bitcast.69), custom_call_target="tpu_custom_call" | custom-call | tf_op jit(solution)/shard_map/finish/pallas_call | solution.py:418
  174.3 2.9 %unpack.1 = (f32[1024,512]{1,0:T(8,128)}, f32[1024,512]{1,0:T(8,128)}, f32[256,256]{1,0:T(8,128)}, f32[4,2,512]{2,1,0:T(2,128)}, f32[4,2,512]{2,1,0:T(2,128)}, /*index=5*/f32[8,8]{1,0:T(8,128)}) custom-call(s32[4]{0:T(128)S(1)} %copy-done.2, bf16[4,144,512]{2,1,0:T(8,128)(2,1)S(1)} %pad_maximum_fusion.refs_0_, ...), custom_call_target="tpu_custom_call" | custom-call | tf_op jit(solution)/shard_map/unpack/pallas_call | solution.py:391
  177.1 5.9 %all-to-all-done.2 = bf16[4,64,1024]{2,1,0:T(8,128)(2,1)S(1)} async-done(((bf16[4,64,1024]{2,1,0:T(8,128)(2,1)}), bf16[4,64,1024]{2,1,0:T(8,128)(2,1)S(1)}, u32[]{:S(2)}, u32[]{:S(2)}) %all-to-all-start.2) | async-done | bytes 524320 | tf_op jit(solution)/shard_map/all_to_all | solution.py:439
  183.0 0.8 copy-done.9
  183.9 2.0 %finish.3 = bf16[2,256,1024]{2,1,0:T(8,128)(2,1)} custom-call(bf16[256,1024]{1,0:T(8,128)(2,1)} %get-tuple-element.130.grad, bf16[256,1024]{1,0:T(8,128)(2,1)} %bitcast.70, bf16[2,256,1024]{2,1,0:T(8,128)(2,1)} %finish.2.refs_0_), custom_call_target="tpu_custom_call", output_to_operand_aliasing={{}: (2, {})} | custom-call | tf_op jit(solution)/shard_map/finish/pallas_call | solution.py:418
  (106 shorter events, 5.3 us)
Async XLA Ops:
  0.6 4.4 %copy-start.3 = (bf16[1,2,256,1024]{3,2,1,0:T(8,128)(2,1)S(1)}, bf16[1,2,256,1024]{3,2,1,0:T(8,128)(2,1)}, u32[]{:S(2)}) copy-start(bf16[1,2,256,1024]{3,2,1,0:T(8,128)(2,1)} %param.8) | copy-start | bytes 3145732
  2.0 8.7 %copy-start.19 = (bf16[8,8]{1,0:T(8,128)(2,1)S(1)}, bf16[8,8]{1,0:T(8,128)(2,1)}, u32[]{:S(2)}) copy-start(bf16[8,8]{1,0:T(8,128)(2,1)} %param.11) | copy-start | bytes 388
  2.0 15.1 %collective-permute-start.3 = (bf16[512,512]{1,0:T(8,128)(2,1)S(1)}, bf16[512,512]{1,0:T(8,128)(2,1)}, u32[]{:S(2)}, u32[]{:S(2)}) collective-permute-start(bf16[512,512]{1,0:T(8,128)(2,1)S(1)} %fusion), channel_id=1, source_target_pairs={{0,1},{1,0},{2,3},{3,2},{4,5},{5,4},{6,7},{7,6},{8,9},{9,8},{10,11... | collective-permute-start | bytes 1572872 | tf_op jit(solution)/shard_map/ppermute | solution.py:435
  5.1 6.3 %copy-start.18 = (bf16[4,4,512]{2,1,0:T(4,128)(2,1)S(1)}, bf16[4,4,512]{2,1,0:T(4,128)(2,1)}, u32[]{:S(2)}) copy-start(bf16[4,4,512]{2,1,0:T(4,128)(2,1)} %param.14) | copy-start | bytes 49156
  6.0 12.8 %copy-start.17 = (bf16[4,4,512]{2,1,0:T(4,128)(2,1)S(1)}, bf16[4,4,512]{2,1,0:T(4,128)(2,1)}, u32[]{:S(2)}) copy-start(bf16[4,4,512]{2,1,0:T(4,128)(2,1)} %param.15) | copy-start | bytes 49156
  6.0 18.4 %collective-permute-start.2 = (bf16[2,64,1024]{2,1,0:T(8,128)(2,1)}, bf16[2,64,1024]{2,1,0:T(8,128)(2,1)S(1)}, u32[]{:S(2)}, u32[]{:S(2)}) collective-permute-start(bf16[2,64,1024]{2,1,0:T(8,128)(2,1)} %get-tuple-element.163), channel_id=1, source_target_pairs={{0,6},{2,0},{4,2},{6,4},{1,7},{3,1},{5,3},{7,5},{8,14},{10,8},{12,... | collective-permute-start | bytes 786440 | tf_op jit(solution)/shard_map/ppermute | solution.py:431
  9.6 14.9 %collective-permute-start = (bf16[2,64,1024]{2,1,0:T(8,128)(2,1)}, bf16[2,64,1024]{2,1,0:T(8,128)(2,1)}, u32[]{:S(2)}, u32[]{:S(2)}) collective-permute-start(bf16[2,64,1024]{2,1,0:T(8,128)(2,1)} %get-tuple-element.164), channel_id=1, source_target_pairs={{0,2},{2,4},{4,6},{6,0},{1,3},{3,5},{5,7},{7,1},{8,10},{10,12},{12... | collective-permute-start | bytes 786440 | tf_op jit(solution)/shard_map/ppermute | solution.py:431
  9.6 22.3 %collective-permute-start.1 = (bf16[2,64,1024]{2,1,0:T(8,128)(2,1)}, bf16[2,64,1024]{2,1,0:T(8,128)(2,1)}, u32[]{:S(2)}, u32[]{:S(2)}) collective-permute-start(bf16[2,64,1024]{2,1,0:T(8,128)(2,1)} %get-tuple-element.166), channel_id=1, source_target_pairs={{0,4},{2,6},{4,0},{6,2},{1,5},{3,7},{5,1},{7,3},{8,12},{10,14},{12... | collective-permute-start | bytes 786440 | tf_op jit(solution)/shard_map/ppermute | solution.py:431
  10.7 8.2 %copy-start.6 = (bf16[1,2,256,1024]{3,2,1,0:T(8,128)(2,1)S(1)}, bf16[1,2,256,1024]{3,2,1,0:T(8,128)(2,1)}, u32[]{:S(2)}) copy-start(bf16[1,2,256,1024]{3,2,1,0:T(8,128)(2,1)} %param.9) | copy-start | bytes 3145732
  17.1 19.4 %collective-permute-start.4 = (bf16[512,512]{1,0:T(8,128)(2,1)}, bf16[512,512]{1,0:T(8,128)(2,1)}, u32[]{:S(2)}, u32[]{:S(2)}) collective-permute-start(bf16[512,512]{1,0:T(8,128)(2,1)} %collective-permute-done.3.refs_2_), channel_id=1, source_target_pairs={{0,16},{8,24},{16,0},{24,8},{1,17},{9,25},{17,1},{25,9},{2,18},{10... | collective-permute-start | bytes 1572872 | tf_op jit(solution)/shard_map/ppermute | solution.py:435
  18.8 38.0 %collective-permute-start.10 = (bf16[2,256,1024]{2,1,0:T(8,128)(2,1)S(1)}, bf16[2,256,1024]{2,1,0:T(8,128)(2,1)S(1)}, u32[]{:S(2)}, u32[]{:S(2)}) collective-permute-start(bf16[2,256,1024]{2,1,0:T(8,128)(2,1)S(1)} %bitcast.65), channel_id=1, source_target_pairs={{0,1},{1,0},{2,3},{3,2},{4,5},{5,4},{6,7},{7,6},{8,9},{9,8},{10,11... | collective-permute-start | bytes 3145736 | tf_op jit(solution)/shard_map/ppermute | solution.py:435
  24.5 9.0 %copy-start.10 = (bf16[2,64,1024]{2,1,0:T(8,128)(2,1)}, bf16[2,64,1024]{2,1,0:T(8,128)(2,1)S(1)}, u32[]{:S(2)}) copy-start(bf16[2,64,1024]{2,1,0:T(8,128)(2,1)S(1)} %collective-permute-done.2) | copy-start | bytes 786436
  36.5 3.8 %collective-permute-start.7 = (bf16[512,512]{1,0:T(8,128)(2,1)}, bf16[512,512]{1,0:T(8,128)(2,1)}, u32[]{:S(2)}, u32[]{:S(2)}) collective-permute-start(bf16[512,512]{1,0:T(8,128)(2,1)} %collective-permute-done.3.refs_2_), channel_id=1, source_target_pairs={{0,8},{8,0},{16,24},{24,16},{1,9},{9,1},{17,25},{25,17},{2,10},{10... | collective-permute-start | bytes 1572872 | tf_op jit(solution)/shard_map/ppermute | solution.py:435
  36.6 3.7 %collective-permute-start.8 = (bf16[512,512]{1,0:T(8,128)(2,1)}, bf16[512,512]{1,0:T(8,128)(2,1)}, u32[]{:S(2)}, u32[]{:S(2)}) collective-permute-start(bf16[512,512]{1,0:T(8,128)(2,1)} %collective-permute-done.4.refs_3_), channel_id=1, source_target_pairs={{0,8},{8,0},{16,24},{24,16},{1,9},{9,1},{17,25},{25,17},{2,10},{10... | collective-permute-start | bytes 1572872 | tf_op jit(solution)/shard_map/ppermute | solution.py:435
  37.1 8.5 %collective-permute-start.5 = (bf16[64,1024]{1,0:T(8,128)(2,1)}, bf16[64,1024]{1,0:T(8,128)(2,1)S(1)}, u32[]{:S(2)}, u32[]{:S(2)}) collective-permute-start(bf16[64,1024]{1,0:T(8,128)(2,1)} %get-tuple-element.99), channel_id=1, source_target_pairs={{0,2},{2,4},{4,6},{6,0},{1,3},{3,5},{5,7},{7,1},{8,10},{10,12},{12... | collective-permute-start | bytes 393224 | tf_op jit(solution)/shard_map/ppermute | solution.py:431
  37.1 14.1 %collective-permute-start.6 = (bf16[64,1024]{1,0:T(8,128)(2,1)}, bf16[64,1024]{1,0:T(8,128)(2,1)S(1)}, u32[]{:S(2)}, u32[]{:S(2)}) collective-permute-start(bf16[64,1024]{1,0:T(8,128)(2,1)} %get-tuple-element.100), channel_id=1, source_target_pairs={{0,4},{2,6},{4,0},{6,2},{1,5},{3,7},{5,1},{7,3},{8,12},{10,14},{12... | collective-permute-start | bytes 393224 | tf_op jit(solution)/shard_map/ppermute | solution.py:431
  40.3 16.6 %collective-permute-start.9 = (bf16[64,1024]{1,0:T(8,128)(2,1)}, bf16[64,1024]{1,0:T(8,128)(2,1)S(1)}, u32[]{:S(2)}, u32[]{:S(2)}) collective-permute-start(bf16[64,1024]{1,0:T(8,128)(2,1)} %get-tuple-element.108), channel_id=1, source_target_pairs={{0,6},{2,0},{4,2},{6,4},{1,7},{3,1},{5,3},{7,5},{8,14},{10,8},{12,... | collective-permute-start | bytes 393224 | tf_op jit(solution)/shard_map/ppermute | solution.py:431
  42.2 18.9 %collective-permute-start.12 = (bf16[64,1024]{1,0:T(8,128)(2,1)}, bf16[64,1024]{1,0:T(8,128)(2,1)S(1)}, u32[]{:S(2)}, u32[]{:S(2)}) collective-permute-start(bf16[64,1024]{1,0:T(8,128)(2,1)} %get-tuple-element.116), channel_id=1, source_target_pairs={{0,2},{2,4},{4,6},{6,0},{1,3},{3,5},{5,7},{7,1},{8,10},{10,12},{12... | collective-permute-start | bytes 393224 | tf_op jit(solution)/shard_map/ppermute | solution.py:431
  45.5 12.0 %copy-start.13 = (bf16[64,1024]{1,0:T(8,128)(2,1)}, bf16[64,1024]{1,0:T(8,128)(2,1)S(1)}, u32[]{:S(2)}) copy-start(bf16[64,1024]{1,0:T(8,128)(2,1)S(1)} %collective-permute-done.5.refs_0_) | copy-start | bytes 393220
  45.5 16.0 %collective-permute-start.13 = (bf16[64,1024]{1,0:T(8,128)(2,1)}, bf16[64,1024]{1,0:T(8,128)(2,1)S(1)}, u32[]{:S(2)}, u32[]{:S(2)}) collective-permute-start(bf16[64,1024]{1,0:T(8,128)(2,1)} %get-tuple-element.117), channel_id=1, source_target_pairs={{0,4},{2,6},{4,0},{6,2},{1,5},{3,7},{5,1},{7,3},{8,12},{10,14},{12... | collective-permute-start | bytes 393224 | tf_op jit(solution)/shard_map/ppermute | solution.py:431
  51.1 5.7 %copy-start.15 = (bf16[64,1024]{1,0:T(8,128)(2,1)}, bf16[64,1024]{1,0:T(8,128)(2,1)S(1)}, u32[]{:S(2)}) copy-start(bf16[64,1024]{1,0:T(8,128)(2,1)S(1)} %collective-permute-done.6.refs_1_) | copy-start | bytes 393220
  51.1 10.4 %collective-permute-start.14 = (bf16[64,1024]{1,0:T(8,128)(2,1)}, bf16[64,1024]{1,0:T(8,128)(2,1)}, u32[]{:S(2)}, u32[]{:S(2)}) collective-permute-start(bf16[64,1024]{1,0:T(8,128)(2,1)} %get-tuple-element.118), channel_id=1, source_target_pairs={{0,6},{2,0},{4,2},{6,4},{1,7},{3,1},{5,3},{7,5},{8,14},{10,8},{12,... | collective-permute-start | bytes 393224 | tf_op jit(solution)/shard_map/ppermute | solution.py:431
  56.8 1.0 copy-start.7
  56.8 0.7 copy-start.16
  57.8 17.0 %copy-start.1 = (bf16[2,512,512]{2,1,0:T(8,128)(2,1)S(1)}, bf16[2,512,512]{2,1,0:T(8,128)(2,1)}, u32[]{:S(2)}) copy-start(bf16[2,512,512]{2,1,0:T(8,128)(2,1)} %wu_own.3) | copy-start | bytes 3145732
  60.5 14.4 %copy-start = (bf16[2,512,512]{2,1,0:T(8,128)(2,1)S(1)}, bf16[2,512,512]{2,1,0:T(8,128)(2,1)}, u32[]{:S(2)}) copy-start(bf16[2,512,512]{2,1,0:T(8,128)(2,1)} %wg_own.3) | copy-start | bytes 3145732
  60.5 14.3 %copy-start.2 = (s32[4]{0:T(128)S(1)}, s32[4]{0:T(128)}, u32[]{:S(2)}) copy-start(s32[4]{0:T(128)} %pad_add_fusion.place.refs_0_) | copy-start | bytes 52
  60.5 14.3 %collective-permute-start.11 = (bf16[256,1024]{1,0:T(8,128)(2,1)}, bf16[256,1024]{1,0:T(8,128)(2,1)}, u32[]{:S(2)}, u32[]{:S(2)}) collective-permute-start(bf16[256,1024]{1,0:T(8,128)(2,1)} %get-tuple-element.114.refs_0_.refs_2_), channel_id=1, source_target_pairs={{0,1},{1,0},{2,3},{3,2},{4,5},{5,4},{6,7},{7,6},{8,9},{9,8},{10,11... | collective-permute-start | bytes 1572872 | tf_op jit(solution)/shard_map/ppermute | solution.py:435
  61.1 0.6 copy-start.12
  61.5 0.6 copy-start.14
  64.6 19.2 %collective-permute-start.15 = (bf16[256,1024]{1,0:T(8,128)(2,1)}, bf16[256,1024]{1,0:T(8,128)(2,1)S(1)}, u32[]{:S(2)}, u32[]{:S(2)}) collective-permute-start(bf16[256,1024]{1,0:T(8,128)(2,1)} %get-tuple-element.120.refs_0_.refs_3_), channel_id=1, source_target_pairs={{0,1},{1,0},{2,3},{3,2},{4,5},{5,4},{6,7},{7,6},{8,9},{9,8},{10,11... | collective-permute-start | bytes 1572872 | tf_op jit(solution)/shard_map/ppermute | solution.py:435
  83.8 0.8 copy-start.11
  84.6 18.4 %all-to-all-start = ((bf16[4,64,1024]{2,1,0:T(8,128)(2,1)}), bf16[4,64,1024]{2,1,0:T(8,128)(2,1)S(1)}, u32[]{:S(2)}, u32[]{:S(2)}) async-start(bf16[4,64,1024]{2,1,0:T(8,128)(2,1)} %bitcast.74), calls=%async_computation | async-start | bytes 1048576 | tf_op jit(solution)/shard_map/all_to_all | solution.py:439
  103.0 7.8 %copy-start.4 = (bf16[4,64,1024]{2,1,0:T(8,128)(2,1)}, bf16[4,64,1024]{2,1,0:T(8,128)(2,1)S(1)}, u32[]{:S(2)}) copy-start(bf16[4,64,1024]{2,1,0:T(8,128)(2,1)S(1)} %all-to-all-done) | copy-start | bytes 1572868
  103.0 5.2 %collective-permute-start.16 = (bf16[8,144,512]{2,1,0:T(8,128)(2,1)}, bf16[8,144,512]{2,1,0:T(8,128)(2,1)S(1)}, u32[]{:S(2)}, u32[]{:S(2)}) collective-permute-start(bf16[8,144,512]{2,1,0:T(8,128)(2,1)} %get-tuple-element.145), channel_id=1, source_target_pairs={{0,8},{8,0},{16,24},{24,16},{1,9},{9,1},{17,25},{25,17},{2,10},{10... | collective-permute-start | bytes 3538952 | tf_op jit(solution)/shard_map/ppermute | solution.py:435
  103.1 20.2 %all-to-all-start.1 = ((bf16[4,64,1024]{2,1,0:T(8,128)(2,1)}), bf16[4,64,1024]{2,1,0:T(8,128)(2,1)S(1)}, u32[]{:S(2)}, u32[]{:S(2)}) async-start(bf16[4,64,1024]{2,1,0:T(8,128)(2,1)} %bitcast.18), calls=%async_computation.1 | async-start | bytes 1048576 | tf_op jit(solution)/shard_map/all_to_all | solution.py:439
  110.8 12.5 %collective-permute-start.17 = (bf16[144,512]{1,0:T(8,128)(2,1)}, bf16[144,512]{1,0:T(8,128)(2,1)S(1)}, u32[]{:S(2)}, u32[]{:S(2)}) collective-permute-start(bf16[144,512]{1,0:T(8,128)(2,1)} %get-tuple-element.146), channel_id=1, source_target_pairs={{0,16},{8,24},{16,0},{24,8},{1,17},{9,25},{17,1},{25,9},{2,18},{10... | collective-permute-start | bytes 442376 | tf_op jit(solution)/shard_map/ppermute | solution.py:435
  112.3 11.0 %collective-permute-start.19 = (bf16[144,512]{1,0:T(8,128)(2,1)}, bf16[144,512]{1,0:T(8,128)(2,1)S(1)}, u32[]{:S(2)}, u32[]{:S(2)}) collective-permute-start(bf16[144,512]{1,0:T(8,128)(2,1)} %get-tuple-element.150), channel_id=1, source_target_pairs={{0,16},{8,24},{16,0},{24,8},{1,17},{9,25},{17,1},{25,9},{2,18},{10... | collective-permute-start | bytes 442376 | tf_op jit(solution)/shard_map/ppermute | solution.py:435
  112.9 11.2 %collective-permute-start.21 = (bf16[144,512]{1,0:T(8,128)(2,1)}, bf16[144,512]{1,0:T(8,128)(2,1)S(1)}, u32[]{:S(2)}, u32[]{:S(2)}) collective-permute-start(bf16[144,512]{1,0:T(8,128)(2,1)} %get-tuple-element.151), channel_id=1, source_target_pairs={{0,16},{8,24},{16,0},{24,8},{1,17},{9,25},{17,1},{25,9},{2,18},{10... | collective-permute-start | bytes 442376 | tf_op jit(solution)/shard_map/ppermute | solution.py:435
  114.4 26.4 %collective-permute-start.23 = (bf16[144,512]{1,0:T(8,128)(2,1)}, bf16[144,512]{1,0:T(8,128)(2,1)S(1)}, u32[]{:S(2)}, u32[]{:S(2)}) collective-permute-start(bf16[144,512]{1,0:T(8,128)(2,1)} %get-tuple-element.152), channel_id=1, source_target_pairs={{0,16},{8,24},{16,0},{24,8},{1,17},{9,25},{17,1},{25,9},{2,18},{10... | collective-permute-start | bytes 442376 | tf_op jit(solution)/shard_map/ppermute | solution.py:435
  123.3 6.9 %copy-start.5 = (bf16[4,64,1024]{2,1,0:T(8,128)(2,1)}, bf16[4,64,1024]{2,1,0:T(8,128)(2,1)S(1)}, u32[]{:S(2)}) copy-start(bf16[4,64,1024]{2,1,0:T(8,128)(2,1)S(1)} %all-to-all-done.1) | copy-start | bytes 1572868
  125.2 15.5 %collective-permute-start.18 = (bf16[144,512]{1,0:T(8,128)(2,1)S(1)}, bf16[144,512]{1,0:T(8,128)(2,1)S(1)}, u32[]{:S(2)}, u32[]{:S(2)}) collective-permute-start(bf16[144,512]{1,0:T(8,128)(2,1)S(1)} %get-tuple-element.167), channel_id=1, source_target_pairs={{0,2},{2,4},{4,6},{6,0},{1,3},{3,5},{5,7},{7,1},{8,10},{10,12},{12... | collective-permute-start | bytes 442376 | tf_op jit(solution)/shard_map/ppermute | solution.py:431
  127.3 13.4 %collective-permute-start.22 = (bf16[144,512]{1,0:T(8,128)(2,1)S(1)}, bf16[144,512]{1,0:T(8,128)(2,1)S(1)}, u32[]{:S(2)}, u32[]{:S(2)}) collective-permute-start(bf16[144,512]{1,0:T(8,128)(2,1)S(1)} %get-tuple-element.168), channel_id=1, source_target_pairs={{0,6},{2,0},{4,2},{6,4},{1,7},{3,1},{5,3},{7,5},{8,14},{10,8},{12,... | collective-permute-start | bytes 442376 | tf_op jit(solution)/shard_map/ppermute | solution.py:431
  129.4 13.7 %collective-permute-start.20 = (bf16[144,512]{1,0:T(8,128)(2,1)S(1)}, bf16[144,512]{1,0:T(8,128)(2,1)S(1)}, u32[]{:S(2)}, u32[]{:S(2)}) collective-permute-start(bf16[144,512]{1,0:T(8,128)(2,1)S(1)} %get-tuple-element.169), channel_id=1, source_target_pairs={{0,4},{2,6},{4,0},{6,2},{1,5},{3,7},{5,1},{7,3},{8,12},{10,14},{12... | collective-permute-start | bytes 442376 | tf_op jit(solution)/shard_map/ppermute | solution.py:431
  136.1 31.0 %all-to-all-start.3 = ((bf16[4,64,1024]{2,1,0:T(8,128)(2,1)}), bf16[4,64,1024]{2,1,0:T(8,128)(2,1)S(1)}, u32[]{:S(2)}, u32[]{:S(2)}) async-start(bf16[4,64,1024]{2,1,0:T(8,128)(2,1)} %bitcast.28), calls=%async_computation.3 | async-start | bytes 1048576 | tf_op jit(solution)/shard_map/all_to_all | solution.py:439
  144.1 3.8 %collective-permute-start.24 = (bf16[16,512]{1,0:T(8,128)(2,1)S(1)}, bf16[16,512]{1,0:T(8,128)(2,1)S(1)}, u32[]{:S(2)}, u32[]{:S(2)}) collective-permute-start(bf16[16,512]{1,0:T(8,128)(2,1)S(1)} %slice.88), channel_id=1, source_target_pairs={{0,1},{1,0},{2,3},{3,2},{4,5},{5,4},{6,7},{7,6},{8,9},{9,8},{10,11... | collective-permute-start | bytes 49160 | tf_op jit(solution)/shard_map/ppermute | solution.py:435
  148.0 6.6 %collective-permute-start.27 = (bf16[144,512]{1,0:T(8,128)(2,1)S(1)}, bf16[144,512]{1,0:T(8,128)(2,1)S(1)}, u32[]{:S(2)}, u32[]{:S(2)}) collective-permute-start(bf16[144,512]{1,0:T(8,128)(2,1)S(1)} %concatenate.37), channel_id=1, source_target_pairs={{0,6},{2,0},{4,2},{6,4},{1,7},{3,1},{5,3},{7,5},{8,14},{10,8},{12,... | collective-permute-start | bytes 442376 | tf_op jit(solution)/shard_map/ppermute | solution.py:431
  151.9 13.1 %collective-permute-start.26 = (bf16[144,512]{1,0:T(8,128)(2,1)S(1)}, bf16[144,512]{1,0:T(8,128)(2,1)S(1)}, u32[]{:S(2)}, u32[]{:S(2)}) collective-permute-start(bf16[144,512]{1,0:T(8,128)(2,1)S(1)} %concatenate.37), channel_id=1, source_target_pairs={{0,4},{2,6},{4,0},{6,2},{1,5},{3,7},{5,1},{7,3},{8,12},{10,14},{12... | collective-permute-start | bytes 442376 | tf_op jit(solution)/shard_map/ppermute | solution.py:431
  151.9 14.6 %collective-permute-start.25 = (bf16[144,512]{1,0:T(8,128)(2,1)S(1)}, bf16[144,512]{1,0:T(8,128)(2,1)S(1)}, u32[]{:S(2)}, u32[]{:S(2)}) collective-permute-start(bf16[144,512]{1,0:T(8,128)(2,1)S(1)} %concatenate.37), channel_id=1, source_target_pairs={{0,2},{2,4},{4,6},{6,0},{1,3},{3,5},{5,7},{7,1},{8,10},{10,12},{12... | collective-permute-start | bytes 442376 | tf_op jit(solution)/shard_map/ppermute | solution.py:431
  152.6 18.1 %collective-permute-start.28 = (bf16[144,512]{1,0:T(8,128)(2,1)S(1)}, bf16[144,512]{1,0:T(8,128)(2,1)S(1)}, u32[]{:S(2)}, u32[]{:S(2)}) collective-permute-start(bf16[144,512]{1,0:T(8,128)(2,1)S(1)} %concatenate.37), channel_id=1, source_target_pairs={{0,16},{8,24},{16,0},{24,8},{1,17},{9,25},{17,1},{25,9},{2,18},{10... | collective-permute-start | bytes 442376 | tf_op jit(solution)/shard_map/ppermute | solution.py:435
  154.7 16.1 %collective-permute-start.31 = (bf16[144,512]{1,0:T(8,128)(2,1)S(1)}, bf16[144,512]{1,0:T(8,128)(2,1)S(1)}, u32[]{:S(2)}, u32[]{:S(2)}) collective-permute-start(bf16[144,512]{1,0:T(8,128)(2,1)S(1)} %collective-permute-done.27), channel_id=1, source_target_pairs={{0,16},{8,24},{16,0},{24,8},{1,17},{9,25},{17,1},{25,9},{2,18},{10... | collective-permute-start | bytes 442376 | tf_op jit(solution)/shard_map/ppermute | solution.py:435
  165.0 5.7 %collective-permute-start.30 = (bf16[144,512]{1,0:T(8,128)(2,1)S(1)}, bf16[144,512]{1,0:T(8,128)(2,1)S(1)}, u32[]{:S(2)}, u32[]{:S(2)}) collective-permute-start(bf16[144,512]{1,0:T(8,128)(2,1)S(1)} %collective-permute-done.26), channel_id=1, source_target_pairs={{0,16},{8,24},{16,0},{24,8},{1,17},{9,25},{17,1},{25,9},{2,18},{10... | collective-permute-start | bytes 442376 | tf_op jit(solution)/shard_map/ppermute | solution.py:435
  166.6 5.5 %collective-permute-start.29 = (bf16[144,512]{1,0:T(8,128)(2,1)S(1)}, bf16[144,512]{1,0:T(8,128)(2,1)S(1)}, u32[]{:S(2)}, u32[]{:S(2)}) collective-permute-start(bf16[144,512]{1,0:T(8,128)(2,1)S(1)} %collective-permute-done.25), channel_id=1, source_target_pairs={{0,16},{8,24},{16,0},{24,8},{1,17},{9,25},{17,1},{25,9},{2,18},{10... | collective-permute-start | bytes 442376 | tf_op jit(solution)/shard_map/ppermute | solution.py:435
  167.1 5.1 %copy-start.8 = (bf16[4,64,1024]{2,1,0:T(8,128)(2,1)}, bf16[4,64,1024]{2,1,0:T(8,128)(2,1)S(1)}, u32[]{:S(2)}) copy-start(bf16[4,64,1024]{2,1,0:T(8,128)(2,1)S(1)} %all-to-all-done.3) | copy-start | bytes 1572868
  167.1 15.9 %all-to-all-start.2 = ((bf16[4,64,1024]{2,1,0:T(8,128)(2,1)}), bf16[4,64,1024]{2,1,0:T(8,128)(2,1)S(1)}, u32[]{:S(2)}, u32[]{:S(2)}) async-start(bf16[4,64,1024]{2,1,0:T(8,128)(2,1)} %bitcast.26), calls=%async_computation.2 | async-start | bytes 1048576 | tf_op jit(solution)/shard_map/all_to_all | solution.py:439
  170.6 3.6 %collective-permute-start.32 = (bf16[4,144,512]{2,1,0:T(8,128)(2,1)S(1)}, bf16[4,144,512]{2,1,0:T(8,128)(2,1)S(1)}, u32[]{:S(2)}, u32[]{:S(2)}) collective-permute-start(bf16[4,144,512]{2,1,0:T(8,128)(2,1)S(1)} %pad_maximum_fusion.refs_0_), channel_id=1, source_target_pairs={{0,8},{8,0},{16,24},{24,16},{1,9},{9,1},{17,25},{25,17},{2,10},{10... | collective-permute-start | bytes 1769480 | tf_op jit(solution)/shard_map/ppermute | solution.py:435
  172.2 2.1 %collective-permute-start.33 = (bf16[4,144,512]{2,1,0:T(8,128)(2,1)S(1)}, bf16[4,144,512]{2,1,0:T(8,128)(2,1)S(1)}, u32[]{:S(2)}, u32[]{:S(2)}) collective-permute-start(bf16[4,144,512]{2,1,0:T(8,128)(2,1)S(1)} %pad_maximum_fusion.1.refs_1_), channel_id=1, source_target_pairs={{0,8},{8,0},{16,24},{24,16},{1,9},{9,1},{17,25},{25,17},{2,10},{10... | collective-permute-start | bytes 1769480 | tf_op jit(solution)/shard_map/ppermute | solution.py:435
  183.0 0.8 copy-start.9

commit v6 on v5

--- a/solution.py
+++ b/solution.py
@@ -283,22 +283,20 @@
 
 def sums_kernel(rows, parts, place, row_sum, *refs):
     hid, back_g, back_u, mix_sum = (refs[i * rows : (i + 1) * rows] for i in range(4))
-    outs = refs[4 * rows :]
-    size = outs[0].shape[-1]
-    local = hid[0].shape[1] // size
-    blocks = 2 * local
+    kept, sent, ready, done = refs[4 * rows :]
+    cols, size = hid[0].shape
+    blocks, local = mix_sum[0].shape[1:3]
     first = (((0,), (0,)), ((), ()))
     high = local * size // parts
     per = size // high
     chan, core = place[1], place[2]
-    for part, out in ((1, outs[1]), (0, outs[0])):
-        k = core if part == 0 else 1 - core
-        spot = pl.ds(pl.multiple_of(k * size, size), size)
+
+    def half(k, out):
         for w, back in enumerate((back_g, back_u)):
             total = None
             for h in range(rows):
                 term = lax.dot_general(
-                    hid[h][:, spot], back[h][:, spot], first, preferred_element_type=F
+                    hid[h][...], back[h][...], first, preferred_element_type=F
                 )
                 total = term if total is None else total + term
             for q in range(per):
@@ -318,18 +316,39 @@
             tail = jnp.concatenate([eight, *lines, jnp.zeros((6, size), F)], axis=0)
             out[q, 2 * high :, :] = tail.astype(BF)
 
+    copy = pltpu.make_async_copy(ready, sent, done.at[0])
+
+    @pl.when(pl.program_id(0) == 0)
+    def _():
+        half(1 - core, ready)
+        copy.start()
+
+    @pl.when(pl.program_id(0) == 1)
+    def _():
+        half(core, kept)
+        copy.wait()
+
 
 def sums(place, parts, row_sum, hid, back_g, back_u, mix_sum):
     rows = len(hid)
+    cols, width = hid[0].shape
     size = mix_sum[0].shape[-1]
-    high = hid[0].shape[1] // parts
+    high = width // parts
     dims = (parts // 2, 2 * high + 16, size)
+    fixed = lambda *shape: pl.BlockSpec(shape, lambda j, at: (0,) * len(shape))
+    side = pl.BlockSpec((cols, size), lambda j, at: (0, at[2] + (1 - j) * (1 - 2 * at[2])))
     return pl.pallas_call(
-        once(functools.partial(sums_kernel, rows, parts)),
+        functools.partial(sums_kernel, rows, parts),
         out_shape=[shape_of(dims)] * 2,
-        grid=(2,),
-        in_specs=[SM] + wholes(row_sum, *hid, *back_g, *back_u, *mix_sum),
-        out_specs=[whole(*dims)] * 2,
+        grid_spec=pltpu.PrefetchScalarGridSpec(
+            num_scalar_prefetch=1,
+            grid=(2,),
+            in_specs=[fixed(*row_sum.shape)]
+            + [side] * (3 * rows)
+            + [fixed(*value.shape) for value in mix_sum],
+            out_specs=[fixed(*dims), pl.BlockSpec(memory_space=pltpu.HBM)],
+            scratch_shapes=[pltpu.VMEM(dims, BF), pltpu.SemaphoreType.DMA((1,))],
+        ),
         compiler_params=PARAMS,
         name="sums",
     )(place, *held_in_hbm(row_sum, *hid, *back_g, *back_u, *mix_sum))
@@ -523,7 +542,10 @@
         for held, value in zip((hidden, mixed), hidden_row(place, rows_in, values, h, got[h])):
             held.append(value)
     weights = (blocks_gate, blocks_up, *lent)
-    others = [swapped(hid, "chan", 1, 2) for hid in hidden]
+    others = [swapped(hidden[0], "chan", 1, 2)]
+    for hid in hidden[1:]:
+        hid, others[-1] = lax.optimization_barrier((hid, others[-1]))
+        others.append(swapped(hid, "chan", 1, 2))
     others[0], hidden[-1] = lax.optimization_barrier((others[0], hidden[-1]))
     grads, back_g, back_u, pieces, mix_sum, rows_sum = [], [], [], [], [], []
     for h in range(rows):

time: 187 us -> 186 us (level)
    ppermute x19, waiting for transfers between devices: 18.9 us -> 12 us  [swapped(): return lax.ppermute(value, axis, [(i, i ^ bit) for i in range(n)])]
    ppermute x15, waiting for transfers between devices: 28.6 us -> 34 us  [shifted(): return lax.ppermute(value, 'seq', [(i, (i + by) % n) for i in range(n)])]
  transfers between devices with their start and end apart: 38 -> 38, of which waited for: 14 -> 15; matrix products, arithmetic and copies ran while one was open for 7% -> 7% of each run, Pallas kernels for 24% -> 23%
where the time goes in v6:
time: 186 us; the launch traced here: 185 us
  starting transfers between devices  60.4 us (32%)
  waiting for transfers between devices  60.3 us (32%)
  Pallas kernels  46.5 us (25%)
  local copies, waits for them, and re-layouts  11.2 us (6%)
  other arithmetic  5.85 us (3%)
    ppermute x15, waiting for transfers between devices, shifted(): return lax.ppermute(value, 'seq', [(i, (i + by) % n) for i in range(n)])  34 us
    ppermute x15, starting transfers between devices, shifted(): return lax.ppermute(value, 'seq', [(i, (i + by) % n) for i in range(n)])  24 us
    ppermute x19, starting transfers between devices, swapped(): return lax.ppermute(value, axis, [(i, i ^ bit) for i in range(n)])  19.9 us
    pallas_call x2, Pallas kernels, channel_row(): pl.pallas_call(functools.partial(channel_kernel, h, count), out_shape=[sh...  18 us
    all_to_all x4, starting transfers between devices, traded(): return lax.all_to_all(value, 'seq', split_axis=0, concat_axis=0, tiled=True)  16.5 us
    all_to_all x4, waiting for transfers between devices, traded(): return lax.all_to_all(value, 'seq', split_axis=0, concat_axis=0, tiled=True)  14.3 us
    ppermute x19, waiting for transfers between devices, swapped(): return lax.ppermute(value, axis, [(i, i ^ bit) for i in range(n)])  12 us
    pallas_call x2, Pallas kernels, column_mix(): pl.pallas_call(functools.partial(column_mix_kernel, len(sources)), out_sh...  5.95 us
  transfers between devices with their start and end apart: 38, of which 15 were waited for; matrix products, arithmetic and copies ran while one was open for 7% of the time, Pallas kernels for 23%

profile of v6, /device:TPU:0, one launch (start us, length us, event | category | flops | bytes accessed | tf_op | source)
XLA Modules:
  0.0 185.3 jit_solution(7941136260309503983)
XLA Ops:
  0.7 1.3 fusion
  2.0 3.0 %collective-permute-start.3 = (bf16[512,512]{1,0:T(8,128)(2,1)S(1)}, bf16[512,512]{1,0:T(8,128)(2,1)}, u32[]{:S(2)}, u32[]{:S(2)}) collective-permute-start(bf16[512,512]{1,0:T(8,128)(2,1)S(1)} %fusion), channel_id=1, source_target_pairs={{0,1},{1,0},{2,3},{3,2},{4,5},{5,4},{6,7},{7,6},{8,9},{9,8},{10,11... | collective-permute-start | bytes 1572872 | tf_op jit(solution)/shard_map/ppermute | solution.py:454
  5.1 1.0 dynamic-slice_bitcast_fusion
  6.0 3.6 %collective-permute-start.2 = (bf16[2,64,1024]{2,1,0:T(8,128)(2,1)}, bf16[2,64,1024]{2,1,0:T(8,128)(2,1)S(1)}, u32[]{:S(2)}, u32[]{:S(2)}) collective-permute-start(bf16[2,64,1024]{2,1,0:T(8,128)(2,1)} %get-tuple-element.167), channel_id=1, source_target_pairs={{0,6},{2,0},{4,2},{6,4},{1,7},{3,1},{5,3},{7,5},{8,14},{10,8},{12,... | collective-permute-start | bytes 786440 | tf_op jit(solution)/shard_map/ppermute | solution.py:450
  9.6 1.0 collective-permute-start.1
  11.3 1.2 broadcast_select_fusion
  12.5 4.6 %collective-permute-done.3.refs_2_ = bf16[512,512]{1,0:T(8,128)(2,1)} collective-permute-done((bf16[512,512]{1,0:T(8,128)(2,1)S(1)}, bf16[512,512]{1,0:T(8,128)(2,1)}, u32[]{:S(2)}, u32[]{:S(2)}) %collective-permute-start.3) | collective-permute-done | bytes 524320 | tf_op jit(solution)/shard_map/ppermute | solution.py:454
  17.1 1.7 collective-permute-start.4
  18.8 1.6 collective-permute-start.13
  20.5 2.6 %select_n.97.table = bf16[512,512]{1,0:T(8,128)(2,1)} reshape(bf16[8,64,8,64]{3,2,1,0:T(8,128)(2,1)} %get-tuple-element.180) | data formatting | bytes 1048576 | tf_op jit(solution)/shard_map/jit(_where)/select_n | solution.py:60
  23.0 1.4 select_n.95.table
  24.5 7.5 %collective-permute-done.1 = bf16[2,64,1024]{2,1,0:T(8,128)(2,1)} collective-permute-done((bf16[2,64,1024]{2,1,0:T(8,128)(2,1)}, bf16[2,64,1024]{2,1,0:T(8,128)(2,1)}, u32[]{:S(2)}, u32[]{:S(2)}) %collective-permute-start.1) | collective-permute-done | bytes 262176 | tf_op jit(solution)/shard_map/ppermute | solution.py:450
  32.0 0.7 broadcast_in_dim.55.refs_7_
  32.7 0.7 broadcast_in_dim.54.refs_6_
  33.5 3.0 %column_mix.1 = (bf16[64,1024]{1,0:T(8,128)(2,1)}, bf16[64,1024]{1,0:T(8,128)(2,1)}, bf16[64,1024]{1,0:T(8,128)(2,1)}, bf16[64,1024]{1,0:T(8,128)(2,1)}, bf16[64...) custom-call(bf16[512,512]{1,0:T(8,128)(2,1)} %select_n.95.table, ...), custom_call_target="tpu_custom_call" | custom-call | tf_op jit(solution)/shard_map/column_mix/pallas_call | solution.py:82
  37.1 3.2 %collective-permute-start.11 = (bf16[64,1024]{1,0:T(8,128)(2,1)}, bf16[64,1024]{1,0:T(8,128)(2,1)S(1)}, u32[]{:S(2)}, u32[]{:S(2)}) collective-permute-start(bf16[64,1024]{1,0:T(8,128)(2,1)} %get-tuple-element.114), channel_id=1, source_target_pairs={{0,4},{2,6},{4,0},{6,2},{1,5},{3,7},{5,1},{7,3},{8,12},{10,14},{12... | collective-permute-start | bytes 393224 | tf_op jit(solution)/shard_map/ppermute | solution.py:450
  40.3 1.9 %collective-permute-start.12 = (bf16[64,1024]{1,0:T(8,128)(2,1)}, bf16[64,1024]{1,0:T(8,128)(2,1)S(1)}, u32[]{:S(2)}, u32[]{:S(2)}) collective-permute-start(bf16[64,1024]{1,0:T(8,128)(2,1)} %get-tuple-element.115), channel_id=1, source_target_pairs={{0,6},{2,0},{4,2},{6,4},{1,7},{3,1},{5,3},{7,5},{8,14},{10,8},{12,... | collective-permute-start | bytes 393224 | tf_op jit(solution)/shard_map/ppermute | solution.py:450
  42.8 2.7 %collective-permute-done.10.refs_0_ = bf16[64,1024]{1,0:T(8,128)(2,1)S(1)} collective-permute-done((bf16[64,1024]{1,0:T(8,128)(2,1)}, bf16[64,1024]{1,0:T(8,128)(2,1)S(1)}, u32[]{:S(2)}, u32[]{:S(2)}) %collective-permute-start.10) | collective-permute-done | bytes 131104 | tf_op jit(solution)/shard_map/ppermute | solution.py:450
  45.5 4.7 %collective-permute-done.11.refs_1_ = bf16[64,1024]{1,0:T(8,128)(2,1)S(1)} collective-permute-done((bf16[64,1024]{1,0:T(8,128)(2,1)}, bf16[64,1024]{1,0:T(8,128)(2,1)S(1)}, u32[]{:S(2)}, u32[]{:S(2)}) %collective-permute-start.11) | collective-permute-done | bytes 131104 | tf_op jit(solution)/shard_map/ppermute | solution.py:450
  51.3 2.6 %hidden_row.3 = (bf16[256,1024]{1,0:T(8,128)(2,1)}, bf16[256,1024]{1,0:T(8,128)(2,1)}) custom-call(s32[4]{0:T(128)} %pad_add_fusion.place.refs_0_, bf16[256,256]{1,0:T(8,128)(2,1)} %refs_10_.3, bf16[2,256,1024]{2,1,0:T(8,128)(2,1)} %bitcast.57, bf16[64,1024]{1,0:T(8,128)(2,1)} %get-tuple-element.117.own, bf16[64,1024]{1,0:T(8,128)(2,1)} %copy-done.12, ...), custom_call_target="tpu_custom_call" | custom-call | tf_op jit(solution)/shard_map/hidden_row/pallas_call | solution.py:140
  54.5 2.3 %collective-permute-start.7 = (bf16[64,1024]{1,0:T(8,128)(2,1)}, bf16[64,1024]{1,0:T(8,128)(2,1)S(1)}, u32[]{:S(2)}, u32[]{:S(2)}) collective-permute-start(bf16[64,1024]{1,0:T(8,128)(2,1)} %get-tuple-element.108), channel_id=1, source_target_pairs={{0,2},{2,4},{4,6},{6,0},{1,3},{3,5},{5,7},{7,1},{8,10},{10,12},{12... | collective-permute-start | bytes 393224 | tf_op jit(solution)/shard_map/ppermute | solution.py:450
  56.8 0.9 collective-permute-start.8
  57.6 1.5 collective-permute-start.9
  59.1 3.8 %collective-permute-done.7.refs_0_ = bf16[64,1024]{1,0:T(8,128)(2,1)S(1)} collective-permute-done((bf16[64,1024]{1,0:T(8,128)(2,1)}, bf16[64,1024]{1,0:T(8,128)(2,1)S(1)}, u32[]{:S(2)}, u32[]{:S(2)}) %collective-permute-start.7) | collective-permute-done | bytes 131104 | tf_op jit(solution)/shard_map/ppermute | solution.py:450
  62.9 3.4 %collective-permute-done.8.refs_1_ = bf16[64,1024]{1,0:T(8,128)(2,1)S(1)} collective-permute-done((bf16[64,1024]{1,0:T(8,128)(2,1)}, bf16[64,1024]{1,0:T(8,128)(2,1)S(1)}, u32[]{:S(2)}, u32[]{:S(2)}) %collective-permute-start.8) | collective-permute-done | bytes 131104 | tf_op jit(solution)/shard_map/ppermute | solution.py:450
  67.0 0.7 copy-done.17
  67.7 2.5 %hidden_row.2 = (bf16[256,1024]{1,0:T(8,128)(2,1)}, bf16[256,1024]{1,0:T(8,128)(2,1)}) custom-call(s32[4]{0:T(128)} %pad_add_fusion.place.refs_0_, bf16[256,256]{1,0:T(8,128)(2,1)} %refs_10_.3, bf16[2,256,1024]{2,1,0:T(8,128)(2,1)} %bitcast.58, bf16[64,1024]{1,0:T(8,128)(2,1)} %get-tuple-element.107.own, bf16[64,1024]{1,0:T(8,128)(2,1)} %copy-done.15, ...), custom_call_target="tpu_custom_call" | custom-call | tf_op jit(solution)/shard_map/hidden_row/pallas_call | solution.py:140
  70.2 1.6 collective-permute-start.15
  71.8 9.0 %channel_row.2 = (bf16[256,1024]{1,0:T(8,128)(2,1)}, bf16[256,1024]{1,0:T(8,128)(2,1)}, bf16[256,1024]{1,0:T(8,128)(2,1)}, bf16[256,1024]{1,0:T(8,128)(2,1)}, f3...) custom-call(s32[4]{0:T(128)S(1)} %copy-done.2, bf16[2,512,512]{2,1,0:T(8,128)(2,1)S(1)} %copy-done, ...), custom_call_target="tpu_custom_call" | custom-call | tf_op jit(solution)/shard_map/channel_row/pallas_call | solution.py:268
  80.7 3.2 %collective-permute-done.15.refs_1_ = bf16[256,1024]{1,0:T(8,128)(2,1)} collective-permute-done((bf16[256,1024]{1,0:T(8,128)(2,1)}, bf16[256,1024]{1,0:T(8,128)(2,1)}, u32[]{:S(2)}, u32[]{:S(2)}) %collective-permute-start.15) | collective-permute-done | bytes 524320 | tf_op jit(solution)/shard_map/ppermute | solution.py:454
  83.9 4.4 %all-to-all-start = ((bf16[4,64,1024]{2,1,0:T(8,128)(2,1)}), bf16[4,64,1024]{2,1,0:T(8,128)(2,1)S(1)}, u32[]{:S(2)}, u32[]{:S(2)}) async-start(bf16[4,64,1024]{2,1,0:T(8,128)(2,1)} %bitcast.74), calls=%async_computation | async-start | bytes 1048576 | tf_op jit(solution)/shard_map/all_to_all | solution.py:458
  88.3 9.0 %channel_row.3 = (bf16[256,1024]{1,0:T(8,128)(2,1)}, bf16[256,1024]{1,0:T(8,128)(2,1)}, bf16[256,1024]{1,0:T(8,128)(2,1)}, bf16[256,1024]{1,0:T(8,128)(2,1)}, f3...) custom-call(s32[4]{0:T(128)S(1)} %copy-done.2, bf16[2,512,512]{2,1,0:T(8,128)(2,1)S(1)} %copy-done, ...), custom_call_target="tpu_custom_call" | custom-call | tf_op jit(solution)/shard_map/channel_row/pallas_call | solution.py:268
  97.3 5.1 %sums.1 = (bf16[8,144,512]{2,1,0:T(8,128)(2,1)}, bf16[8,144,512]{2,1,0:T(8,128)(2,1)}) custom-call(s32[4]{0:T(128)S(1)} %copy-done.2, f32[256,256]{1,0:T(8,128)} %get-tuple-element.139.row_sum, bf16[256,1024]{1,0:T(8,128)(2,1)} %get-tuple-element.121.refs_0_, bf16[256,1024]{1,0:T(8,128)(2,1)} %get-tuple-element.124.refs_0_.refs_1_, ...), custom_call_target="tpu_custom_call" | custom-call | tf_op jit(solution)/shard_map/sums/pallas_call | solution.py:340
  102.6 5.1 %all-to-all-start.1 = ((bf16[4,64,1024]{2,1,0:T(8,128)(2,1)}), bf16[4,64,1024]{2,1,0:T(8,128)(2,1)S(1)}, u32[]{:S(2)}, u32[]{:S(2)}) async-start(bf16[4,64,1024]{2,1,0:T(8,128)(2,1)} %bitcast.18), calls=%async_computation.1 | async-start | bytes 1048576 | tf_op jit(solution)/shard_map/all_to_all | solution.py:458
  107.7 2.6 %core_add.1 = (bf16[144,512]{1,0:T(8,128)(2,1)}, bf16[144,512]{1,0:T(8,128)(2,1)}, bf16[144,512]{1,0:T(8,128)(2,1)}, bf16[144,512]{1,0:T(8,128)(2,1)}, bf16[4,144,512]{2,1,0:T(8,128)(2,1)}) custom-call(s32[4]{0:T(128)S(1)} %copy-done.2, bf16[8,144,512]{2,1,0:T(8,128)(2,1)} %get-tuple-element.146.refs_1_, bf16[8,144,512]{2,1,0:T(8,128)(2,1)S(1)} %collective-permute-done.16.refs_2_), custom_call_target="tpu_custom_call" | custom-call | tf_op jit(solution)/shard_map/core_add/pallas_call | solution.py:368
  110.3 1.5 collective-permute-start.17
  112.4 1.5 collective-permute-start.21
  114.4 8.4 %all-to-all-done.1 = bf16[4,64,1024]{2,1,0:T(8,128)(2,1)S(1)} async-done(((bf16[4,64,1024]{2,1,0:T(8,128)(2,1)}), bf16[4,64,1024]{2,1,0:T(8,128)(2,1)S(1)}, u32[]{:S(2)}, u32[]{:S(2)}) %all-to-all-start.1) | async-done | bytes 524320 | tf_op jit(solution)/shard_map/all_to_all | solution.py:458
  122.8 0.7 collective-permute-done.21
  123.5 1.2 fusion.4
  124.7 2.1 %collective-permute-start.18 = (bf16[144,512]{1,0:T(8,128)(2,1)S(1)}, bf16[144,512]{1,0:T(8,128)(2,1)S(1)}, u32[]{:S(2)}, u32[]{:S(2)}) collective-permute-start(bf16[144,512]{1,0:T(8,128)(2,1)S(1)} %get-tuple-element.171), channel_id=1, source_target_pairs={{0,2},{2,4},{4,6},{6,0},{1,3},{3,5},{5,7},{7,1},{8,10},{10,12},{12... | collective-permute-start | bytes 442376 | tf_op jit(solution)/shard_map/ppermute | solution.py:450
  126.8 2.0 %collective-permute-start.22 = (bf16[144,512]{1,0:T(8,128)(2,1)S(1)}, bf16[144,512]{1,0:T(8,128)(2,1)S(1)}, u32[]{:S(2)}, u32[]{:S(2)}) collective-permute-start(bf16[144,512]{1,0:T(8,128)(2,1)S(1)} %get-tuple-element.172), channel_id=1, source_target_pairs={{0,6},{2,0},{4,2},{6,4},{1,7},{3,1},{5,3},{7,5},{8,14},{10,8},{12,... | collective-permute-start | bytes 442376 | tf_op jit(solution)/shard_map/ppermute | solution.py:450
  128.9 0.9 collective-permute-start.20
  129.7 3.0 %column_back.1 = (bf16[256,1024]{1,0:T(8,128)(2,1)}, bf16[256,1024]{1,0:T(8,128)(2,1)}) custom-call(bf16[512,512]{1,0:T(8,128)(2,1)} %select_n.97.table, bf16[256,1024]{1,0:T(8,128)(2,1)} %bitcast.59, bf16[256,1024]{1,0:T(8,128)(2,1)} %bitcast.61), custom_call_target="tpu_custom_call" | custom-call | tf_op jit(solution)/shard_map/column_back/pallas_call | solution.py:82
  132.7 2.9 %column_sum.1 = f32[8,512]{1,0:T(8,128)} custom-call(bf16[256,1024]{1,0:T(8,128)(2,1)} %bitcast.60, bf16[256,1024]{1,0:T(8,128)(2,1)} %bitcast.62, bf16[128,1024]{1,0:T(8,128)(2,1)} %bitcast.68, bf16[128,1024]{1,0:T(8,128)(2,1)} %bitcast.7.refs_1_.refs_3_, bf16[128,1024]{1,0:T(8,128)(2,1)} %bitcast.9.refs_2_.refs_4_, bf16[128,1024]{1,0:T(8,128)(2,1)} %bitcast.72), custom_call_target="tpu_custom_call" | custom-call | tf_op jit(solution)/shard_map/column_sum/pallas_call | solution.py:112
  135.6 3.5 %all-to-all-start.3 = ((bf16[4,64,1024]{2,1,0:T(8,128)(2,1)}), bf16[4,64,1024]{2,1,0:T(8,128)(2,1)S(1)}, u32[]{:S(2)}, u32[]{:S(2)}) async-start(bf16[4,64,1024]{2,1,0:T(8,128)(2,1)} %bitcast.28), calls=%async_computation.3 | async-start | bytes 1048576 | tf_op jit(solution)/shard_map/all_to_all | solution.py:458
  139.1 0.8 reshape.112
  140.3 2.3 %collective-permute-done.20 = bf16[144,512]{1,0:T(8,128)(2,1)S(1)} collective-permute-done((bf16[144,512]{1,0:T(8,128)(2,1)S(1)}, bf16[144,512]{1,0:T(8,128)(2,1)S(1)}, u32[]{:S(2)}, u32[]{:S(2)}) %collective-permute-start.20) | collective-permute-done | bytes 147488 | tf_op jit(solution)/shard_map/ppermute | solution.py:450
  142.6 1.0 add_convert_fusion
  143.6 1.6 collective-permute-start.24
  145.2 2.2 %collective-permute-done.24 = bf16[16,512]{1,0:T(8,128)(2,1)S(1)} collective-permute-done((bf16[16,512]{1,0:T(8,128)(2,1)S(1)}, bf16[16,512]{1,0:T(8,128)(2,1)S(1)}, u32[]{:S(2)}, u32[]{:S(2)}) %collective-permute-start.24) | collective-permute-done | bytes 16416 | tf_op jit(solution)/shard_map/ppermute | solution.py:454
  147.5 3.9 %collective-permute-start.27 = (bf16[144,512]{1,0:T(8,128)(2,1)S(1)}, bf16[144,512]{1,0:T(8,128)(2,1)S(1)}, u32[]{:S(2)}, u32[]{:S(2)}) collective-permute-start(bf16[144,512]{1,0:T(8,128)(2,1)S(1)} %concatenate.37), channel_id=1, source_target_pairs={{0,6},{2,0},{4,2},{6,4},{1,7},{3,1},{5,3},{7,5},{8,14},{10,8},{12,... | collective-permute-start | bytes 442376 | tf_op jit(solution)/shard_map/ppermute | solution.py:450
  151.4 0.6 collective-permute-start.25
  152.1 1.5 collective-permute-start.28
  154.1 1.5 collective-permute-start.31
  155.6 8.9 %collective-permute-done.26 = bf16[144,512]{1,0:T(8,128)(2,1)S(1)} collective-permute-done((bf16[144,512]{1,0:T(8,128)(2,1)S(1)}, bf16[144,512]{1,0:T(8,128)(2,1)S(1)}, u32[]{:S(2)}, u32[]{:S(2)}) %collective-permute-start.26) | collective-permute-done | bytes 147488 | tf_op jit(solution)/shard_map/ppermute | solution.py:450
  164.5 1.5 collective-permute-start.30
  166.6 3.5 %all-to-all-start.2 = ((bf16[4,64,1024]{2,1,0:T(8,128)(2,1)}), bf16[4,64,1024]{2,1,0:T(8,128)(2,1)S(1)}, u32[]{:S(2)}, u32[]{:S(2)}) async-start(bf16[4,64,1024]{2,1,0:T(8,128)(2,1)} %bitcast.26), calls=%async_computation.2 | async-start | bytes 1048576 | tf_op jit(solution)/shard_map/all_to_all | solution.py:458
  170.2 1.3 collective-permute-done.29
  171.7 2.0 %finish.2.refs_0_ = bf16[2,256,1024]{2,1,0:T(8,128)(2,1)} custom-call(bf16[256,1024]{1,0:T(8,128)(2,1)} %get-tuple-element.160.grad, bf16[256,1024]{1,0:T(8,128)(2,1)} %bitcast.69), custom_call_target="tpu_custom_call" | custom-call | tf_op jit(solution)/shard_map/finish/pallas_call | solution.py:437
  173.7 2.9 %unpack.1 = (f32[1024,512]{1,0:T(8,128)}, f32[1024,512]{1,0:T(8,128)}, f32[256,256]{1,0:T(8,128)}, f32[4,2,512]{2,1,0:T(2,128)}, f32[4,2,512]{2,1,0:T(2,128)}, /*index=5*/f32[8,8]{1,0:T(8,128)}) custom-call(s32[4]{0:T(128)S(1)} %copy-done.2, bf16[4,144,512]{2,1,0:T(8,128)(2,1)S(1)} %pad_maximum_fusion.refs_0_, ...), custom_call_target="tpu_custom_call" | custom-call | tf_op jit(solution)/shard_map/unpack/pallas_call | solution.py:410
  176.6 5.9 %all-to-all-done.2 = bf16[4,64,1024]{2,1,0:T(8,128)(2,1)S(1)} async-done(((bf16[4,64,1024]{2,1,0:T(8,128)(2,1)}), bf16[4,64,1024]{2,1,0:T(8,128)(2,1)S(1)}, u32[]{:S(2)}, u32[]{:S(2)}) %all-to-all-start.2) | async-done | bytes 524320 | tf_op jit(solution)/shard_map/all_to_all | solution.py:458
  182.5 0.8 copy-done.9
  183.3 2.0 %finish.3 = bf16[2,256,1024]{2,1,0:T(8,128)(2,1)} custom-call(bf16[256,1024]{1,0:T(8,128)(2,1)} %get-tuple-element.134.grad, bf16[256,1024]{1,0:T(8,128)(2,1)} %bitcast.70, bf16[2,256,1024]{2,1,0:T(8,128)(2,1)} %finish.2.refs_0_), custom_call_target="tpu_custom_call", output_to_operand_aliasing={{}: (2, {})} | custom-call | tf_op jit(solution)/shard_map/finish/pallas_call | solution.py:437
  (108 shorter events, 7.2 us)
Async XLA Ops:
  0.6 4.4 %copy-start.3 = (bf16[1,2,256,1024]{3,2,1,0:T(8,128)(2,1)S(1)}, bf16[1,2,256,1024]{3,2,1,0:T(8,128)(2,1)}, u32[]{:S(2)}) copy-start(bf16[1,2,256,1024]{3,2,1,0:T(8,128)(2,1)} %param.8) | copy-start | bytes 3145732
  2.0 8.7 %copy-start.20 = (bf16[8,8]{1,0:T(8,128)(2,1)S(1)}, bf16[8,8]{1,0:T(8,128)(2,1)}, u32[]{:S(2)}) copy-start(bf16[8,8]{1,0:T(8,128)(2,1)} %param.11) | copy-start | bytes 388
  2.0 15.1 %collective-permute-start.3 = (bf16[512,512]{1,0:T(8,128)(2,1)S(1)}, bf16[512,512]{1,0:T(8,128)(2,1)}, u32[]{:S(2)}, u32[]{:S(2)}) collective-permute-start(bf16[512,512]{1,0:T(8,128)(2,1)S(1)} %fusion), channel_id=1, source_target_pairs={{0,1},{1,0},{2,3},{3,2},{4,5},{5,4},{6,7},{7,6},{8,9},{9,8},{10,11... | collective-permute-start | bytes 1572872 | tf_op jit(solution)/shard_map/ppermute | solution.py:454
  5.1 6.3 %copy-start.19 = (bf16[4,4,512]{2,1,0:T(4,128)(2,1)S(1)}, bf16[4,4,512]{2,1,0:T(4,128)(2,1)}, u32[]{:S(2)}) copy-start(bf16[4,4,512]{2,1,0:T(4,128)(2,1)} %param.14) | copy-start | bytes 49156
  6.0 12.8 %copy-start.18 = (bf16[4,4,512]{2,1,0:T(4,128)(2,1)S(1)}, bf16[4,4,512]{2,1,0:T(4,128)(2,1)}, u32[]{:S(2)}) copy-start(bf16[4,4,512]{2,1,0:T(4,128)(2,1)} %param.15) | copy-start | bytes 49156
  6.0 18.4 %collective-permute-start.2 = (bf16[2,64,1024]{2,1,0:T(8,128)(2,1)}, bf16[2,64,1024]{2,1,0:T(8,128)(2,1)S(1)}, u32[]{:S(2)}, u32[]{:S(2)}) collective-permute-start(bf16[2,64,1024]{2,1,0:T(8,128)(2,1)} %get-tuple-element.167), channel_id=1, source_target_pairs={{0,6},{2,0},{4,2},{6,4},{1,7},{3,1},{5,3},{7,5},{8,14},{10,8},{12,... | collective-permute-start | bytes 786440 | tf_op jit(solution)/shard_map/ppermute | solution.py:450
  9.6 14.9 %collective-permute-start = (bf16[2,64,1024]{2,1,0:T(8,128)(2,1)}, bf16[2,64,1024]{2,1,0:T(8,128)(2,1)}, u32[]{:S(2)}, u32[]{:S(2)}) collective-permute-start(bf16[2,64,1024]{2,1,0:T(8,128)(2,1)} %get-tuple-element.168), channel_id=1, source_target_pairs={{0,2},{2,4},{4,6},{6,0},{1,3},{3,5},{5,7},{7,1},{8,10},{10,12},{12... | collective-permute-start | bytes 786440 | tf_op jit(solution)/shard_map/ppermute | solution.py:450
  9.6 22.3 %collective-permute-start.1 = (bf16[2,64,1024]{2,1,0:T(8,128)(2,1)}, bf16[2,64,1024]{2,1,0:T(8,128)(2,1)}, u32[]{:S(2)}, u32[]{:S(2)}) collective-permute-start(bf16[2,64,1024]{2,1,0:T(8,128)(2,1)} %get-tuple-element.170), channel_id=1, source_target_pairs={{0,4},{2,6},{4,0},{6,2},{1,5},{3,7},{5,1},{7,3},{8,12},{10,14},{12... | collective-permute-start | bytes 786440 | tf_op jit(solution)/shard_map/ppermute | solution.py:450
  10.7 8.2 %copy-start.6 = (bf16[1,2,256,1024]{3,2,1,0:T(8,128)(2,1)S(1)}, bf16[1,2,256,1024]{3,2,1,0:T(8,128)(2,1)}, u32[]{:S(2)}) copy-start(bf16[1,2,256,1024]{3,2,1,0:T(8,128)(2,1)} %param.9) | copy-start | bytes 3145732
  17.1 19.4 %collective-permute-start.4 = (bf16[512,512]{1,0:T(8,128)(2,1)}, bf16[512,512]{1,0:T(8,128)(2,1)}, u32[]{:S(2)}, u32[]{:S(2)}) collective-permute-start(bf16[512,512]{1,0:T(8,128)(2,1)} %collective-permute-done.3.refs_2_), channel_id=1, source_target_pairs={{0,16},{8,24},{16,0},{24,8},{1,17},{9,25},{17,1},{25,9},{2,18},{10... | collective-permute-start | bytes 1572872 | tf_op jit(solution)/shard_map/ppermute | solution.py:454
  18.8 31.4 %collective-permute-start.13 = (bf16[2,256,1024]{2,1,0:T(8,128)(2,1)S(1)}, bf16[2,256,1024]{2,1,0:T(8,128)(2,1)S(1)}, u32[]{:S(2)}, u32[]{:S(2)}) collective-permute-start(bf16[2,256,1024]{2,1,0:T(8,128)(2,1)S(1)} %bitcast.65), channel_id=1, source_target_pairs={{0,1},{1,0},{2,3},{3,2},{4,5},{5,4},{6,7},{7,6},{8,9},{9,8},{10,11... | collective-permute-start | bytes 3145736 | tf_op jit(solution)/shard_map/ppermute | solution.py:454
  24.5 9.0 %copy-start.10 = (bf16[2,64,1024]{2,1,0:T(8,128)(2,1)}, bf16[2,64,1024]{2,1,0:T(8,128)(2,1)S(1)}, u32[]{:S(2)}) copy-start(bf16[2,64,1024]{2,1,0:T(8,128)(2,1)S(1)} %collective-permute-done.2) | copy-start | bytes 786436
  36.5 3.8 %collective-permute-start.5 = (bf16[512,512]{1,0:T(8,128)(2,1)}, bf16[512,512]{1,0:T(8,128)(2,1)}, u32[]{:S(2)}, u32[]{:S(2)}) collective-permute-start(bf16[512,512]{1,0:T(8,128)(2,1)} %collective-permute-done.3.refs_2_), channel_id=1, source_target_pairs={{0,8},{8,0},{16,24},{24,16},{1,9},{9,1},{17,25},{25,17},{2,10},{10... | collective-permute-start | bytes 1572872 | tf_op jit(solution)/shard_map/ppermute | solution.py:454
  36.6 3.7 %collective-permute-start.6 = (bf16[512,512]{1,0:T(8,128)(2,1)}, bf16[512,512]{1,0:T(8,128)(2,1)}, u32[]{:S(2)}, u32[]{:S(2)}) collective-permute-start(bf16[512,512]{1,0:T(8,128)(2,1)} %collective-permute-done.4.refs_3_), channel_id=1, source_target_pairs={{0,8},{8,0},{16,24},{24,16},{1,9},{9,1},{17,25},{25,17},{2,10},{10... | collective-permute-start | bytes 1572872 | tf_op jit(solution)/shard_map/ppermute | solution.py:454
  37.1 8.5 %collective-permute-start.10 = (bf16[64,1024]{1,0:T(8,128)(2,1)}, bf16[64,1024]{1,0:T(8,128)(2,1)S(1)}, u32[]{:S(2)}, u32[]{:S(2)}) collective-permute-start(bf16[64,1024]{1,0:T(8,128)(2,1)} %get-tuple-element.113), channel_id=1, source_target_pairs={{0,2},{2,4},{4,6},{6,0},{1,3},{3,5},{5,7},{7,1},{8,10},{10,12},{12... | collective-permute-start | bytes 393224 | tf_op jit(solution)/shard_map/ppermute | solution.py:450
  37.1 13.2 %collective-permute-start.11 = (bf16[64,1024]{1,0:T(8,128)(2,1)}, bf16[64,1024]{1,0:T(8,128)(2,1)S(1)}, u32[]{:S(2)}, u32[]{:S(2)}) collective-permute-start(bf16[64,1024]{1,0:T(8,128)(2,1)} %get-tuple-element.114), channel_id=1, source_target_pairs={{0,4},{2,6},{4,0},{6,2},{1,5},{3,7},{5,1},{7,3},{8,12},{10,14},{12... | collective-permute-start | bytes 393224 | tf_op jit(solution)/shard_map/ppermute | solution.py:450
  40.3 10.0 %collective-permute-start.12 = (bf16[64,1024]{1,0:T(8,128)(2,1)}, bf16[64,1024]{1,0:T(8,128)(2,1)S(1)}, u32[]{:S(2)}, u32[]{:S(2)}) collective-permute-start(bf16[64,1024]{1,0:T(8,128)(2,1)} %get-tuple-element.115), channel_id=1, source_target_pairs={{0,6},{2,0},{4,2},{6,4},{1,7},{3,1},{5,3},{7,5},{8,14},{10,8},{12,... | collective-permute-start | bytes 393224 | tf_op jit(solution)/shard_map/ppermute | solution.py:450
  45.5 4.7 %copy-start.12 = (bf16[64,1024]{1,0:T(8,128)(2,1)}, bf16[64,1024]{1,0:T(8,128)(2,1)S(1)}, u32[]{:S(2)}) copy-start(bf16[64,1024]{1,0:T(8,128)(2,1)S(1)} %collective-permute-done.10.refs_0_) | copy-start | bytes 393220
  50.3 0.7 copy-start.13
  50.3 1.0 copy-start.7
  50.3 1.0 copy-start.14
  51.3 20.5 %copy-start.1 = (bf16[2,512,512]{2,1,0:T(8,128)(2,1)S(1)}, bf16[2,512,512]{2,1,0:T(8,128)(2,1)}, u32[]{:S(2)}) copy-start(bf16[2,512,512]{2,1,0:T(8,128)(2,1)} %wu_own.3) | copy-start | bytes 3145732
  53.9 17.9 %copy-start = (bf16[2,512,512]{2,1,0:T(8,128)(2,1)S(1)}, bf16[2,512,512]{2,1,0:T(8,128)(2,1)}, u32[]{:S(2)}) copy-start(bf16[2,512,512]{2,1,0:T(8,128)(2,1)} %wg_own.3) | copy-start | bytes 3145732
  53.9 17.9 %copy-start.2 = (s32[4]{0:T(128)S(1)}, s32[4]{0:T(128)}, u32[]{:S(2)}) copy-start(s32[4]{0:T(128)} %pad_add_fusion.place.refs_0_) | copy-start | bytes 52
  53.9 16.3 %collective-permute-start.14 = (bf16[256,1024]{1,0:T(8,128)(2,1)}, bf16[256,1024]{1,0:T(8,128)(2,1)S(1)}, u32[]{:S(2)}, u32[]{:S(2)}) collective-permute-start(bf16[256,1024]{1,0:T(8,128)(2,1)} %get-tuple-element.121.refs_0_), channel_id=1, source_target_pairs={{0,1},{1,0},{2,3},{3,2},{4,5},{5,4},{6,7},{7,6},{8,9},{9,8},{10,11... | collective-permute-start | bytes 1572872 | tf_op jit(solution)/shard_map/ppermute | solution.py:454
  54.5 8.4 %collective-permute-start.7 = (bf16[64,1024]{1,0:T(8,128)(2,1)}, bf16[64,1024]{1,0:T(8,128)(2,1)S(1)}, u32[]{:S(2)}, u32[]{:S(2)}) collective-permute-start(bf16[64,1024]{1,0:T(8,128)(2,1)} %get-tuple-element.108), channel_id=1, source_target_pairs={{0,2},{2,4},{4,6},{6,0},{1,3},{3,5},{5,7},{7,1},{8,10},{10,12},{12... | collective-permute-start | bytes 393224 | tf_op jit(solution)/shard_map/ppermute | solution.py:450
  56.8 9.6 %collective-permute-start.8 = (bf16[64,1024]{1,0:T(8,128)(2,1)}, bf16[64,1024]{1,0:T(8,128)(2,1)S(1)}, u32[]{:S(2)}, u32[]{:S(2)}) collective-permute-start(bf16[64,1024]{1,0:T(8,128)(2,1)} %get-tuple-element.109), channel_id=1, source_target_pairs={{0,4},{2,6},{4,0},{6,2},{1,5},{3,7},{5,1},{7,3},{8,12},{10,14},{12... | collective-permute-start | bytes 393224 | tf_op jit(solution)/shard_map/ppermute | solution.py:450
  57.6 8.8 %collective-permute-start.9 = (bf16[64,1024]{1,0:T(8,128)(2,1)}, bf16[64,1024]{1,0:T(8,128)(2,1)S(1)}, u32[]{:S(2)}, u32[]{:S(2)}) collective-permute-start(bf16[64,1024]{1,0:T(8,128)(2,1)} %get-tuple-element.110), channel_id=1, source_target_pairs={{0,6},{2,0},{4,2},{6,4},{1,7},{3,1},{5,3},{7,5},{8,14},{10,8},{12,... | collective-permute-start | bytes 393224 | tf_op jit(solution)/shard_map/ppermute | solution.py:450
  62.9 3.5 %copy-start.15 = (bf16[64,1024]{1,0:T(8,128)(2,1)}, bf16[64,1024]{1,0:T(8,128)(2,1)S(1)}, u32[]{:S(2)}) copy-start(bf16[64,1024]{1,0:T(8,128)(2,1)S(1)} %collective-permute-done.7.refs_0_) | copy-start | bytes 393220
  66.4 0.6 copy-start.16
  67.0 0.7 copy-start.17
  70.2 1.6 copy-start.11
  70.2 13.7 %collective-permute-start.15 = (bf16[256,1024]{1,0:T(8,128)(2,1)}, bf16[256,1024]{1,0:T(8,128)(2,1)}, u32[]{:S(2)}, u32[]{:S(2)}) collective-permute-start(bf16[256,1024]{1,0:T(8,128)(2,1)} %get-tuple-element.124.refs_0_.refs_1_), channel_id=1, source_target_pairs={{0,1},{1,0},{2,3},{3,2},{4,5},{5,4},{6,7},{7,6},{8,9},{9,8},{10,11... | collective-permute-start | bytes 1572872 | tf_op jit(solution)/shard_map/ppermute | solution.py:454
  83.9 18.6 %all-to-all-start = ((bf16[4,64,1024]{2,1,0:T(8,128)(2,1)}), bf16[4,64,1024]{2,1,0:T(8,128)(2,1)S(1)}, u32[]{:S(2)}, u32[]{:S(2)}) async-start(bf16[4,64,1024]{2,1,0:T(8,128)(2,1)} %bitcast.74), calls=%async_computation | async-start | bytes 1048576 | tf_op jit(solution)/shard_map/all_to_all | solution.py:458
  102.5 7.8 %copy-start.4 = (bf16[4,64,1024]{2,1,0:T(8,128)(2,1)}, bf16[4,64,1024]{2,1,0:T(8,128)(2,1)S(1)}, u32[]{:S(2)}) copy-start(bf16[4,64,1024]{2,1,0:T(8,128)(2,1)S(1)} %all-to-all-done) | copy-start | bytes 1572868
  102.5 5.2 %collective-permute-start.16 = (bf16[8,144,512]{2,1,0:T(8,128)(2,1)}, bf16[8,144,512]{2,1,0:T(8,128)(2,1)S(1)}, u32[]{:S(2)}, u32[]{:S(2)}) collective-permute-start(bf16[8,144,512]{2,1,0:T(8,128)(2,1)} %get-tuple-element.149), channel_id=1, source_target_pairs={{0,8},{8,0},{16,24},{24,16},{1,9},{9,1},{17,25},{25,17},{2,10},{10... | collective-permute-start | bytes 3538952 | tf_op jit(solution)/shard_map/ppermute | solution.py:454
  102.6 20.2 %all-to-all-start.1 = ((bf16[4,64,1024]{2,1,0:T(8,128)(2,1)}), bf16[4,64,1024]{2,1,0:T(8,128)(2,1)S(1)}, u32[]{:S(2)}, u32[]{:S(2)}) async-start(bf16[4,64,1024]{2,1,0:T(8,128)(2,1)} %bitcast.18), calls=%async_computation.1 | async-start | bytes 1048576 | tf_op jit(solution)/shard_map/all_to_all | solution.py:458
  110.3 12.5 %collective-permute-start.17 = (bf16[144,512]{1,0:T(8,128)(2,1)}, bf16[144,512]{1,0:T(8,128)(2,1)S(1)}, u32[]{:S(2)}, u32[]{:S(2)}) collective-permute-start(bf16[144,512]{1,0:T(8,128)(2,1)} %get-tuple-element.150), channel_id=1, source_target_pairs={{0,16},{8,24},{16,0},{24,8},{1,17},{9,25},{17,1},{25,9},{2,18},{10... | collective-permute-start | bytes 442376 | tf_op jit(solution)/shard_map/ppermute | solution.py:454
  111.8 11.0 %collective-permute-start.19 = (bf16[144,512]{1,0:T(8,128)(2,1)}, bf16[144,512]{1,0:T(8,128)(2,1)S(1)}, u32[]{:S(2)}, u32[]{:S(2)}) collective-permute-start(bf16[144,512]{1,0:T(8,128)(2,1)} %get-tuple-element.154), channel_id=1, source_target_pairs={{0,16},{8,24},{16,0},{24,8},{1,17},{9,25},{17,1},{25,9},{2,18},{10... | collective-permute-start | bytes 442376 | tf_op jit(solution)/shard_map/ppermute | solution.py:454
  112.4 11.2 %collective-permute-start.21 = (bf16[144,512]{1,0:T(8,128)(2,1)}, bf16[144,512]{1,0:T(8,128)(2,1)S(1)}, u32[]{:S(2)}, u32[]{:S(2)}) collective-permute-start(bf16[144,512]{1,0:T(8,128)(2,1)} %get-tuple-element.155), channel_id=1, source_target_pairs={{0,16},{8,24},{16,0},{24,8},{1,17},{9,25},{17,1},{25,9},{2,18},{10... | collective-permute-start | bytes 442376 | tf_op jit(solution)/shard_map/ppermute | solution.py:454
  113.9 26.4 %collective-permute-start.23 = (bf16[144,512]{1,0:T(8,128)(2,1)}, bf16[144,512]{1,0:T(8,128)(2,1)S(1)}, u32[]{:S(2)}, u32[]{:S(2)}) collective-permute-start(bf16[144,512]{1,0:T(8,128)(2,1)} %get-tuple-element.156), channel_id=1, source_target_pairs={{0,16},{8,24},{16,0},{24,8},{1,17},{9,25},{17,1},{25,9},{2,18},{10... | collective-permute-start | bytes 442376 | tf_op jit(solution)/shard_map/ppermute | solution.py:454
  122.8 6.9 %copy-start.5 = (bf16[4,64,1024]{2,1,0:T(8,128)(2,1)}, bf16[4,64,1024]{2,1,0:T(8,128)(2,1)S(1)}, u32[]{:S(2)}) copy-start(bf16[4,64,1024]{2,1,0:T(8,128)(2,1)S(1)} %all-to-all-done.1) | copy-start | bytes 1572868
  124.7 15.5 %collective-permute-start.18 = (bf16[144,512]{1,0:T(8,128)(2,1)S(1)}, bf16[144,512]{1,0:T(8,128)(2,1)S(1)}, u32[]{:S(2)}, u32[]{:S(2)}) collective-permute-start(bf16[144,512]{1,0:T(8,128)(2,1)S(1)} %get-tuple-element.171), channel_id=1, source_target_pairs={{0,2},{2,4},{4,6},{6,0},{1,3},{3,5},{5,7},{7,1},{8,10},{10,12},{12... | collective-permute-start | bytes 442376 | tf_op jit(solution)/shard_map/ppermute | solution.py:450
  126.8 13.4 %collective-permute-start.22 = (bf16[144,512]{1,0:T(8,128)(2,1)S(1)}, bf16[144,512]{1,0:T(8,128)(2,1)S(1)}, u32[]{:S(2)}, u32[]{:S(2)}) collective-permute-start(bf16[144,512]{1,0:T(8,128)(2,1)S(1)} %get-tuple-element.172), channel_id=1, source_target_pairs={{0,6},{2,0},{4,2},{6,4},{1,7},{3,1},{5,3},{7,5},{8,14},{10,8},{12,... | collective-permute-start | bytes 442376 | tf_op jit(solution)/shard_map/ppermute | solution.py:450
  128.9 13.7 %collective-permute-start.20 = (bf16[144,512]{1,0:T(8,128)(2,1)S(1)}, bf16[144,512]{1,0:T(8,128)(2,1)S(1)}, u32[]{:S(2)}, u32[]{:S(2)}) collective-permute-start(bf16[144,512]{1,0:T(8,128)(2,1)S(1)} %get-tuple-element.173), channel_id=1, source_target_pairs={{0,4},{2,6},{4,0},{6,2},{1,5},{3,7},{5,1},{7,3},{8,12},{10,14},{12... | collective-permute-start | bytes 442376 | tf_op jit(solution)/shard_map/ppermute | solution.py:450
  135.6 31.0 %all-to-all-start.3 = ((bf16[4,64,1024]{2,1,0:T(8,128)(2,1)}), bf16[4,64,1024]{2,1,0:T(8,128)(2,1)S(1)}, u32[]{:S(2)}, u32[]{:S(2)}) async-start(bf16[4,64,1024]{2,1,0:T(8,128)(2,1)} %bitcast.28), calls=%async_computation.3 | async-start | bytes 1048576 | tf_op jit(solution)/shard_map/all_to_all | solution.py:458
  143.6 3.8 %collective-permute-start.24 = (bf16[16,512]{1,0:T(8,128)(2,1)S(1)}, bf16[16,512]{1,0:T(8,128)(2,1)S(1)}, u32[]{:S(2)}, u32[]{:S(2)}) collective-permute-start(bf16[16,512]{1,0:T(8,128)(2,1)S(1)} %slice.88), channel_id=1, source_target_pairs={{0,1},{1,0},{2,3},{3,2},{4,5},{5,4},{6,7},{7,6},{8,9},{9,8},{10,11... | collective-permute-start | bytes 49160 | tf_op jit(solution)/shard_map/ppermute | solution.py:454
  147.5 6.6 %collective-permute-start.27 = (bf16[144,512]{1,0:T(8,128)(2,1)S(1)}, bf16[144,512]{1,0:T(8,128)(2,1)S(1)}, u32[]{:S(2)}, u32[]{:S(2)}) collective-permute-start(bf16[144,512]{1,0:T(8,128)(2,1)S(1)} %concatenate.37), channel_id=1, source_target_pairs={{0,6},{2,0},{4,2},{6,4},{1,7},{3,1},{5,3},{7,5},{8,14},{10,8},{12,... | collective-permute-start | bytes 442376 | tf_op jit(solution)/shard_map/ppermute | solution.py:450
  151.4 13.1 %collective-permute-start.26 = (bf16[144,512]{1,0:T(8,128)(2,1)S(1)}, bf16[144,512]{1,0:T(8,128)(2,1)S(1)}, u32[]{:S(2)}, u32[]{:S(2)}) collective-permute-start(bf16[144,512]{1,0:T(8,128)(2,1)S(1)} %concatenate.37), channel_id=1, source_target_pairs={{0,4},{2,6},{4,0},{6,2},{1,5},{3,7},{5,1},{7,3},{8,12},{10,14},{12... | collective-permute-start | bytes 442376 | tf_op jit(solution)/shard_map/ppermute | solution.py:450
  151.4 14.6 %collective-permute-start.25 = (bf16[144,512]{1,0:T(8,128)(2,1)S(1)}, bf16[144,512]{1,0:T(8,128)(2,1)S(1)}, u32[]{:S(2)}, u32[]{:S(2)}) collective-permute-start(bf16[144,512]{1,0:T(8,128)(2,1)S(1)} %concatenate.37), channel_id=1, source_target_pairs={{0,2},{2,4},{4,6},{6,0},{1,3},{3,5},{5,7},{7,1},{8,10},{10,12},{12... | collective-permute-start | bytes 442376 | tf_op jit(solution)/shard_map/ppermute | solution.py:450
  152.1 18.2 %collective-permute-start.28 = (bf16[144,512]{1,0:T(8,128)(2,1)S(1)}, bf16[144,512]{1,0:T(8,128)(2,1)S(1)}, u32[]{:S(2)}, u32[]{:S(2)}) collective-permute-start(bf16[144,512]{1,0:T(8,128)(2,1)S(1)} %concatenate.37), channel_id=1, source_target_pairs={{0,16},{8,24},{16,0},{24,8},{1,17},{9,25},{17,1},{25,9},{2,18},{10... | collective-permute-start | bytes 442376 | tf_op jit(solution)/shard_map/ppermute | solution.py:454
  154.1 16.1 %collective-permute-start.31 = (bf16[144,512]{1,0:T(8,128)(2,1)S(1)}, bf16[144,512]{1,0:T(8,128)(2,1)S(1)}, u32[]{:S(2)}, u32[]{:S(2)}) collective-permute-start(bf16[144,512]{1,0:T(8,128)(2,1)S(1)} %collective-permute-done.27), channel_id=1, source_target_pairs={{0,16},{8,24},{16,0},{24,8},{1,17},{9,25},{17,1},{25,9},{2,18},{10... | collective-permute-start | bytes 442376 | tf_op jit(solution)/shard_map/ppermute | solution.py:454
  164.5 5.7 %collective-permute-start.30 = (bf16[144,512]{1,0:T(8,128)(2,1)S(1)}, bf16[144,512]{1,0:T(8,128)(2,1)S(1)}, u32[]{:S(2)}, u32[]{:S(2)}) collective-permute-start(bf16[144,512]{1,0:T(8,128)(2,1)S(1)} %collective-permute-done.26), channel_id=1, source_target_pairs={{0,16},{8,24},{16,0},{24,8},{1,17},{9,25},{17,1},{25,9},{2,18},{10... | collective-permute-start | bytes 442376 | tf_op jit(solution)/shard_map/ppermute | solution.py:454
  166.0 5.5 %collective-permute-start.29 = (bf16[144,512]{1,0:T(8,128)(2,1)S(1)}, bf16[144,512]{1,0:T(8,128)(2,1)S(1)}, u32[]{:S(2)}, u32[]{:S(2)}) collective-permute-start(bf16[144,512]{1,0:T(8,128)(2,1)S(1)} %collective-permute-done.25), channel_id=1, source_target_pairs={{0,16},{8,24},{16,0},{24,8},{1,17},{9,25},{17,1},{25,9},{2,18},{10... | collective-permute-start | bytes 442376 | tf_op jit(solution)/shard_map/ppermute | solution.py:454
  166.6 5.1 %copy-start.8 = (bf16[4,64,1024]{2,1,0:T(8,128)(2,1)}, bf16[4,64,1024]{2,1,0:T(8,128)(2,1)S(1)}, u32[]{:S(2)}) copy-start(bf16[4,64,1024]{2,1,0:T(8,128)(2,1)S(1)} %all-to-all-done.3) | copy-start | bytes 1572868
  166.6 15.9 %all-to-all-start.2 = ((bf16[4,64,1024]{2,1,0:T(8,128)(2,1)}), bf16[4,64,1024]{2,1,0:T(8,128)(2,1)S(1)}, u32[]{:S(2)}, u32[]{:S(2)}) async-start(bf16[4,64,1024]{2,1,0:T(8,128)(2,1)} %bitcast.26), calls=%async_computation.2 | async-start | bytes 1048576 | tf_op jit(solution)/shard_map/all_to_all | solution.py:458
  170.1 3.6 %collective-permute-start.32 = (bf16[4,144,512]{2,1,0:T(8,128)(2,1)S(1)}, bf16[4,144,512]{2,1,0:T(8,128)(2,1)S(1)}, u32[]{:S(2)}, u32[]{:S(2)}) collective-permute-start(bf16[4,144,512]{2,1,0:T(8,128)(2,1)S(1)} %pad_maximum_fusion.refs_0_), channel_id=1, source_target_pairs={{0,8},{8,0},{16,24},{24,16},{1,9},{9,1},{17,25},{25,17},{2,10},{10... | collective-permute-start | bytes 1769480 | tf_op jit(solution)/shard_map/ppermute | solution.py:454
  171.6 2.1 %collective-permute-start.33 = (bf16[4,144,512]{2,1,0:T(8,128)(2,1)S(1)}, bf16[4,144,512]{2,1,0:T(8,128)(2,1)S(1)}, u32[]{:S(2)}, u32[]{:S(2)}) collective-permute-start(bf16[4,144,512]{2,1,0:T(8,128)(2,1)S(1)} %pad_maximum_fusion.1.refs_1_), channel_id=1, source_target_pairs={{0,8},{8,0},{16,24},{24,16},{1,9},{9,1},{17,25},{25,17},{2,10},{10... | collective-permute-start | bytes 1769480 | tf_op jit(solution)/shard_map/ppermute | solution.py:454
  182.5 0.8 copy-start.9
